TPU v7x, 512 devices: a whole 4x8x8 slice. The times are simulated.
512 devices in a mesh: view: 8 (over z_hi, x), col: 64 (over y, z_lo, core).
Axes of the slice: x: 4, y: 8, z: 8 (z_hi: 2, z_lo: 4; z = z_hi * 4 + z_lo), core: 2. Of those that a mesh axis runs over, the one named last changes fastest.
Arguments:
- estimate: float32 [2048, 64, 128], P('col', 'view'), may hold values from 0.5 to 2
- observed: float32 [8, 2048, 64, 128], P('view', 'col'), may hold values from 0.5 to 2
- psf_taps: float32 [8, 3, 31], replicated, as said below
- intersection: int32 [8, 16], replicated, may hold values 0 or 1
Outputs:
- deconvolved: float32 [2048, 64, 128], P('col', 'view')
Inputs may be any that keep to these rules, and one draw needn't show every extreme that they name: `psf_taps`: every tap is positive.
All inputs are finite; a program needn't handle non-finite values.
Results may differ from a plain program's by a relative error of at most 0.0003.
Values sent between devices are 32-bit elements; how exact they have to be, the bound alone decides.
No kernel may reach another device: no remote copies, remote signals or barrier semaphores. Data moves between devices by JAX's collectives and lax.ppermute only.
A program may use at most 64 MiB of HBM per device.

v0:
```python
from functools import partial

import jax
import jax.numpy as jnp
from jax import lax
from jax.sharding import PartitionSpec as P

TX = 128
ITERS = 2


HIGH = lax.Precision.HIGHEST


def extended_2(block, sides, width):
    for axis, dim in sides:
        count = lax.axis_size(axis)
        forward = [(i, i + 1) for i in range(count - 1)]
        backward = [(target, source) for source, target in forward]
        low = lax.ppermute(
            lax.slice_in_dim(block, block.shape[dim] - width, None, axis=dim), axis, forward
        )
        high = lax.ppermute(lax.slice_in_dim(block, 0, width, axis=dim), axis, backward)
        block = jnp.concatenate([low, block, high], axis=dim)
    return block


def banded(kernel, length):
    tap_count = kernel.shape[0]
    half_width = (tap_count - 1) // 2
    offsets = jnp.arange(length)[:, None] - jnp.arange(length)[None, :] + half_width
    onehot = (offsets[:, :, None] == jnp.arange(tap_count)[None, None, :]).astype(jnp.float32)
    return jnp.einsum("iok,k->io", onehot, kernel, precision=HIGH)


def column_weights(kernel, length):
    return jnp.sum(banded(kernel, length), axis=0)


def row_matrix(kernel, row_count, row_span):
    tap_count = kernel.shape[-1]
    offsets = jnp.arange(row_span)[None, :] - jnp.arange(row_count)[:, None]
    onehot = (offsets[:, :, None] == jnp.arange(tap_count)[None, None, :]).astype(jnp.float32)
    return jnp.einsum("xjk,k->xj", onehot, kernel, precision=HIGH)


def along_rows(extended, kernel):
    row_span = extended.shape[0]
    row_count = row_span - (kernel.shape[0] - 1)
    matrix = row_matrix(kernel, row_count, row_span)
    flattened = extended.reshape(row_span, -1)
    result = jnp.dot(matrix, flattened, precision=HIGH)
    return result.reshape((row_count,) + extended.shape[1:])


def across(field, kernels):
    result = jnp.einsum("xyz,yw->xwz", field, banded(kernels[1], field.shape[1]), precision=HIGH)
    return jnp.dot(result, banded(kernels[2], field.shape[2]), precision=HIGH)


def view_masks(intersection, first_row, row_count, tile_rows):
    global_rows = first_row + jnp.arange(row_count, dtype=jnp.int32)
    tile_index = jnp.floor_divide(global_rows, tile_rows)
    onehot = (
        tile_index[:, None] == jnp.arange(intersection.shape[1], dtype=jnp.int32)[None, :]
    ).astype(jnp.float32)
    return jnp.dot(intersection.astype(jnp.float32), onehot.T, precision=HIGH)


def body(estimate, observed, psf_taps, intersection):
    slab_rows = observed.shape[1]
    full_width = observed.shape[2]
    depth = observed.shape[3]
    own_width = estimate.shape[1]
    view_index = lax.axis_index("view")
    col_index = lax.axis_index("col")
    first_row = col_index * slab_rows
    kernels = psf_taps / jnp.sum(psf_taps, axis=2, keepdims=True)
    mirrored = kernels[:, :, ::-1]
    halo_rows = (kernels.shape[2] - 1) // 2
    picker = (jnp.arange(kernels.shape[0], dtype=jnp.int32) == view_index).astype(jnp.float32)
    own_kernels = jnp.einsum("v,vdk->dk", picker, kernels, precision=HIGH)
    own_mirror = own_kernels[:, ::-1]
    masks_all = view_masks(intersection, first_row - halo_rows, slab_rows + 2 * halo_rows, TX)
    row_mats = jax.vmap(
        partial(row_matrix, row_count=slab_rows, row_span=slab_rows + 2 * halo_rows)
    )(mirrored[:, 0])
    weight_rows = jnp.einsum("vxj,vj->vx", row_mats, masks_all, precision=HIGH)
    weight_cols = jax.vmap(partial(column_weights, length=full_width))(mirrored[:, 1])
    weight_depth = jax.vmap(partial(column_weights, length=depth))(mirrored[:, 2])
    weight_full = jnp.einsum(
        "vx,vy,vz->xyz", weight_rows, weight_cols, weight_depth, precision=HIGH
    )
    weight_own = lax.dynamic_slice_in_dim(weight_full, view_index * own_width, own_width, 1)
    mask_outer = jnp.dot(picker, masks_all, precision=HIGH)
    mask_inner = mask_outer[halo_rows : halo_rows + slab_rows]
    image_used = observed[0]
    current = estimate
    for iteration in range(ITERS):
        full_estimate = lax.all_gather(current, "view", axis=1, tiled=True)
        extended = extended_2(full_estimate, (("col", 0),), halo_rows)
        blurred = across(along_rows(extended, own_kernels[0]), own_kernels)
        inside = mask_inner[:, None, None] > 0
        ratio = jnp.where(inside, image_used / jnp.where(inside, blurred, 1.0), 0.0)
        padded_ratio = extended_2(ratio, (("col", 0),), halo_rows)
        summed = lax.psum_scatter(
            across(along_rows(padded_ratio, own_mirror[0]), own_mirror),
            "view",
            scatter_dimension=1,
            tiled=True,
        )
        current = current * (summed + 1.0) / (weight_own + 1.0)
    return current


def solution(mesh):
    return jax.shard_map(
        body,
        mesh=mesh,
        in_specs=(P("col", "view", None), P("view", "col", None, None), P(), P()),
        out_specs=P("col", "view", None),
        check_vma=False,
    )
```

profile of v0, /device:TPU:57, one launch (start us, length us, event | category | flops | bytes accessed | tf_op | source)
XLA Modules:
  0.0 431.0 jit_solution(17454508880146930062)
XLA Ops:
  6.5 0.7 all-gather.3.cloned.1.call-update
  7.3 0.8 reduce_sum.27
  8.1 0.8 broadcast_divide_fusion
  9.0 0.9 fusion.34
  9.9 0.1 convolution_bitcast_fusion.4
  10.2 0.3 fusion.27
  10.5 0.1 iota_compare_fusion.1
  10.6 0.5 fusion.21
  11.2 69.5 %all-gather.3.cloned.1.call-done = f32[32,64,128]{2,1,0:T(8,128)} async-done(((f32[32,8,128]{2,1,0:T(8,128)}), f32[32,64,128]{2,1,0:T(8,128)}) %all-gather.3.cloned.1.call-update) | async-done | bytes 1048592 | tf_op jit(solution)/shard_map/all_gather | solution.py:100
  80.7 1.3 fusion.64
  82.0 4.0 collective-permute-start
  86.0 1.9 collective-permute-start.1
  88.1 0.3 iota_compare_fusion
  88.4 1.2 fusion.14
  89.5 2.2 collective-permute-done
  91.8 9.8 %collective-permute-done.1 = f32[15,64,128]{2,1,0:T(8,128)} collective-permute-done((f32[15,64,128]{2,1,0:T(8,128)S(1)}, f32[15,64,128]{2,1,0:T(8,128)}, u32[]{:S(2)}, u32[]{:S(2)}) %collective-permute-start.1) | collective-permute-done | bytes 491552 | tf_op jit(solution)/shard_map/ppermute | solution.py:23
  101.5 1.2 pad_maximum_fusion
  102.7 0.2 slice_bitcast_fusion.3
  103.0 2.3 fusion.6
  105.3 1.6 convolution_bitcast_fusion.3
  106.9 1.0 fusion.9
  108.0 1.9 collective-permute-start.2
  109.9 2.6 collective-permute-start.3
  112.5 0.3 fusion.28
  113.0 0.5 fusion.23
  113.6 1.2 fusion.12
  114.7 0.9 collective-permute-done.2
  115.7 7.3 %collective-permute-done.3 = f32[15,64,128]{2,1,0:T(8,128)} collective-permute-done((f32[15,64,128]{2,1,0:T(8,128)S(1)}, f32[15,64,128]{2,1,0:T(8,128)}, u32[]{:S(2)}, u32[]{:S(2)}) %collective-permute-start.3) | collective-permute-done | bytes 491552 | tf_op jit(solution)/shard_map/ppermute | solution.py:23
  122.9 1.2 pad_maximum_fusion.1
  124.1 0.2 slice_bitcast_fusion.2
  124.3 2.3 fusion.4
  126.7 1.6 convolution_bitcast_fusion.2
  128.3 2.0 fusion.67
  130.6 0.6 convolution_reduce_fusion.1
  131.2 0.3 fusion.26
  131.5 0.3 fusion.32
  131.8 0.1 broadcast_multiply_fusion
  132.0 0.2 copy.38
  132.1 1.2 convolution_reduce_fusion
  133.3 1.8 fusion.36
  135.1 84.2 %reduce-scatter.3.cloned.1.call-done = f32[32,8,128]{2,1,0:T(8,128)} async-done(((f32[32,64,128]{2,1,0:T(8,128)}), f32[32,8,128]{2,1,0:T(8,128)}) %reduce-scatter.3.cloned.1.call-update) | async-done | bytes 131088 | tf_op jit(solution)/shard_map/reduce_scatter | solution.py:106
  219.4 1.6 bitcast_divide_fusion.1
  221.0 65.1 %all-gather.5.cloned.1.call-done = f32[32,64,128]{2,1,0:T(8,128)} async-done(((f32[32,8,128]{2,1,0:T(8,128)}), f32[32,64,128]{2,1,0:T(8,128)}) %all-gather.5.cloned.1.call-update) | async-done | bytes 1048592 | tf_op jit(solution)/shard_map/all_gather | solution.py:100
  286.1 1.4 fusion.62
  287.5 4.0 collective-permute-start.4
  291.5 2.1 collective-permute-start.5
  293.7 3.6 collective-permute-done.4
  297.3 9.7 %collective-permute-done.5 = f32[15,64,128]{2,1,0:T(8,128)S(1)} collective-permute-done((f32[15,64,128]{2,1,0:T(8,128)S(1)}, f32[15,64,128]{2,1,0:T(8,128)S(1)}, u32[]{:S(2)}, u32[]{:S(2)}) %collective-permute-start.5) | collective-permute-done | bytes 491552 | tf_op jit(solution)/shard_map/ppermute | solution.py:23
  306.9 0.2 pad_maximum_fusion.2
  307.2 0.2 slice_bitcast_fusion.1
  307.4 2.3 fusion.2
  309.7 1.6 convolution_bitcast_fusion.1
  311.4 1.0 fusion.11
  312.5 1.9 collective-permute-start.6
  314.4 2.4 collective-permute-start.7
  316.8 3.3 collective-permute-done.6
  320.1 7.2 %collective-permute-done.7 = f32[15,64,128]{2,1,0:T(8,128)S(1)} collective-permute-done((f32[15,64,128]{2,1,0:T(8,128)S(1)}, f32[15,64,128]{2,1,0:T(8,128)S(1)}, u32[]{:S(2)}, u32[]{:S(2)}) %collective-permute-start.7) | collective-permute-done | bytes 491552 | tf_op jit(solution)/shard_map/ppermute | solution.py:23
  327.3 0.2 pad_maximum_fusion.3
  327.5 0.2 slice_bitcast_fusion
  327.8 2.3 fusion
  330.1 1.6 convolution_bitcast_fusion
  331.7 2.0 fusion.68
  333.7 89.2 %reduce-scatter.5.cloned.1.call-done = f32[32,8,128]{2,1,0:T(8,128)} async-done(((f32[32,64,128]{2,1,0:T(8,128)}), f32[32,8,128]{2,1,0:T(8,128)}) %reduce-scatter.5.cloned.1.call-update) | async-done | bytes 131088 | tf_op jit(solution)/shard_map/reduce_scatter | solution.py:106
  422.9 1.6 bitcast_divide_fusion
  (49 shorter events, 1.2 us)
Async XLA Ops:
  6.5 74.2 %all-gather.3.cloned.1.call-start = ((), (), s32[]{:S(2)}) async-start(), calls=%async_computation.2 | async-start | bytes 1179648 | tf_op jit(solution)/shard_map/all_gather | solution.py:100
  7.3 212.1 %reduce-scatter.3.cloned.1.call-start = ((), (), s32[]{:S(2)}) async-start(), calls=%async_computation.3 | async-start | bytes 1179648 | tf_op jit(solution)/shard_map/reduce_scatter | solution.py:106
  10.6 102.4 %copy-start.4 = (pred[64,64,31]{1,0,2:T(32,128)(4,1)}, pred[64,64,31]{1,0,2:T(32,128)(4,1)S(1)}, u32[]{:S(2)}) copy-start(pred[64,64,31]{1,0,2:T(32,128)(4,1)S(1)} %iota_compare_fusion.1) | copy-start | bytes 380932
  11.2 94.1 %copy-start.6 = (f32[1,64,64]{2,0,1:T(1,128)}, f32[1,64,64]{2,0,1:T(1,128)S(1)}, u32[]{:S(2)}) copy-start(f32[1,64,64]{2,0,1:T(1,128)S(1)} %fusion.21) | copy-start | bytes 49156
  80.7 20.9 %copy-start = (f32[32,64,128]{2,1,0:T(8,128)S(1)}, f32[32,64,128]{2,1,0:T(8,128)}, u32[]{:S(2)}) copy-start(f32[32,64,128]{2,1,0:T(8,128)} %all-gather.3.cloned.1.call-done) | copy-start | bytes 3145732
  82.0 9.7 %collective-permute-start = (f32[15,64,128]{2,1,0:T(8,128)S(1)}, f32[15,64,128]{2,1,0:T(8,128)S(1)}, u32[]{:S(2)}, u32[]{:S(2)}) collective-permute-start(f32[15,64,128]{2,1,0:T(8,128)S(1)} %get-tuple-element.11), channel_id=1, source_target_pairs={{0,1},{1,2},{2,3},{3,4},{4,5},{5,6},{6,7},{7,8},{8,9},{9,10},{10,1... | collective-permute-start | bytes 1474568 | tf_op jit(solution)/shard_map/ppermute | solution.py:20
  86.0 15.5 %collective-permute-start.1 = (f32[15,64,128]{2,1,0:T(8,128)S(1)}, f32[15,64,128]{2,1,0:T(8,128)}, u32[]{:S(2)}, u32[]{:S(2)}) collective-permute-start(f32[15,64,128]{2,1,0:T(8,128)S(1)} %get-tuple-element.12), channel_id=1, source_target_pairs={{1,0},{2,1},{3,2},{4,3},{5,4},{6,5},{7,6},{8,7},{9,8},{10,9},{11,1... | collective-permute-start | bytes 1474568 | tf_op jit(solution)/shard_map/ppermute | solution.py:23
  103.0 3.9 copy-start.10
  108.0 7.7 %collective-permute-start.2 = (f32[15,64,128]{2,1,0:T(8,128)S(1)}, f32[15,64,128]{2,1,0:T(8,128)S(1)}, u32[]{:S(2)}, u32[]{:S(2)}) collective-permute-start(f32[15,64,128]{2,1,0:T(8,128)S(1)} %get-tuple-element.9), channel_id=1, source_target_pairs={{0,1},{1,2},{2,3},{3,4},{4,5},{5,6},{6,7},{7,8},{8,9},{9,10},{10,1... | collective-permute-start | bytes 1474568 | tf_op jit(solution)/shard_map/ppermute | solution.py:20
  109.9 13.0 %collective-permute-start.3 = (f32[15,64,128]{2,1,0:T(8,128)S(1)}, f32[15,64,128]{2,1,0:T(8,128)}, u32[]{:S(2)}, u32[]{:S(2)}) collective-permute-start(f32[15,64,128]{2,1,0:T(8,128)S(1)} %get-tuple-element.10), channel_id=1, source_target_pairs={{1,0},{2,1},{3,2},{4,3},{5,4},{6,5},{7,6},{8,7},{9,8},{10,9},{11,1... | collective-permute-start | bytes 1474568 | tf_op jit(solution)/shard_map/ppermute | solution.py:23
  113.6 13.1 %copy-start.8 = (f32[1,64,64]{2,0,1:T(1,128)}, f32[1,64,64]{2,0,1:T(1,128)S(1)}, u32[]{:S(2)}) copy-start(f32[1,64,64]{2,0,1:T(1,128)S(1)} %fusion.23) | copy-start | bytes 49156
  128.3 2.3 copy-start.5
  130.3 155.9 %all-gather.5.cloned.1.call-start = ((), (), s32[]{:S(2)}) async-start(), calls=%async_computation.4 | async-start | bytes 1179648 | tf_op jit(solution)/shard_map/all_gather | solution.py:100
  131.1 88.3 %copy-start.3 = (f32[32,8,128]{2,1,0:T(8,128)S(1)}, f32[32,8,128]{2,1,0:T(8,128)}, u32[]{:S(2)}) copy-start(f32[32,8,128]{2,1,0:T(8,128)} %param.4) | copy-start | bytes 393220
  221.0 201.9 %reduce-scatter.5.cloned.1.call-start = ((), (), s32[]{:S(2)}) async-start(), calls=%async_computation.5 | async-start | bytes 1179648 | tf_op jit(solution)/shard_map/reduce_scatter | solution.py:106
  286.1 20.8 %copy-start.1 = (f32[32,64,128]{2,1,0:T(8,128)S(1)}, f32[32,64,128]{2,1,0:T(8,128)}, u32[]{:S(2)}) copy-start(f32[32,64,128]{2,1,0:T(8,128)} %all-gather.5.cloned.1.call-done) | copy-start | bytes 3145732
  287.5 9.7 %collective-permute-start.4 = (f32[15,64,128]{2,1,0:T(8,128)S(1)}, f32[15,64,128]{2,1,0:T(8,128)S(1)}, u32[]{:S(2)}, u32[]{:S(2)}) collective-permute-start(f32[15,64,128]{2,1,0:T(8,128)S(1)} %get-tuple-element.7), channel_id=1, source_target_pairs={{0,1},{1,2},{2,3},{3,4},{4,5},{5,6},{6,7},{7,8},{8,9},{9,10},{10,1... | collective-permute-start | bytes 1474568 | tf_op jit(solution)/shard_map/ppermute | solution.py:20
  291.5 15.4 %collective-permute-start.5 = (f32[15,64,128]{2,1,0:T(8,128)S(1)}, f32[15,64,128]{2,1,0:T(8,128)S(1)}, u32[]{:S(2)}, u32[]{:S(2)}) collective-permute-start(f32[15,64,128]{2,1,0:T(8,128)S(1)} %get-tuple-element.8), channel_id=1, source_target_pairs={{1,0},{2,1},{3,2},{4,3},{5,4},{6,5},{7,6},{8,7},{9,8},{10,9},{11,1... | collective-permute-start | bytes 1474568 | tf_op jit(solution)/shard_map/ppermute | solution.py:23
  307.4 2.3 copy-start.7
  307.4 3.9 copy-start.11
  312.5 7.7 %collective-permute-start.6 = (f32[15,64,128]{2,1,0:T(8,128)S(1)}, f32[15,64,128]{2,1,0:T(8,128)S(1)}, u32[]{:S(2)}, u32[]{:S(2)}) collective-permute-start(f32[15,64,128]{2,1,0:T(8,128)S(1)} %get-tuple-element.5), channel_id=1, source_target_pairs={{0,1},{1,2},{2,3},{3,4},{4,5},{5,6},{6,7},{7,8},{8,9},{9,10},{10,1... | collective-permute-start | bytes 1474568 | tf_op jit(solution)/shard_map/ppermute | solution.py:20
  314.4 12.9 %collective-permute-start.7 = (f32[15,64,128]{2,1,0:T(8,128)S(1)}, f32[15,64,128]{2,1,0:T(8,128)S(1)}, u32[]{:S(2)}, u32[]{:S(2)}) collective-permute-start(f32[15,64,128]{2,1,0:T(8,128)S(1)} %get-tuple-element.6), channel_id=1, source_target_pairs={{1,0},{2,1},{3,2},{4,3},{5,4},{6,5},{7,6},{8,7},{9,8},{10,9},{11,1... | collective-permute-start | bytes 1474568 | tf_op jit(solution)/shard_map/ppermute | solution.py:23
  327.8 2.3 copy-start.9
  331.7 91.2 %copy-start.2 = (f32[32,8,128]{2,1,0:T(8,128)S(1)}, f32[32,8,128]{2,1,0:T(8,128)}, u32[]{:S(2)}) copy-start(f32[32,8,128]{2,1,0:T(8,128)} %bitcast_divide_fusion.1) | copy-start | bytes 393220
Sparse Core Ops, SparseCore 0:
  10.4 70.2 all-gather.2
  130.4 88.9 reduce-scatter.2
  222.9 63.2 all-gather.4
  333.8 89.0 reduce-scatter.4
where the time goes:
time: 434 us; the launch traced here: 431 us
  waiting for transfers between devices  353 us (81%)
  matrix products  30.9 us (7%)
  starting transfers between devices  21 us (5%)
  between operations  13.6 us (3%)
  other arithmetic  8.23 us (2%)
  local copies, waits for them, and re-layouts  4.58 us (1%)
    reduce_scatter x2, waiting for transfers between devices, body(): lax.psum_scatter(across(along_rows(padded_ratio, own_mirror[0]), own_mirr...  173 us
    all_gather x2, waiting for transfers between devices, body(): full_estimate = lax.all_gather(current, 'view', axis=1, tiled=True)  135 us
    ppermute x4, waiting for transfers between devices, extended_2(): lax.ppermute(lax.slice_in_dim(block, 0, width, axis=dim), axis, backward)  33.8 us
    ppermute x4, starting transfers between devices, extended_2(): lax.ppermute(lax.slice_in_dim(block, block.shape[dim] - width, None, axis...  11.8 us
    ppermute x4, waiting for transfers between devices, extended_2(): lax.ppermute(lax.slice_in_dim(block, block.shape[dim] - width, None, axis...  10.1 us
    dot_general x4, matrix products, along_rows(): result = jnp.dot(matrix, flattened, precision=HIGH)  9.19 us
    ppermute x4, starting transfers between devices, extended_2(): lax.ppermute(lax.slice_in_dim(block, 0, width, axis=dim), axis, backward)  9.06 us
  transfers between devices with their start and end apart: 12, of which 12 were waited for; matrix products, arithmetic and copies ran while one was open for 3% of the time, Pallas kernels for 0%

commit v1 on v0

v1 whole, which is shorter than its diff:
```python
import jax
import jax.numpy as jnp
from jax import lax
from jax.sharding import PartitionSpec as P

TX = 128
ITERS = 2
HIGH = lax.Precision.HIGH
HIGHEST = lax.Precision.HIGHEST
AXES = ("view", "col")
SLAB = 16
COLS = 64


def device(h, x, c):
    return (h * 4 + x) * COLS + c


def chip_x(column, p):
    return (p - column % 4) % 4


def spread_pairs(turn):
    pairs = []
    for h in range(2):
        for column in range(COLS // 2):
            for x in range(4):
                for k in range(2):
                    p = 2 * k + (x + turn) % 2
                    pairs.append(
                        (device(h, x, 2 * column + k), device(h, chip_x(column, p), 2 * column + x // 2))
                    )
    return pairs


def chip_pairs(step):
    pairs = []
    chips = COLS // 2 * 4
    for h in range(2):
        for chip in range(chips):
            if 0 <= chip + step < chips:
                for core in range(2):
                    ends = []
                    for q in (chip, chip + step):
                        column, p = divmod(q, 4)
                        ends.append(device(h, chip_x(column, p), 2 * column + core))
                    pairs.append(tuple(ends))
    return pairs


def swap_pairs(across):
    pairs = []
    for h in range(2):
        for x in range(4):
            for c in range(COLS):
                other = device(1 - h, x, c) if across == "h" else device(h, x, c ^ 1)
                pairs.append((device(h, x, c), other))
    return pairs


def reverse(pairs):
    return [(b, a) for a, b in pairs]


SPREAD = [spread_pairs(0), spread_pairs(1)]
UP = chip_pairs(1)
DOWN = chip_pairs(-1)
SWAP_H = swap_pairs("h")
SWAP_CORE = swap_pairs("core")


def send(value, pairs):
    return lax.ppermute(value, AXES, pairs)


def tap_matrix(kernel, taps):
    count = kernel.shape[1]
    onehot = (taps[:, :, None] == jnp.arange(count, dtype=jnp.int32)).astype(jnp.float32)
    return jnp.einsum("ijk,uk->uij", onehot, kernel, precision=HIGHEST)


def body(estimate, observed, psf_taps, intersection):
    rows = intersection.shape[1] * TX
    full_width = observed.shape[2]
    depth = observed.shape[3]
    view_index = lax.axis_index("view")
    col_index = lax.axis_index("col")
    h, x = view_index // 4, view_index % 4
    column, k = col_index // 2, col_index % 2
    p = (x + column % 4) % 4
    core = k
    first_row = column * (4 * SLAB) + p * SLAB
    taps = psf_taps.shape[2]
    half = (taps - 1) // 2

    def spread(block, turn):
        return send(lax.dynamic_slice_in_dim(block, SLAB * ((x + turn) % 2), SLAB, 0), SPREAD[turn])

    even = p % 2 == 0
    est = [spread(estimate, turn) for turn in (0, 1)]
    quarter = jnp.where(even, jnp.concatenate(est, 1), jnp.concatenate(est[::-1], 1))
    current = jnp.concatenate([quarter, send(quarter, SWAP_H)], 1)
    images = jnp.stack([spread(observed[0], turn) for turn in (0, 1)])

    kernels = psf_taps / jnp.sum(psf_taps, axis=2, keepdims=True)
    views = jnp.arange(kernels.shape[0], dtype=jnp.int32)
    own_views = 4 * h + 2 * core + jnp.stack([p % 2, (p + 1) % 2])
    picker = (own_views[:, None] == views[None, :]).astype(jnp.float32)
    own = jnp.einsum("uv,vdk->udk", picker, kernels, precision=HIGHEST)
    quarters = jnp.stack([2 * h + core, 2 * (1 - h) + core, 2 * h + 1 - core, 2 * (1 - h) + 1 - core])
    quarter_width = full_width // 4
    local_y = (quarters[:, None] * quarter_width + jnp.arange(quarter_width, dtype=jnp.int32)[None, :]).reshape(-1)
    all_y = jnp.arange(full_width, dtype=jnp.int32)
    all_z = jnp.arange(depth, dtype=jnp.int32)
    slab = jnp.arange(SLAB, dtype=jnp.int32)
    wide = jnp.arange(3 * SLAB, dtype=jnp.int32) - SLAB
    mat_x = tap_matrix(own[:, 0], wide[None, :] - slab[:, None] + half)
    mat_y = tap_matrix(own[:, 1], local_y[None, :] - all_y[:, None] + half)
    mat_z = tap_matrix(own[:, 2], all_z[:, None] - all_z[None, :] + half)

    wide_rows = first_row + wide
    tile = (wide_rows // TX)[:, None] == jnp.arange(intersection.shape[1], dtype=jnp.int32)[None, :]
    tile = jnp.logical_and(tile, jnp.logical_and(wide_rows >= 0, wide_rows < rows)[:, None]).astype(jnp.float32)
    masks = jnp.einsum("vt,jt->vj", intersection.astype(jnp.float32), tile, precision=HIGHEST)
    weight_rows = jnp.einsum(
        "vrj,vj->vr", tap_matrix(kernels[:, 0], slab[:, None] - wide[None, :] + half), masks, precision=HIGHEST
    )

    def coverage(kernel, places, length):
        source = places[:, None] - jnp.arange(taps, dtype=jnp.int32)[None, :] + half
        inside = jnp.logical_and(source >= 0, source < length).astype(jnp.float32)
        return jnp.einsum("yk,vk->vy", inside, kernel, precision=HIGHEST)

    weight_cols = coverage(kernels[:, 1], local_y[: 2 * quarter_width], full_width)
    weight_depth = coverage(kernels[:, 2], all_z, depth)
    weight_plane = weight_rows[:, :, None] * weight_cols[:, None, :]
    weights = jnp.einsum("vxy,vz->xyz", weight_plane, weight_depth, precision=HIGHEST)
    own_masks = jnp.einsum("uv,vj->uj", picker, masks[:, SLAB : 2 * SLAB], precision=HIGHEST)
    inside = own_masks[:, :, None, None] > 0

    width = 2 * quarter_width
    for iteration in range(ITERS):
        low = send(current, UP)
        high = send(current, DOWN)
        extended = jnp.concatenate([low, current, high], 0)
        extended = jnp.concatenate([extended, send(extended, SWAP_CORE)], 1)
        blurred = jnp.einsum("urj,jyz->uryz", mat_x, extended, precision=HIGH)
        blurred = jnp.einsum("urjz,uyj->uryz", blurred, mat_y, precision=HIGH)
        blurred = jnp.einsum("uryz,uzw->uryw", blurred, mat_z, precision=HIGH)
        ratio = jnp.where(inside, images / jnp.where(inside, blurred, 1.0), 0.0)
        back = jnp.einsum("uryw,uzw->uryz", ratio, mat_z, precision=HIGH)
        back = jnp.einsum("uryz,uyj->urjz", back, mat_y, precision=HIGH)
        back = jnp.einsum("urj,uryz->jyz", mat_x, back, precision=HIGH)
        part = back[:, :width] + send(back[:, width:], SWAP_CORE)
        part = (
            part[SLAB : 2 * SLAB]
            + send(part[:SLAB], DOWN)
            + send(part[2 * SLAB :], UP)
        )
        if iteration < ITERS - 1:
            other = send(part, SWAP_H)
            total = part + jnp.concatenate([other[:, quarter_width:], other[:, :quarter_width]], 1)
            current = current * (total + 1.0) / (weights + 1.0)
        else:
            total = part[:, :quarter_width] + send(part[:, quarter_width:], SWAP_H)
            quarter = current[:, :quarter_width] * (total + 1.0) / (weights[:, :quarter_width] + 1.0)

    block = quarter_width // 2
    first, second = quarter[:, :block], quarter[:, block:]
    pieces = []
    for turn in (0, 1):
        chosen = jnp.where((p + turn) % 2 == 0, first, second)
        pieces.append(send(chosen, reverse(SPREAD[turn])))
    return jnp.where(x % 2 == 0, jnp.concatenate(pieces, 0), jnp.concatenate(pieces[::-1], 0))


def solution(mesh):
    return jax.shard_map(
        body,
        mesh=mesh,
        in_specs=(P("col", "view", None), P("view", "col", None, None), P(), P()),
        out_specs=P("col", "view", None),
        check_vma=False,
    )
```

time: 434 us -> 168 us (0.39)
  the two profiles are of different devices: /device:TPU:57 before, /device:TPU:32 now
where the time goes in v1:
time: 168 us; the launch traced here: 167 us
  starting transfers between devices  85.2 us (51%)
  waiting for transfers between devices  60 us (36%)
  matrix products  16.5 us (10%)
  local copies, waits for them, and re-layouts  3.7 us (2%)
    ppermute x21, starting transfers between devices, send(): return lax.ppermute(value, AXES, pairs)  85.2 us
    ppermute x21, waiting for transfers between devices, send(): return lax.ppermute(value, AXES, pairs)  60 us
    dot_general x2, matrix products, body(): blurred = jnp.einsum('uryz,uzw->uryw', blurred, mat_z, precision=HIGH)  3.69 us
  transfers between devices with their start and end apart: 21, of which 16 were waited for; matrix products, arithmetic and copies ran while one was open for 5% of the time, Pallas kernels for 0%

profile of v1, /device:TPU:32, one launch (start us, length us, event | category | flops | bytes accessed | tf_op | source)
XLA Modules:
  0.0 167.1 jit_solution(2370009760021514075)
XLA Ops:
  0.0 0.9 constant_dynamic-slice_fusion.1
  0.9 0.7 collective-permute-start
  1.6 3.4 %collective-permute-start.1 = (f32[16,8,128]{2,0,1:T(8,128)S(1)}, f32[16,8,128]{2,0,1:T(8,128)S(1)}, u32[]{:S(2)}, u32[]{:S(2)}) collective-permute-start(f32[16,8,128]{2,0,1:T(8,128)S(1)} %copy.35), channel_id=1, source_target_pairs={{0,64},{1,192},{64,0},{65,128},{128,65},{129,193},{192,1},{193,129... | collective-permute-start | bytes 196616 | tf_op jit(solution)/shard_map/ppermute | solution.py:73
  5.0 1.3 dynamic-slice_bitcast_fusion.1
  6.3 1.5 collective-permute-start.3
  7.8 2.4 %collective-permute-start.4 = (f32[16,64,128]{2,1,0:T(8,128)S(1)}, f32[16,64,128]{2,1,0:T(8,128)}, u32[]{:S(2)}, u32[]{:S(2)}) collective-permute-start(f32[16,64,128]{2,1,0:T(8,128)S(1)} %get-tuple-element.6), channel_id=1, source_target_pairs={{0,64},{1,192},{64,0},{65,128},{128,65},{129,193},{192,1},{193,129... | collective-permute-start | bytes 1572872 | tf_op jit(solution)/shard_map/ppermute | solution.py:73
  10.6 0.2 fusion.77
  10.8 0.2 fusion.56
  11.2 10.9 %collective-permute-start.2 = (f32[16,16,128]{2,0,1:T(8,128)S(1)}, f32[16,16,128]{2,0,1:T(8,128)S(1)}, u32[]{:S(2)}, u32[]{:S(2)}) collective-permute-start(f32[16,16,128]{2,0,1:T(8,128)S(1)} %maximum_select_fusion), channel_id=1, source_target_pairs={{0,256},{1,257},{2,258},{3,259},{4,260},{5,261},{6,262},{7,263},{8... | collective-permute-start | bytes 393224 | tf_op jit(solution)/shard_map/ppermute | solution.py:73
  22.2 2.8 %collective-permute-done.2 = f32[16,16,128]{2,0,1:T(8,128)S(1)} collective-permute-done((f32[16,16,128]{2,0,1:T(8,128)S(1)}, f32[16,16,128]{2,0,1:T(8,128)S(1)}, u32[]{:S(2)}, u32[]{:S(2)}) %collective-permute-start.2) | collective-permute-done | bytes 131104 | tf_op jit(solution)/shard_map/ppermute | solution.py:73
  25.0 3.4 %collective-permute-start.5 = (f32[16,32,128]{2,0,1:T(8,128)S(1)}, f32[16,32,128]{2,0,1:T(8,128)S(1)}, u32[]{:S(2)}, u32[]{:S(2)}) collective-permute-start(f32[16,32,128]{2,0,1:T(8,128)S(1)} %pad_maximum_fusion.3), channel_id=1, source_target_pairs={{0,64},{1,65},{64,128},{65,129},{128,192},{129,193},{192,194},{193... | collective-permute-start | bytes 786440 | tf_op jit(solution)/shard_map/ppermute | solution.py:73
  28.4 10.4 %collective-permute-start.6 = (f32[16,32,128]{2,0,1:T(8,128)S(1)}, f32[16,32,128]{2,0,1:T(8,128)S(1)}, u32[]{:S(2)}, u32[]{:S(2)}) collective-permute-start(f32[16,32,128]{2,0,1:T(8,128)S(1)} %pad_maximum_fusion.3), channel_id=1, source_target_pairs={{64,0},{65,1},{128,64},{129,65},{192,128},{193,129},{194,192},{195... | collective-permute-start | bytes 786440 | tf_op jit(solution)/shard_map/ppermute | solution.py:73
  38.8 0.8 fusion.21
  39.7 4.3 %collective-permute-done.5 = f32[16,32,128]{2,0,1:T(8,128)S(1)} collective-permute-done((f32[16,32,128]{2,0,1:T(8,128)S(1)}, f32[16,32,128]{2,0,1:T(8,128)S(1)}, u32[]{:S(2)}, u32[]{:S(2)}) %collective-permute-start.5) | collective-permute-done | bytes 262176 | tf_op jit(solution)/shard_map/ppermute | solution.py:73
  44.0 1.3 collective-permute-done.6
  45.3 1.9 %collective-permute-start.7 = (f32[48,32,128]{2,0,1:T(8,128)S(1)}, f32[48,32,128]{2,0,1:T(8,128)}, u32[]{:S(2)}, u32[]{:S(2)}) collective-permute-start(f32[48,32,128]{2,0,1:T(8,128)S(1)} %pad_maximum_fusion.1), channel_id=1, source_target_pairs={{0,1},{1,0},{2,3},{3,2},{4,5},{5,4},{6,7},{7,6},{8,9},{9,8},{10,11... | collective-permute-start | bytes 2359304 | tf_op jit(solution)/shard_map/ppermute | solution.py:73
  47.3 0.4 convolution_bitcast_fusion.4
  47.9 0.2 convolution_compare_fusion
  48.1 0.2 fusion.36
  48.3 1.3 collective-permute-done.7
  49.6 1.7 %fusion.1 = f32[2,16,64,128]{3,1,2,0:T(8,128)S(1)} fusion(f32[48,32,128]{2,0,1:T(8,128)} %collective-permute-done.7, f32[16,32,128]{2,0,1:T(8,128)S(1)} %collective-permute-done.6, f32[16,16,128]{2,0,1:T(8,128)S(1)} %collective-permute-done.2, f32[16,16,128]{2,0,1:T(8,128)S(1)} %maximum_select_fusion, f32[16,32,128]{2,0,1:T(8,128)S(1)} %collective-permute-done.5, ...), kind=kOutput, calls=%fused_computation.3 | convolution fusion | flops 77070336 | bytes 2627584 | tf_op jit(solution)/shard_map/urj,jyz->uryz/dot_general | solution.py:147
  51.3 0.9 convolution_bitcast_fusion.3
  52.3 1.8 %fusion.18 = f32[2,16,64,128]{3,2,1,0:T(8,128)S(1)} fusion(f32[2,16,64,128]{3,2,1,0:T(8,128)S(1)} %convolution_bitcast_fusion.3, f32[1,16,64,128]{3,2,1,0:T(8,128)} %bitcast.17, f32[1,16,64,128]{3,2,1,0:T(8,128)} %bitcast.15, pred[2,16]{1,0:T(4,128)(4,1)S(1)} %convolution_compare_fusion, f32[2,128,128,1]{2,0,1,3:T(2,128)S(1)} %fusion.21), kind=kOutput, calls=%fused_computation.27 | convolution fusion | flops 202375168 | bytes 3276832 | tf_op jit(solution)/shard_map/uryz,uzw->uryw/dot_general | solution.py:149
  54.1 0.6 fusion.92
  54.7 0.6 fusion.93
  55.2 1.4 convolution_bitcast_fusion.1
  56.7 2.0 %collective-permute-start.8 = (f32[48,32,128]{2,0,1:T(8,128)S(1)}, f32[48,32,128]{2,0,1:T(8,128)S(1)}, u32[]{:S(2)}, u32[]{:S(2)}) collective-permute-start(f32[48,32,128]{2,0,1:T(8,128)S(1)} %slice.109), channel_id=1, source_target_pairs={{0,1},{1,0},{2,3},{3,2},{4,5},{5,4},{6,7},{7,6},{8,9},{9,8},{10,11... | collective-permute-start | bytes 2359304 | tf_op jit(solution)/shard_map/ppermute | solution.py:73
  58.7 0.7 fusion.30
  59.4 1.4 collective-permute-done.8
  61.0 1.9 %collective-permute-start.10 = (f32[16,32,128]{2,0,1:T(8,128)S(1)}, f32[16,32,128]{2,0,1:T(8,128)S(1)}, u32[]{:S(2)}, u32[]{:S(2)}) collective-permute-start(f32[16,32,128]{2,0,1:T(8,128)S(1)} %get-tuple-element.10), channel_id=1, source_target_pairs={{0,64},{1,65},{64,128},{65,129},{128,192},{129,193},{192,194},{193... | collective-permute-start | bytes 786440 | tf_op jit(solution)/shard_map/ppermute | solution.py:73
  62.9 8.3 %collective-permute-start.9 = (f32[16,32,128]{2,0,1:T(8,128)S(1)}, f32[16,32,128]{2,0,1:T(8,128)S(1)}, u32[]{:S(2)}, u32[]{:S(2)}) collective-permute-start(f32[16,32,128]{2,0,1:T(8,128)S(1)} %get-tuple-element.9), channel_id=1, source_target_pairs={{64,0},{65,1},{128,64},{129,65},{192,128},{193,129},{194,192},{195... | collective-permute-start | bytes 786440 | tf_op jit(solution)/shard_map/ppermute | solution.py:73
  71.2 0.2 fusion.44
  71.6 0.2 fusion.63
  71.8 4.1 %collective-permute-done.10 = f32[16,32,128]{2,0,1:T(8,128)S(1)} collective-permute-done((f32[16,32,128]{2,0,1:T(8,128)S(1)}, f32[16,32,128]{2,0,1:T(8,128)S(1)}, u32[]{:S(2)}, u32[]{:S(2)}) %collective-permute-start.10) | collective-permute-done | bytes 262176 | tf_op jit(solution)/shard_map/ppermute | solution.py:73
  75.9 1.2 collective-permute-done.9
  77.1 7.3 %collective-permute-start.11 = (f32[16,32,128]{2,0,1:T(8,128)S(1)}, f32[16,32,128]{2,0,1:T(8,128)S(1)}, u32[]{:S(2)}, u32[]{:S(2)}) collective-permute-start(f32[16,32,128]{2,0,1:T(8,128)S(1)} %fusion.32), channel_id=1, source_target_pairs={{0,256},{1,257},{2,258},{3,259},{4,260},{5,261},{6,262},{7,263},{8... | collective-permute-start | bytes 786440 | tf_op jit(solution)/shard_map/ppermute | solution.py:73
  84.5 0.1 copy.25
  84.6 0.1 convolution_bitcast_fusion.5
  84.8 11.3 %collective-permute-done.11 = f32[16,32,128]{2,0,1:T(8,128)S(1)} collective-permute-done((f32[16,32,128]{2,0,1:T(8,128)S(1)}, f32[16,32,128]{2,0,1:T(8,128)S(1)}, u32[]{:S(2)}, u32[]{:S(2)}) %collective-permute-start.11) | collective-permute-done | bytes 262176 | tf_op jit(solution)/shard_map/ppermute | solution.py:73
  96.1 0.6 fusion.35
  96.7 1.9 %collective-permute-start.12 = (f32[16,32,128]{2,0,1:T(8,128)S(1)}, f32[16,32,128]{2,0,1:T(8,128)S(1)}, u32[]{:S(2)}, u32[]{:S(2)}) collective-permute-start(f32[16,32,128]{2,0,1:T(8,128)S(1)} %get-tuple-element.19), channel_id=1, source_target_pairs={{0,64},{1,65},{64,128},{65,129},{128,192},{129,193},{192,194},{193... | collective-permute-start | bytes 786440 | tf_op jit(solution)/shard_map/ppermute | solution.py:73
  98.7 7.8 %collective-permute-start.13 = (f32[16,32,128]{2,0,1:T(8,128)S(1)}, f32[16,32,128]{2,0,1:T(8,128)S(1)}, u32[]{:S(2)}, u32[]{:S(2)}) collective-permute-start(f32[16,32,128]{2,0,1:T(8,128)S(1)} %get-tuple-element.19), channel_id=1, source_target_pairs={{64,0},{65,1},{128,64},{129,65},{192,128},{193,129},{194,192},{195... | collective-permute-start | bytes 786440 | tf_op jit(solution)/shard_map/ppermute | solution.py:73
  106.5 4.1 %collective-permute-done.12 = f32[16,32,128]{2,0,1:T(8,128)S(1)} collective-permute-done((f32[16,32,128]{2,0,1:T(8,128)S(1)}, f32[16,32,128]{2,0,1:T(8,128)S(1)}, u32[]{:S(2)}, u32[]{:S(2)}) %collective-permute-start.12) | collective-permute-done | bytes 262176 | tf_op jit(solution)/shard_map/ppermute | solution.py:73
  110.6 1.2 collective-permute-done.13
  111.8 2.1 %collective-permute-start.14 = (f32[48,32,128]{2,0,1:T(8,128)S(1)}, f32[48,32,128]{2,0,1:T(8,128)S(1)}, u32[]{:S(2)}, u32[]{:S(2)}) collective-permute-start(f32[48,32,128]{2,0,1:T(8,128)S(1)} %pad_maximum_fusion.2), channel_id=1, source_target_pairs={{0,1},{1,0},{2,3},{3,2},{4,5},{5,4},{6,7},{7,6},{8,9},{9,8},{10,11... | collective-permute-start | bytes 2359304 | tf_op jit(solution)/shard_map/ppermute | solution.py:73
  113.9 2.1 %collective-permute-done.14 = f32[48,32,128]{2,0,1:T(8,128)S(1)} collective-permute-done((f32[48,32,128]{2,0,1:T(8,128)S(1)}, f32[48,32,128]{2,0,1:T(8,128)S(1)}, u32[]{:S(2)}, u32[]{:S(2)}) %collective-permute-start.14) | collective-permute-done | bytes 786464 | tf_op jit(solution)/shard_map/ppermute | solution.py:73
  116.0 0.6 fusion.10
  116.6 0.9 convolution_bitcast_fusion.2
  117.5 1.8 %fusion.20 = f32[2,16,64,128]{3,2,1,0:T(8,128)S(1)} fusion(f32[2,16,64,128]{3,2,1,0:T(8,128)S(1)} %convolution_bitcast_fusion.2, f32[1,16,64,128]{3,2,1,0:T(8,128)} %bitcast.17, f32[1,16,64,128]{3,2,1,0:T(8,128)} %bitcast.15, pred[2,16]{1,0:T(4,128)(4,1)S(1)} %convolution_compare_fusion, f32[2,128,128,1]{2,0,1,3:T(2,128)S(1)} %fusion.21), kind=kOutput, calls=%fused_computation.29 | convolution fusion | flops 202375168 | bytes 3276832 | tf_op jit(solution)/shard_map/uryz,uzw->uryw/dot_general | solution.py:149
  119.3 0.6 fusion.94
  119.9 0.6 fusion.95
  120.5 1.4 convolution_bitcast_fusion
  121.9 2.0 %collective-permute-start.15 = (f32[48,32,128]{2,0,1:T(8,128)S(1)}, f32[48,32,128]{2,0,1:T(8,128)S(1)}, u32[]{:S(2)}, u32[]{:S(2)}) collective-permute-start(f32[48,32,128]{2,0,1:T(8,128)S(1)} %slice.120), channel_id=1, source_target_pairs={{0,1},{1,0},{2,3},{3,2},{4,5},{5,4},{6,7},{7,6},{8,9},{9,8},{10,11... | collective-permute-start | bytes 2359304 | tf_op jit(solution)/shard_map/ppermute | solution.py:73
  123.9 2.1 %collective-permute-done.15 = f32[48,32,128]{2,0,1:T(8,128)S(1)} collective-permute-done((f32[48,32,128]{2,0,1:T(8,128)S(1)}, f32[48,32,128]{2,0,1:T(8,128)S(1)}, u32[]{:S(2)}, u32[]{:S(2)}) %collective-permute-start.15) | collective-permute-done | bytes 786464 | tf_op jit(solution)/shard_map/ppermute | solution.py:73
  126.2 8.3 %collective-permute-start.16 = (f32[16,32,128]{2,0,1:T(8,128)S(1)}, f32[16,32,128]{2,0,1:T(8,128)S(1)}, u32[]{:S(2)}, u32[]{:S(2)}) collective-permute-start(f32[16,32,128]{2,0,1:T(8,128)S(1)} %get-tuple-element.7), channel_id=1, source_target_pairs={{64,0},{65,1},{128,64},{129,65},{192,128},{193,129},{194,192},{195... | collective-permute-start | bytes 786440 | tf_op jit(solution)/shard_map/ppermute | solution.py:73
  134.5 1.9 %collective-permute-start.17 = (f32[16,32,128]{2,0,1:T(8,128)S(1)}, f32[16,32,128]{2,0,1:T(8,128)S(1)}, u32[]{:S(2)}, u32[]{:S(2)}) collective-permute-start(f32[16,32,128]{2,0,1:T(8,128)S(1)} %get-tuple-element.8), channel_id=1, source_target_pairs={{0,64},{1,65},{64,128},{65,129},{128,192},{129,193},{192,194},{193... | collective-permute-start | bytes 786440 | tf_op jit(solution)/shard_map/ppermute | solution.py:73
  136.4 3.9 %collective-permute-done.16 = f32[16,32,128]{2,0,1:T(8,128)S(1)} collective-permute-done((f32[16,32,128]{2,0,1:T(8,128)S(1)}, f32[16,32,128]{2,0,1:T(8,128)S(1)}, u32[]{:S(2)}, u32[]{:S(2)}) %collective-permute-start.16) | collective-permute-done | bytes 262176 | tf_op jit(solution)/shard_map/ppermute | solution.py:73
  140.3 8.2 %collective-permute-done.17 = f32[16,32,128]{2,0,1:T(8,128)S(1)} collective-permute-done((f32[16,32,128]{2,0,1:T(8,128)S(1)}, f32[16,32,128]{2,0,1:T(8,128)S(1)}, u32[]{:S(2)}, u32[]{:S(2)}) %collective-permute-start.17) | collective-permute-done | bytes 262176 | tf_op jit(solution)/shard_map/ppermute | solution.py:73
  148.6 4.4 %collective-permute-start.18 = (f32[16,16,128]{2,0,1:T(8,128)S(1)}, f32[16,16,128]{2,0,1:T(8,128)S(1)}, u32[]{:S(2)}, u32[]{:S(2)}) collective-permute-start(f32[16,16,128]{2,0,1:T(8,128)S(1)} %slice.125), channel_id=1, source_target_pairs={{0,256},{1,257},{2,258},{3,259},{4,260},{5,261},{6,262},{7,263},{8... | collective-permute-start | bytes 393224 | tf_op jit(solution)/shard_map/ppermute | solution.py:73
  153.0 6.4 %collective-permute-done.18 = f32[16,16,128]{2,0,1:T(8,128)S(1)} collective-permute-done((f32[16,16,128]{2,0,1:T(8,128)S(1)}, f32[16,16,128]{2,0,1:T(8,128)S(1)}, u32[]{:S(2)}, u32[]{:S(2)}) %collective-permute-start.18) | collective-permute-done | bytes 131104 | tf_op jit(solution)/shard_map/ppermute | solution.py:73
  159.5 0.7 collective-permute-start.19
  160.1 1.9 %collective-permute-start.20 = (f32[16,8,128]{2,0,1:T(8,128)S(1)}, f32[16,8,128]{2,0,1:T(8,128)S(1)}, u32[]{:S(2)}, u32[]{:S(2)}) collective-permute-start(f32[16,8,128]{2,0,1:T(8,128)S(1)} %get-tuple-element.14), channel_id=1, source_target_pairs={{64,0},{192,1},{0,64},{128,65},{65,128},{193,129},{1,192},{129,193... | collective-permute-start | bytes 196616 | tf_op jit(solution)/shard_map/ppermute | solution.py:73
  162.1 4.2 %collective-permute-done.20 = f32[16,8,128]{2,0,1:T(8,128)S(1)} collective-permute-done((f32[16,8,128]{2,0,1:T(8,128)S(1)}, f32[16,8,128]{2,0,1:T(8,128)S(1)}, u32[]{:S(2)}, u32[]{:S(2)}) %collective-permute-start.20) | collective-permute-done | bytes 65568 | tf_op jit(solution)/shard_map/ppermute | solution.py:73
  166.3 0.7 copy.11
  (46 shorter events, 1.7 us)
Async XLA Ops:
  0.0 10.4 %copy-start = (f32[8,3,31]{2,0,1:T(8,128)S(1)}, f32[8,3,31]{2,0,1:T(8,128)}, u32[]{:S(2)}) copy-start(f32[8,3,31]{2,0,1:T(8,128)} %param.6) | copy-start | bytes 8932
  0.0 10.8 %copy-start.1 = (s32[8,16]{1,0:T(8,128)S(1)}, s32[8,16]{1,0:T(8,128)}, u32[]{:S(2)}) copy-start(s32[8,16]{1,0:T(8,128)} %param.7) | copy-start | bytes 1540
  0.9 10.2 %collective-permute-start = (f32[16,8,128]{2,0,1:T(8,128)S(1)}, f32[16,8,128]{2,0,1:T(8,128)S(1)}, u32[]{:S(2)}, u32[]{:S(2)}) collective-permute-start(f32[16,8,128]{2,0,1:T(8,128)S(1)} %copy.34), channel_id=1, source_target_pairs={{0,0},{1,128},{64,64},{65,192},{128,1},{129,129},{192,65},{193,193... | collective-permute-start | bytes 196616 | tf_op jit(solution)/shard_map/ppermute | solution.py:73
  1.6 9.5 %collective-permute-start.1 = (f32[16,8,128]{2,0,1:T(8,128)S(1)}, f32[16,8,128]{2,0,1:T(8,128)S(1)}, u32[]{:S(2)}, u32[]{:S(2)}) collective-permute-start(f32[16,8,128]{2,0,1:T(8,128)S(1)} %copy.35), channel_id=1, source_target_pairs={{0,64},{1,192},{64,0},{65,128},{128,65},{129,193},{192,1},{193,129... | collective-permute-start | bytes 196616 | tf_op jit(solution)/shard_map/ppermute | solution.py:73
  6.3 45.9 %collective-permute-start.3 = (f32[16,64,128]{2,1,0:T(8,128)S(1)}, f32[16,64,128]{2,1,0:T(8,128)}, u32[]{:S(2)}, u32[]{:S(2)}) collective-permute-start(f32[16,64,128]{2,1,0:T(8,128)S(1)} %get-tuple-element.5), channel_id=1, source_target_pairs={{0,0},{1,128},{64,64},{65,192},{128,1},{129,129},{192,65},{193,193... | collective-permute-start | bytes 1572872 | tf_op jit(solution)/shard_map/ppermute | solution.py:73
  7.8 44.5 %collective-permute-start.4 = (f32[16,64,128]{2,1,0:T(8,128)S(1)}, f32[16,64,128]{2,1,0:T(8,128)}, u32[]{:S(2)}, u32[]{:S(2)}) collective-permute-start(f32[16,64,128]{2,1,0:T(8,128)S(1)} %get-tuple-element.6), channel_id=1, source_target_pairs={{0,64},{1,192},{64,0},{65,128},{128,65},{129,193},{192,1},{193,129... | collective-permute-start | bytes 1572872 | tf_op jit(solution)/shard_map/ppermute | solution.py:73
  11.2 13.9 %collective-permute-start.2 = (f32[16,16,128]{2,0,1:T(8,128)S(1)}, f32[16,16,128]{2,0,1:T(8,128)S(1)}, u32[]{:S(2)}, u32[]{:S(2)}) collective-permute-start(f32[16,16,128]{2,0,1:T(8,128)S(1)} %maximum_select_fusion), channel_id=1, source_target_pairs={{0,256},{1,257},{2,258},{3,259},{4,260},{5,261},{6,262},{7,263},{8... | collective-permute-start | bytes 393224 | tf_op jit(solution)/shard_map/ppermute | solution.py:73
  25.0 18.9 %collective-permute-start.5 = (f32[16,32,128]{2,0,1:T(8,128)S(1)}, f32[16,32,128]{2,0,1:T(8,128)S(1)}, u32[]{:S(2)}, u32[]{:S(2)}) collective-permute-start(f32[16,32,128]{2,0,1:T(8,128)S(1)} %pad_maximum_fusion.3), channel_id=1, source_target_pairs={{0,64},{1,65},{64,128},{65,129},{128,192},{129,193},{192,194},{193... | collective-permute-start | bytes 786440 | tf_op jit(solution)/shard_map/ppermute | solution.py:73
  28.4 16.8 %collective-permute-start.6 = (f32[16,32,128]{2,0,1:T(8,128)S(1)}, f32[16,32,128]{2,0,1:T(8,128)S(1)}, u32[]{:S(2)}, u32[]{:S(2)}) collective-permute-start(f32[16,32,128]{2,0,1:T(8,128)S(1)} %pad_maximum_fusion.3), channel_id=1, source_target_pairs={{64,0},{65,1},{128,64},{129,65},{192,128},{193,129},{194,192},{195... | collective-permute-start | bytes 786440 | tf_op jit(solution)/shard_map/ppermute | solution.py:73
  45.3 4.3 %collective-permute-start.7 = (f32[48,32,128]{2,0,1:T(8,128)S(1)}, f32[48,32,128]{2,0,1:T(8,128)}, u32[]{:S(2)}, u32[]{:S(2)}) collective-permute-start(f32[48,32,128]{2,0,1:T(8,128)S(1)} %pad_maximum_fusion.1), channel_id=1, source_target_pairs={{0,1},{1,0},{2,3},{3,2},{4,5},{5,4},{6,7},{7,6},{8,9},{9,8},{10,11... | collective-permute-start | bytes 2359304 | tf_op jit(solution)/shard_map/ppermute | solution.py:73
  56.7 4.2 %collective-permute-start.8 = (f32[48,32,128]{2,0,1:T(8,128)S(1)}, f32[48,32,128]{2,0,1:T(8,128)S(1)}, u32[]{:S(2)}, u32[]{:S(2)}) collective-permute-start(f32[48,32,128]{2,0,1:T(8,128)S(1)} %slice.109), channel_id=1, source_target_pairs={{0,1},{1,0},{2,3},{3,2},{4,5},{5,4},{6,7},{7,6},{8,9},{9,8},{10,11... | collective-permute-start | bytes 2359304 | tf_op jit(solution)/shard_map/ppermute | solution.py:73
  61.0 14.9 %collective-permute-start.10 = (f32[16,32,128]{2,0,1:T(8,128)S(1)}, f32[16,32,128]{2,0,1:T(8,128)S(1)}, u32[]{:S(2)}, u32[]{:S(2)}) collective-permute-start(f32[16,32,128]{2,0,1:T(8,128)S(1)} %get-tuple-element.10), channel_id=1, source_target_pairs={{0,64},{1,65},{64,128},{65,129},{128,192},{129,193},{192,194},{193... | collective-permute-start | bytes 786440 | tf_op jit(solution)/shard_map/ppermute | solution.py:73
  62.9 14.1 %collective-permute-start.9 = (f32[16,32,128]{2,0,1:T(8,128)S(1)}, f32[16,32,128]{2,0,1:T(8,128)S(1)}, u32[]{:S(2)}, u32[]{:S(2)}) collective-permute-start(f32[16,32,128]{2,0,1:T(8,128)S(1)} %get-tuple-element.9), channel_id=1, source_target_pairs={{64,0},{65,1},{128,64},{129,65},{192,128},{193,129},{194,192},{195... | collective-permute-start | bytes 786440 | tf_op jit(solution)/shard_map/ppermute | solution.py:73
  77.1 19.0 %collective-permute-start.11 = (f32[16,32,128]{2,0,1:T(8,128)S(1)}, f32[16,32,128]{2,0,1:T(8,128)S(1)}, u32[]{:S(2)}, u32[]{:S(2)}) collective-permute-start(f32[16,32,128]{2,0,1:T(8,128)S(1)} %fusion.32), channel_id=1, source_target_pairs={{0,256},{1,257},{2,258},{3,259},{4,260},{5,261},{6,262},{7,263},{8... | collective-permute-start | bytes 786440 | tf_op jit(solution)/shard_map/ppermute | solution.py:73
  96.7 13.9 %collective-permute-start.12 = (f32[16,32,128]{2,0,1:T(8,128)S(1)}, f32[16,32,128]{2,0,1:T(8,128)S(1)}, u32[]{:S(2)}, u32[]{:S(2)}) collective-permute-start(f32[16,32,128]{2,0,1:T(8,128)S(1)} %get-tuple-element.19), channel_id=1, source_target_pairs={{0,64},{1,65},{64,128},{65,129},{128,192},{129,193},{192,194},{193... | collective-permute-start | bytes 786440 | tf_op jit(solution)/shard_map/ppermute | solution.py:73
  98.7 13.1 %collective-permute-start.13 = (f32[16,32,128]{2,0,1:T(8,128)S(1)}, f32[16,32,128]{2,0,1:T(8,128)S(1)}, u32[]{:S(2)}, u32[]{:S(2)}) collective-permute-start(f32[16,32,128]{2,0,1:T(8,128)S(1)} %get-tuple-element.19), channel_id=1, source_target_pairs={{64,0},{65,1},{128,64},{129,65},{192,128},{193,129},{194,192},{195... | collective-permute-start | bytes 786440 | tf_op jit(solution)/shard_map/ppermute | solution.py:73
  111.8 4.2 %collective-permute-start.14 = (f32[48,32,128]{2,0,1:T(8,128)S(1)}, f32[48,32,128]{2,0,1:T(8,128)S(1)}, u32[]{:S(2)}, u32[]{:S(2)}) collective-permute-start(f32[48,32,128]{2,0,1:T(8,128)S(1)} %pad_maximum_fusion.2), channel_id=1, source_target_pairs={{0,1},{1,0},{2,3},{3,2},{4,5},{5,4},{6,7},{7,6},{8,9},{9,8},{10,11... | collective-permute-start | bytes 2359304 | tf_op jit(solution)/shard_map/ppermute | solution.py:73
  121.9 4.2 %collective-permute-start.15 = (f32[48,32,128]{2,0,1:T(8,128)S(1)}, f32[48,32,128]{2,0,1:T(8,128)S(1)}, u32[]{:S(2)}, u32[]{:S(2)}) collective-permute-start(f32[48,32,128]{2,0,1:T(8,128)S(1)} %slice.120), channel_id=1, source_target_pairs={{0,1},{1,0},{2,3},{3,2},{4,5},{5,4},{6,7},{7,6},{8,9},{9,8},{10,11... | collective-permute-start | bytes 2359304 | tf_op jit(solution)/shard_map/ppermute | solution.py:73
  126.2 14.1 %collective-permute-start.16 = (f32[16,32,128]{2,0,1:T(8,128)S(1)}, f32[16,32,128]{2,0,1:T(8,128)S(1)}, u32[]{:S(2)}, u32[]{:S(2)}) collective-permute-start(f32[16,32,128]{2,0,1:T(8,128)S(1)} %get-tuple-element.7), channel_id=1, source_target_pairs={{64,0},{65,1},{128,64},{129,65},{192,128},{193,129},{194,192},{195... | collective-permute-start | bytes 786440 | tf_op jit(solution)/shard_map/ppermute | solution.py:73
  134.5 14.1 %collective-permute-start.17 = (f32[16,32,128]{2,0,1:T(8,128)S(1)}, f32[16,32,128]{2,0,1:T(8,128)S(1)}, u32[]{:S(2)}, u32[]{:S(2)}) collective-permute-start(f32[16,32,128]{2,0,1:T(8,128)S(1)} %get-tuple-element.8), channel_id=1, source_target_pairs={{0,64},{1,65},{64,128},{65,129},{128,192},{129,193},{192,194},{193... | collective-permute-start | bytes 786440 | tf_op jit(solution)/shard_map/ppermute | solution.py:73
  148.6 10.8 %collective-permute-start.18 = (f32[16,16,128]{2,0,1:T(8,128)S(1)}, f32[16,16,128]{2,0,1:T(8,128)S(1)}, u32[]{:S(2)}, u32[]{:S(2)}) collective-permute-start(f32[16,16,128]{2,0,1:T(8,128)S(1)} %slice.125), channel_id=1, source_target_pairs={{0,256},{1,257},{2,258},{3,259},{4,260},{5,261},{6,262},{7,263},{8... | collective-permute-start | bytes 393224 | tf_op jit(solution)/shard_map/ppermute | solution.py:73
  159.5 2.6 %collective-permute-start.19 = (f32[16,8,128]{2,0,1:T(8,128)S(1)}, f32[16,8,128]{2,0,1:T(8,128)S(1)}, u32[]{:S(2)}, u32[]{:S(2)}) collective-permute-start(f32[16,8,128]{2,0,1:T(8,128)S(1)} %get-tuple-element.13), channel_id=1, source_target_pairs={{0,0},{128,1},{64,64},{192,65},{1,128},{129,129},{65,192},{193,193... | collective-permute-start | bytes 196616 | tf_op jit(solution)/shard_map/ppermute | solution.py:73
  160.1 6.2 %collective-permute-start.20 = (f32[16,8,128]{2,0,1:T(8,128)S(1)}, f32[16,8,128]{2,0,1:T(8,128)S(1)}, u32[]{:S(2)}, u32[]{:S(2)}) collective-permute-start(f32[16,8,128]{2,0,1:T(8,128)S(1)} %get-tuple-element.14), channel_id=1, source_target_pairs={{64,0},{192,1},{0,64},{128,65},{65,128},{193,129},{1,192},{129,193... | collective-permute-start | bytes 196616 | tf_op jit(solution)/shard_map/ppermute | solution.py:73

commit v2 on v1

--- a/solution.py
+++ b/solution.py
@@ -20,7 +20,7 @@
     return (p - column % 4) % 4
 
 
-def spread_pairs(turn):
+def spread_pairs(turn, cross=0):
     pairs = []
     for h in range(2):
         for column in range(COLS // 2):
@@ -28,23 +28,23 @@
                 for k in range(2):
                     p = 2 * k + (x + turn) % 2
                     pairs.append(
-                        (device(h, x, 2 * column + k), device(h, chip_x(column, p), 2 * column + x // 2))
+                        (
+                            device(h, x, 2 * column + k),
+                            device(h ^ cross, chip_x(column, p), 2 * column + x // 2),
+                        )
                     )
     return pairs
 
 
-def chip_pairs(step):
+def chip_pairs(first):
     pairs = []
-    chips = COLS // 2 * 4
     for h in range(2):
-        for chip in range(chips):
-            if 0 <= chip + step < chips:
-                for core in range(2):
-                    ends = []
-                    for q in (chip, chip + step):
-                        column, p = divmod(q, 4)
-                        ends.append(device(h, chip_x(column, p), 2 * column + core))
-                    pairs.append(tuple(ends))
+        for chip in range(first, COLS // 2 * 4 - 1, 2):
+            for core in range(2):
+                low, high = (
+                    device(h, chip_x(q // 4, q % 4), 2 * (q // 4) + core) for q in (chip, chip + 1)
+                )
+                pairs += [(low, high), (high, low)]
     return pairs
 
 
@@ -63,8 +63,9 @@
 
 
 SPREAD = [spread_pairs(0), spread_pairs(1)]
-UP = chip_pairs(1)
-DOWN = chip_pairs(-1)
+SPREAD_CROSS = [spread_pairs(0, 1), spread_pairs(1, 1)]
+ODD = chip_pairs(1)
+EVEN = chip_pairs(0)
 SWAP_H = swap_pairs("h")
 SWAP_CORE = swap_pairs("core")
 
@@ -93,14 +94,17 @@
     taps = psf_taps.shape[2]
     half = (taps - 1) // 2
 
-    def spread(block, turn):
-        return send(lax.dynamic_slice_in_dim(block, SLAB * ((x + turn) % 2), SLAB, 0), SPREAD[turn])
+    def piece(block, turn):
+        return lax.dynamic_slice_in_dim(block, SLAB * ((x + turn) % 2), SLAB, 0)
 
     even = p % 2 == 0
-    est = [spread(estimate, turn) for turn in (0, 1)]
+    est = [send(piece(estimate, turn), SPREAD[turn]) for turn in (0, 1)]
     quarter = jnp.where(even, jnp.concatenate(est, 1), jnp.concatenate(est[::-1], 1))
     current = jnp.concatenate([quarter, send(quarter, SWAP_H)], 1)
-    images = jnp.stack([spread(observed[0], turn) for turn in (0, 1)])
+    images = [piece(observed[0], turn) for turn in (0, 1)]
+    *images, _ = lax.optimization_barrier((*images, quarter))
+    images = [send(image, route) for image, route in zip(images, SPREAD)]
+    current, images[0] = lax.optimization_barrier((current, images[0]))
 
     kernels = psf_taps / jnp.sum(psf_taps, axis=2, keepdims=True)
     views = jnp.arange(kernels.shape[0], dtype=jnp.int32)
@@ -113,7 +117,8 @@
     all_y = jnp.arange(full_width, dtype=jnp.int32)
     all_z = jnp.arange(depth, dtype=jnp.int32)
     slab = jnp.arange(SLAB, dtype=jnp.int32)
-    wide = jnp.arange(3 * SLAB, dtype=jnp.int32) - SLAB
+    side = jnp.where(even, SLAB, -SLAB)
+    wide = jnp.concatenate([slab - side, slab, slab + side])
     mat_x = tap_matrix(own[:, 0], wide[None, :] - slab[:, None] + half)
     mat_y = tap_matrix(own[:, 1], local_y[None, :] - all_y[:, None] + half)
     mat_z = tap_matrix(own[:, 2], all_z[:, None] - all_z[None, :] + half)
@@ -139,10 +144,12 @@
     inside = own_masks[:, :, None, None] > 0
 
     width = 2 * quarter_width
+    scale = 1.0 / (weights + 1.0)
     for iteration in range(ITERS):
-        low = send(current, UP)
-        high = send(current, DOWN)
-        extended = jnp.concatenate([low, current, high], 0)
+        extended = jnp.concatenate([send(current, ODD), current, send(current, EVEN)], 0)
+        if iteration == 0:
+            extended, images[1] = lax.optimization_barrier((extended, images[1]))
+            images = jnp.stack(images)
         extended = jnp.concatenate([extended, send(extended, SWAP_CORE)], 1)
         blurred = jnp.einsum("urj,jyz->uryz", mat_x, extended, precision=HIGH)
         blurred = jnp.einsum("urjz,uyj->uryz", blurred, mat_y, precision=HIGH)
@@ -152,26 +159,29 @@
         back = jnp.einsum("uryz,uyj->urjz", back, mat_y, precision=HIGH)
         back = jnp.einsum("urj,uryz->jyz", mat_x, back, precision=HIGH)
         part = back[:, :width] + send(back[:, width:], SWAP_CORE)
-        part = (
-            part[SLAB : 2 * SLAB]
-            + send(part[:SLAB], DOWN)
-            + send(part[2 * SLAB :], UP)
-        )
+        part = part[SLAB : 2 * SLAB] + send(part[:SLAB], ODD) + send(part[2 * SLAB :], EVEN)
         if iteration < ITERS - 1:
             other = send(part, SWAP_H)
             total = part + jnp.concatenate([other[:, quarter_width:], other[:, :quarter_width]], 1)
-            current = current * (total + 1.0) / (weights + 1.0)
-        else:
-            total = part[:, :quarter_width] + send(part[:, quarter_width:], SWAP_H)
-            quarter = current[:, :quarter_width] * (total + 1.0) / (weights[:, :quarter_width] + 1.0)
+            current = current * (total + 1.0) * scale
 
+    factor = current * scale
+    halves = [
+        (factor * part)[:, quarter_width:],
+        (factor * (part + 1.0))[:, :quarter_width],
+    ]
     block = quarter_width // 2
-    first, second = quarter[:, :block], quarter[:, block:]
     pieces = []
-    for turn in (0, 1):
-        chosen = jnp.where((p + turn) % 2 == 0, first, second)
-        pieces.append(send(chosen, reverse(SPREAD[turn])))
-    return jnp.where(x % 2 == 0, jnp.concatenate(pieces, 0), jnp.concatenate(pieces[::-1], 0))
+    for half_part, routes in zip(halves, (SPREAD_CROSS, SPREAD)):
+        first, second = half_part[:, :block], half_part[:, block:]
+        pieces.append(
+            [
+                send(jnp.where((p + turn) % 2 == 0, first, second), reverse(routes[turn]))
+                for turn in (0, 1)
+            ]
+        )
+    one, two = (pieces[0][turn] + pieces[1][turn] for turn in (0, 1))
+    return jnp.where(x % 2 == 0, jnp.concatenate([one, two], 0), jnp.concatenate([two, one], 0))
 
 
 def solution(mesh):

time: 168 us -> 161 us (0.958)
  the two profiles are of different devices: /device:TPU:32 before, /device:TPU:57 now
where the time goes in v2:
time: 161 us; the launch traced here: 160 us
  starting transfers between devices  90.3 us (56%)
  waiting for transfers between devices  49.3 us (31%)
  matrix products  13 us (8%)
  local copies, waits for them, and re-layouts  3.81 us (2%)
  other arithmetic  2.55 us (2%)
    ppermute x22, starting transfers between devices, send(): return lax.ppermute(value, AXES, pairs)  90.3 us
    ppermute x22, waiting for transfers between devices, send(): return lax.ppermute(value, AXES, pairs)  49.3 us
  transfers between devices with their start and end apart: 22, of which 14 were waited for; matrix products, arithmetic and copies ran while one was open for 5% of the time, Pallas kernels for 0%

profile of v2, /device:TPU:57, one launch (start us, length us, event | category | flops | bytes accessed | tf_op | source)
XLA Modules:
  0.0 159.6 jit_solution(12993523265680646903)
XLA Ops:
  0.0 0.9 constant_dynamic-slice_fusion.1
  0.9 5.2 %collective-permute-start = (f32[16,8,128]{2,0,1:T(8,128)S(1)}, f32[16,8,128]{2,0,1:T(8,128)S(1)}, u32[]{:S(2)}, u32[]{:S(2)}) collective-permute-start(f32[16,8,128]{2,0,1:T(8,128)S(1)} %copy.33), channel_id=1, source_target_pairs={{0,0},{1,128},{64,64},{65,192},{128,1},{129,129},{192,65},{193,193... | collective-permute-start | bytes 196616 | tf_op jit(solution)/shard_map/ppermute | solution.py:74
  6.2 2.5 %collective-permute-start.1 = (f32[16,8,128]{2,0,1:T(8,128)S(1)}, f32[16,8,128]{2,0,1:T(8,128)S(1)}, u32[]{:S(2)}, u32[]{:S(2)}) collective-permute-start(f32[16,8,128]{2,0,1:T(8,128)S(1)} %copy.34), channel_id=1, source_target_pairs={{0,64},{1,192},{64,0},{65,128},{128,65},{129,193},{192,1},{193,129... | collective-permute-start | bytes 196616 | tf_op jit(solution)/shard_map/ppermute | solution.py:74
  8.7 0.8 reduce_sum.9
  9.5 0.8 broadcast_divide_fusion
  10.7 0.2 fusion.69
  10.9 1.3 dynamic-slice_bitcast_fusion
  12.2 0.8 collective-permute-done.1
  13.0 2.9 %collective-permute-start.3 = (f32[16,64,128]{2,1,0:T(8,128)S(1)}, f32[16,64,128]{2,1,0:T(8,128)S(1)}, u32[]{:S(2)}, u32[]{:S(2)}) collective-permute-start(f32[16,64,128]{2,1,0:T(8,128)S(1)} %get-tuple-element.11), channel_id=1, source_target_pairs={{0,0},{1,128},{64,64},{65,192},{128,1},{129,129},{192,65},{193,193... | collective-permute-start | bytes 1572872 | tf_op jit(solution)/shard_map/ppermute | solution.py:74
  15.9 0.4 convolution_bitcast_fusion.4
  16.4 10.6 %collective-permute-start.2 = (f32[16,16,128]{2,0,1:T(8,128)S(1)}, f32[16,16,128]{2,0,1:T(8,128)S(1)}, u32[]{:S(2)}, u32[]{:S(2)}) collective-permute-start(f32[16,16,128]{2,0,1:T(8,128)S(1)} %maximum_select_fusion), channel_id=1, source_target_pairs={{0,256},{1,257},{2,258},{3,259},{4,260},{5,261},{6,262},{7,263},{8... | collective-permute-start | bytes 393224 | tf_op jit(solution)/shard_map/ppermute | solution.py:74
  27.1 0.8 fusion.16
  27.8 2.9 %collective-permute-start.6 = (f32[16,64,128]{2,1,0:T(8,128)S(1)}, f32[16,64,128]{2,1,0:T(8,128)S(1)}, u32[]{:S(2)}, u32[]{:S(2)}) collective-permute-start(f32[16,64,128]{2,1,0:T(8,128)S(1)} %get-tuple-element.14), channel_id=1, source_target_pairs={{0,64},{1,192},{64,0},{65,128},{128,65},{129,193},{192,1},{193,129... | collective-permute-start | bytes 1572872 | tf_op jit(solution)/shard_map/ppermute | solution.py:74
  30.8 5.1 %collective-permute-start.4 = (f32[16,32,128]{2,0,1:T(8,128)S(1)}, f32[16,32,128]{2,0,1:T(8,128)S(1)}, u32[]{:S(2)}, u32[]{:S(2)}) collective-permute-start(f32[16,32,128]{2,0,1:T(8,128)S(1)} %pad_maximum_fusion.3), channel_id=1, source_target_pairs={{64,128},{128,64},{65,129},{129,65},{192,194},{194,192},{193,195},... | collective-permute-start | bytes 786440 | tf_op jit(solution)/shard_map/ppermute | solution.py:74
  35.9 1.9 %collective-permute-start.5 = (f32[16,32,128]{2,0,1:T(8,128)S(1)}, f32[16,32,128]{2,0,1:T(8,128)S(1)}, u32[]{:S(2)}, u32[]{:S(2)}) collective-permute-start(f32[16,32,128]{2,0,1:T(8,128)S(1)} %pad_maximum_fusion.3), channel_id=1, source_target_pairs={{0,64},{64,0},{1,65},{65,1},{128,192},{192,128},{129,193},{193,129... | collective-permute-start | bytes 786440 | tf_op jit(solution)/shard_map/ppermute | solution.py:74
  38.2 5.0 %collective-permute-done.4 = f32[16,32,128]{2,0,1:T(8,128)S(1)} collective-permute-done((f32[16,32,128]{2,0,1:T(8,128)S(1)}, f32[16,32,128]{2,0,1:T(8,128)S(1)}, u32[]{:S(2)}, u32[]{:S(2)}) %collective-permute-start.4) | collective-permute-done | bytes 262176 | tf_op jit(solution)/shard_map/ppermute | solution.py:74
  43.2 1.7 %collective-permute-done.5 = f32[16,32,128]{2,0,1:T(8,128)S(1)} collective-permute-done((f32[16,32,128]{2,0,1:T(8,128)S(1)}, f32[16,32,128]{2,0,1:T(8,128)S(1)}, u32[]{:S(2)}, u32[]{:S(2)}) %collective-permute-start.5) | collective-permute-done | bytes 262176 | tf_op jit(solution)/shard_map/ppermute | solution.py:74
  45.0 3.6 %collective-permute-start.7 = (f32[48,32,128]{2,0,1:T(8,128)S(1)}, f32[48,32,128]{2,0,1:T(8,128)S(1)}, u32[]{:S(2)}, u32[]{:S(2)}) collective-permute-start(f32[48,32,128]{2,0,1:T(8,128)S(1)} %pad_maximum_fusion.1), channel_id=1, source_target_pairs={{0,1},{1,0},{2,3},{3,2},{4,5},{5,4},{6,7},{7,6},{8,9},{9,8},{10,11... | collective-permute-start | bytes 2359304 | tf_op jit(solution)/shard_map/ppermute | solution.py:74
  48.6 0.2 fusion.48
  48.7 0.2 convolution_compare_fusion
  49.0 0.2 fusion.31
  49.2 1.2 collective-permute-done.7
  50.4 0.6 fusion.1
  51.0 0.9 convolution_bitcast_fusion.3
  51.9 0.7 fusion.12
  52.6 0.6 fusion.84
  53.1 0.6 fusion.85
  53.7 1.4 convolution_bitcast_fusion.1
  55.1 2.3 %collective-permute-start.8 = (f32[48,32,128]{2,0,1:T(8,128)S(1)}, f32[48,32,128]{2,0,1:T(8,128)S(1)}, u32[]{:S(2)}, u32[]{:S(2)}) collective-permute-start(f32[48,32,128]{2,0,1:T(8,128)S(1)} %slice.107), channel_id=1, source_target_pairs={{0,1},{1,0},{2,3},{3,2},{4,5},{5,4},{6,7},{7,6},{8,9},{9,8},{10,11... | collective-permute-start | bytes 2359304 | tf_op jit(solution)/shard_map/ppermute | solution.py:74
  57.4 0.7 fusion.25
  58.1 1.2 collective-permute-done.8
  59.4 1.9 %collective-permute-start.10 = (f32[16,32,128]{2,0,1:T(8,128)S(1)}, f32[16,32,128]{2,0,1:T(8,128)S(1)}, u32[]{:S(2)}, u32[]{:S(2)}) collective-permute-start(f32[16,32,128]{2,0,1:T(8,128)S(1)} %get-tuple-element.26), channel_id=1, source_target_pairs={{0,64},{64,0},{1,65},{65,1},{128,192},{192,128},{129,193},{193,129... | collective-permute-start | bytes 786440 | tf_op jit(solution)/shard_map/ppermute | solution.py:74
  61.4 7.6 %collective-permute-start.9 = (f32[16,32,128]{2,0,1:T(8,128)S(1)}, f32[16,32,128]{2,0,1:T(8,128)S(1)}, u32[]{:S(2)}, u32[]{:S(2)}) collective-permute-start(f32[16,32,128]{2,0,1:T(8,128)S(1)} %get-tuple-element.25), channel_id=1, source_target_pairs={{64,128},{128,64},{65,129},{129,65},{192,194},{194,192},{193,195},... | collective-permute-start | bytes 786440 | tf_op jit(solution)/shard_map/ppermute | solution.py:74
  69.0 0.2 fusion.36
  69.4 0.2 fusion.55
  69.6 5.5 %collective-permute-done.9 = f32[16,32,128]{2,0,1:T(8,128)S(1)} collective-permute-done((f32[16,32,128]{2,0,1:T(8,128)S(1)}, f32[16,32,128]{2,0,1:T(8,128)S(1)}, u32[]{:S(2)}, u32[]{:S(2)}) %collective-permute-start.9) | collective-permute-done | bytes 262176 | tf_op jit(solution)/shard_map/ppermute | solution.py:74
  75.1 5.9 %collective-permute-start.11 = (f32[16,32,128]{2,0,1:T(8,128)S(1)}, f32[16,32,128]{2,0,1:T(8,128)S(1)}, u32[]{:S(2)}, u32[]{:S(2)}) collective-permute-start(f32[16,32,128]{2,0,1:T(8,128)S(1)} %fusion.27), channel_id=1, source_target_pairs={{0,256},{1,257},{2,258},{3,259},{4,260},{5,261},{6,262},{7,263},{8... | collective-permute-start | bytes 786440 | tf_op jit(solution)/shard_map/ppermute | solution.py:74
  81.3 13.1 %collective-permute-done.11 = f32[16,32,128]{2,0,1:T(8,128)S(1)} collective-permute-done((f32[16,32,128]{2,0,1:T(8,128)S(1)}, f32[16,32,128]{2,0,1:T(8,128)S(1)}, u32[]{:S(2)}, u32[]{:S(2)}) %collective-permute-start.11) | collective-permute-done | bytes 262176 | tf_op jit(solution)/shard_map/ppermute | solution.py:74
  94.5 0.6 fusion.30
  95.2 5.7 %collective-permute-start.12 = (f32[16,32,128]{2,0,1:T(8,128)S(1)}, f32[16,32,128]{2,0,1:T(8,128)S(1)}, u32[]{:S(2)}, u32[]{:S(2)}) collective-permute-start(f32[16,32,128]{2,0,1:T(8,128)S(1)} %get-tuple-element.37), channel_id=1, source_target_pairs={{64,128},{128,64},{65,129},{129,65},{192,194},{194,192},{193,195},... | collective-permute-start | bytes 786440 | tf_op jit(solution)/shard_map/ppermute | solution.py:74
  100.8 1.9 %collective-permute-start.13 = (f32[16,32,128]{2,0,1:T(8,128)S(1)}, f32[16,32,128]{2,0,1:T(8,128)S(1)}, u32[]{:S(2)}, u32[]{:S(2)}) collective-permute-start(f32[16,32,128]{2,0,1:T(8,128)S(1)} %get-tuple-element.37), channel_id=1, source_target_pairs={{0,64},{64,0},{1,65},{65,1},{128,192},{192,128},{129,193},{193,129... | collective-permute-start | bytes 786440 | tf_op jit(solution)/shard_map/ppermute | solution.py:74
  102.8 4.3 %collective-permute-done.12 = f32[16,32,128]{2,0,1:T(8,128)S(1)} collective-permute-done((f32[16,32,128]{2,0,1:T(8,128)S(1)}, f32[16,32,128]{2,0,1:T(8,128)S(1)}, u32[]{:S(2)}, u32[]{:S(2)}) %collective-permute-start.12) | collective-permute-done | bytes 262176 | tf_op jit(solution)/shard_map/ppermute | solution.py:74
  107.1 2.7 %collective-permute-done.13 = f32[16,32,128]{2,0,1:T(8,128)S(1)} collective-permute-done((f32[16,32,128]{2,0,1:T(8,128)S(1)}, f32[16,32,128]{2,0,1:T(8,128)S(1)}, u32[]{:S(2)}, u32[]{:S(2)}) %collective-permute-start.13) | collective-permute-done | bytes 262176 | tf_op jit(solution)/shard_map/ppermute | solution.py:74
  109.9 3.8 %collective-permute-start.14 = (f32[48,32,128]{2,0,1:T(8,128)S(1)}, f32[48,32,128]{2,0,1:T(8,128)S(1)}, u32[]{:S(2)}, u32[]{:S(2)}) collective-permute-start(f32[48,32,128]{2,0,1:T(8,128)S(1)} %pad_maximum_fusion.2), channel_id=1, source_target_pairs={{0,1},{1,0},{2,3},{3,2},{4,5},{5,4},{6,7},{7,6},{8,9},{9,8},{10,11... | collective-permute-start | bytes 2359304 | tf_op jit(solution)/shard_map/ppermute | solution.py:74
  113.6 1.7 %collective-permute-done.14 = f32[48,32,128]{2,0,1:T(8,128)S(1)} collective-permute-done((f32[48,32,128]{2,0,1:T(8,128)S(1)}, f32[48,32,128]{2,0,1:T(8,128)S(1)}, u32[]{:S(2)}, u32[]{:S(2)}) %collective-permute-start.14) | collective-permute-done | bytes 786464 | tf_op jit(solution)/shard_map/ppermute | solution.py:74
  115.3 0.6 fusion.4
  115.9 0.9 convolution_bitcast_fusion.2
  116.8 0.1 copy-done.1
  116.9 0.7 fusion.14
  117.6 0.6 fusion.86
  118.2 0.6 fusion.87
  118.7 1.4 convolution_bitcast_fusion
  120.2 2.3 %collective-permute-start.15 = (f32[48,32,128]{2,0,1:T(8,128)S(1)}, f32[48,32,128]{2,0,1:T(8,128)S(1)}, u32[]{:S(2)}, u32[]{:S(2)}) collective-permute-start(f32[48,32,128]{2,0,1:T(8,128)S(1)} %slice.117), channel_id=1, source_target_pairs={{0,1},{1,0},{2,3},{3,2},{4,5},{5,4},{6,7},{7,6},{8,9},{9,8},{10,11... | collective-permute-start | bytes 2359304 | tf_op jit(solution)/shard_map/ppermute | solution.py:74
  122.5 1.9 %collective-permute-done.15 = f32[48,32,128]{2,0,1:T(8,128)S(1)} collective-permute-done((f32[48,32,128]{2,0,1:T(8,128)S(1)}, f32[48,32,128]{2,0,1:T(8,128)S(1)}, u32[]{:S(2)}, u32[]{:S(2)}) %collective-permute-start.15) | collective-permute-done | bytes 786464 | tf_op jit(solution)/shard_map/ppermute | solution.py:74
  124.5 3.5 %collective-permute-start.16 = (f32[16,32,128]{2,0,1:T(8,128)S(1)}, f32[16,32,128]{2,0,1:T(8,128)S(1)}, u32[]{:S(2)}, u32[]{:S(2)}) collective-permute-start(f32[16,32,128]{2,0,1:T(8,128)S(1)} %get-tuple-element.23), channel_id=1, source_target_pairs={{64,128},{128,64},{65,129},{129,65},{192,194},{194,192},{193,195},... | collective-permute-start | bytes 786440 | tf_op jit(solution)/shard_map/ppermute | solution.py:74
  128.0 1.9 %collective-permute-start.17 = (f32[16,32,128]{2,0,1:T(8,128)S(1)}, f32[16,32,128]{2,0,1:T(8,128)S(1)}, u32[]{:S(2)}, u32[]{:S(2)}) collective-permute-start(f32[16,32,128]{2,0,1:T(8,128)S(1)} %get-tuple-element.24), channel_id=1, source_target_pairs={{0,64},{64,0},{1,65},{65,1},{128,192},{192,128},{129,193},{193,129... | collective-permute-start | bytes 786440 | tf_op jit(solution)/shard_map/ppermute | solution.py:74
  129.9 6.7 %collective-permute-done.16 = f32[16,32,128]{2,0,1:T(8,128)S(1)} collective-permute-done((f32[16,32,128]{2,0,1:T(8,128)S(1)}, f32[16,32,128]{2,0,1:T(8,128)S(1)}, u32[]{:S(2)}, u32[]{:S(2)}) %collective-permute-start.16) | collective-permute-done | bytes 262176 | tf_op jit(solution)/shard_map/ppermute | solution.py:74
  136.6 0.5 collective-permute-done.17
  137.2 3.5 %collective-permute-start.19 = (f32[16,8,128]{2,0,1:T(8,128)S(1)}, f32[16,8,128]{2,0,1:T(8,128)S(1)}, u32[]{:S(2)}, u32[]{:S(2)}) collective-permute-start(f32[16,8,128]{2,0,1:T(8,128)S(1)} %get-tuple-element.27), channel_id=1, source_target_pairs={{0,0},{128,1},{64,64},{192,65},{1,128},{129,129},{65,192},{193,193... | collective-permute-start | bytes 196616 | tf_op jit(solution)/shard_map/ppermute | solution.py:74
  140.7 4.0 %collective-permute-start.18 = (f32[16,8,128]{2,0,1:T(8,128)S(1)}, f32[16,8,128]{2,0,1:T(8,128)S(1)}, u32[]{:S(2)}, u32[]{:S(2)}) collective-permute-start(f32[16,8,128]{2,0,1:T(8,128)S(1)} %get-tuple-element.29), channel_id=1, source_target_pairs={{256,0},{384,1},{320,64},{448,65},{257,128},{385,129},{321,192},{4... | collective-permute-start | bytes 196616 | tf_op jit(solution)/shard_map/ppermute | solution.py:74
  144.7 2.6 %collective-permute-start.21 = (f32[16,8,128]{2,0,1:T(8,128)S(1)}, f32[16,8,128]{2,0,1:T(8,128)S(1)}, u32[]{:S(2)}, u32[]{:S(2)}) collective-permute-start(f32[16,8,128]{2,0,1:T(8,128)S(1)} %get-tuple-element.28), channel_id=1, source_target_pairs={{64,0},{192,1},{0,64},{128,65},{65,128},{193,129},{1,192},{129,193... | collective-permute-start | bytes 196616 | tf_op jit(solution)/shard_map/ppermute | solution.py:74
  147.3 8.6 %collective-permute-start.20 = (f32[16,8,128]{2,0,1:T(8,128)S(1)}, f32[16,8,128]{2,0,1:T(8,128)S(1)}, u32[]{:S(2)}, u32[]{:S(2)}) collective-permute-start(f32[16,8,128]{2,0,1:T(8,128)S(1)} %get-tuple-element.30), channel_id=1, source_target_pairs={{320,0},{448,1},{256,64},{384,65},{321,128},{449,129},{257,192},{3... | collective-permute-start | bytes 196616 | tf_op jit(solution)/shard_map/ppermute | solution.py:74
  155.9 2.9 %collective-permute-done.20 = f32[16,8,128]{2,0,1:T(8,128)S(1)} collective-permute-done((f32[16,8,128]{2,0,1:T(8,128)S(1)}, f32[16,8,128]{2,0,1:T(8,128)S(1)}, u32[]{:S(2)}, u32[]{:S(2)}) %collective-permute-start.20) | collective-permute-done | bytes 65568 | tf_op jit(solution)/shard_map/ppermute | solution.py:74
  158.9 0.7 copy.10
  (52 shorter events, 1.9 us)
Async XLA Ops:
  0.9 11.2 %collective-permute-start = (f32[16,8,128]{2,0,1:T(8,128)S(1)}, f32[16,8,128]{2,0,1:T(8,128)S(1)}, u32[]{:S(2)}, u32[]{:S(2)}) collective-permute-start(f32[16,8,128]{2,0,1:T(8,128)S(1)} %copy.33), channel_id=1, source_target_pairs={{0,0},{1,128},{64,64},{65,192},{128,1},{129,129},{192,65},{193,193... | collective-permute-start | bytes 196616 | tf_op jit(solution)/shard_map/ppermute | solution.py:74
  6.2 6.8 %collective-permute-start.1 = (f32[16,8,128]{2,0,1:T(8,128)S(1)}, f32[16,8,128]{2,0,1:T(8,128)S(1)}, u32[]{:S(2)}, u32[]{:S(2)}) collective-permute-start(f32[16,8,128]{2,0,1:T(8,128)S(1)} %copy.34), channel_id=1, source_target_pairs={{0,64},{1,192},{64,0},{65,128},{128,65},{129,193},{192,1},{193,129... | collective-permute-start | bytes 196616 | tf_op jit(solution)/shard_map/ppermute | solution.py:74
  13.0 17.8 %collective-permute-start.3 = (f32[16,64,128]{2,1,0:T(8,128)S(1)}, f32[16,64,128]{2,1,0:T(8,128)S(1)}, u32[]{:S(2)}, u32[]{:S(2)}) collective-permute-start(f32[16,64,128]{2,1,0:T(8,128)S(1)} %get-tuple-element.11), channel_id=1, source_target_pairs={{0,0},{1,128},{64,64},{65,192},{128,1},{129,129},{192,65},{193,193... | collective-permute-start | bytes 1572872 | tf_op jit(solution)/shard_map/ppermute | solution.py:74
  15.9 32.6 %copy-start.2 = (s32[8,16]{1,0:T(8,128)S(1)}, s32[8,16]{1,0:T(8,128)}, u32[]{:S(2)}) copy-start(s32[8,16]{1,0:T(8,128)} %param.7) | copy-start | bytes 1540
  16.4 14.4 %collective-permute-start.2 = (f32[16,16,128]{2,0,1:T(8,128)S(1)}, f32[16,16,128]{2,0,1:T(8,128)S(1)}, u32[]{:S(2)}, u32[]{:S(2)}) collective-permute-start(f32[16,16,128]{2,0,1:T(8,128)S(1)} %maximum_select_fusion), channel_id=1, source_target_pairs={{0,256},{1,257},{2,258},{3,259},{4,260},{5,261},{6,262},{7,263},{8... | collective-permute-start | bytes 393224 | tf_op jit(solution)/shard_map/ppermute | solution.py:74
  27.8 17.1 %collective-permute-start.6 = (f32[16,64,128]{2,1,0:T(8,128)S(1)}, f32[16,64,128]{2,1,0:T(8,128)S(1)}, u32[]{:S(2)}, u32[]{:S(2)}) collective-permute-start(f32[16,64,128]{2,1,0:T(8,128)S(1)} %get-tuple-element.14), channel_id=1, source_target_pairs={{0,64},{1,192},{64,0},{65,128},{128,65},{129,193},{192,1},{193,129... | collective-permute-start | bytes 1572872 | tf_op jit(solution)/shard_map/ppermute | solution.py:74
  30.8 12.4 %collective-permute-start.4 = (f32[16,32,128]{2,0,1:T(8,128)S(1)}, f32[16,32,128]{2,0,1:T(8,128)S(1)}, u32[]{:S(2)}, u32[]{:S(2)}) collective-permute-start(f32[16,32,128]{2,0,1:T(8,128)S(1)} %pad_maximum_fusion.3), channel_id=1, source_target_pairs={{64,128},{128,64},{65,129},{129,65},{192,194},{194,192},{193,195},... | collective-permute-start | bytes 786440 | tf_op jit(solution)/shard_map/ppermute | solution.py:74
  35.9 9.0 %collective-permute-start.5 = (f32[16,32,128]{2,0,1:T(8,128)S(1)}, f32[16,32,128]{2,0,1:T(8,128)S(1)}, u32[]{:S(2)}, u32[]{:S(2)}) collective-permute-start(f32[16,32,128]{2,0,1:T(8,128)S(1)} %pad_maximum_fusion.3), channel_id=1, source_target_pairs={{0,64},{64,0},{1,65},{65,1},{128,192},{192,128},{129,193},{193,129... | collective-permute-start | bytes 786440 | tf_op jit(solution)/shard_map/ppermute | solution.py:74
  45.0 6.9 %copy-start = (f32[16,64,128]{2,1,0:T(8,128)}, f32[16,64,128]{2,1,0:T(8,128)S(1)}, u32[]{:S(2)}) copy-start(f32[16,64,128]{2,1,0:T(8,128)S(1)} %collective-permute-done.6) | copy-start | bytes 1572868
  45.0 5.5 %collective-permute-start.7 = (f32[48,32,128]{2,0,1:T(8,128)S(1)}, f32[48,32,128]{2,0,1:T(8,128)S(1)}, u32[]{:S(2)}, u32[]{:S(2)}) collective-permute-start(f32[48,32,128]{2,0,1:T(8,128)S(1)} %pad_maximum_fusion.1), channel_id=1, source_target_pairs={{0,1},{1,0},{2,3},{3,2},{4,5},{5,4},{6,7},{7,6},{8,9},{9,8},{10,11... | collective-permute-start | bytes 2359304 | tf_op jit(solution)/shard_map/ppermute | solution.py:74
  55.1 4.2 %collective-permute-start.8 = (f32[48,32,128]{2,0,1:T(8,128)S(1)}, f32[48,32,128]{2,0,1:T(8,128)S(1)}, u32[]{:S(2)}, u32[]{:S(2)}) collective-permute-start(f32[48,32,128]{2,0,1:T(8,128)S(1)} %slice.107), channel_id=1, source_target_pairs={{0,1},{1,0},{2,3},{3,2},{4,5},{5,4},{6,7},{7,6},{8,9},{9,8},{10,11... | collective-permute-start | bytes 2359304 | tf_op jit(solution)/shard_map/ppermute | solution.py:74
  59.4 10.2 %collective-permute-start.10 = (f32[16,32,128]{2,0,1:T(8,128)S(1)}, f32[16,32,128]{2,0,1:T(8,128)S(1)}, u32[]{:S(2)}, u32[]{:S(2)}) collective-permute-start(f32[16,32,128]{2,0,1:T(8,128)S(1)} %get-tuple-element.26), channel_id=1, source_target_pairs={{0,64},{64,0},{1,65},{65,1},{128,192},{192,128},{129,193},{193,129... | collective-permute-start | bytes 786440 | tf_op jit(solution)/shard_map/ppermute | solution.py:74
  61.4 13.7 %collective-permute-start.9 = (f32[16,32,128]{2,0,1:T(8,128)S(1)}, f32[16,32,128]{2,0,1:T(8,128)S(1)}, u32[]{:S(2)}, u32[]{:S(2)}) collective-permute-start(f32[16,32,128]{2,0,1:T(8,128)S(1)} %get-tuple-element.25), channel_id=1, source_target_pairs={{64,128},{128,64},{65,129},{129,65},{192,194},{194,192},{193,195},... | collective-permute-start | bytes 786440 | tf_op jit(solution)/shard_map/ppermute | solution.py:74
  75.1 19.4 %collective-permute-start.11 = (f32[16,32,128]{2,0,1:T(8,128)S(1)}, f32[16,32,128]{2,0,1:T(8,128)S(1)}, u32[]{:S(2)}, u32[]{:S(2)}) collective-permute-start(f32[16,32,128]{2,0,1:T(8,128)S(1)} %fusion.27), channel_id=1, source_target_pairs={{0,256},{1,257},{2,258},{3,259},{4,260},{5,261},{6,262},{7,263},{8... | collective-permute-start | bytes 786440 | tf_op jit(solution)/shard_map/ppermute | solution.py:74
  95.2 12.0 %collective-permute-start.12 = (f32[16,32,128]{2,0,1:T(8,128)S(1)}, f32[16,32,128]{2,0,1:T(8,128)S(1)}, u32[]{:S(2)}, u32[]{:S(2)}) collective-permute-start(f32[16,32,128]{2,0,1:T(8,128)S(1)} %get-tuple-element.37), channel_id=1, source_target_pairs={{64,128},{128,64},{65,129},{129,65},{192,194},{194,192},{193,195},... | collective-permute-start | bytes 786440 | tf_op jit(solution)/shard_map/ppermute | solution.py:74
  100.8 9.0 %collective-permute-start.13 = (f32[16,32,128]{2,0,1:T(8,128)S(1)}, f32[16,32,128]{2,0,1:T(8,128)S(1)}, u32[]{:S(2)}, u32[]{:S(2)}) collective-permute-start(f32[16,32,128]{2,0,1:T(8,128)S(1)} %get-tuple-element.37), channel_id=1, source_target_pairs={{0,64},{64,0},{1,65},{65,1},{128,192},{192,128},{129,193},{193,129... | collective-permute-start | bytes 786440 | tf_op jit(solution)/shard_map/ppermute | solution.py:74
  109.9 5.5 %collective-permute-start.14 = (f32[48,32,128]{2,0,1:T(8,128)S(1)}, f32[48,32,128]{2,0,1:T(8,128)S(1)}, u32[]{:S(2)}, u32[]{:S(2)}) collective-permute-start(f32[48,32,128]{2,0,1:T(8,128)S(1)} %pad_maximum_fusion.2), channel_id=1, source_target_pairs={{0,1},{1,0},{2,3},{3,2},{4,5},{5,4},{6,7},{7,6},{8,9},{9,8},{10,11... | collective-permute-start | bytes 2359304 | tf_op jit(solution)/shard_map/ppermute | solution.py:74
  115.9 1.0 copy-start.1
  120.2 4.2 %collective-permute-start.15 = (f32[48,32,128]{2,0,1:T(8,128)S(1)}, f32[48,32,128]{2,0,1:T(8,128)S(1)}, u32[]{:S(2)}, u32[]{:S(2)}) collective-permute-start(f32[48,32,128]{2,0,1:T(8,128)S(1)} %slice.117), channel_id=1, source_target_pairs={{0,1},{1,0},{2,3},{3,2},{4,5},{5,4},{6,7},{7,6},{8,9},{9,8},{10,11... | collective-permute-start | bytes 2359304 | tf_op jit(solution)/shard_map/ppermute | solution.py:74
  124.5 12.1 %collective-permute-start.16 = (f32[16,32,128]{2,0,1:T(8,128)S(1)}, f32[16,32,128]{2,0,1:T(8,128)S(1)}, u32[]{:S(2)}, u32[]{:S(2)}) collective-permute-start(f32[16,32,128]{2,0,1:T(8,128)S(1)} %get-tuple-element.23), channel_id=1, source_target_pairs={{64,128},{128,64},{65,129},{129,65},{192,194},{194,192},{193,195},... | collective-permute-start | bytes 786440 | tf_op jit(solution)/shard_map/ppermute | solution.py:74
  128.0 9.1 %collective-permute-start.17 = (f32[16,32,128]{2,0,1:T(8,128)S(1)}, f32[16,32,128]{2,0,1:T(8,128)S(1)}, u32[]{:S(2)}, u32[]{:S(2)}) collective-permute-start(f32[16,32,128]{2,0,1:T(8,128)S(1)} %get-tuple-element.24), channel_id=1, source_target_pairs={{0,64},{64,0},{1,65},{65,1},{128,192},{192,128},{129,193},{193,129... | collective-permute-start | bytes 786440 | tf_op jit(solution)/shard_map/ppermute | solution.py:74
  137.2 18.7 %collective-permute-start.19 = (f32[16,8,128]{2,0,1:T(8,128)S(1)}, f32[16,8,128]{2,0,1:T(8,128)S(1)}, u32[]{:S(2)}, u32[]{:S(2)}) collective-permute-start(f32[16,8,128]{2,0,1:T(8,128)S(1)} %get-tuple-element.27), channel_id=1, source_target_pairs={{0,0},{128,1},{64,64},{192,65},{1,128},{129,129},{65,192},{193,193... | collective-permute-start | bytes 196616 | tf_op jit(solution)/shard_map/ppermute | solution.py:74
  140.7 15.2 %collective-permute-start.18 = (f32[16,8,128]{2,0,1:T(8,128)S(1)}, f32[16,8,128]{2,0,1:T(8,128)S(1)}, u32[]{:S(2)}, u32[]{:S(2)}) collective-permute-start(f32[16,8,128]{2,0,1:T(8,128)S(1)} %get-tuple-element.29), channel_id=1, source_target_pairs={{256,0},{384,1},{320,64},{448,65},{257,128},{385,129},{321,192},{4... | collective-permute-start | bytes 196616 | tf_op jit(solution)/shard_map/ppermute | solution.py:74
  144.7 11.2 %collective-permute-start.21 = (f32[16,8,128]{2,0,1:T(8,128)S(1)}, f32[16,8,128]{2,0,1:T(8,128)S(1)}, u32[]{:S(2)}, u32[]{:S(2)}) collective-permute-start(f32[16,8,128]{2,0,1:T(8,128)S(1)} %get-tuple-element.28), channel_id=1, source_target_pairs={{64,0},{192,1},{0,64},{128,65},{65,128},{193,129},{1,192},{129,193... | collective-permute-start | bytes 196616 | tf_op jit(solution)/shard_map/ppermute | solution.py:74
  147.3 11.6 %collective-permute-start.20 = (f32[16,8,128]{2,0,1:T(8,128)S(1)}, f32[16,8,128]{2,0,1:T(8,128)S(1)}, u32[]{:S(2)}, u32[]{:S(2)}) collective-permute-start(f32[16,8,128]{2,0,1:T(8,128)S(1)} %get-tuple-element.30), channel_id=1, source_target_pairs={{320,0},{448,1},{256,64},{384,65},{321,128},{449,129},{257,192},{3... | collective-permute-start | bytes 196616 | tf_op jit(solution)/shard_map/ppermute | solution.py:74

commit v3 on v1

v3 whole, which is shorter than its diff:
```python
import jax
import jax.numpy as jnp
from jax import lax
from jax.sharding import PartitionSpec as P

TX = 128
ITERS = 2
HIGH = lax.Precision.HIGH
HIGHEST = lax.Precision.HIGHEST
AXES = ("view", "col")
SLAB = 8
COLS = 64
SLABS = 256


def device(h, x, c):
    return (h * 4 + x) * COLS + c


def holder(h, d):
    column, rest = divmod(d, 8)
    p, core = divmod(rest, 2)
    return device(h, (p - column) % 4, 2 * column + core)


def spread_pairs(turn):
    return [
        (device(h, x, 2 * column + k), holder(h, 8 * column + 4 * k + (x + turn) % 4))
        for h in range(2)
        for column in range(COLS // 2)
        for x in range(4)
        for k in range(2)
    ]


def slab_swaps(step, members):
    pairs = []
    for h in range(2):
        for d in range(SLABS - step):
            if d % 4 in members:
                low, high = holder(h, d), holder(h, d + step)
                pairs += [(low, high), (high, low)]
    return pairs


SPREAD = [spread_pairs(turn) for turn in range(4)]
RETURN = [[(b, a) for a, b in pairs] for pairs in SPREAD]
SWAP_H = [(device(h, x, c), device(1 - h, x, c)) for h in range(2) for x in range(4) for c in range(COLS)]
NEAR = [slab_swaps(2, (2, 3)), slab_swaps(1, (1, 3)), slab_swaps(2, (0, 1)), slab_swaps(1, (0, 2))]


def send(value, pairs):
    return lax.ppermute(value, AXES, pairs)


def tap_matrix(kernel, taps):
    count = kernel.shape[1]
    onehot = (taps[:, :, None] == jnp.arange(count, dtype=jnp.int32)).astype(jnp.float32)
    return jnp.einsum("ijk,uk->uij", onehot, kernel, precision=HIGHEST)


def body(estimate, observed, psf_taps, intersection):
    rows = intersection.shape[1] * TX
    full_width = observed.shape[2]
    depth = observed.shape[3]
    block = estimate.shape[1]
    view_index = lax.axis_index("view")
    col_index = lax.axis_index("col")
    h, x = view_index // 4, view_index % 4
    column, core = col_index // 2, col_index % 2
    p = (x + column) % 4
    j = 2 * (p % 2) + core
    first_row = column * (8 * SLAB) + p * (2 * SLAB) + core * SLAB
    taps = psf_taps.shape[2]
    half = (taps - 1) // 2

    def piece(value, turn):
        return lax.dynamic_slice_in_dim(value, SLAB * ((x + turn) % 4), SLAB, 0)

    other = send(estimate, SWAP_H)
    paired = jnp.where(h == 0, jnp.concatenate([estimate, other], 1), jnp.concatenate([other, estimate], 1))
    est = [send(piece(paired, turn), SPREAD[turn]) for turn in range(4)]
    current = jnp.concatenate(est[::-1] + est[:0:-1], 1)
    current = lax.dynamic_slice_in_dim(current, 2 * block * ((3 - j) % 4), full_width, 1)
    images = [send(piece(observed[0], turn), SPREAD[turn]) for turn in range(4)]

    kernels = psf_taps / jnp.sum(psf_taps, axis=2, keepdims=True)
    views = jnp.arange(kernels.shape[0], dtype=jnp.int32)
    own_views = 4 * h + (j - jnp.arange(4, dtype=jnp.int32)) % 4
    picker = (own_views[:, None] == views[None, :]).astype(jnp.float32)
    own = jnp.einsum("uv,vdk->udk", picker, kernels, precision=HIGHEST)
    all_y = jnp.arange(full_width, dtype=jnp.int32)
    local_y = all_y // (2 * block) * block + all_y % (2 * block) // block * (full_width // 2) + all_y % block
    all_z = jnp.arange(depth, dtype=jnp.int32)
    slab = jnp.arange(SLAB, dtype=jnp.int32)
    two = jnp.where(p % 2 == 0, 2 * SLAB, -2 * SLAB)
    one = jnp.where(core == 0, SLAB, -SLAB)
    wide = jnp.concatenate([slab - two, slab - one, slab + two, slab + one, slab])
    mat_x = tap_matrix(own[:, 0], wide[None, :] - slab[:, None] + half)
    mat_y = tap_matrix(own[:, 1], local_y[None, :] - all_y[:, None] + half)
    mat_z = tap_matrix(own[:, 2], all_z[:, None] - all_z[None, :] + half)

    wide_rows = first_row + wide
    tile = (wide_rows // TX)[:, None] == jnp.arange(intersection.shape[1], dtype=jnp.int32)[None, :]
    tile = jnp.logical_and(tile, jnp.logical_and(wide_rows >= 0, wide_rows < rows)[:, None]).astype(jnp.float32)
    masks = jnp.einsum("vt,jt->vj", intersection.astype(jnp.float32), tile, precision=HIGHEST)
    weight_rows = jnp.einsum(
        "vrj,vj->vr", tap_matrix(kernels[:, 0], slab[:, None] - wide[None, :] + half), masks, precision=HIGHEST
    )

    def coverage(kernel, places, length):
        source = places[:, None] - jnp.arange(taps, dtype=jnp.int32)[None, :] + half
        inside = jnp.logical_and(source >= 0, source < length).astype(jnp.float32)
        return jnp.einsum("yk,vk->vy", inside, kernel, precision=HIGHEST)

    weight_cols = coverage(kernels[:, 1], local_y, full_width)
    weight_depth = coverage(kernels[:, 2], all_z, depth)
    weight_plane = weight_rows[:, :, None] * weight_cols[:, None, :]
    weights = jnp.einsum("vxy,vz->xyz", weight_plane, weight_depth, precision=HIGHEST)
    scale = 1.0 / (weights + 1.0)
    own_masks = jnp.einsum("uv,vj->uj", picker, masks[:, 4 * SLAB :], precision=HIGHEST)
    inside = own_masks[:, :, None, None] > 0

    def own_half(value, mine):
        blocks = value.reshape(SLAB, 4, 2, block, depth)
        return jnp.where((h == 0) == mine, blocks[:, :, 0], blocks[:, :, 1])

    for iteration in range(ITERS):
        extended = jnp.concatenate([send(current, pairs) for pairs in NEAR] + [current], 0)
        if iteration == 0:
            *images, extended = lax.optimization_barrier((*images, extended))
            images = jnp.stack(images)
        blurred = jnp.einsum("urj,jyz->uryz", mat_x, extended, precision=HIGH)
        blurred = jnp.einsum("urjz,uyj->uryz", blurred, mat_y, precision=HIGH)
        blurred = jnp.einsum("uryz,uzw->uryw", blurred, mat_z, precision=HIGH)
        ratio = jnp.where(inside, images / jnp.where(inside, blurred, 1.0), 0.0)
        back = jnp.einsum("uryw,uzw->uryz", ratio, mat_z, precision=HIGH)
        back = jnp.einsum("uryz,uyj->urjz", back, mat_y, precision=HIGH)
        back = jnp.einsum("urj,uryz->jyz", mat_x, back, precision=HIGH)
        part = back[4 * SLAB :]
        for place, pairs in enumerate(NEAR):
            part = part + send(back[place * SLAB : (place + 1) * SLAB], pairs)
        if iteration < ITERS - 1:
            current = current * (part + send(part, SWAP_H) + 1.0) * scale
        else:
            total = own_half(part, True) + send(own_half(part, False), SWAP_H)
            result = own_half(current, True) * (total + 1.0) * own_half(scale, True)

    pieces = [
        send(lax.dynamic_index_in_dim(result, (j - turn) % 4, 1, keepdims=False), RETURN[turn])
        for turn in range(4)
    ]
    joined = jnp.concatenate(pieces + pieces[:3], 0)
    return lax.dynamic_slice_in_dim(joined, SLAB * ((4 - x) % 4), 4 * SLAB, 0)


def solution(mesh):
    return jax.shard_map(
        body,
        mesh=mesh,
        in_specs=(P("col", "view", None), P("view", "col", None, None), P(), P()),
        out_specs=P("col", "view", None),
        check_vma=False,
    )
```

time: 168 us -> 183 us (1.089)
  the two profiles are of different devices: /device:TPU:32 before, /device:TPU:57 now
where the time goes in v3:
time: 183 us; the launch traced here: 181 us
  starting transfers between devices  114 us (62%)
  waiting for transfers between devices  43.4 us (24%)
  matrix products  14.8 us (8%)
  local copies, waits for them, and re-layouts  6.05 us (3%)
    ppermute x31, starting transfers between devices, send(): return lax.ppermute(value, AXES, pairs)  114 us
    ppermute x31, waiting for transfers between devices, send(): return lax.ppermute(value, AXES, pairs)  43.4 us
  transfers between devices with their start and end apart: 31, of which 13 were waited for; matrix products, arithmetic and copies ran while one was open for 3% of the time, Pallas kernels for 0%

profile of v3, /device:TPU:57, one launch (start us, length us, event | category | flops | bytes accessed | tf_op | source)
XLA Modules:
  0.0 181.2 jit_solution(12561036017453424120)
XLA Ops:
  0.0 0.9 copy.6
  1.0 10.6 %collective-permute-start = (f32[32,8,128]{2,0,1:T(8,128)S(1)}, f32[32,8,128]{2,0,1:T(8,128)S(1)}, u32[]{:S(2)}, u32[]{:S(2)}) collective-permute-start(f32[32,8,128]{2,0,1:T(8,128)S(1)} %copy.6), channel_id=1, source_target_pairs={{0,256},{1,257},{2,258},{3,259},{4,260},{5,261},{6,262},{7,263},{8... | collective-permute-start | bytes 393224 | tf_op jit(solution)/shard_map/ppermute | solution.py:53
  11.7 1.3 dynamic-slice_bitcast_fusion
  13.0 5.5 %collective-permute-start.5 = (f32[8,64,128]{2,1,0:T(8,128)S(1)}, f32[8,64,128]{2,1,0:T(8,128)}, u32[]{:S(2)}, u32[]{:S(2)}) collective-permute-start(f32[8,64,128]{2,1,0:T(8,128)S(1)} %get-tuple-element.25), channel_id=1, source_target_pairs={{0,0},{1,128},{64,1},{65,129},{128,64},{129,192},{192,65},{193,193... | collective-permute-start | bytes 786440 | tf_op jit(solution)/shard_map/ppermute | solution.py:53
  18.5 2.8 %collective-permute-start.6 = (f32[8,64,128]{2,1,0:T(8,128)S(1)}, f32[8,64,128]{2,1,0:T(8,128)}, u32[]{:S(2)}, u32[]{:S(2)}) collective-permute-start(f32[8,64,128]{2,1,0:T(8,128)S(1)} %get-tuple-element.24), channel_id=1, source_target_pairs={{0,1},{1,129},{64,64},{65,192},{128,65},{129,193},{192,0},{193,128... | collective-permute-start | bytes 786440 | tf_op jit(solution)/shard_map/ppermute | solution.py:53
  22.0 0.4 fusion.25
  23.1 1.9 %collective-permute-start.1 = (f32[8,16,128]{2,0,1:T(8,128)S(1)}, f32[8,16,128]{2,0,1:T(8,128)S(1)}, u32[]{:S(2)}, u32[]{:S(2)}) collective-permute-start(f32[8,16,128]{2,0,1:T(8,128)S(1)} %get-tuple-element.30), channel_id=1, source_target_pairs={{0,65},{1,193},{64,0},{65,128},{128,1},{129,129},{192,64},{193,192... | collective-permute-start | bytes 196616 | tf_op jit(solution)/shard_map/ppermute | solution.py:53
  25.2 1.9 %collective-permute-start.2 = (f32[8,16,128]{2,0,1:T(8,128)S(1)}, f32[8,16,128]{2,0,1:T(8,128)S(1)}, u32[]{:S(2)}, u32[]{:S(2)}) collective-permute-start(f32[8,16,128]{2,0,1:T(8,128)S(1)} %get-tuple-element.29), channel_id=1, source_target_pairs={{0,64},{1,192},{64,65},{65,193},{128,0},{129,128},{192,1},{193,129... | collective-permute-start | bytes 196616 | tf_op jit(solution)/shard_map/ppermute | solution.py:53
  27.1 5.2 %collective-permute-start.3 = (f32[8,16,128]{2,0,1:T(8,128)S(1)}, f32[8,16,128]{2,0,1:T(8,128)S(1)}, u32[]{:S(2)}, u32[]{:S(2)}) collective-permute-start(f32[8,16,128]{2,0,1:T(8,128)S(1)} %get-tuple-element.28), channel_id=1, source_target_pairs={{0,1},{1,129},{64,64},{65,192},{128,65},{129,193},{192,0},{193,128... | collective-permute-start | bytes 196616 | tf_op jit(solution)/shard_map/ppermute | solution.py:53
  32.4 2.0 %collective-permute-start.4 = (f32[8,16,128]{2,0,1:T(8,128)S(1)}, f32[8,16,128]{2,0,1:T(8,128)S(1)}, u32[]{:S(2)}, u32[]{:S(2)}) collective-permute-start(f32[8,16,128]{2,0,1:T(8,128)S(1)} %get-tuple-element.27), channel_id=1, source_target_pairs={{0,0},{1,128},{64,1},{65,129},{128,64},{129,192},{192,65},{193,193... | collective-permute-start | bytes 196616 | tf_op jit(solution)/shard_map/ppermute | solution.py:53
  34.5 3.5 %collective-permute-done.4 = f32[8,16,128]{2,0,1:T(8,128)S(1)} collective-permute-done((f32[8,16,128]{2,0,1:T(8,128)S(1)}, f32[8,16,128]{2,0,1:T(8,128)S(1)}, u32[]{:S(2)}, u32[]{:S(2)}) %collective-permute-start.4) | collective-permute-done | bytes 65568 | tf_op jit(solution)/shard_map/ppermute | solution.py:53
  38.1 5.9 %collective-permute-start.9 = (f32[8,64,128]{2,0,1:T(8,128)S(1)}, f32[8,64,128]{2,0,1:T(8,128)S(1)}, u32[]{:S(2)}, u32[]{:S(2)}) collective-permute-start(f32[8,64,128]{2,0,1:T(8,128)S(1)} %constant_dynamic-slice_fusion.5), channel_id=1, source_target_pairs={{64,128},{128,64},{65,129},{129,65},{192,194},{194,192},{193,195},... | collective-permute-start | bytes 786440 | tf_op jit(solution)/shard_map/ppermute | solution.py:53
  44.0 1.9 %collective-permute-start.10 = (f32[8,64,128]{2,0,1:T(8,128)S(1)}, f32[8,64,128]{2,0,1:T(8,128)S(1)}, u32[]{:S(2)}, u32[]{:S(2)}) collective-permute-start(f32[8,64,128]{2,0,1:T(8,128)S(1)} %constant_dynamic-slice_fusion.5), channel_id=1, source_target_pairs={{1,64},{64,1},{65,128},{128,65},{129,192},{192,129},{193,194},{194... | collective-permute-start | bytes 786440 | tf_op jit(solution)/shard_map/ppermute | solution.py:53
  45.9 0.8 fusion.9
  46.7 1.9 %collective-permute-start.11 = (f32[8,64,128]{2,0,1:T(8,128)S(1)}, f32[8,64,128]{2,0,1:T(8,128)S(1)}, u32[]{:S(2)}, u32[]{:S(2)}) collective-permute-start(f32[8,64,128]{2,0,1:T(8,128)S(1)} %constant_dynamic-slice_fusion.5), channel_id=1, source_target_pairs={{0,64},{64,0},{1,65},{65,1},{128,192},{192,128},{129,193},{193,129... | collective-permute-start | bytes 786440 | tf_op jit(solution)/shard_map/ppermute | solution.py:53
  48.6 0.4 convolution_bitcast_fusion.6
  49.3 1.4 collective-permute-done.9
  50.7 2.6 %collective-permute-start.12 = (f32[8,64,128]{2,0,1:T(8,128)S(1)}, f32[8,64,128]{2,0,1:T(8,128)S(1)}, u32[]{:S(2)}, u32[]{:S(2)}) collective-permute-start(f32[8,64,128]{2,0,1:T(8,128)S(1)} %constant_dynamic-slice_fusion.5), channel_id=1, source_target_pairs={{0,1},{1,0},{64,65},{65,64},{128,129},{129,128},{192,193},{193,192... | collective-permute-start | bytes 786440 | tf_op jit(solution)/shard_map/ppermute | solution.py:53
  53.4 1.9 %collective-permute-start.7 = (f32[8,64,128]{2,1,0:T(8,128)S(1)}, f32[8,64,128]{2,1,0:T(8,128)S(1)}, u32[]{:S(2)}, u32[]{:S(2)}) collective-permute-start(f32[8,64,128]{2,1,0:T(8,128)S(1)} %get-tuple-element.26), channel_id=1, source_target_pairs={{0,64},{1,192},{64,65},{65,193},{128,0},{129,128},{192,1},{193,129... | collective-permute-start | bytes 786440 | tf_op jit(solution)/shard_map/ppermute | solution.py:53
  55.3 1.6 collective-permute-done.11
  56.9 1.9 %collective-permute-start.8 = (f32[8,64,128]{2,1,0:T(8,128)S(1)}, f32[8,64,128]{2,1,0:T(8,128)S(1)}, u32[]{:S(2)}, u32[]{:S(2)}) collective-permute-start(f32[8,64,128]{2,1,0:T(8,128)S(1)} %get-tuple-element.23), channel_id=1, source_target_pairs={{0,65},{1,193},{64,0},{65,128},{128,1},{129,129},{192,64},{193,192... | collective-permute-start | bytes 786440 | tf_op jit(solution)/shard_map/ppermute | solution.py:53
  59.0 8.9 %collective-permute-done.7 = f32[8,64,128]{2,1,0:T(8,128)S(1)} collective-permute-done((f32[8,64,128]{2,1,0:T(8,128)S(1)}, f32[8,64,128]{2,1,0:T(8,128)S(1)}, u32[]{:S(2)}, u32[]{:S(2)}) %collective-permute-start.7) | collective-permute-done | bytes 262176 | tf_op jit(solution)/shard_map/ppermute | solution.py:53
  67.9 0.8 fusion.7
  68.7 0.6 convolution_bitcast_fusion.5
  69.3 1.7 fusion.2
  71.0 0.6 fusion.84
  71.5 0.6 convolution_bitcast_fusion.4
  72.1 1.6 convolution_bitcast_fusion.1
  73.7 0.9 fusion.83
  74.6 1.9 %collective-permute-start.13 = (f32[8,64,128]{2,0,1:T(8,128)}, f32[8,64,128]{2,0,1:T(8,128)S(1)}, u32[]{:S(2)}, u32[]{:S(2)}) collective-permute-start(f32[8,64,128]{2,0,1:T(8,128)} %get-tuple-element.19), channel_id=1, source_target_pairs={{64,128},{128,64},{65,129},{129,65},{192,194},{194,192},{193,195},... | collective-permute-start | bytes 786440 | tf_op jit(solution)/shard_map/ppermute | solution.py:53
  76.5 1.9 %collective-permute-start.14 = (f32[8,64,128]{2,0,1:T(8,128)}, f32[8,64,128]{2,0,1:T(8,128)S(1)}, u32[]{:S(2)}, u32[]{:S(2)}) collective-permute-start(f32[8,64,128]{2,0,1:T(8,128)} %get-tuple-element.22), channel_id=1, source_target_pairs={{1,64},{64,1},{65,128},{128,65},{129,192},{192,129},{193,194},{194... | collective-permute-start | bytes 786440 | tf_op jit(solution)/shard_map/ppermute | solution.py:53
  78.5 3.3 %collective-permute-start.15 = (f32[8,64,128]{2,0,1:T(8,128)}, f32[8,64,128]{2,0,1:T(8,128)}, u32[]{:S(2)}, u32[]{:S(2)}) collective-permute-start(f32[8,64,128]{2,0,1:T(8,128)} %get-tuple-element.21), channel_id=1, source_target_pairs={{0,64},{64,0},{1,65},{65,1},{128,192},{192,128},{129,193},{193,129... | collective-permute-start | bytes 786440 | tf_op jit(solution)/shard_map/ppermute | solution.py:53
  81.8 5.1 %collective-permute-start.16 = (f32[8,64,128]{2,0,1:T(8,128)S(1)}, f32[8,64,128]{2,0,1:T(8,128)}, u32[]{:S(2)}, u32[]{:S(2)}) collective-permute-start(f32[8,64,128]{2,0,1:T(8,128)S(1)} %get-tuple-element.20), channel_id=1, source_target_pairs={{0,1},{1,0},{64,65},{65,64},{128,129},{129,128},{192,193},{193,192... | collective-permute-start | bytes 786440 | tf_op jit(solution)/shard_map/ppermute | solution.py:53
  87.6 0.6 collective-permute-done.16
  88.1 1.1 fusion.22
  89.2 2.2 %collective-permute-start.17 = (f32[8,64,128]{2,0,1:T(8,128)S(1)}, f32[8,64,128]{2,0,1:T(8,128)S(1)}, u32[]{:S(2)}, u32[]{:S(2)}) collective-permute-start(f32[8,64,128]{2,0,1:T(8,128)S(1)} %fusion.22), channel_id=1, source_target_pairs={{0,256},{1,257},{2,258},{3,259},{4,260},{5,261},{6,262},{7,263},{8... | collective-permute-start | bytes 786440 | tf_op jit(solution)/shard_map/ppermute | solution.py:53
  92.1 8.2 %collective-permute-done.17 = f32[8,64,128]{2,0,1:T(8,128)S(1)} collective-permute-done((f32[8,64,128]{2,0,1:T(8,128)S(1)}, f32[8,64,128]{2,0,1:T(8,128)S(1)}, u32[]{:S(2)}, u32[]{:S(2)}) %collective-permute-start.17) | collective-permute-done | bytes 262176 | tf_op jit(solution)/shard_map/ppermute | solution.py:53
  100.4 15.6 %collective-permute-start.18 = (f32[8,64,128]{2,0,1:T(8,128)S(1)}, f32[8,64,128]{2,0,1:T(8,128)S(1)}, u32[]{:S(2)}, u32[]{:S(2)}) collective-permute-start(f32[8,64,128]{2,0,1:T(8,128)S(1)} %multiply_multiply_fusion), channel_id=1, source_target_pairs={{64,128},{128,64},{65,129},{129,65},{192,194},{194,192},{193,195},... | collective-permute-start | bytes 786440 | tf_op jit(solution)/shard_map/ppermute | solution.py:53
  116.1 1.9 %collective-permute-start.19 = (f32[8,64,128]{2,0,1:T(8,128)S(1)}, f32[8,64,128]{2,0,1:T(8,128)S(1)}, u32[]{:S(2)}, u32[]{:S(2)}) collective-permute-start(f32[8,64,128]{2,0,1:T(8,128)S(1)} %multiply_multiply_fusion), channel_id=1, source_target_pairs={{1,64},{64,1},{65,128},{128,65},{129,192},{192,129},{193,194},{194... | collective-permute-start | bytes 786440 | tf_op jit(solution)/shard_map/ppermute | solution.py:53
  118.0 1.9 %collective-permute-start.20 = (f32[8,64,128]{2,0,1:T(8,128)S(1)}, f32[8,64,128]{2,0,1:T(8,128)S(1)}, u32[]{:S(2)}, u32[]{:S(2)}) collective-permute-start(f32[8,64,128]{2,0,1:T(8,128)S(1)} %multiply_multiply_fusion), channel_id=1, source_target_pairs={{0,64},{64,0},{1,65},{65,1},{128,192},{192,128},{129,193},{193,129... | collective-permute-start | bytes 786440 | tf_op jit(solution)/shard_map/ppermute | solution.py:53
  119.9 4.2 %collective-permute-start.21 = (f32[8,64,128]{2,0,1:T(8,128)S(1)}, f32[8,64,128]{2,0,1:T(8,128)S(1)}, u32[]{:S(2)}, u32[]{:S(2)}) collective-permute-start(f32[8,64,128]{2,0,1:T(8,128)S(1)} %multiply_multiply_fusion), channel_id=1, source_target_pairs={{0,1},{1,0},{64,65},{65,64},{128,129},{129,128},{192,193},{193,192... | collective-permute-start | bytes 786440 | tf_op jit(solution)/shard_map/ppermute | solution.py:53
  124.2 1.3 collective-permute-done.19
  125.5 2.8 %collective-permute-done.20 = f32[8,64,128]{2,0,1:T(8,128)S(1)} collective-permute-done((f32[8,64,128]{2,0,1:T(8,128)S(1)}, f32[8,64,128]{2,0,1:T(8,128)S(1)}, u32[]{:S(2)}, u32[]{:S(2)}) %collective-permute-start.20) | collective-permute-done | bytes 262176 | tf_op jit(solution)/shard_map/ppermute | solution.py:53
  128.3 0.8 fusion.5
  129.1 0.6 convolution_bitcast_fusion.3
  130.1 1.7 fusion.4
  131.8 0.6 fusion.85
  132.4 0.6 convolution_bitcast_fusion.2
  133.0 1.6 convolution_bitcast_fusion
  134.6 0.9 fusion.82
  135.4 5.4 %collective-permute-start.22 = (f32[8,64,128]{2,0,1:T(8,128)}, f32[8,64,128]{2,0,1:T(8,128)S(1)}, u32[]{:S(2)}, u32[]{:S(2)}) collective-permute-start(f32[8,64,128]{2,0,1:T(8,128)} %get-tuple-element.15), channel_id=1, source_target_pairs={{64,128},{128,64},{65,129},{129,65},{192,194},{194,192},{193,195},... | collective-permute-start | bytes 786440 | tf_op jit(solution)/shard_map/ppermute | solution.py:53
  140.8 1.9 %collective-permute-start.23 = (f32[8,64,128]{2,0,1:T(8,128)}, f32[8,64,128]{2,0,1:T(8,128)S(1)}, u32[]{:S(2)}, u32[]{:S(2)}) collective-permute-start(f32[8,64,128]{2,0,1:T(8,128)} %get-tuple-element.18), channel_id=1, source_target_pairs={{1,64},{64,1},{65,128},{128,65},{129,192},{192,129},{193,194},{194... | collective-permute-start | bytes 786440 | tf_op jit(solution)/shard_map/ppermute | solution.py:53
  142.8 1.9 %collective-permute-start.24 = (f32[8,64,128]{2,0,1:T(8,128)S(1)}, f32[8,64,128]{2,0,1:T(8,128)S(1)}, u32[]{:S(2)}, u32[]{:S(2)}) collective-permute-start(f32[8,64,128]{2,0,1:T(8,128)S(1)} %get-tuple-element.17), channel_id=1, source_target_pairs={{0,64},{64,0},{1,65},{65,1},{128,192},{192,128},{129,193},{193,129... | collective-permute-start | bytes 786440 | tf_op jit(solution)/shard_map/ppermute | solution.py:53
  144.7 4.0 %collective-permute-start.25 = (f32[8,64,128]{2,0,1:T(8,128)S(1)}, f32[8,64,128]{2,0,1:T(8,128)S(1)}, u32[]{:S(2)}, u32[]{:S(2)}) collective-permute-start(f32[8,64,128]{2,0,1:T(8,128)S(1)} %get-tuple-element.16), channel_id=1, source_target_pairs={{0,1},{1,0},{64,65},{65,64},{128,129},{129,128},{192,193},{193,192... | collective-permute-start | bytes 786440 | tf_op jit(solution)/shard_map/ppermute | solution.py:53
  148.7 1.9 %collective-permute-done.23 = f32[8,64,128]{2,0,1:T(8,128)S(1)} collective-permute-done((f32[8,64,128]{2,0,1:T(8,128)}, f32[8,64,128]{2,0,1:T(8,128)S(1)}, u32[]{:S(2)}, u32[]{:S(2)}) %collective-permute-start.23) | collective-permute-done | bytes 262176 | tf_op jit(solution)/shard_map/ppermute | solution.py:53
  150.7 2.3 %collective-permute-done.24 = f32[8,64,128]{2,0,1:T(8,128)S(1)} collective-permute-done((f32[8,64,128]{2,0,1:T(8,128)S(1)}, f32[8,64,128]{2,0,1:T(8,128)S(1)}, u32[]{:S(2)}, u32[]{:S(2)}) %collective-permute-start.24) | collective-permute-done | bytes 262176 | tf_op jit(solution)/shard_map/ppermute | solution.py:53
  153.1 2.9 %collective-permute-start.26 = (f32[8,4,8,128]{3,0,2,1:T(8,128)S(1)}, f32[8,4,8,128]{3,0,2,1:T(8,128)S(1)}, u32[]{:S(2)}, u32[]{:S(2)}) collective-permute-start(f32[8,4,8,128]{3,0,2,1:T(8,128)S(1)} %select_bitcast_fusion), channel_id=1, source_target_pairs={{0,256},{1,257},{2,258},{3,259},{4,260},{5,261},{6,262},{7,263},{8... | collective-permute-start | bytes 393224 | tf_op jit(solution)/shard_map/ppermute | solution.py:53
  156.0 6.7 %collective-permute-done.26 = f32[8,4,8,128]{3,0,2,1:T(8,128)S(1)} collective-permute-done((f32[8,4,8,128]{3,0,2,1:T(8,128)S(1)}, f32[8,4,8,128]{3,0,2,1:T(8,128)S(1)}, u32[]{:S(2)}, u32[]{:S(2)}) %collective-permute-start.26) | collective-permute-done | bytes 131104 | tf_op jit(solution)/shard_map/ppermute | solution.py:53
  162.8 4.4 %collective-permute-start.27 = (f32[8,8,128]{2,1,0:T(8,128)S(1)}, f32[8,8,128]{2,1,0:T(8,128)S(1)}, u32[]{:S(2)}, u32[]{:S(2)}) collective-permute-start(f32[8,8,128]{2,1,0:T(8,128)S(1)} %bitcast.163), channel_id=1, source_target_pairs={{0,0},{128,1},{1,64},{129,65},{64,128},{192,129},{65,192},{193,193... | collective-permute-start | bytes 98312 | tf_op jit(solution)/shard_map/ppermute | solution.py:53
  167.3 1.9 %collective-permute-start.28 = (f32[8,8,128]{2,1,0:T(8,128)S(1)}, f32[8,8,128]{2,1,0:T(8,128)S(1)}, u32[]{:S(2)}, u32[]{:S(2)}) collective-permute-start(f32[8,8,128]{2,1,0:T(8,128)S(1)} %bitcast.164), channel_id=1, source_target_pairs={{1,0},{129,1},{64,64},{192,65},{65,128},{193,129},{0,192},{128,193... | collective-permute-start | bytes 98312 | tf_op jit(solution)/shard_map/ppermute | solution.py:53
  169.2 5.3 %collective-permute-start.29 = (f32[8,8,128]{2,1,0:T(8,128)S(1)}, f32[8,8,128]{2,1,0:T(8,128)S(1)}, u32[]{:S(2)}, u32[]{:S(2)}) collective-permute-start(f32[8,8,128]{2,1,0:T(8,128)S(1)} %bitcast.165), channel_id=1, source_target_pairs={{64,0},{192,1},{65,64},{193,65},{0,128},{128,129},{1,192},{129,193... | collective-permute-start | bytes 98312 | tf_op jit(solution)/shard_map/ppermute | solution.py:53
  174.6 1.9 %collective-permute-start.30 = (f32[8,8,128]{2,1,0:T(8,128)S(1)}, f32[8,8,128]{2,1,0:T(8,128)S(1)}, u32[]{:S(2)}, u32[]{:S(2)}) collective-permute-start(f32[8,8,128]{2,1,0:T(8,128)S(1)} %bitcast.166), channel_id=1, source_target_pairs={{65,0},{193,1},{0,64},{128,65},{1,128},{129,129},{64,192},{192,193... | collective-permute-start | bytes 98312 | tf_op jit(solution)/shard_map/ppermute | solution.py:53
  176.6 3.9 %collective-permute-done.30 = f32[8,8,128]{2,1,0:T(8,128)S(1)} collective-permute-done((f32[8,8,128]{2,1,0:T(8,128)S(1)}, f32[8,8,128]{2,1,0:T(8,128)S(1)}, u32[]{:S(2)}, u32[]{:S(2)}) %collective-permute-start.30) | collective-permute-done | bytes 32800 | tf_op jit(solution)/shard_map/ppermute | solution.py:53
  180.5 0.7 constant_dynamic-slice_fusion
  (93 shorter events, 3.9 us)
Async XLA Ops:
  0.0 21.6 %copy-start = (f32[8,3,31]{2,0,1:T(8,128)S(1)}, f32[8,3,31]{2,0,1:T(8,128)}, u32[]{:S(2)}) copy-start(f32[8,3,31]{2,0,1:T(8,128)} %param.6) | copy-start | bytes 8932
  0.9 21.5 %copy-start.5 = (s32[8,16]{1,0:T(8,128)S(1)}, s32[8,16]{1,0:T(8,128)}, u32[]{:S(2)}) copy-start(s32[8,16]{1,0:T(8,128)} %param.7) | copy-start | bytes 1540
  1.0 22.0 %collective-permute-start = (f32[32,8,128]{2,0,1:T(8,128)S(1)}, f32[32,8,128]{2,0,1:T(8,128)S(1)}, u32[]{:S(2)}, u32[]{:S(2)}) collective-permute-start(f32[32,8,128]{2,0,1:T(8,128)S(1)} %copy.6), channel_id=1, source_target_pairs={{0,256},{1,257},{2,258},{3,259},{4,260},{5,261},{6,262},{7,263},{8... | collective-permute-start | bytes 393224 | tf_op jit(solution)/shard_map/ppermute | solution.py:53
  13.0 46.0 %collective-permute-start.5 = (f32[8,64,128]{2,1,0:T(8,128)S(1)}, f32[8,64,128]{2,1,0:T(8,128)}, u32[]{:S(2)}, u32[]{:S(2)}) collective-permute-start(f32[8,64,128]{2,1,0:T(8,128)S(1)} %get-tuple-element.25), channel_id=1, source_target_pairs={{0,0},{1,128},{64,1},{65,129},{128,64},{129,192},{192,65},{193,193... | collective-permute-start | bytes 786440 | tf_op jit(solution)/shard_map/ppermute | solution.py:53
  18.5 40.5 %collective-permute-start.6 = (f32[8,64,128]{2,1,0:T(8,128)S(1)}, f32[8,64,128]{2,1,0:T(8,128)}, u32[]{:S(2)}, u32[]{:S(2)}) collective-permute-start(f32[8,64,128]{2,1,0:T(8,128)S(1)} %get-tuple-element.24), channel_id=1, source_target_pairs={{0,1},{1,129},{64,64},{65,192},{128,65},{129,193},{192,0},{193,128... | collective-permute-start | bytes 786440 | tf_op jit(solution)/shard_map/ppermute | solution.py:53
  23.1 9.3 %collective-permute-start.1 = (f32[8,16,128]{2,0,1:T(8,128)S(1)}, f32[8,16,128]{2,0,1:T(8,128)S(1)}, u32[]{:S(2)}, u32[]{:S(2)}) collective-permute-start(f32[8,16,128]{2,0,1:T(8,128)S(1)} %get-tuple-element.30), channel_id=1, source_target_pairs={{0,65},{1,193},{64,0},{65,128},{128,1},{129,129},{192,64},{193,192... | collective-permute-start | bytes 196616 | tf_op jit(solution)/shard_map/ppermute | solution.py:53
  25.2 9.3 %collective-permute-start.2 = (f32[8,16,128]{2,0,1:T(8,128)S(1)}, f32[8,16,128]{2,0,1:T(8,128)S(1)}, u32[]{:S(2)}, u32[]{:S(2)}) collective-permute-start(f32[8,16,128]{2,0,1:T(8,128)S(1)} %get-tuple-element.29), channel_id=1, source_target_pairs={{0,64},{1,192},{64,65},{65,193},{128,0},{129,128},{192,1},{193,129... | collective-permute-start | bytes 196616 | tf_op jit(solution)/shard_map/ppermute | solution.py:53
  27.1 7.4 %collective-permute-start.3 = (f32[8,16,128]{2,0,1:T(8,128)S(1)}, f32[8,16,128]{2,0,1:T(8,128)S(1)}, u32[]{:S(2)}, u32[]{:S(2)}) collective-permute-start(f32[8,16,128]{2,0,1:T(8,128)S(1)} %get-tuple-element.28), channel_id=1, source_target_pairs={{0,1},{1,129},{64,64},{65,192},{128,65},{129,193},{192,0},{193,128... | collective-permute-start | bytes 196616 | tf_op jit(solution)/shard_map/ppermute | solution.py:53
  32.4 5.6 %collective-permute-start.4 = (f32[8,16,128]{2,0,1:T(8,128)S(1)}, f32[8,16,128]{2,0,1:T(8,128)S(1)}, u32[]{:S(2)}, u32[]{:S(2)}) collective-permute-start(f32[8,16,128]{2,0,1:T(8,128)S(1)} %get-tuple-element.27), channel_id=1, source_target_pairs={{0,0},{1,128},{64,1},{65,129},{128,64},{129,192},{192,65},{193,193... | collective-permute-start | bytes 196616 | tf_op jit(solution)/shard_map/ppermute | solution.py:53
  38.1 12.6 %collective-permute-start.9 = (f32[8,64,128]{2,0,1:T(8,128)S(1)}, f32[8,64,128]{2,0,1:T(8,128)S(1)}, u32[]{:S(2)}, u32[]{:S(2)}) collective-permute-start(f32[8,64,128]{2,0,1:T(8,128)S(1)} %constant_dynamic-slice_fusion.5), channel_id=1, source_target_pairs={{64,128},{128,64},{65,129},{129,65},{192,194},{194,192},{193,195},... | collective-permute-start | bytes 786440 | tf_op jit(solution)/shard_map/ppermute | solution.py:53
  44.0 9.4 %collective-permute-start.10 = (f32[8,64,128]{2,0,1:T(8,128)S(1)}, f32[8,64,128]{2,0,1:T(8,128)S(1)}, u32[]{:S(2)}, u32[]{:S(2)}) collective-permute-start(f32[8,64,128]{2,0,1:T(8,128)S(1)} %constant_dynamic-slice_fusion.5), channel_id=1, source_target_pairs={{1,64},{64,1},{65,128},{128,65},{129,192},{192,129},{193,194},{194... | collective-permute-start | bytes 786440 | tf_op jit(solution)/shard_map/ppermute | solution.py:53
  46.7 10.3 %collective-permute-start.11 = (f32[8,64,128]{2,0,1:T(8,128)S(1)}, f32[8,64,128]{2,0,1:T(8,128)S(1)}, u32[]{:S(2)}, u32[]{:S(2)}) collective-permute-start(f32[8,64,128]{2,0,1:T(8,128)S(1)} %constant_dynamic-slice_fusion.5), channel_id=1, source_target_pairs={{0,64},{64,0},{1,65},{65,1},{128,192},{192,128},{129,193},{193,129... | collective-permute-start | bytes 786440 | tf_op jit(solution)/shard_map/ppermute | solution.py:53
  50.7 8.2 %collective-permute-start.12 = (f32[8,64,128]{2,0,1:T(8,128)S(1)}, f32[8,64,128]{2,0,1:T(8,128)S(1)}, u32[]{:S(2)}, u32[]{:S(2)}) collective-permute-start(f32[8,64,128]{2,0,1:T(8,128)S(1)} %constant_dynamic-slice_fusion.5), channel_id=1, source_target_pairs={{0,1},{1,0},{64,65},{65,64},{128,129},{129,128},{192,193},{193,192... | collective-permute-start | bytes 786440 | tf_op jit(solution)/shard_map/ppermute | solution.py:53
  53.4 14.5 %collective-permute-start.7 = (f32[8,64,128]{2,1,0:T(8,128)S(1)}, f32[8,64,128]{2,1,0:T(8,128)S(1)}, u32[]{:S(2)}, u32[]{:S(2)}) collective-permute-start(f32[8,64,128]{2,1,0:T(8,128)S(1)} %get-tuple-element.26), channel_id=1, source_target_pairs={{0,64},{1,192},{64,65},{65,193},{128,0},{129,128},{192,1},{193,129... | collective-permute-start | bytes 786440 | tf_op jit(solution)/shard_map/ppermute | solution.py:53
  56.9 10.9 %collective-permute-start.8 = (f32[8,64,128]{2,1,0:T(8,128)S(1)}, f32[8,64,128]{2,1,0:T(8,128)S(1)}, u32[]{:S(2)}, u32[]{:S(2)}) collective-permute-start(f32[8,64,128]{2,1,0:T(8,128)S(1)} %get-tuple-element.23), channel_id=1, source_target_pairs={{0,65},{1,193},{64,0},{65,128},{128,1},{129,129},{192,64},{193,192... | collective-permute-start | bytes 786440 | tf_op jit(solution)/shard_map/ppermute | solution.py:53
  67.9 1.4 copy-start.1
  67.9 1.4 copy-start.3
  74.6 12.6 %collective-permute-start.13 = (f32[8,64,128]{2,0,1:T(8,128)}, f32[8,64,128]{2,0,1:T(8,128)S(1)}, u32[]{:S(2)}, u32[]{:S(2)}) collective-permute-start(f32[8,64,128]{2,0,1:T(8,128)} %get-tuple-element.19), channel_id=1, source_target_pairs={{64,128},{128,64},{65,129},{129,65},{192,194},{194,192},{193,195},... | collective-permute-start | bytes 786440 | tf_op jit(solution)/shard_map/ppermute | solution.py:53
  76.5 10.7 %collective-permute-start.14 = (f32[8,64,128]{2,0,1:T(8,128)}, f32[8,64,128]{2,0,1:T(8,128)S(1)}, u32[]{:S(2)}, u32[]{:S(2)}) collective-permute-start(f32[8,64,128]{2,0,1:T(8,128)} %get-tuple-element.22), channel_id=1, source_target_pairs={{1,64},{64,1},{65,128},{128,65},{129,192},{192,129},{193,194},{194... | collective-permute-start | bytes 786440 | tf_op jit(solution)/shard_map/ppermute | solution.py:53
  78.5 9.1 %collective-permute-start.15 = (f32[8,64,128]{2,0,1:T(8,128)}, f32[8,64,128]{2,0,1:T(8,128)}, u32[]{:S(2)}, u32[]{:S(2)}) collective-permute-start(f32[8,64,128]{2,0,1:T(8,128)} %get-tuple-element.21), channel_id=1, source_target_pairs={{0,64},{64,0},{1,65},{65,1},{128,192},{192,128},{129,193},{193,129... | collective-permute-start | bytes 786440 | tf_op jit(solution)/shard_map/ppermute | solution.py:53
  81.8 6.4 %collective-permute-start.16 = (f32[8,64,128]{2,0,1:T(8,128)S(1)}, f32[8,64,128]{2,0,1:T(8,128)}, u32[]{:S(2)}, u32[]{:S(2)}) collective-permute-start(f32[8,64,128]{2,0,1:T(8,128)S(1)} %get-tuple-element.20), channel_id=1, source_target_pairs={{0,1},{1,0},{64,65},{65,64},{128,129},{129,128},{192,193},{193,192... | collective-permute-start | bytes 786440 | tf_op jit(solution)/shard_map/ppermute | solution.py:53
  89.2 11.2 %collective-permute-start.17 = (f32[8,64,128]{2,0,1:T(8,128)S(1)}, f32[8,64,128]{2,0,1:T(8,128)S(1)}, u32[]{:S(2)}, u32[]{:S(2)}) collective-permute-start(f32[8,64,128]{2,0,1:T(8,128)S(1)} %fusion.22), channel_id=1, source_target_pairs={{0,256},{1,257},{2,258},{3,259},{4,260},{5,261},{6,262},{7,263},{8... | collective-permute-start | bytes 786440 | tf_op jit(solution)/shard_map/ppermute | solution.py:53
  100.4 23.7 %collective-permute-start.18 = (f32[8,64,128]{2,0,1:T(8,128)S(1)}, f32[8,64,128]{2,0,1:T(8,128)S(1)}, u32[]{:S(2)}, u32[]{:S(2)}) collective-permute-start(f32[8,64,128]{2,0,1:T(8,128)S(1)} %multiply_multiply_fusion), channel_id=1, source_target_pairs={{64,128},{128,64},{65,129},{129,65},{192,194},{194,192},{193,195},... | collective-permute-start | bytes 786440 | tf_op jit(solution)/shard_map/ppermute | solution.py:53
  116.1 9.4 %collective-permute-start.19 = (f32[8,64,128]{2,0,1:T(8,128)S(1)}, f32[8,64,128]{2,0,1:T(8,128)S(1)}, u32[]{:S(2)}, u32[]{:S(2)}) collective-permute-start(f32[8,64,128]{2,0,1:T(8,128)S(1)} %multiply_multiply_fusion), channel_id=1, source_target_pairs={{1,64},{64,1},{65,128},{128,65},{129,192},{192,129},{193,194},{194... | collective-permute-start | bytes 786440 | tf_op jit(solution)/shard_map/ppermute | solution.py:53
  118.0 10.3 %collective-permute-start.20 = (f32[8,64,128]{2,0,1:T(8,128)S(1)}, f32[8,64,128]{2,0,1:T(8,128)S(1)}, u32[]{:S(2)}, u32[]{:S(2)}) collective-permute-start(f32[8,64,128]{2,0,1:T(8,128)S(1)} %multiply_multiply_fusion), channel_id=1, source_target_pairs={{0,64},{64,0},{1,65},{65,1},{128,192},{192,128},{129,193},{193,129... | collective-permute-start | bytes 786440 | tf_op jit(solution)/shard_map/ppermute | solution.py:53
  119.9 8.4 %collective-permute-start.21 = (f32[8,64,128]{2,0,1:T(8,128)S(1)}, f32[8,64,128]{2,0,1:T(8,128)S(1)}, u32[]{:S(2)}, u32[]{:S(2)}) collective-permute-start(f32[8,64,128]{2,0,1:T(8,128)S(1)} %multiply_multiply_fusion), channel_id=1, source_target_pairs={{0,1},{1,0},{64,65},{65,64},{128,129},{129,128},{192,193},{193,192... | collective-permute-start | bytes 786440 | tf_op jit(solution)/shard_map/ppermute | solution.py:53
  129.1 1.0 copy-start.2
  129.1 1.0 copy-start.4
  135.4 13.3 %collective-permute-start.22 = (f32[8,64,128]{2,0,1:T(8,128)}, f32[8,64,128]{2,0,1:T(8,128)S(1)}, u32[]{:S(2)}, u32[]{:S(2)}) collective-permute-start(f32[8,64,128]{2,0,1:T(8,128)} %get-tuple-element.15), channel_id=1, source_target_pairs={{64,128},{128,64},{65,129},{129,65},{192,194},{194,192},{193,195},... | collective-permute-start | bytes 786440 | tf_op jit(solution)/shard_map/ppermute | solution.py:53
  140.8 9.8 %collective-permute-start.23 = (f32[8,64,128]{2,0,1:T(8,128)}, f32[8,64,128]{2,0,1:T(8,128)S(1)}, u32[]{:S(2)}, u32[]{:S(2)}) collective-permute-start(f32[8,64,128]{2,0,1:T(8,128)} %get-tuple-element.18), channel_id=1, source_target_pairs={{1,64},{64,1},{65,128},{128,65},{129,192},{192,129},{193,194},{194... | collective-permute-start | bytes 786440 | tf_op jit(solution)/shard_map/ppermute | solution.py:53
  142.8 10.2 %collective-permute-start.24 = (f32[8,64,128]{2,0,1:T(8,128)S(1)}, f32[8,64,128]{2,0,1:T(8,128)S(1)}, u32[]{:S(2)}, u32[]{:S(2)}) collective-permute-start(f32[8,64,128]{2,0,1:T(8,128)S(1)} %get-tuple-element.17), channel_id=1, source_target_pairs={{0,64},{64,0},{1,65},{65,1},{128,192},{192,128},{129,193},{193,129... | collective-permute-start | bytes 786440 | tf_op jit(solution)/shard_map/ppermute | solution.py:53
  144.7 8.3 %collective-permute-start.25 = (f32[8,64,128]{2,0,1:T(8,128)S(1)}, f32[8,64,128]{2,0,1:T(8,128)S(1)}, u32[]{:S(2)}, u32[]{:S(2)}) collective-permute-start(f32[8,64,128]{2,0,1:T(8,128)S(1)} %get-tuple-element.16), channel_id=1, source_target_pairs={{0,1},{1,0},{64,65},{65,64},{128,129},{129,128},{192,193},{193,192... | collective-permute-start | bytes 786440 | tf_op jit(solution)/shard_map/ppermute | solution.py:53
  153.1 9.6 %collective-permute-start.26 = (f32[8,4,8,128]{3,0,2,1:T(8,128)S(1)}, f32[8,4,8,128]{3,0,2,1:T(8,128)S(1)}, u32[]{:S(2)}, u32[]{:S(2)}) collective-permute-start(f32[8,4,8,128]{3,0,2,1:T(8,128)S(1)} %select_bitcast_fusion), channel_id=1, source_target_pairs={{0,256},{1,257},{2,258},{3,259},{4,260},{5,261},{6,262},{7,263},{8... | collective-permute-start | bytes 393224 | tf_op jit(solution)/shard_map/ppermute | solution.py:53
  162.8 13.7 %collective-permute-start.27 = (f32[8,8,128]{2,1,0:T(8,128)S(1)}, f32[8,8,128]{2,1,0:T(8,128)S(1)}, u32[]{:S(2)}, u32[]{:S(2)}) collective-permute-start(f32[8,8,128]{2,1,0:T(8,128)S(1)} %bitcast.163), channel_id=1, source_target_pairs={{0,0},{128,1},{1,64},{129,65},{64,128},{192,129},{65,192},{193,193... | collective-permute-start | bytes 98312 | tf_op jit(solution)/shard_map/ppermute | solution.py:53
  167.3 9.2 %collective-permute-start.28 = (f32[8,8,128]{2,1,0:T(8,128)S(1)}, f32[8,8,128]{2,1,0:T(8,128)S(1)}, u32[]{:S(2)}, u32[]{:S(2)}) collective-permute-start(f32[8,8,128]{2,1,0:T(8,128)S(1)} %bitcast.164), channel_id=1, source_target_pairs={{1,0},{129,1},{64,64},{192,65},{65,128},{193,129},{0,192},{128,193... | collective-permute-start | bytes 98312 | tf_op jit(solution)/shard_map/ppermute | solution.py:53
  169.2 7.3 %collective-permute-start.29 = (f32[8,8,128]{2,1,0:T(8,128)S(1)}, f32[8,8,128]{2,1,0:T(8,128)S(1)}, u32[]{:S(2)}, u32[]{:S(2)}) collective-permute-start(f32[8,8,128]{2,1,0:T(8,128)S(1)} %bitcast.165), channel_id=1, source_target_pairs={{64,0},{192,1},{65,64},{193,65},{0,128},{128,129},{1,192},{129,193... | collective-permute-start | bytes 98312 | tf_op jit(solution)/shard_map/ppermute | solution.py:53
  174.6 5.9 %collective-permute-start.30 = (f32[8,8,128]{2,1,0:T(8,128)S(1)}, f32[8,8,128]{2,1,0:T(8,128)S(1)}, u32[]{:S(2)}, u32[]{:S(2)}) collective-permute-start(f32[8,8,128]{2,1,0:T(8,128)S(1)} %bitcast.166), channel_id=1, source_target_pairs={{65,0},{193,1},{0,64},{128,65},{1,128},{129,129},{64,192},{192,193... | collective-permute-start | bytes 98312 | tf_op jit(solution)/shard_map/ppermute | solution.py:53

commit v4 on v2

--- a/solution.py
+++ b/solution.py
@@ -20,7 +20,7 @@
     return (p - column % 4) % 4
 
 
-def spread_pairs(turn, cross=0):
+def spread_pairs(turn):
     pairs = []
     for h in range(2):
         for column in range(COLS // 2):
@@ -30,7 +30,7 @@
                     pairs.append(
                         (
                             device(h, x, 2 * column + k),
-                            device(h ^ cross, chip_x(column, p), 2 * column + x // 2),
+                            device(h, chip_x(column, p), 2 * column + x // 2),
                         )
                     )
     return pairs
@@ -42,7 +42,8 @@
         for chip in range(first, COLS // 2 * 4 - 1, 2):
             for core in range(2):
                 low, high = (
-                    device(h, chip_x(q // 4, q % 4), 2 * (q // 4) + core) for q in (chip, chip + 1)
+                    device((h + q // 16) % 2, chip_x(q // 4, q % 4), 2 * (q // 4) + core)
+                    for q in (chip, chip + 1)
                 )
                 pairs += [(low, high), (high, low)]
     return pairs
@@ -63,7 +64,6 @@
 
 
 SPREAD = [spread_pairs(0), spread_pairs(1)]
-SPREAD_CROSS = [spread_pairs(0, 1), spread_pairs(1, 1)]
 ODD = chip_pairs(1)
 EVEN = chip_pairs(0)
 SWAP_H = swap_pairs("h")
@@ -78,6 +78,10 @@
     count = kernel.shape[1]
     onehot = (taps[:, :, None] == jnp.arange(count, dtype=jnp.int32)).astype(jnp.float32)
     return jnp.einsum("ijk,uk->uij", onehot, kernel, precision=HIGHEST)
+
+
+def by_h(own, other, h):
+    return jnp.where(h == 0, jnp.concatenate([own, other], 1), jnp.concatenate([other, own], 1))
 
 
 def body(estimate, observed, psf_taps, intersection):
@@ -100,7 +104,7 @@
     even = p % 2 == 0
     est = [send(piece(estimate, turn), SPREAD[turn]) for turn in (0, 1)]
     quarter = jnp.where(even, jnp.concatenate(est, 1), jnp.concatenate(est[::-1], 1))
-    current = jnp.concatenate([quarter, send(quarter, SWAP_H)], 1)
+    current = by_h(quarter, send(quarter, SWAP_H), h)
     images = [piece(observed[0], turn) for turn in (0, 1)]
     *images, _ = lax.optimization_barrier((*images, quarter))
     images = [send(image, route) for image, route in zip(images, SPREAD)]
@@ -111,7 +115,7 @@
     own_views = 4 * h + 2 * core + jnp.stack([p % 2, (p + 1) % 2])
     picker = (own_views[:, None] == views[None, :]).astype(jnp.float32)
     own = jnp.einsum("uv,vdk->udk", picker, kernels, precision=HIGHEST)
-    quarters = jnp.stack([2 * h + core, 2 * (1 - h) + core, 2 * h + 1 - core, 2 * (1 - h) + 1 - core])
+    quarters = jnp.stack([core, 2 + core, 1 - core, 3 - core])
     quarter_width = full_width // 4
     local_y = (quarters[:, None] * quarter_width + jnp.arange(quarter_width, dtype=jnp.int32)[None, :]).reshape(-1)
     all_y = jnp.arange(full_width, dtype=jnp.int32)
@@ -161,26 +165,18 @@
         part = back[:, :width] + send(back[:, width:], SWAP_CORE)
         part = part[SLAB : 2 * SLAB] + send(part[:SLAB], ODD) + send(part[2 * SLAB :], EVEN)
         if iteration < ITERS - 1:
-            other = send(part, SWAP_H)
-            total = part + jnp.concatenate([other[:, quarter_width:], other[:, :quarter_width]], 1)
-            current = current * (total + 1.0) * scale
+            current = current * (part + send(part, SWAP_H) + 1.0) * scale
 
-    factor = current * scale
-    halves = [
-        (factor * part)[:, quarter_width:],
-        (factor * (part + 1.0))[:, :quarter_width],
-    ]
+    def own_half(value, mine):
+        return jnp.where((h == 0) == mine, value[:, :quarter_width], value[:, quarter_width:])
+
+    total = own_half(part, True) + send(own_half(part, False), SWAP_H)
+    quarter = own_half(current, True) * (total + 1.0) * own_half(scale, True)
+
     block = quarter_width // 2
-    pieces = []
-    for half_part, routes in zip(halves, (SPREAD_CROSS, SPREAD)):
-        first, second = half_part[:, :block], half_part[:, block:]
-        pieces.append(
-            [
-                send(jnp.where((p + turn) % 2 == 0, first, second), reverse(routes[turn]))
-                for turn in (0, 1)
-            ]
-        )
-    one, two = (pieces[0][turn] + pieces[1][turn] for turn in (0, 1))
+    first, second = quarter[:, :block], quarter[:, block:]
+    chosen = [jnp.where(even, first, second), jnp.where(even, second, first)]
+    one, two = (send(value, reverse(route)) for value, route in zip(chosen, SPREAD))
     return jnp.where(x % 2 == 0, jnp.concatenate([one, two], 0), jnp.concatenate([two, one], 0))
 
 

time: 161 us -> 162 us (level)
  starting transfers between devices: 90.3 us -> 81.1 us
  waiting for transfers between devices: 49.3 us -> 52.8 us
  matrix products: 13 us -> 16.4 us
  local copies, waits for them, and re-layouts: 3.81 us -> 6.9 us
    ppermute x22 -> x21, starting transfers between devices: 90.3 us -> 81.1 us  [send(): return lax.ppermute(value, AXES, pairs)]
    ppermute x22 -> x21, waiting for transfers between devices: 49.3 us -> 52.8 us  [send(): return lax.ppermute(value, AXES, pairs)]
  transfers between devices with their start and end apart: 22 -> 21, of which waited for: 14 -> 16; matrix products, arithmetic and copies ran while one was open for 5% -> 9% of each run, Pallas kernels for 0% -> 0%
where the time goes in v4:
time: 162 us; the launch traced here: 161 us
  starting transfers between devices  81.1 us (50%)
  waiting for transfers between devices  52.8 us (33%)
  matrix products  16.4 us (10%)
  local copies, waits for them, and re-layouts  6.9 us (4%)
  other arithmetic  3.22 us (2%)
    ppermute x21, starting transfers between devices, send(): return lax.ppermute(value, AXES, pairs)  81.1 us
    ppermute x21, waiting for transfers between devices, send(): return lax.ppermute(value, AXES, pairs)  52.8 us
  transfers between devices with their start and end apart: 21, of which 16 were waited for; matrix products, arithmetic and copies ran while one was open for 9% of the time, Pallas kernels for 0%

profile of v4, /device:TPU:57, one launch (start us, length us, event | category | flops | bytes accessed | tf_op | source)
XLA Modules:
  0.0 161.3 jit_solution(10375021427302307013)
XLA Ops:
  0.0 0.9 constant_dynamic-slice_fusion.1
  0.9 5.2 %collective-permute-start = (f32[16,8,128]{2,0,1:T(8,128)S(1)}, f32[16,8,128]{2,0,1:T(8,128)S(1)}, u32[]{:S(2)}, u32[]{:S(2)}) collective-permute-start(f32[16,8,128]{2,0,1:T(8,128)S(1)} %copy.33), channel_id=1, source_target_pairs={{0,0},{1,128},{64,64},{65,192},{128,1},{129,129},{192,65},{193,193... | collective-permute-start | bytes 196616 | tf_op jit(solution)/shard_map/ppermute | solution.py:74
  6.2 2.5 %collective-permute-start.1 = (f32[16,8,128]{2,0,1:T(8,128)S(1)}, f32[16,8,128]{2,0,1:T(8,128)S(1)}, u32[]{:S(2)}, u32[]{:S(2)}) collective-permute-start(f32[16,8,128]{2,0,1:T(8,128)S(1)} %copy.34), channel_id=1, source_target_pairs={{0,64},{1,192},{64,0},{65,128},{128,65},{129,193},{192,1},{193,129... | collective-permute-start | bytes 196616 | tf_op jit(solution)/shard_map/ppermute | solution.py:74
  8.7 0.8 reduce_sum.9
  9.5 0.8 broadcast_divide_fusion
  10.9 1.3 dynamic-slice_bitcast_fusion
  12.2 0.8 collective-permute-done.1
  13.0 3.0 %collective-permute-start.3 = (f32[16,64,128]{2,1,0:T(8,128)S(1)}, f32[16,64,128]{2,1,0:T(8,128)S(1)}, u32[]{:S(2)}, u32[]{:S(2)}) collective-permute-start(f32[16,64,128]{2,1,0:T(8,128)S(1)} %get-tuple-element.11), channel_id=1, source_target_pairs={{0,0},{1,128},{64,64},{65,192},{128,1},{129,129},{192,65},{193,193... | collective-permute-start | bytes 1572872 | tf_op jit(solution)/shard_map/ppermute | solution.py:74
  16.4 10.6 %collective-permute-start.2 = (f32[16,16,128]{2,0,1:T(8,128)S(1)}, f32[16,16,128]{2,0,1:T(8,128)S(1)}, u32[]{:S(2)}, u32[]{:S(2)}) collective-permute-start(f32[16,16,128]{2,0,1:T(8,128)S(1)} %maximum_select_fusion.1), channel_id=1, source_target_pairs={{0,256},{1,257},{2,258},{3,259},{4,260},{5,261},{6,262},{7,263},{8... | collective-permute-start | bytes 393224 | tf_op jit(solution)/shard_map/ppermute | solution.py:74
  27.1 0.8 fusion.16
  27.9 2.9 %collective-permute-start.6 = (f32[16,64,128]{2,1,0:T(8,128)S(1)}, f32[16,64,128]{2,1,0:T(8,128)S(1)}, u32[]{:S(2)}, u32[]{:S(2)}) collective-permute-start(f32[16,64,128]{2,1,0:T(8,128)S(1)} %get-tuple-element.14), channel_id=1, source_target_pairs={{0,64},{1,192},{64,0},{65,128},{128,65},{129,193},{192,1},{193,129... | collective-permute-start | bytes 1572872 | tf_op jit(solution)/shard_map/ppermute | solution.py:74
  30.9 8.0 %collective-permute-start.4 = (f32[16,32,128]{2,0,1:T(8,128)S(1)}, f32[16,32,128]{2,0,1:T(8,128)S(1)}, u32[]{:S(2)}, u32[]{:S(2)}) collective-permute-start(f32[16,32,128]{2,0,1:T(8,128)S(1)} %maximum_select_fusion), channel_id=1, source_target_pairs={{64,128},{128,64},{65,129},{129,65},{192,194},{194,192},{193,195},... | collective-permute-start | bytes 786440 | tf_op jit(solution)/shard_map/ppermute | solution.py:74
  38.9 1.9 %collective-permute-start.5 = (f32[16,32,128]{2,0,1:T(8,128)S(1)}, f32[16,32,128]{2,0,1:T(8,128)S(1)}, u32[]{:S(2)}, u32[]{:S(2)}) collective-permute-start(f32[16,32,128]{2,0,1:T(8,128)S(1)} %maximum_select_fusion), channel_id=1, source_target_pairs={{0,64},{64,0},{1,65},{65,1},{128,192},{192,128},{129,193},{193,129... | collective-permute-start | bytes 786440 | tf_op jit(solution)/shard_map/ppermute | solution.py:74
  41.1 3.2 %collective-permute-done.4 = f32[16,32,128]{2,0,1:T(8,128)S(1)} collective-permute-done((f32[16,32,128]{2,0,1:T(8,128)S(1)}, f32[16,32,128]{2,0,1:T(8,128)S(1)}, u32[]{:S(2)}, u32[]{:S(2)}) %collective-permute-start.4) | collective-permute-done | bytes 262176 | tf_op jit(solution)/shard_map/ppermute | solution.py:74
  44.3 3.9 %collective-permute-done.5 = f32[16,32,128]{2,0,1:T(8,128)S(1)} collective-permute-done((f32[16,32,128]{2,0,1:T(8,128)S(1)}, f32[16,32,128]{2,0,1:T(8,128)S(1)}, u32[]{:S(2)}, u32[]{:S(2)}) %collective-permute-start.5) | collective-permute-done | bytes 262176 | tf_op jit(solution)/shard_map/ppermute | solution.py:74
  48.4 2.2 %collective-permute-start.7 = (f32[48,32,128]{2,0,1:T(8,128)S(1)}, f32[48,32,128]{2,0,1:T(8,128)S(1)}, u32[]{:S(2)}, u32[]{:S(2)}) collective-permute-start(f32[48,32,128]{2,0,1:T(8,128)S(1)} %pad_maximum_fusion.1), channel_id=1, source_target_pairs={{0,1},{1,0},{2,3},{3,2},{4,5},{5,4},{6,7},{7,6},{8,9},{9,8},{10,11... | collective-permute-start | bytes 2359304 | tf_op jit(solution)/shard_map/ppermute | solution.py:74
  50.9 0.6 subtract_add_fusion.5
  51.8 0.8 collective-permute-done.7
  52.5 0.6 fusion.1
  53.1 0.9 convolution_bitcast_fusion.3
  54.0 0.7 fusion.12
  54.7 0.6 fusion.82
  55.3 0.6 fusion.83
  55.9 1.4 convolution_bitcast_fusion.1
  57.3 2.2 %collective-permute-start.8 = (f32[48,32,128]{2,0,1:T(8,128)S(1)}, f32[48,32,128]{2,0,1:T(8,128)S(1)}, u32[]{:S(2)}, u32[]{:S(2)}) collective-permute-start(f32[48,32,128]{2,0,1:T(8,128)S(1)} %slice.111), channel_id=1, source_target_pairs={{0,1},{1,0},{2,3},{3,2},{4,5},{5,4},{6,7},{7,6},{8,9},{9,8},{10,11... | collective-permute-start | bytes 2359304 | tf_op jit(solution)/shard_map/ppermute | solution.py:74
  59.5 0.6 slice.92
  60.1 1.3 sub.139
  61.4 1.4 fusion.25
  62.8 1.5 fusion.35
  64.4 1.9 %collective-permute-start.10 = (f32[16,32,128]{2,0,1:T(8,128)S(1)}, f32[16,32,128]{2,0,1:T(8,128)S(1)}, u32[]{:S(2)}, u32[]{:S(2)}) collective-permute-start(f32[16,32,128]{2,0,1:T(8,128)S(1)} %get-tuple-element.24), channel_id=1, source_target_pairs={{0,64},{64,0},{1,65},{65,1},{128,192},{192,128},{129,193},{193,129... | collective-permute-start | bytes 786440 | tf_op jit(solution)/shard_map/ppermute | solution.py:74
  66.4 5.2 %collective-permute-start.9 = (f32[16,32,128]{2,0,1:T(8,128)S(1)}, f32[16,32,128]{2,0,1:T(8,128)S(1)}, u32[]{:S(2)}, u32[]{:S(2)}) collective-permute-start(f32[16,32,128]{2,0,1:T(8,128)S(1)} %get-tuple-element.23), channel_id=1, source_target_pairs={{64,128},{128,64},{65,129},{129,65},{192,194},{194,192},{193,195},... | collective-permute-start | bytes 786440 | tf_op jit(solution)/shard_map/ppermute | solution.py:74
  71.6 0.9 fusion.54
  72.5 0.8 copy.23
  73.3 0.7 collective-permute-done.10
  74.0 4.0 %collective-permute-done.9 = f32[16,32,128]{2,0,1:T(8,128)S(1)} collective-permute-done((f32[16,32,128]{2,0,1:T(8,128)S(1)}, f32[16,32,128]{2,0,1:T(8,128)S(1)}, u32[]{:S(2)}, u32[]{:S(2)}) %collective-permute-start.9) | collective-permute-done | bytes 262176 | tf_op jit(solution)/shard_map/ppermute | solution.py:74
  78.0 5.4 %collective-permute-start.11 = (f32[16,32,128]{2,0,1:T(8,128)S(1)}, f32[16,32,128]{2,0,1:T(8,128)S(1)}, u32[]{:S(2)}, u32[]{:S(2)}) collective-permute-start(f32[16,32,128]{2,0,1:T(8,128)S(1)} %fusion.27), channel_id=1, source_target_pairs={{0,256},{1,257},{2,258},{3,259},{4,260},{5,261},{6,262},{7,263},{8... | collective-permute-start | bytes 786440 | tf_op jit(solution)/shard_map/ppermute | solution.py:74
  83.5 0.8 convolution_bitcast_fusion.5
  84.5 0.6 fusion.15
  85.1 12.6 %collective-permute-done.11 = f32[16,32,128]{2,0,1:T(8,128)S(1)} collective-permute-done((f32[16,32,128]{2,0,1:T(8,128)S(1)}, f32[16,32,128]{2,0,1:T(8,128)S(1)}, u32[]{:S(2)}, u32[]{:S(2)}) %collective-permute-start.11) | collective-permute-done | bytes 262176 | tf_op jit(solution)/shard_map/ppermute | solution.py:74
  97.7 3.7 %collective-permute-start.12 = (f32[16,32,128]{2,0,1:T(8,128)S(1)}, f32[16,32,128]{2,0,1:T(8,128)S(1)}, u32[]{:S(2)}, u32[]{:S(2)}) collective-permute-start(f32[16,32,128]{2,0,1:T(8,128)S(1)} %multiply_multiply_fusion), channel_id=1, source_target_pairs={{64,128},{128,64},{65,129},{129,65},{192,194},{194,192},{193,195},... | collective-permute-start | bytes 786440 | tf_op jit(solution)/shard_map/ppermute | solution.py:74
  101.5 1.9 %collective-permute-start.13 = (f32[16,32,128]{2,0,1:T(8,128)S(1)}, f32[16,32,128]{2,0,1:T(8,128)S(1)}, u32[]{:S(2)}, u32[]{:S(2)}) collective-permute-start(f32[16,32,128]{2,0,1:T(8,128)S(1)} %multiply_multiply_fusion), channel_id=1, source_target_pairs={{0,64},{64,0},{1,65},{65,1},{128,192},{192,128},{129,193},{193,129... | collective-permute-start | bytes 786440 | tf_op jit(solution)/shard_map/ppermute | solution.py:74
  103.4 5.7 %collective-permute-done.12 = f32[16,32,128]{2,0,1:T(8,128)S(1)} collective-permute-done((f32[16,32,128]{2,0,1:T(8,128)S(1)}, f32[16,32,128]{2,0,1:T(8,128)S(1)}, u32[]{:S(2)}, u32[]{:S(2)}) %collective-permute-start.12) | collective-permute-done | bytes 262176 | tf_op jit(solution)/shard_map/ppermute | solution.py:74
  109.1 1.4 collective-permute-done.13
  110.5 3.9 %collective-permute-start.14 = (f32[48,32,128]{2,0,1:T(8,128)S(1)}, f32[48,32,128]{2,0,1:T(8,128)S(1)}, u32[]{:S(2)}, u32[]{:S(2)}) collective-permute-start(f32[48,32,128]{2,0,1:T(8,128)S(1)} %pad_maximum_fusion.2), channel_id=1, source_target_pairs={{0,1},{1,0},{2,3},{3,2},{4,5},{5,4},{6,7},{7,6},{8,9},{9,8},{10,11... | collective-permute-start | bytes 2359304 | tf_op jit(solution)/shard_map/ppermute | solution.py:74
  114.4 1.7 %collective-permute-done.14 = f32[48,32,128]{2,0,1:T(8,128)S(1)} collective-permute-done((f32[48,32,128]{2,0,1:T(8,128)S(1)}, f32[48,32,128]{2,0,1:T(8,128)S(1)}, u32[]{:S(2)}, u32[]{:S(2)}) %collective-permute-start.14) | collective-permute-done | bytes 786464 | tf_op jit(solution)/shard_map/ppermute | solution.py:74
  116.1 0.6 fusion.4
  116.7 0.9 convolution_bitcast_fusion.2
  117.9 0.6 fusion.14
  118.6 0.6 fusion.84
  119.4 0.6 fusion.85
  120.0 1.4 convolution_bitcast_fusion
  121.4 2.3 %collective-permute-start.15 = (f32[48,32,128]{2,0,1:T(8,128)S(1)}, f32[48,32,128]{2,0,1:T(8,128)S(1)}, u32[]{:S(2)}, u32[]{:S(2)}) collective-permute-start(f32[48,32,128]{2,0,1:T(8,128)S(1)} %slice.121), channel_id=1, source_target_pairs={{0,1},{1,0},{2,3},{3,2},{4,5},{5,4},{6,7},{7,6},{8,9},{9,8},{10,11... | collective-permute-start | bytes 2359304 | tf_op jit(solution)/shard_map/ppermute | solution.py:74
  123.7 1.9 %collective-permute-done.15 = f32[48,32,128]{2,0,1:T(8,128)S(1)} collective-permute-done((f32[48,32,128]{2,0,1:T(8,128)S(1)}, f32[48,32,128]{2,0,1:T(8,128)S(1)}, u32[]{:S(2)}, u32[]{:S(2)}) %collective-permute-start.15) | collective-permute-done | bytes 786464 | tf_op jit(solution)/shard_map/ppermute | solution.py:74
  125.8 4.9 %collective-permute-start.16 = (f32[16,32,128]{2,0,1:T(8,128)S(1)}, f32[16,32,128]{2,0,1:T(8,128)S(1)}, u32[]{:S(2)}, u32[]{:S(2)}) collective-permute-start(f32[16,32,128]{2,0,1:T(8,128)S(1)} %get-tuple-element.21), channel_id=1, source_target_pairs={{64,128},{128,64},{65,129},{129,65},{192,194},{194,192},{193,195},... | collective-permute-start | bytes 786440 | tf_op jit(solution)/shard_map/ppermute | solution.py:74
  130.6 1.9 %collective-permute-start.17 = (f32[16,32,128]{2,0,1:T(8,128)S(1)}, f32[16,32,128]{2,0,1:T(8,128)S(1)}, u32[]{:S(2)}, u32[]{:S(2)}) collective-permute-start(f32[16,32,128]{2,0,1:T(8,128)S(1)} %get-tuple-element.22), channel_id=1, source_target_pairs={{0,64},{64,0},{1,65},{65,1},{128,192},{192,128},{129,193},{193,129... | collective-permute-start | bytes 786440 | tf_op jit(solution)/shard_map/ppermute | solution.py:74
  132.6 4.7 %collective-permute-done.16 = f32[16,32,128]{2,0,1:T(8,128)S(1)} collective-permute-done((f32[16,32,128]{2,0,1:T(8,128)S(1)}, f32[16,32,128]{2,0,1:T(8,128)S(1)}, u32[]{:S(2)}, u32[]{:S(2)}) %collective-permute-start.16) | collective-permute-done | bytes 262176 | tf_op jit(solution)/shard_map/ppermute | solution.py:74
  137.3 2.4 %collective-permute-done.17 = f32[16,32,128]{2,0,1:T(8,128)S(1)} collective-permute-done((f32[16,32,128]{2,0,1:T(8,128)S(1)}, f32[16,32,128]{2,0,1:T(8,128)S(1)}, u32[]{:S(2)}, u32[]{:S(2)}) %collective-permute-start.17) | collective-permute-done | bytes 262176 | tf_op jit(solution)/shard_map/ppermute | solution.py:74
  139.8 4.7 %collective-permute-start.18 = (f32[16,16,128]{2,0,1:T(8,128)S(1)}, f32[16,16,128]{2,0,1:T(8,128)S(1)}, u32[]{:S(2)}, u32[]{:S(2)}) collective-permute-start(f32[16,16,128]{2,0,1:T(8,128)S(1)} %slice_select_fusion.2), channel_id=1, source_target_pairs={{0,256},{1,257},{2,258},{3,259},{4,260},{5,261},{6,262},{7,263},{8... | collective-permute-start | bytes 393224 | tf_op jit(solution)/shard_map/ppermute | solution.py:74
  144.5 4.9 %collective-permute-done.18 = f32[16,16,128]{2,0,1:T(8,128)S(1)} collective-permute-done((f32[16,16,128]{2,0,1:T(8,128)S(1)}, f32[16,16,128]{2,0,1:T(8,128)S(1)}, u32[]{:S(2)}, u32[]{:S(2)}) %collective-permute-start.18) | collective-permute-done | bytes 131104 | tf_op jit(solution)/shard_map/ppermute | solution.py:74
  149.5 4.2 %collective-permute-start.19 = (f32[16,8,128]{2,0,1:T(8,128)S(1)}, f32[16,8,128]{2,0,1:T(8,128)S(1)}, u32[]{:S(2)}, u32[]{:S(2)}) collective-permute-start(f32[16,8,128]{2,0,1:T(8,128)S(1)} %get-tuple-element.25), channel_id=1, source_target_pairs={{0,0},{128,1},{64,64},{192,65},{1,128},{129,129},{65,192},{193,193... | collective-permute-start | bytes 196616 | tf_op jit(solution)/shard_map/ppermute | solution.py:74
  153.7 2.6 %collective-permute-start.20 = (f32[16,8,128]{2,0,1:T(8,128)S(1)}, f32[16,8,128]{2,0,1:T(8,128)S(1)}, u32[]{:S(2)}, u32[]{:S(2)}) collective-permute-start(f32[16,8,128]{2,0,1:T(8,128)S(1)} %get-tuple-element.26), channel_id=1, source_target_pairs={{64,0},{192,1},{0,64},{128,65},{65,128},{193,129},{1,192},{129,193... | collective-permute-start | bytes 196616 | tf_op jit(solution)/shard_map/ppermute | solution.py:74
  156.4 0.5 collective-permute-done.19
  156.9 3.7 %collective-permute-done.20 = f32[16,8,128]{2,0,1:T(8,128)S(1)} collective-permute-done((f32[16,8,128]{2,0,1:T(8,128)S(1)}, f32[16,8,128]{2,0,1:T(8,128)S(1)}, u32[]{:S(2)}, u32[]{:S(2)}) %collective-permute-start.20) | collective-permute-done | bytes 65568 | tf_op jit(solution)/shard_map/ppermute | solution.py:74
  160.6 0.7 copy.10
  (79 shorter events, 3.6 us)
Async XLA Ops:
  0.9 11.3 %collective-permute-start = (f32[16,8,128]{2,0,1:T(8,128)S(1)}, f32[16,8,128]{2,0,1:T(8,128)S(1)}, u32[]{:S(2)}, u32[]{:S(2)}) collective-permute-start(f32[16,8,128]{2,0,1:T(8,128)S(1)} %copy.33), channel_id=1, source_target_pairs={{0,0},{1,128},{64,64},{65,192},{128,1},{129,129},{192,65},{193,193... | collective-permute-start | bytes 196616 | tf_op jit(solution)/shard_map/ppermute | solution.py:74
  6.2 6.8 %collective-permute-start.1 = (f32[16,8,128]{2,0,1:T(8,128)S(1)}, f32[16,8,128]{2,0,1:T(8,128)S(1)}, u32[]{:S(2)}, u32[]{:S(2)}) collective-permute-start(f32[16,8,128]{2,0,1:T(8,128)S(1)} %copy.34), channel_id=1, source_target_pairs={{0,64},{1,192},{64,0},{65,128},{128,65},{129,193},{192,1},{193,129... | collective-permute-start | bytes 196616 | tf_op jit(solution)/shard_map/ppermute | solution.py:74
  10.3 17.5 %copy-start.8 = (f32[8,3,31]{2,0,1:T(8,128)}, f32[8,3,31]{2,0,1:T(8,128)S(1)}, u32[]{:S(2)}) copy-start(f32[8,3,31]{2,0,1:T(8,128)S(1)} %broadcast_divide_fusion) | copy-start | bytes 8932
  10.5 17.4 %copy-start.6 = (s32[4,16]{1,0:T(4,128)}, s32[4,16]{1,0:T(4,128)S(1)}, u32[]{:S(2)}) copy-start(s32[4,16]{1,0:T(4,128)S(1)} %iota_add_fusion) | copy-start | bytes 772
  13.0 17.9 %collective-permute-start.3 = (f32[16,64,128]{2,1,0:T(8,128)S(1)}, f32[16,64,128]{2,1,0:T(8,128)S(1)}, u32[]{:S(2)}, u32[]{:S(2)}) collective-permute-start(f32[16,64,128]{2,1,0:T(8,128)S(1)} %get-tuple-element.11), channel_id=1, source_target_pairs={{0,0},{1,128},{64,64},{65,192},{128,1},{129,129},{192,65},{193,193... | collective-permute-start | bytes 1572872 | tf_op jit(solution)/shard_map/ppermute | solution.py:74
  16.0 34.6 %copy-start.14 = (s32[8,16]{1,0:T(8,128)S(1)}, s32[8,16]{1,0:T(8,128)}, u32[]{:S(2)}) copy-start(s32[8,16]{1,0:T(8,128)} %param.7) | copy-start | bytes 1540
  16.4 36.7 %copy-start = (f32[2,64,64,1]{2,0,1,3:T(2,128)}, f32[2,64,64,1]{2,0,1,3:T(2,128)S(1)}, u32[]{:S(2)}) copy-start(f32[2,64,64,1]{2,0,1,3:T(2,128)S(1)} %convolution_bitcast_fusion.4) | copy-start | bytes 98308
  16.4 14.4 %collective-permute-start.2 = (f32[16,16,128]{2,0,1:T(8,128)S(1)}, f32[16,16,128]{2,0,1:T(8,128)S(1)}, u32[]{:S(2)}, u32[]{:S(2)}) collective-permute-start(f32[16,16,128]{2,0,1:T(8,128)S(1)} %maximum_select_fusion.1), channel_id=1, source_target_pairs={{0,256},{1,257},{2,258},{3,259},{4,260},{5,261},{6,262},{7,263},{8... | collective-permute-start | bytes 393224 | tf_op jit(solution)/shard_map/ppermute | solution.py:74
  27.9 26.1 %copy-start.4 = (f32[2,128,128,1]{2,0,1,3:T(2,128)}, f32[2,128,128,1]{2,0,1,3:T(2,128)S(1)}, u32[]{:S(2)}) copy-start(f32[2,128,128,1]{2,0,1,3:T(2,128)S(1)} %fusion.16) | copy-start | bytes 393220
  27.9 20.4 %collective-permute-start.6 = (f32[16,64,128]{2,1,0:T(8,128)S(1)}, f32[16,64,128]{2,1,0:T(8,128)S(1)}, u32[]{:S(2)}, u32[]{:S(2)}) collective-permute-start(f32[16,64,128]{2,1,0:T(8,128)S(1)} %get-tuple-element.14), channel_id=1, source_target_pairs={{0,64},{1,192},{64,0},{65,128},{128,65},{129,193},{192,1},{193,129... | collective-permute-start | bytes 1572872 | tf_op jit(solution)/shard_map/ppermute | solution.py:74
  30.8 23.2 %copy-start.10 = (f32[16,64,128]{2,1,0:T(8,128)}, f32[16,64,128]{2,1,0:T(8,128)S(1)}, u32[]{:S(2)}) copy-start(f32[16,64,128]{2,1,0:T(8,128)S(1)} %collective-permute-done.3) | copy-start | bytes 1572868
  30.9 13.5 %collective-permute-start.4 = (f32[16,32,128]{2,0,1:T(8,128)S(1)}, f32[16,32,128]{2,0,1:T(8,128)S(1)}, u32[]{:S(2)}, u32[]{:S(2)}) collective-permute-start(f32[16,32,128]{2,0,1:T(8,128)S(1)} %maximum_select_fusion), channel_id=1, source_target_pairs={{64,128},{128,64},{65,129},{129,65},{192,194},{194,192},{193,195},... | collective-permute-start | bytes 786440 | tf_op jit(solution)/shard_map/ppermute | solution.py:74
  38.9 9.4 %collective-permute-start.5 = (f32[16,32,128]{2,0,1:T(8,128)S(1)}, f32[16,32,128]{2,0,1:T(8,128)S(1)}, u32[]{:S(2)}, u32[]{:S(2)}) collective-permute-start(f32[16,32,128]{2,0,1:T(8,128)S(1)} %maximum_select_fusion), channel_id=1, source_target_pairs={{0,64},{64,0},{1,65},{65,1},{128,192},{192,128},{129,193},{193,129... | collective-permute-start | bytes 786440 | tf_op jit(solution)/shard_map/ppermute | solution.py:74
  41.1 14.2 %copy-start.2 = (f32[2,64,64,1]{1,2,3,0:T(8,128)}, f32[2,64,64,1]{1,2,3,0:T(8,128)S(1)}, u32[]{:S(2)}) copy-start(f32[2,64,64,1]{1,2,3,0:T(8,128)S(1)} %copy.18) | copy-start | bytes 98308
  48.3 6.4 %copy-start.12 = (f32[16,64,128]{2,1,0:T(8,128)}, f32[16,64,128]{2,1,0:T(8,128)S(1)}, u32[]{:S(2)}) copy-start(f32[16,64,128]{2,1,0:T(8,128)S(1)} %collective-permute-done.6) | copy-start | bytes 1572868
  48.4 4.2 %collective-permute-start.7 = (f32[48,32,128]{2,0,1:T(8,128)S(1)}, f32[48,32,128]{2,0,1:T(8,128)S(1)}, u32[]{:S(2)}, u32[]{:S(2)}) collective-permute-start(f32[48,32,128]{2,0,1:T(8,128)S(1)} %pad_maximum_fusion.1), channel_id=1, source_target_pairs={{0,1},{1,0},{2,3},{3,2},{4,5},{5,4},{6,7},{7,6},{8,9},{9,8},{10,11... | collective-permute-start | bytes 2359304 | tf_op jit(solution)/shard_map/ppermute | solution.py:74
  50.7 0.8 copy-start.9
  50.9 3.1 %copy-start.16 = (pred[2,16]{1,0:T(4,128)(4,1)}, pred[2,16]{1,0:T(4,128)(4,1)S(1)}, u32[]{:S(2)}) copy-start(pred[2,16]{1,0:T(4,128)(4,1)S(1)} %convolution_compare_fusion) | copy-start | bytes 100
  55.9 3.6 %copy-start.7 = (s32[4,16]{1,0:T(4,128)S(1)}, s32[4,16]{1,0:T(4,128)}, u32[]{:S(2)}) copy-start(s32[4,16]{1,0:T(4,128)} %copy-done.6) | copy-start | bytes 772
  57.3 7.0 %collective-permute-start.8 = (f32[48,32,128]{2,0,1:T(8,128)S(1)}, f32[48,32,128]{2,0,1:T(8,128)S(1)}, u32[]{:S(2)}, u32[]{:S(2)}) collective-permute-start(f32[48,32,128]{2,0,1:T(8,128)S(1)} %slice.111), channel_id=1, source_target_pairs={{0,1},{1,0},{2,3},{3,2},{4,5},{5,4},{6,7},{7,6},{8,9},{9,8},{10,11... | collective-permute-start | bytes 2359304 | tf_op jit(solution)/shard_map/ppermute | solution.py:74
  64.3 7.3 %copy-start.15 = (s32[32]{0:T(128)S(1)}, s32[32]{0:T(128)}, u32[]{:S(2)}) copy-start(s32[32]{0:T(128)} %sub.139) | copy-start | bytes 388
  64.4 9.5 %collective-permute-start.10 = (f32[16,32,128]{2,0,1:T(8,128)S(1)}, f32[16,32,128]{2,0,1:T(8,128)S(1)}, u32[]{:S(2)}, u32[]{:S(2)}) collective-permute-start(f32[16,32,128]{2,0,1:T(8,128)S(1)} %get-tuple-element.24), channel_id=1, source_target_pairs={{0,64},{64,0},{1,65},{65,1},{128,192},{192,128},{129,193},{193,129... | collective-permute-start | bytes 786440 | tf_op jit(solution)/shard_map/ppermute | solution.py:74
  66.4 11.6 %collective-permute-start.9 = (f32[16,32,128]{2,0,1:T(8,128)S(1)}, f32[16,32,128]{2,0,1:T(8,128)S(1)}, u32[]{:S(2)}, u32[]{:S(2)}) collective-permute-start(f32[16,32,128]{2,0,1:T(8,128)S(1)} %get-tuple-element.23), channel_id=1, source_target_pairs={{64,128},{128,64},{65,129},{129,65},{192,194},{194,192},{193,195},... | collective-permute-start | bytes 786440 | tf_op jit(solution)/shard_map/ppermute | solution.py:74
  78.0 19.6 %collective-permute-start.11 = (f32[16,32,128]{2,0,1:T(8,128)S(1)}, f32[16,32,128]{2,0,1:T(8,128)S(1)}, u32[]{:S(2)}, u32[]{:S(2)}) collective-permute-start(f32[16,32,128]{2,0,1:T(8,128)S(1)} %fusion.27), channel_id=1, source_target_pairs={{0,256},{1,257},{2,258},{3,259},{4,260},{5,261},{6,262},{7,263},{8... | collective-permute-start | bytes 786440 | tf_op jit(solution)/shard_map/ppermute | solution.py:74
  97.7 11.3 %collective-permute-start.12 = (f32[16,32,128]{2,0,1:T(8,128)S(1)}, f32[16,32,128]{2,0,1:T(8,128)S(1)}, u32[]{:S(2)}, u32[]{:S(2)}) collective-permute-start(f32[16,32,128]{2,0,1:T(8,128)S(1)} %multiply_multiply_fusion), channel_id=1, source_target_pairs={{64,128},{128,64},{65,129},{129,65},{192,194},{194,192},{193,195},... | collective-permute-start | bytes 786440 | tf_op jit(solution)/shard_map/ppermute | solution.py:74
  101.5 9.0 %collective-permute-start.13 = (f32[16,32,128]{2,0,1:T(8,128)S(1)}, f32[16,32,128]{2,0,1:T(8,128)S(1)}, u32[]{:S(2)}, u32[]{:S(2)}) collective-permute-start(f32[16,32,128]{2,0,1:T(8,128)S(1)} %multiply_multiply_fusion), channel_id=1, source_target_pairs={{0,64},{64,0},{1,65},{65,1},{128,192},{192,128},{129,193},{193,129... | collective-permute-start | bytes 786440 | tf_op jit(solution)/shard_map/ppermute | solution.py:74
  110.5 6.2 %copy-start.1 = (f32[2,64,64,1]{2,0,1,3:T(2,128)S(1)}, f32[2,64,64,1]{2,0,1,3:T(2,128)}, u32[]{:S(2)}) copy-start(f32[2,64,64,1]{2,0,1,3:T(2,128)} %copy-done) | copy-start | bytes 98308
  110.5 5.6 %collective-permute-start.14 = (f32[48,32,128]{2,0,1:T(8,128)S(1)}, f32[48,32,128]{2,0,1:T(8,128)S(1)}, u32[]{:S(2)}, u32[]{:S(2)}) collective-permute-start(f32[48,32,128]{2,0,1:T(8,128)S(1)} %pad_maximum_fusion.2), channel_id=1, source_target_pairs={{0,1},{1,0},{2,3},{3,2},{4,5},{5,4},{6,7},{7,6},{8,9},{9,8},{10,11... | collective-permute-start | bytes 2359304 | tf_op jit(solution)/shard_map/ppermute | solution.py:74
  116.7 0.9 copy-start.5
  116.7 1.1 copy-start.11
  116.7 1.3 copy-start.13
  116.7 1.3 copy-start.17
  118.6 0.8 copy-start.3
  121.4 4.2 %collective-permute-start.15 = (f32[48,32,128]{2,0,1:T(8,128)S(1)}, f32[48,32,128]{2,0,1:T(8,128)S(1)}, u32[]{:S(2)}, u32[]{:S(2)}) collective-permute-start(f32[48,32,128]{2,0,1:T(8,128)S(1)} %slice.121), channel_id=1, source_target_pairs={{0,1},{1,0},{2,3},{3,2},{4,5},{5,4},{6,7},{7,6},{8,9},{9,8},{10,11... | collective-permute-start | bytes 2359304 | tf_op jit(solution)/shard_map/ppermute | solution.py:74
  125.8 11.5 %collective-permute-start.16 = (f32[16,32,128]{2,0,1:T(8,128)S(1)}, f32[16,32,128]{2,0,1:T(8,128)S(1)}, u32[]{:S(2)}, u32[]{:S(2)}) collective-permute-start(f32[16,32,128]{2,0,1:T(8,128)S(1)} %get-tuple-element.21), channel_id=1, source_target_pairs={{64,128},{128,64},{65,129},{129,65},{192,194},{194,192},{193,195},... | collective-permute-start | bytes 786440 | tf_op jit(solution)/shard_map/ppermute | solution.py:74
  130.6 9.1 %collective-permute-start.17 = (f32[16,32,128]{2,0,1:T(8,128)S(1)}, f32[16,32,128]{2,0,1:T(8,128)S(1)}, u32[]{:S(2)}, u32[]{:S(2)}) collective-permute-start(f32[16,32,128]{2,0,1:T(8,128)S(1)} %get-tuple-element.22), channel_id=1, source_target_pairs={{0,64},{64,0},{1,65},{65,1},{128,192},{192,128},{129,193},{193,129... | collective-permute-start | bytes 786440 | tf_op jit(solution)/shard_map/ppermute | solution.py:74
  139.8 9.6 %collective-permute-start.18 = (f32[16,16,128]{2,0,1:T(8,128)S(1)}, f32[16,16,128]{2,0,1:T(8,128)S(1)}, u32[]{:S(2)}, u32[]{:S(2)}) collective-permute-start(f32[16,16,128]{2,0,1:T(8,128)S(1)} %slice_select_fusion.2), channel_id=1, source_target_pairs={{0,256},{1,257},{2,258},{3,259},{4,260},{5,261},{6,262},{7,263},{8... | collective-permute-start | bytes 393224 | tf_op jit(solution)/shard_map/ppermute | solution.py:74
  149.5 7.3 %collective-permute-start.19 = (f32[16,8,128]{2,0,1:T(8,128)S(1)}, f32[16,8,128]{2,0,1:T(8,128)S(1)}, u32[]{:S(2)}, u32[]{:S(2)}) collective-permute-start(f32[16,8,128]{2,0,1:T(8,128)S(1)} %get-tuple-element.25), channel_id=1, source_target_pairs={{0,0},{128,1},{64,64},{192,65},{1,128},{129,129},{65,192},{193,193... | collective-permute-start | bytes 196616 | tf_op jit(solution)/shard_map/ppermute | solution.py:74
  153.7 6.8 %collective-permute-start.20 = (f32[16,8,128]{2,0,1:T(8,128)S(1)}, f32[16,8,128]{2,0,1:T(8,128)S(1)}, u32[]{:S(2)}, u32[]{:S(2)}) collective-permute-start(f32[16,8,128]{2,0,1:T(8,128)S(1)} %get-tuple-element.26), channel_id=1, source_target_pairs={{64,0},{192,1},{0,64},{128,65},{65,128},{193,129},{1,192},{129,193... | collective-permute-start | bytes 196616 | tf_op jit(solution)/shard_map/ppermute | solution.py:74

commit v5 on v4

--- a/solution.py
+++ b/solution.py
@@ -81,7 +81,7 @@
 
 
 def by_h(own, other, h):
-    return jnp.where(h == 0, jnp.concatenate([own, other], 1), jnp.concatenate([other, own], 1))
+    return jnp.where(h == 0, jnp.concatenate([own, other], 0), jnp.concatenate([other, own], 0))
 
 
 def body(estimate, observed, psf_taps, intersection):
@@ -98,26 +98,32 @@
     taps = psf_taps.shape[2]
     half = (taps - 1) // 2
 
-    def piece(block, turn):
-        return lax.dynamic_slice_in_dim(block, SLAB * ((x + turn) % 2), SLAB, 0)
+    def piece(value, turn, axis):
+        return lax.dynamic_slice_in_dim(value, SLAB * ((x + turn) % 2), SLAB, axis)
+
+    def ordered(pair, first):
+        one, two = pair
+        return jnp.where(first, one, two), jnp.where(first, two, one)
 
     even = p % 2 == 0
-    est = [send(piece(estimate, turn), SPREAD[turn]) for turn in (0, 1)]
-    quarter = jnp.where(even, jnp.concatenate(est, 1), jnp.concatenate(est[::-1], 1))
-    current = by_h(quarter, send(quarter, SWAP_H), h)
-    images = [piece(observed[0], turn) for turn in (0, 1)]
-    *images, _ = lax.optimization_barrier((*images, quarter))
-    images = [send(image, route) for image, route in zip(images, SPREAD)]
-    current, images[0] = lax.optimization_barrier((current, images[0]))
+    flipped = jnp.swapaxes(estimate, 0, 1)
+    both = by_h(flipped, send(flipped, SWAP_H), h)
+    current = jnp.concatenate(
+        ordered([send(piece(both, turn, 1), SPREAD[turn]) for turn in (0, 1)], even), 0
+    )
+    images = [send(piece(observed[0], turn, 0), SPREAD[turn]) for turn in (0, 1)]
+    psf_taps, intersection, current = lax.optimization_barrier((psf_taps, intersection, current))
 
     kernels = psf_taps / jnp.sum(psf_taps, axis=2, keepdims=True)
     views = jnp.arange(kernels.shape[0], dtype=jnp.int32)
     own_views = 4 * h + 2 * core + jnp.stack([p % 2, (p + 1) % 2])
     picker = (own_views[:, None] == views[None, :]).astype(jnp.float32)
     own = jnp.einsum("uv,vdk->udk", picker, kernels, precision=HIGHEST)
-    quarters = jnp.stack([core, 2 + core, 1 - core, 3 - core])
-    quarter_width = full_width // 4
-    local_y = (quarters[:, None] * quarter_width + jnp.arange(quarter_width, dtype=jnp.int32)[None, :]).reshape(-1)
+    width = full_width // 2
+    block = estimate.shape[1]
+    place = jnp.arange(width, dtype=jnp.int32)
+    place = place // (2 * block) * block + place // block % 2 * width + place % block
+    local_y = jnp.concatenate([place + core * (width // 2), place + (1 - core) * (width // 2)])
     all_y = jnp.arange(full_width, dtype=jnp.int32)
     all_z = jnp.arange(depth, dtype=jnp.int32)
     slab = jnp.arange(SLAB, dtype=jnp.int32)
@@ -140,44 +146,41 @@
         inside = jnp.logical_and(source >= 0, source < length).astype(jnp.float32)
         return jnp.einsum("yk,vk->vy", inside, kernel, precision=HIGHEST)
 
-    weight_cols = coverage(kernels[:, 1], local_y[: 2 * quarter_width], full_width)
+    weight_cols = coverage(kernels[:, 1], local_y[:width], full_width)
     weight_depth = coverage(kernels[:, 2], all_z, depth)
-    weight_plane = weight_rows[:, :, None] * weight_cols[:, None, :]
-    weights = jnp.einsum("vxy,vz->xyz", weight_plane, weight_depth, precision=HIGHEST)
+    weight_plane = weight_cols[:, :, None] * weight_rows[:, None, :]
+    weights = jnp.einsum("vyx,vz->yxz", weight_plane, weight_depth, precision=HIGHEST)
     own_masks = jnp.einsum("uv,vj->uj", picker, masks[:, SLAB : 2 * SLAB], precision=HIGHEST)
     inside = own_masks[:, :, None, None] > 0
 
-    width = 2 * quarter_width
     scale = 1.0 / (weights + 1.0)
     for iteration in range(ITERS):
-        extended = jnp.concatenate([send(current, ODD), current, send(current, EVEN)], 0)
+        extended = jnp.concatenate([send(current, ODD), current, send(current, EVEN)], 1)
         if iteration == 0:
-            extended, images[1] = lax.optimization_barrier((extended, images[1]))
+            extended, scale, inside, mat_x, mat_y, mat_z, *images = lax.optimization_barrier(
+                (extended, scale, inside, mat_x, mat_y, mat_z, *images)
+            )
             images = jnp.stack(images)
-        extended = jnp.concatenate([extended, send(extended, SWAP_CORE)], 1)
-        blurred = jnp.einsum("urj,jyz->uryz", mat_x, extended, precision=HIGH)
+        extended = jnp.concatenate([extended, send(extended, SWAP_CORE)], 0)
+        blurred = jnp.einsum("urj,yjz->uryz", mat_x, extended, precision=HIGH)
         blurred = jnp.einsum("urjz,uyj->uryz", blurred, mat_y, precision=HIGH)
         blurred = jnp.einsum("uryz,uzw->uryw", blurred, mat_z, precision=HIGH)
         ratio = jnp.where(inside, images / jnp.where(inside, blurred, 1.0), 0.0)
         back = jnp.einsum("uryw,uzw->uryz", ratio, mat_z, precision=HIGH)
         back = jnp.einsum("uryz,uyj->urjz", back, mat_y, precision=HIGH)
-        back = jnp.einsum("urj,uryz->jyz", mat_x, back, precision=HIGH)
-        part = back[:, :width] + send(back[:, width:], SWAP_CORE)
-        part = part[SLAB : 2 * SLAB] + send(part[:SLAB], ODD) + send(part[2 * SLAB :], EVEN)
+        back = jnp.einsum("urj,uryz->yjz", mat_x, back, precision=HIGH)
+        part = back[:width] + send(back[width:], SWAP_CORE)
+        part = part[:, SLAB : 2 * SLAB] + send(part[:, :SLAB], ODD) + send(part[:, 2 * SLAB :], EVEN)
         if iteration < ITERS - 1:
             current = current * (part + send(part, SWAP_H) + 1.0) * scale
 
-    def own_half(value, mine):
-        return jnp.where((h == 0) == mine, value[:, :quarter_width], value[:, quarter_width:])
-
-    total = own_half(part, True) + send(own_half(part, False), SWAP_H)
-    quarter = own_half(current, True) * (total + 1.0) * own_half(scale, True)
-
-    block = quarter_width // 2
-    first, second = quarter[:, :block], quarter[:, block:]
-    chosen = [jnp.where(even, first, second), jnp.where(even, second, first)]
-    one, two = (send(value, reverse(route)) for value, route in zip(chosen, SPREAD))
-    return jnp.where(x % 2 == 0, jnp.concatenate([one, two], 0), jnp.concatenate([two, one], 0))
+    own_h = (place // width == h)[:, None, None]
+    terms = current * scale * jnp.where(own_h, part + 1.0, part)
+    terms = ordered([terms[: 2 * block], terms[2 * block :]], even)
+    terms = [send(value, reverse(route)) for value, route in zip(terms, SPREAD)]
+    terms = jnp.concatenate(ordered(terms, x % 2 == 0), 1)
+    mine, other = ordered([terms[:block], terms[block:]], h == 0)
+    return jnp.swapaxes(mine + send(other, SWAP_H), 0, 1)
 
 
 def solution(mesh):

time: 162 us -> 162 us (level)
  waiting for transfers between devices: 52.8 us -> 60.7 us
  local copies, waits for them, and re-layouts: 6.9 us -> 3.35 us
  starting transfers between devices: 81.1 us -> 78.5 us
  other arithmetic: 3.22 us -> 1.11 us
    ppermute x21, waiting for transfers between devices: 52.8 us -> 60.7 us  [send(): return lax.ppermute(value, AXES, pairs)]
    ppermute x21, starting transfers between devices: 81.1 us -> 78.5 us  [send(): return lax.ppermute(value, AXES, pairs)]
    dot_general x2, matrix products: 1.3 us -> 3.68 us  [body(): blurred = jnp.einsum('uryz,uzw->uryw', blurred, mat_z, precision=HIGH)]
  transfers between devices with their start and end apart: 21 -> 21, of which waited for: 16 -> 17; matrix products, arithmetic and copies ran while one was open for 9% -> 4% of each run, Pallas kernels for 0% -> 0%
where the time goes in v5:
time: 162 us; the launch traced here: 160 us
  starting transfers between devices  78.5 us (48%)
  waiting for transfers between devices  60.7 us (37%)
  matrix products  15.6 us (10%)
  local copies, waits for them, and re-layouts  3.35 us (2%)
    ppermute x21, starting transfers between devices, send(): return lax.ppermute(value, AXES, pairs)  78.5 us
    ppermute x21, waiting for transfers between devices, send(): return lax.ppermute(value, AXES, pairs)  60.7 us
    dot_general x2, matrix products, body(): blurred = jnp.einsum('uryz,uzw->uryw', blurred, mat_z, precision=HIGH)  3.68 us
  transfers between devices with their start and end apart: 21, of which 17 were waited for; matrix products, arithmetic and copies ran while one was open for 4% of the time, Pallas kernels for 0%

profile of v5, /device:TPU:57, one launch (start us, length us, event | category | flops | bytes accessed | tf_op | source)
XLA Modules:
  0.0 160.0 jit_solution(18060112161587882059)
XLA Ops:
  0.0 0.9 copy.64
  0.9 10.6 %collective-permute-start = (f32[8,32,128]{2,1,0:T(8,128)S(1)}, f32[8,32,128]{2,1,0:T(8,128)S(1)}, u32[]{:S(2)}, u32[]{:S(2)}) collective-permute-start(f32[8,32,128]{2,1,0:T(8,128)S(1)} %bitcast.101), channel_id=1, source_target_pairs={{0,256},{1,257},{2,258},{3,259},{4,260},{5,261},{6,262},{7,263},{8... | collective-permute-start | bytes 393224 | tf_op jit(solution)/shard_map/ppermute | solution.py:74
  11.6 1.3 dynamic-slice_bitcast_fusion
  12.9 5.2 %collective-permute-start.6 = (f32[16,64,128]{2,1,0:T(8,128)S(1)}, f32[16,64,128]{2,1,0:T(8,128)}, u32[]{:S(2)}, u32[]{:S(2)}) collective-permute-start(f32[16,64,128]{2,1,0:T(8,128)S(1)} %get-tuple-element.29), channel_id=1, source_target_pairs={{0,64},{1,192},{64,0},{65,128},{128,65},{129,193},{192,1},{193,129... | collective-permute-start | bytes 1572872 | tf_op jit(solution)/shard_map/ppermute | solution.py:74
  18.2 2.2 %collective-permute-start.5 = (f32[16,64,128]{2,1,0:T(8,128)S(1)}, f32[16,64,128]{2,1,0:T(8,128)}, u32[]{:S(2)}, u32[]{:S(2)}) collective-permute-start(f32[16,64,128]{2,1,0:T(8,128)S(1)} %get-tuple-element.30), channel_id=1, source_target_pairs={{0,0},{1,128},{64,64},{65,192},{128,1},{129,129},{192,65},{193,193... | collective-permute-start | bytes 1572872 | tf_op jit(solution)/shard_map/ppermute | solution.py:74
  20.8 4.9 %collective-permute-start.1 = (f32[16,16,128]{2,1,0:T(8,128)S(1)}, f32[16,16,128]{2,1,0:T(8,128)S(1)}, u32[]{:S(2)}, u32[]{:S(2)}) collective-permute-start(f32[16,16,128]{2,1,0:T(8,128)S(1)} %get-tuple-element.41), channel_id=1, source_target_pairs={{0,0},{1,128},{64,64},{65,192},{128,1},{129,129},{192,65},{193,193... | collective-permute-start | bytes 393224 | tf_op jit(solution)/shard_map/ppermute | solution.py:74
  25.7 1.9 %collective-permute-start.2 = (f32[16,16,128]{2,1,0:T(8,128)S(1)}, f32[16,16,128]{2,1,0:T(8,128)S(1)}, u32[]{:S(2)}, u32[]{:S(2)}) collective-permute-start(f32[16,16,128]{2,1,0:T(8,128)S(1)} %get-tuple-element.42), channel_id=1, source_target_pairs={{0,64},{1,192},{64,0},{65,128},{128,65},{129,193},{192,1},{193,129... | collective-permute-start | bytes 393224 | tf_op jit(solution)/shard_map/ppermute | solution.py:74
  27.7 6.1 %collective-permute-done.1 = f32[16,16,128]{2,1,0:T(8,128)S(1)} collective-permute-done((f32[16,16,128]{2,1,0:T(8,128)S(1)}, f32[16,16,128]{2,1,0:T(8,128)S(1)}, u32[]{:S(2)}, u32[]{:S(2)}) %collective-permute-start.1) | collective-permute-done | bytes 131104 | tf_op jit(solution)/shard_map/ppermute | solution.py:74
  33.8 1.0 collective-permute-done.2
  34.9 1.9 %collective-permute-start.4 = (f32[32,16,128]{2,1,0:T(8,128)S(1)}, f32[32,16,128]{2,1,0:T(8,128)S(1)}, u32[]{:S(2)}, u32[]{:S(2)}) collective-permute-start(f32[32,16,128]{2,1,0:T(8,128)S(1)} %pad_maximum_fusion.3), channel_id=1, source_target_pairs={{0,64},{64,0},{1,65},{65,1},{128,192},{192,128},{129,193},{193,129... | collective-permute-start | bytes 786440 | tf_op jit(solution)/shard_map/ppermute | solution.py:74
  36.9 1.9 %collective-permute-start.3 = (f32[32,16,128]{2,1,0:T(8,128)S(1)}, f32[32,16,128]{2,1,0:T(8,128)S(1)}, u32[]{:S(2)}, u32[]{:S(2)}) collective-permute-start(f32[32,16,128]{2,1,0:T(8,128)S(1)} %pad_maximum_fusion.3), channel_id=1, source_target_pairs={{64,128},{128,64},{65,129},{129,65},{192,194},{194,192},{193,195},... | collective-permute-start | bytes 786440 | tf_op jit(solution)/shard_map/ppermute | solution.py:74
  39.0 0.2 fusion.58
  39.2 0.2 fusion.72
  39.4 0.2 fusion.30
  39.6 0.4 fusion.24
  40.0 0.7 fusion.26
  40.7 0.8 fusion
  41.5 0.2 fusion.51
  41.7 0.3 fusion.37
  42.0 0.1 convolution_bitcast_fusion.4
  42.1 0.2 fusion.16
  42.3 0.8 fusion.15
  43.1 5.2 %collective-permute-done.3 = f32[32,16,128]{2,1,0:T(8,128)S(1)} collective-permute-done((f32[32,16,128]{2,1,0:T(8,128)S(1)}, f32[32,16,128]{2,1,0:T(8,128)S(1)}, u32[]{:S(2)}, u32[]{:S(2)}) %collective-permute-start.3) | collective-permute-done | bytes 262176 | tf_op jit(solution)/shard_map/ppermute | solution.py:74
  48.4 2.0 %collective-permute-start.7 = (f32[32,48,128]{2,1,0:T(8,128)S(1)}, f32[32,48,128]{2,1,0:T(8,128)S(1)}, u32[]{:S(2)}, u32[]{:S(2)}) collective-permute-start(f32[32,48,128]{2,1,0:T(8,128)S(1)} %pad_maximum_fusion.1), channel_id=1, source_target_pairs={{0,1},{1,0},{2,3},{3,2},{4,5},{5,4},{6,7},{7,6},{8,9},{9,8},{10,11... | collective-permute-start | bytes 2359304 | tf_op jit(solution)/shard_map/ppermute | solution.py:74
  50.6 1.9 %collective-permute-done.7 = f32[32,48,128]{2,1,0:T(8,128)S(1)} collective-permute-done((f32[32,48,128]{2,1,0:T(8,128)S(1)}, f32[32,48,128]{2,1,0:T(8,128)S(1)}, u32[]{:S(2)}, u32[]{:S(2)}) %collective-permute-start.7) | collective-permute-done | bytes 786464 | tf_op jit(solution)/shard_map/ppermute | solution.py:74
  52.5 0.6 fusion.1
  53.1 0.9 convolution_bitcast_fusion.3
  54.0 1.8 %fusion.12 = f32[2,16,64,128]{3,2,1,0:T(8,128)S(1)} fusion(f32[2,16,64,128]{3,2,1,0:T(8,128)S(1)} %convolution_bitcast_fusion.3, f32[1,16,64,128]{3,2,1,0:T(8,128)} %bitcast.25, f32[1,16,64,128]{3,2,1,0:T(8,128)} %bitcast.24, pred[2,16]{1,0:T(4,128)(4,1)S(1)} %bitcast.110, f32[2,128,128,1]{2,0,1,3:T(2,128)S(1)} %bitcast.106), kind=kOutput, calls=%fused_computation.21 | convolution fusion | flops 202375168 | bytes 3276832 | tf_op jit(solution)/shard_map/uryz,uzw->uryw/dot_general | solution.py:167
  55.8 0.6 fusion.92
  56.4 0.6 fusion.93
  57.0 1.4 convolution_bitcast_fusion.1
  58.4 2.0 %collective-permute-start.8 = (f32[32,48,128]{2,1,0:T(8,128)S(1)}, f32[32,48,128]{2,1,0:T(8,128)S(1)}, u32[]{:S(2)}, u32[]{:S(2)}) collective-permute-start(f32[32,48,128]{2,1,0:T(8,128)S(1)} %slice.91), channel_id=1, source_target_pairs={{0,1},{1,0},{2,3},{3,2},{4,5},{5,4},{6,7},{7,6},{8,9},{9,8},{10,11... | collective-permute-start | bytes 2359304 | tf_op jit(solution)/shard_map/ppermute | solution.py:74
  60.5 2.1 %collective-permute-done.8 = f32[32,48,128]{2,1,0:T(8,128)S(1)} collective-permute-done((f32[32,48,128]{2,1,0:T(8,128)S(1)}, f32[32,48,128]{2,1,0:T(8,128)S(1)}, u32[]{:S(2)}, u32[]{:S(2)}) %collective-permute-start.8) | collective-permute-done | bytes 786464 | tf_op jit(solution)/shard_map/ppermute | solution.py:74
  62.7 3.3 %collective-permute-start.9 = (f32[32,16,128]{2,1,0:T(8,128)S(1)}, f32[32,16,128]{2,1,0:T(8,128)S(1)}, u32[]{:S(2)}, u32[]{:S(2)}) collective-permute-start(f32[32,16,128]{2,1,0:T(8,128)S(1)} %get-tuple-element.33), channel_id=1, source_target_pairs={{64,128},{128,64},{65,129},{129,65},{192,194},{194,192},{193,195},... | collective-permute-start | bytes 786440 | tf_op jit(solution)/shard_map/ppermute | solution.py:74
  66.0 1.9 %collective-permute-start.10 = (f32[32,16,128]{2,1,0:T(8,128)S(1)}, f32[32,16,128]{2,1,0:T(8,128)S(1)}, u32[]{:S(2)}, u32[]{:S(2)}) collective-permute-start(f32[32,16,128]{2,1,0:T(8,128)S(1)} %get-tuple-element.34), channel_id=1, source_target_pairs={{0,64},{64,0},{1,65},{65,1},{128,192},{192,128},{129,193},{193,129... | collective-permute-start | bytes 786440 | tf_op jit(solution)/shard_map/ppermute | solution.py:74
  67.9 6.6 %collective-permute-done.9 = f32[32,16,128]{2,1,0:T(8,128)S(1)} collective-permute-done((f32[32,16,128]{2,1,0:T(8,128)S(1)}, f32[32,16,128]{2,1,0:T(8,128)S(1)}, u32[]{:S(2)}, u32[]{:S(2)}) %collective-permute-start.9) | collective-permute-done | bytes 262176 | tf_op jit(solution)/shard_map/ppermute | solution.py:74
  74.5 0.6 collective-permute-done.10
  75.2 7.6 %collective-permute-start.11 = (f32[32,16,128]{2,1,0:T(8,128)S(1)}, f32[32,16,128]{2,1,0:T(8,128)S(1)}, u32[]{:S(2)}, u32[]{:S(2)}) collective-permute-start(f32[32,16,128]{2,1,0:T(8,128)S(1)} %fusion.29), channel_id=1, source_target_pairs={{0,256},{1,257},{2,258},{3,259},{4,260},{5,261},{6,262},{7,263},{8... | collective-permute-start | bytes 786440 | tf_op jit(solution)/shard_map/ppermute | solution.py:74
  82.7 11.3 %collective-permute-done.11 = f32[32,16,128]{2,1,0:T(8,128)S(1)} collective-permute-done((f32[32,16,128]{2,1,0:T(8,128)S(1)}, f32[32,16,128]{2,1,0:T(8,128)S(1)}, u32[]{:S(2)}, u32[]{:S(2)}) %collective-permute-start.11) | collective-permute-done | bytes 262176 | tf_op jit(solution)/shard_map/ppermute | solution.py:74
  94.1 2.2 %collective-permute-start.13 = (f32[32,16,128]{2,1,0:T(8,128)S(1)}, f32[32,16,128]{2,1,0:T(8,128)S(1)}, u32[]{:S(2)}, u32[]{:S(2)}) collective-permute-start(f32[32,16,128]{2,1,0:T(8,128)S(1)} %multiply_multiply_fusion), channel_id=1, source_target_pairs={{0,64},{64,0},{1,65},{65,1},{128,192},{192,128},{129,193},{193,129... | collective-permute-start | bytes 786440 | tf_op jit(solution)/shard_map/ppermute | solution.py:74
  96.3 6.1 %collective-permute-start.12 = (f32[32,16,128]{2,1,0:T(8,128)S(1)}, f32[32,16,128]{2,1,0:T(8,128)S(1)}, u32[]{:S(2)}, u32[]{:S(2)}) collective-permute-start(f32[32,16,128]{2,1,0:T(8,128)S(1)} %multiply_multiply_fusion), channel_id=1, source_target_pairs={{64,128},{128,64},{65,129},{129,65},{192,194},{194,192},{193,195},... | collective-permute-start | bytes 786440 | tf_op jit(solution)/shard_map/ppermute | solution.py:74
  102.4 1.0 collective-permute-done.13
  103.4 4.6 %collective-permute-done.12 = f32[32,16,128]{2,1,0:T(8,128)S(1)} collective-permute-done((f32[32,16,128]{2,1,0:T(8,128)S(1)}, f32[32,16,128]{2,1,0:T(8,128)S(1)}, u32[]{:S(2)}, u32[]{:S(2)}) %collective-permute-start.12) | collective-permute-done | bytes 262176 | tf_op jit(solution)/shard_map/ppermute | solution.py:74
  108.0 3.8 %collective-permute-start.14 = (f32[32,48,128]{2,1,0:T(8,128)S(1)}, f32[32,48,128]{2,1,0:T(8,128)S(1)}, u32[]{:S(2)}, u32[]{:S(2)}) collective-permute-start(f32[32,48,128]{2,1,0:T(8,128)S(1)} %pad_maximum_fusion.2), channel_id=1, source_target_pairs={{0,1},{1,0},{2,3},{3,2},{4,5},{5,4},{6,7},{7,6},{8,9},{9,8},{10,11... | collective-permute-start | bytes 2359304 | tf_op jit(solution)/shard_map/ppermute | solution.py:74
  111.8 1.7 %collective-permute-done.14 = f32[32,48,128]{2,1,0:T(8,128)S(1)} collective-permute-done((f32[32,48,128]{2,1,0:T(8,128)S(1)}, f32[32,48,128]{2,1,0:T(8,128)S(1)}, u32[]{:S(2)}, u32[]{:S(2)}) %collective-permute-start.14) | collective-permute-done | bytes 786464 | tf_op jit(solution)/shard_map/ppermute | solution.py:74
  113.5 0.6 fusion.4
  114.1 0.9 convolution_bitcast_fusion.2
  115.0 1.8 %fusion.14 = f32[2,16,64,128]{3,2,1,0:T(8,128)S(1)} fusion(f32[2,16,64,128]{3,2,1,0:T(8,128)S(1)} %convolution_bitcast_fusion.2, f32[1,16,64,128]{3,2,1,0:T(8,128)} %bitcast.25, f32[1,16,64,128]{3,2,1,0:T(8,128)} %bitcast.24, pred[2,16]{1,0:T(4,128)(4,1)S(1)} %bitcast.111, f32[2,128,128,1]{2,0,1,3:T(2,128)S(1)} %bitcast.107), kind=kOutput, calls=%fused_computation.23 | convolution fusion | flops 202375168 | bytes 3276832 | tf_op jit(solution)/shard_map/uryz,uzw->uryw/dot_general | solution.py:167
  116.8 0.6 fusion.94
  117.4 0.6 fusion.95
  117.9 1.4 convolution_bitcast_fusion
  119.4 2.3 %collective-permute-start.15 = (f32[32,48,128]{2,1,0:T(8,128)S(1)}, f32[32,48,128]{2,1,0:T(8,128)S(1)}, u32[]{:S(2)}, u32[]{:S(2)}) collective-permute-start(f32[32,48,128]{2,1,0:T(8,128)S(1)} %slice.96), channel_id=1, source_target_pairs={{0,1},{1,0},{2,3},{3,2},{4,5},{5,4},{6,7},{7,6},{8,9},{9,8},{10,11... | collective-permute-start | bytes 2359304 | tf_op jit(solution)/shard_map/ppermute | solution.py:74
  121.7 1.9 %collective-permute-done.15 = f32[32,48,128]{2,1,0:T(8,128)S(1)} collective-permute-done((f32[32,48,128]{2,1,0:T(8,128)S(1)}, f32[32,48,128]{2,1,0:T(8,128)S(1)}, u32[]{:S(2)}, u32[]{:S(2)}) %collective-permute-start.15) | collective-permute-done | bytes 786464 | tf_op jit(solution)/shard_map/ppermute | solution.py:74
  123.7 5.5 %collective-permute-start.16 = (f32[32,16,128]{2,1,0:T(8,128)S(1)}, f32[32,16,128]{2,1,0:T(8,128)S(1)}, u32[]{:S(2)}, u32[]{:S(2)}) collective-permute-start(f32[32,16,128]{2,1,0:T(8,128)S(1)} %get-tuple-element.31), channel_id=1, source_target_pairs={{64,128},{128,64},{65,129},{129,65},{192,194},{194,192},{193,195},... | collective-permute-start | bytes 786440 | tf_op jit(solution)/shard_map/ppermute | solution.py:74
  129.2 1.9 %collective-permute-start.17 = (f32[32,16,128]{2,1,0:T(8,128)S(1)}, f32[32,16,128]{2,1,0:T(8,128)S(1)}, u32[]{:S(2)}, u32[]{:S(2)}) collective-permute-start(f32[32,16,128]{2,1,0:T(8,128)S(1)} %get-tuple-element.32), channel_id=1, source_target_pairs={{0,64},{64,0},{1,65},{65,1},{128,192},{192,128},{129,193},{193,129... | collective-permute-start | bytes 786440 | tf_op jit(solution)/shard_map/ppermute | solution.py:74
  131.1 4.1 %collective-permute-done.16 = f32[32,16,128]{2,1,0:T(8,128)S(1)} collective-permute-done((f32[32,16,128]{2,1,0:T(8,128)S(1)}, f32[32,16,128]{2,1,0:T(8,128)S(1)}, u32[]{:S(2)}, u32[]{:S(2)}) %collective-permute-start.16) | collective-permute-done | bytes 262176 | tf_op jit(solution)/shard_map/ppermute | solution.py:74
  135.2 3.1 %collective-permute-done.17 = f32[32,16,128]{2,1,0:T(8,128)S(1)} collective-permute-done((f32[32,16,128]{2,1,0:T(8,128)S(1)}, f32[32,16,128]{2,1,0:T(8,128)S(1)}, u32[]{:S(2)}, u32[]{:S(2)}) %collective-permute-start.17) | collective-permute-done | bytes 262176 | tf_op jit(solution)/shard_map/ppermute | solution.py:74
  138.4 1.9 %collective-permute-start.18 = (f32[16,16,128]{2,1,0:T(8,128)S(1)}, f32[16,16,128]{2,1,0:T(8,128)S(1)}, u32[]{:S(2)}, u32[]{:S(2)}) collective-permute-start(f32[16,16,128]{2,1,0:T(8,128)S(1)} %get-tuple-element.37), channel_id=1, source_target_pairs={{0,0},{128,1},{64,64},{192,65},{1,128},{129,129},{65,192},{193,193... | collective-permute-start | bytes 393224 | tf_op jit(solution)/shard_map/ppermute | solution.py:74
  140.3 4.9 %collective-permute-start.19 = (f32[16,16,128]{2,1,0:T(8,128)S(1)}, f32[16,16,128]{2,1,0:T(8,128)S(1)}, u32[]{:S(2)}, u32[]{:S(2)}) collective-permute-start(f32[16,16,128]{2,1,0:T(8,128)S(1)} %get-tuple-element.38), channel_id=1, source_target_pairs={{64,0},{192,1},{0,64},{128,65},{65,128},{193,129},{1,192},{129,193... | collective-permute-start | bytes 393224 | tf_op jit(solution)/shard_map/ppermute | solution.py:74
  145.3 1.0 collective-permute-done.18
  146.2 1.7 %collective-permute-done.19 = f32[16,16,128]{2,1,0:T(8,128)S(1)} collective-permute-done((f32[16,16,128]{2,1,0:T(8,128)S(1)}, f32[16,16,128]{2,1,0:T(8,128)S(1)}, u32[]{:S(2)}, u32[]{:S(2)}) %collective-permute-start.19) | collective-permute-done | bytes 131104 | tf_op jit(solution)/shard_map/ppermute | solution.py:74
  147.9 4.4 %collective-permute-start.20 = (f32[8,32,128]{2,1,0:T(8,128)S(1)}, f32[8,32,128]{2,1,0:T(8,128)S(1)}, u32[]{:S(2)}, u32[]{:S(2)}) collective-permute-start(f32[8,32,128]{2,1,0:T(8,128)S(1)} %broadcast_select_fusion.4), channel_id=1, source_target_pairs={{0,256},{1,257},{2,258},{3,259},{4,260},{5,261},{6,262},{7,263},{8... | collective-permute-start | bytes 393224 | tf_op jit(solution)/shard_map/ppermute | solution.py:74
  152.3 6.9 %collective-permute-done.20 = f32[8,32,128]{2,1,0:T(8,128)S(1)} collective-permute-done((f32[8,32,128]{2,1,0:T(8,128)S(1)}, f32[8,32,128]{2,1,0:T(8,128)S(1)}, u32[]{:S(2)}, u32[]{:S(2)}) %collective-permute-start.20) | collective-permute-done | bytes 131104 | tf_op jit(solution)/shard_map/ppermute | solution.py:74
  159.2 0.7 copy.8
  (42 shorter events, 1.5 us)
Async XLA Ops:
  0.9 19.8 %collective-permute-start = (f32[8,32,128]{2,1,0:T(8,128)S(1)}, f32[8,32,128]{2,1,0:T(8,128)S(1)}, u32[]{:S(2)}, u32[]{:S(2)}) collective-permute-start(f32[8,32,128]{2,1,0:T(8,128)S(1)} %bitcast.101), channel_id=1, source_target_pairs={{0,256},{1,257},{2,258},{3,259},{4,260},{5,261},{6,262},{7,263},{8... | collective-permute-start | bytes 393224 | tf_op jit(solution)/shard_map/ppermute | solution.py:74
  12.9 25.9 %copy-start = (f32[8,3,31]{2,0,1:T(8,128)S(1)}, f32[8,3,31]{2,0,1:T(8,128)}, u32[]{:S(2)}) copy-start(f32[8,3,31]{2,0,1:T(8,128)} %param.6) | copy-start | bytes 8932
  12.9 35.4 %collective-permute-start.6 = (f32[16,64,128]{2,1,0:T(8,128)S(1)}, f32[16,64,128]{2,1,0:T(8,128)}, u32[]{:S(2)}, u32[]{:S(2)}) collective-permute-start(f32[16,64,128]{2,1,0:T(8,128)S(1)} %get-tuple-element.29), channel_id=1, source_target_pairs={{0,64},{1,192},{64,0},{65,128},{128,65},{129,193},{192,1},{193,129... | collective-permute-start | bytes 1572872 | tf_op jit(solution)/shard_map/ppermute | solution.py:74
  18.2 30.2 %collective-permute-start.5 = (f32[16,64,128]{2,1,0:T(8,128)S(1)}, f32[16,64,128]{2,1,0:T(8,128)}, u32[]{:S(2)}, u32[]{:S(2)}) collective-permute-start(f32[16,64,128]{2,1,0:T(8,128)S(1)} %get-tuple-element.30), channel_id=1, source_target_pairs={{0,0},{1,128},{64,64},{65,192},{128,1},{129,129},{192,65},{193,193... | collective-permute-start | bytes 1572872 | tf_op jit(solution)/shard_map/ppermute | solution.py:74
  20.7 20.8 %copy-start.1 = (s32[8,16]{1,0:T(8,128)S(1)}, s32[8,16]{1,0:T(8,128)}, u32[]{:S(2)}) copy-start(s32[8,16]{1,0:T(8,128)} %param.7) | copy-start | bytes 1540
  20.8 13.0 %collective-permute-start.1 = (f32[16,16,128]{2,1,0:T(8,128)S(1)}, f32[16,16,128]{2,1,0:T(8,128)S(1)}, u32[]{:S(2)}, u32[]{:S(2)}) collective-permute-start(f32[16,16,128]{2,1,0:T(8,128)S(1)} %get-tuple-element.41), channel_id=1, source_target_pairs={{0,0},{1,128},{64,64},{65,192},{128,1},{129,129},{192,65},{193,193... | collective-permute-start | bytes 393224 | tf_op jit(solution)/shard_map/ppermute | solution.py:74
  25.7 9.2 %collective-permute-start.2 = (f32[16,16,128]{2,1,0:T(8,128)S(1)}, f32[16,16,128]{2,1,0:T(8,128)S(1)}, u32[]{:S(2)}, u32[]{:S(2)}) collective-permute-start(f32[16,16,128]{2,1,0:T(8,128)S(1)} %get-tuple-element.42), channel_id=1, source_target_pairs={{0,64},{1,192},{64,0},{65,128},{128,65},{129,193},{192,1},{193,129... | collective-permute-start | bytes 393224 | tf_op jit(solution)/shard_map/ppermute | solution.py:74
  34.9 8.1 %collective-permute-start.4 = (f32[32,16,128]{2,1,0:T(8,128)S(1)}, f32[32,16,128]{2,1,0:T(8,128)S(1)}, u32[]{:S(2)}, u32[]{:S(2)}) collective-permute-start(f32[32,16,128]{2,1,0:T(8,128)S(1)} %pad_maximum_fusion.3), channel_id=1, source_target_pairs={{0,64},{64,0},{1,65},{65,1},{128,192},{192,128},{129,193},{193,129... | collective-permute-start | bytes 786440 | tf_op jit(solution)/shard_map/ppermute | solution.py:74
  36.9 11.4 %collective-permute-start.3 = (f32[32,16,128]{2,1,0:T(8,128)S(1)}, f32[32,16,128]{2,1,0:T(8,128)S(1)}, u32[]{:S(2)}, u32[]{:S(2)}) collective-permute-start(f32[32,16,128]{2,1,0:T(8,128)S(1)} %pad_maximum_fusion.3), channel_id=1, source_target_pairs={{64,128},{128,64},{65,129},{129,65},{192,194},{194,192},{193,195},... | collective-permute-start | bytes 786440 | tf_op jit(solution)/shard_map/ppermute | solution.py:74
  48.4 4.2 %collective-permute-start.7 = (f32[32,48,128]{2,1,0:T(8,128)S(1)}, f32[32,48,128]{2,1,0:T(8,128)S(1)}, u32[]{:S(2)}, u32[]{:S(2)}) collective-permute-start(f32[32,48,128]{2,1,0:T(8,128)S(1)} %pad_maximum_fusion.1), channel_id=1, source_target_pairs={{0,1},{1,0},{2,3},{3,2},{4,5},{5,4},{6,7},{7,6},{8,9},{9,8},{10,11... | collective-permute-start | bytes 2359304 | tf_op jit(solution)/shard_map/ppermute | solution.py:74
  58.4 4.2 %collective-permute-start.8 = (f32[32,48,128]{2,1,0:T(8,128)S(1)}, f32[32,48,128]{2,1,0:T(8,128)S(1)}, u32[]{:S(2)}, u32[]{:S(2)}) collective-permute-start(f32[32,48,128]{2,1,0:T(8,128)S(1)} %slice.91), channel_id=1, source_target_pairs={{0,1},{1,0},{2,3},{3,2},{4,5},{5,4},{6,7},{7,6},{8,9},{9,8},{10,11... | collective-permute-start | bytes 2359304 | tf_op jit(solution)/shard_map/ppermute | solution.py:74
  62.7 11.8 %collective-permute-start.9 = (f32[32,16,128]{2,1,0:T(8,128)S(1)}, f32[32,16,128]{2,1,0:T(8,128)S(1)}, u32[]{:S(2)}, u32[]{:S(2)}) collective-permute-start(f32[32,16,128]{2,1,0:T(8,128)S(1)} %get-tuple-element.33), channel_id=1, source_target_pairs={{64,128},{128,64},{65,129},{129,65},{192,194},{194,192},{193,195},... | collective-permute-start | bytes 786440 | tf_op jit(solution)/shard_map/ppermute | solution.py:74
  66.0 9.1 %collective-permute-start.10 = (f32[32,16,128]{2,1,0:T(8,128)S(1)}, f32[32,16,128]{2,1,0:T(8,128)S(1)}, u32[]{:S(2)}, u32[]{:S(2)}) collective-permute-start(f32[32,16,128]{2,1,0:T(8,128)S(1)} %get-tuple-element.34), channel_id=1, source_target_pairs={{0,64},{64,0},{1,65},{65,1},{128,192},{192,128},{129,193},{193,129... | collective-permute-start | bytes 786440 | tf_op jit(solution)/shard_map/ppermute | solution.py:74
  75.2 18.9 %collective-permute-start.11 = (f32[32,16,128]{2,1,0:T(8,128)S(1)}, f32[32,16,128]{2,1,0:T(8,128)S(1)}, u32[]{:S(2)}, u32[]{:S(2)}) collective-permute-start(f32[32,16,128]{2,1,0:T(8,128)S(1)} %fusion.29), channel_id=1, source_target_pairs={{0,256},{1,257},{2,258},{3,259},{4,260},{5,261},{6,262},{7,263},{8... | collective-permute-start | bytes 786440 | tf_op jit(solution)/shard_map/ppermute | solution.py:74
  94.1 9.3 %collective-permute-start.13 = (f32[32,16,128]{2,1,0:T(8,128)S(1)}, f32[32,16,128]{2,1,0:T(8,128)S(1)}, u32[]{:S(2)}, u32[]{:S(2)}) collective-permute-start(f32[32,16,128]{2,1,0:T(8,128)S(1)} %multiply_multiply_fusion), channel_id=1, source_target_pairs={{0,64},{64,0},{1,65},{65,1},{128,192},{192,128},{129,193},{193,129... | collective-permute-start | bytes 786440 | tf_op jit(solution)/shard_map/ppermute | solution.py:74
  96.3 11.6 %collective-permute-start.12 = (f32[32,16,128]{2,1,0:T(8,128)S(1)}, f32[32,16,128]{2,1,0:T(8,128)S(1)}, u32[]{:S(2)}, u32[]{:S(2)}) collective-permute-start(f32[32,16,128]{2,1,0:T(8,128)S(1)} %multiply_multiply_fusion), channel_id=1, source_target_pairs={{64,128},{128,64},{65,129},{129,65},{192,194},{194,192},{193,195},... | collective-permute-start | bytes 786440 | tf_op jit(solution)/shard_map/ppermute | solution.py:74
  108.0 5.5 %collective-permute-start.14 = (f32[32,48,128]{2,1,0:T(8,128)S(1)}, f32[32,48,128]{2,1,0:T(8,128)S(1)}, u32[]{:S(2)}, u32[]{:S(2)}) collective-permute-start(f32[32,48,128]{2,1,0:T(8,128)S(1)} %pad_maximum_fusion.2), channel_id=1, source_target_pairs={{0,1},{1,0},{2,3},{3,2},{4,5},{5,4},{6,7},{7,6},{8,9},{9,8},{10,11... | collective-permute-start | bytes 2359304 | tf_op jit(solution)/shard_map/ppermute | solution.py:74
  119.4 4.2 %collective-permute-start.15 = (f32[32,48,128]{2,1,0:T(8,128)S(1)}, f32[32,48,128]{2,1,0:T(8,128)S(1)}, u32[]{:S(2)}, u32[]{:S(2)}) collective-permute-start(f32[32,48,128]{2,1,0:T(8,128)S(1)} %slice.96), channel_id=1, source_target_pairs={{0,1},{1,0},{2,3},{3,2},{4,5},{5,4},{6,7},{7,6},{8,9},{9,8},{10,11... | collective-permute-start | bytes 2359304 | tf_op jit(solution)/shard_map/ppermute | solution.py:74
  123.7 11.5 %collective-permute-start.16 = (f32[32,16,128]{2,1,0:T(8,128)S(1)}, f32[32,16,128]{2,1,0:T(8,128)S(1)}, u32[]{:S(2)}, u32[]{:S(2)}) collective-permute-start(f32[32,16,128]{2,1,0:T(8,128)S(1)} %get-tuple-element.31), channel_id=1, source_target_pairs={{64,128},{128,64},{65,129},{129,65},{192,194},{194,192},{193,195},... | collective-permute-start | bytes 786440 | tf_op jit(solution)/shard_map/ppermute | solution.py:74
  129.2 9.1 %collective-permute-start.17 = (f32[32,16,128]{2,1,0:T(8,128)S(1)}, f32[32,16,128]{2,1,0:T(8,128)S(1)}, u32[]{:S(2)}, u32[]{:S(2)}) collective-permute-start(f32[32,16,128]{2,1,0:T(8,128)S(1)} %get-tuple-element.32), channel_id=1, source_target_pairs={{0,64},{64,0},{1,65},{65,1},{128,192},{192,128},{129,193},{193,129... | collective-permute-start | bytes 786440 | tf_op jit(solution)/shard_map/ppermute | solution.py:74
  138.4 7.8 %collective-permute-start.18 = (f32[16,16,128]{2,1,0:T(8,128)S(1)}, f32[16,16,128]{2,1,0:T(8,128)S(1)}, u32[]{:S(2)}, u32[]{:S(2)}) collective-permute-start(f32[16,16,128]{2,1,0:T(8,128)S(1)} %get-tuple-element.37), channel_id=1, source_target_pairs={{0,0},{128,1},{64,64},{192,65},{1,128},{129,129},{65,192},{193,193... | collective-permute-start | bytes 393224 | tf_op jit(solution)/shard_map/ppermute | solution.py:74
  140.3 7.5 %collective-permute-start.19 = (f32[16,16,128]{2,1,0:T(8,128)S(1)}, f32[16,16,128]{2,1,0:T(8,128)S(1)}, u32[]{:S(2)}, u32[]{:S(2)}) collective-permute-start(f32[16,16,128]{2,1,0:T(8,128)S(1)} %get-tuple-element.38), channel_id=1, source_target_pairs={{64,0},{192,1},{0,64},{128,65},{65,128},{193,129},{1,192},{129,193... | collective-permute-start | bytes 393224 | tf_op jit(solution)/shard_map/ppermute | solution.py:74
  147.9 11.3 %collective-permute-start.20 = (f32[8,32,128]{2,1,0:T(8,128)S(1)}, f32[8,32,128]{2,1,0:T(8,128)S(1)}, u32[]{:S(2)}, u32[]{:S(2)}) collective-permute-start(f32[8,32,128]{2,1,0:T(8,128)S(1)} %broadcast_select_fusion.4), channel_id=1, source_target_pairs={{0,256},{1,257},{2,258},{3,259},{4,260},{5,261},{6,262},{7,263},{8... | collective-permute-start | bytes 393224 | tf_op jit(solution)/shard_map/ppermute | solution.py:74

commit v6 on v5

--- a/solution.py
+++ b/solution.py
@@ -111,12 +111,18 @@
     current = jnp.concatenate(
         ordered([send(piece(both, turn, 1), SPREAD[turn]) for turn in (0, 1)], even), 0
     )
-    images = [send(piece(observed[0], turn, 0), SPREAD[turn]) for turn in (0, 1)]
-    psf_taps, intersection, current = lax.optimization_barrier((psf_taps, intersection, current))
+    images = [piece(observed[0], turn, 0) for turn in (0, 1)]
+    *others, _ = lax.optimization_barrier((*images, both))
+    images = [send(image, SPREAD[turn]) for turn, image in enumerate(images)] + [
+        send(send(image, SWAP_H), SPREAD[turn]) for turn, image in enumerate(others)
+    ]
+    psf_taps, intersection, current, *images[:2] = lax.optimization_barrier(
+        (psf_taps, intersection, current, *images[:2])
+    )
 
     kernels = psf_taps / jnp.sum(psf_taps, axis=2, keepdims=True)
     views = jnp.arange(kernels.shape[0], dtype=jnp.int32)
-    own_views = 4 * h + 2 * core + jnp.stack([p % 2, (p + 1) % 2])
+    own_views = 2 * core + jnp.stack([4 * g + turn for g in (h, 1 - h) for turn in (p % 2, (p + 1) % 2)])
     picker = (own_views[:, None] == views[None, :]).astype(jnp.float32)
     own = jnp.einsum("uv,vdk->udk", picker, kernels, precision=HIGHEST)
     width = full_width // 2
@@ -157,11 +163,14 @@
     for iteration in range(ITERS):
         extended = jnp.concatenate([send(current, ODD), current, send(current, EVEN)], 1)
         if iteration == 0:
-            extended, scale, inside, mat_x, mat_y, mat_z, *images = lax.optimization_barrier(
-                (extended, scale, inside, mat_x, mat_y, mat_z, *images)
+            extended, scale, inside, mat_x, mat_y, mat_z, *images[:3] = lax.optimization_barrier(
+                (extended, scale, inside, mat_x, mat_y, mat_z, *images[:3])
             )
+        swapped = send(extended, SWAP_CORE)
+        if iteration == 0:
+            swapped, images[3] = lax.optimization_barrier((swapped, images[3]))
             images = jnp.stack(images)
-        extended = jnp.concatenate([extended, send(extended, SWAP_CORE)], 0)
+        extended = jnp.concatenate([extended, swapped], 0)
         blurred = jnp.einsum("urj,yjz->uryz", mat_x, extended, precision=HIGH)
         blurred = jnp.einsum("urjz,uyj->uryz", blurred, mat_y, precision=HIGH)
         blurred = jnp.einsum("uryz,uzw->uryw", blurred, mat_z, precision=HIGH)
@@ -172,15 +181,16 @@
         part = back[:width] + send(back[width:], SWAP_CORE)
         part = part[:, SLAB : 2 * SLAB] + send(part[:, :SLAB], ODD) + send(part[:, 2 * SLAB :], EVEN)
         if iteration < ITERS - 1:
-            current = current * (part + send(part, SWAP_H) + 1.0) * scale
-
-    own_h = (place // width == h)[:, None, None]
-    terms = current * scale * jnp.where(own_h, part + 1.0, part)
-    terms = ordered([terms[: 2 * block], terms[2 * block :]], even)
-    terms = [send(value, reverse(route)) for value, route in zip(terms, SPREAD)]
-    terms = jnp.concatenate(ordered(terms, x % 2 == 0), 1)
-    mine, other = ordered([terms[:block], terms[block:]], h == 0)
-    return jnp.swapaxes(mine + send(other, SWAP_H), 0, 1)
+            current = current * (part + 1.0) * scale
+
+    def own_half(value):
+        value = value.reshape(2, 2, block, SLAB, depth)
+        return jnp.where(h == 0, value[:, 0], value[:, 1])
+
+    result = own_half(current) * (own_half(part) + 1.0) * own_half(scale)
+    result = ordered([result[0], result[1]], even)
+    result = [send(value, reverse(route)) for value, route in zip(result, SPREAD)]
+    return jnp.swapaxes(jnp.concatenate(ordered(result, x % 2 == 0), 1), 0, 1)
 
 
 def solution(mesh):

time: 162 us -> 182 us (1.12); the launches traced: 160 us -> 178 us
  starting transfers between devices: 78.5 us -> 85.9 us
  matrix products: 15.6 us -> 21.9 us
  waiting for transfers between devices: 60.7 us -> 64 us
    ppermute x21 -> x23, starting transfers between devices: 78.5 us -> 85.9 us  [send(): return lax.ppermute(value, AXES, pairs)]
    dot_general x2, matrix products: 1.12 us -> 4.58 us  [body(): back = jnp.einsum('uryw,uzw->uryz', ratio, mat_z, precision=HIGH)]
    ppermute x21 -> x23, waiting for transfers between devices: 60.7 us -> 64 us  [send(): return lax.ppermute(value, AXES, pairs)]
  transfers between devices with their start and end apart: 21 -> 23, of which waited for: 17 -> 16; matrix products, arithmetic and copies ran while one was open for 4% -> 3% of each run, Pallas kernels for 0% -> 0%
where the time goes in v6:
time: 182 us; the launch traced here: 178 us
  starting transfers between devices  85.9 us (47%)
  waiting for transfers between devices  64 us (35%)
  matrix products  21.9 us (12%)
  local copies, waits for them, and re-layouts  3.68 us (2%)
  other arithmetic  1.85 us (1%)
    ppermute x23, starting transfers between devices, send(): return lax.ppermute(value, AXES, pairs)  85.9 us
    ppermute x23, waiting for transfers between devices, send(): return lax.ppermute(value, AXES, pairs)  64 us
    dot_general x2, matrix products, body(): back = jnp.einsum('uryw,uzw->uryz', ratio, mat_z, precision=HIGH)  4.58 us
    dot_general x2, matrix products, body(): back = jnp.einsum('urj,uryz->yjz', mat_x, back, precision=HIGH)  3.91 us
  transfers between devices with their start and end apart: 23, of which 16 were waited for; matrix products, arithmetic and copies ran while one was open for 3% of the time, Pallas kernels for 0%

profile of v6, /device:TPU:57, one launch (start us, length us, event | category | flops | bytes accessed | tf_op | source)
XLA Modules:
  0.0 178.0 jit_solution(12241015188670561185)
XLA Ops:
  0.0 0.9 copy.95
  0.9 10.6 %collective-permute-start = (f32[8,32,128]{2,1,0:T(8,128)S(1)}, f32[8,32,128]{2,1,0:T(8,128)S(1)}, u32[]{:S(2)}, u32[]{:S(2)}) collective-permute-start(f32[8,32,128]{2,1,0:T(8,128)S(1)} %bitcast.122), channel_id=1, source_target_pairs={{0,256},{1,257},{2,258},{3,259},{4,260},{5,261},{6,262},{7,263},{8... | collective-permute-start | bytes 393224 | tf_op jit(solution)/shard_map/ppermute | solution.py:74
  11.7 1.3 dynamic-slice_bitcast_fusion
  12.9 5.5 %collective-permute-start.3 = (f32[16,64,128]{2,1,0:T(8,128)S(1)}, f32[16,64,128]{2,1,0:T(8,128)S(1)}, u32[]{:S(2)}, u32[]{:S(2)}) collective-permute-start(f32[16,64,128]{2,1,0:T(8,128)S(1)} %get-tuple-element.28), channel_id=1, source_target_pairs={{0,0},{1,128},{64,64},{65,192},{128,1},{129,129},{192,65},{193,193... | collective-permute-start | bytes 1572872 | tf_op jit(solution)/shard_map/ppermute | solution.py:74
  18.4 2.2 %collective-permute-start.4 = (f32[16,64,128]{2,1,0:T(8,128)S(1)}, f32[16,64,128]{2,1,0:T(8,128)}, u32[]{:S(2)}, u32[]{:S(2)}) collective-permute-start(f32[16,64,128]{2,1,0:T(8,128)S(1)} %get-tuple-element.35), channel_id=1, source_target_pairs={{0,64},{1,192},{64,0},{65,128},{128,65},{129,193},{192,1},{193,129... | collective-permute-start | bytes 1572872 | tf_op jit(solution)/shard_map/ppermute | solution.py:74
  21.1 4.0 %collective-permute-start.1 = (f32[16,16,128]{2,1,0:T(8,128)S(1)}, f32[16,16,128]{2,1,0:T(8,128)S(1)}, u32[]{:S(2)}, u32[]{:S(2)}) collective-permute-start(f32[16,16,128]{2,1,0:T(8,128)S(1)} %get-tuple-element.57), channel_id=1, source_target_pairs={{0,0},{1,128},{64,64},{65,192},{128,1},{129,129},{192,65},{193,193... | collective-permute-start | bytes 393224 | tf_op jit(solution)/shard_map/ppermute | solution.py:74
  25.1 2.5 %collective-permute-start.2 = (f32[16,16,128]{2,1,0:T(8,128)S(1)}, f32[16,16,128]{2,1,0:T(8,128)S(1)}, u32[]{:S(2)}, u32[]{:S(2)}) collective-permute-start(f32[16,16,128]{2,1,0:T(8,128)S(1)} %get-tuple-element.58), channel_id=1, source_target_pairs={{0,64},{1,192},{64,0},{65,128},{128,65},{129,193},{192,1},{193,129... | collective-permute-start | bytes 393224 | tf_op jit(solution)/shard_map/ppermute | solution.py:74
  27.7 5.0 %collective-permute-start.7 = (f32[16,64,128]{2,1,0:T(8,128)S(1)}, f32[16,64,128]{2,1,0:T(8,128)}, u32[]{:S(2)}, u32[]{:S(2)}) collective-permute-start(f32[16,64,128]{2,1,0:T(8,128)S(1)} %get-tuple-element.28), channel_id=1, source_target_pairs={{0,256},{1,257},{2,258},{3,259},{4,260},{5,261},{6,262},{7,263},{8... | collective-permute-start | bytes 1572872 | tf_op jit(solution)/shard_map/ppermute | solution.py:74
  32.7 1.0 collective-permute-done.1
  33.7 3.2 %collective-permute-start.10 = (f32[16,64,128]{2,1,0:T(8,128)S(1)}, f32[16,64,128]{2,1,0:T(8,128)}, u32[]{:S(2)}, u32[]{:S(2)}) collective-permute-start(f32[16,64,128]{2,1,0:T(8,128)S(1)} %get-tuple-element.35), channel_id=1, source_target_pairs={{0,256},{1,257},{2,258},{3,259},{4,260},{5,261},{6,262},{7,263},{8... | collective-permute-start | bytes 1572872 | tf_op jit(solution)/shard_map/ppermute | solution.py:74
  37.0 0.8 copy-done.1
  37.8 5.8 %collective-permute-start.5 = (f32[32,16,128]{2,1,0:T(8,128)S(1)}, f32[32,16,128]{2,1,0:T(8,128)S(1)}, u32[]{:S(2)}, u32[]{:S(2)}) collective-permute-start(f32[32,16,128]{2,1,0:T(8,128)S(1)} %pad_maximum_fusion.5), channel_id=1, source_target_pairs={{64,128},{128,64},{65,129},{129,65},{192,194},{194,192},{193,195},... | collective-permute-start | bytes 786440 | tf_op jit(solution)/shard_map/ppermute | solution.py:74
  43.6 1.9 %collective-permute-start.6 = (f32[32,16,128]{2,1,0:T(8,128)S(1)}, f32[32,16,128]{2,1,0:T(8,128)S(1)}, u32[]{:S(2)}, u32[]{:S(2)}) collective-permute-start(f32[32,16,128]{2,1,0:T(8,128)S(1)} %pad_maximum_fusion.5), channel_id=1, source_target_pairs={{0,64},{64,0},{1,65},{65,1},{128,192},{192,128},{129,193},{193,129... | collective-permute-start | bytes 786440 | tf_op jit(solution)/shard_map/ppermute | solution.py:74
  45.7 0.2 fusion.90
  45.9 0.2 fusion.101
  46.1 0.7 fusion.50
  46.8 0.2 fusion.85
  47.0 0.3 fusion.67
  47.4 0.8 fusion.39
  48.2 0.8 fusion.22
  49.0 2.9 %collective-permute-start.8 = (f32[16,64,128]{2,1,0:T(8,128)}, f32[16,64,128]{2,1,0:T(8,128)S(1)}, u32[]{:S(2)}, u32[]{:S(2)}) collective-permute-start(f32[16,64,128]{2,1,0:T(8,128)} %collective-permute-done.7), channel_id=1, source_target_pairs={{0,0},{1,128},{64,64},{65,192},{128,1},{129,129},{192,65},{193,193... | collective-permute-start | bytes 1572872 | tf_op jit(solution)/shard_map/ppermute | solution.py:74
  51.9 0.4 fusion.48
  52.7 4.4 %collective-permute-done.5 = f32[32,16,128]{2,1,0:T(8,128)S(1)} collective-permute-done((f32[32,16,128]{2,1,0:T(8,128)S(1)}, f32[32,16,128]{2,1,0:T(8,128)S(1)}, u32[]{:S(2)}, u32[]{:S(2)}) %collective-permute-start.5) | collective-permute-done | bytes 262176 | tf_op jit(solution)/shard_map/ppermute | solution.py:74
  57.2 4.0 %collective-permute-done.8 = f32[16,64,128]{2,1,0:T(8,128)S(1)} collective-permute-done((f32[16,64,128]{2,1,0:T(8,128)}, f32[16,64,128]{2,1,0:T(8,128)S(1)}, u32[]{:S(2)}, u32[]{:S(2)}) %collective-permute-start.8) | collective-permute-done | bytes 524320 | tf_op jit(solution)/shard_map/ppermute | solution.py:74
  61.2 1.9 %collective-permute-start.9 = (f32[32,48,128]{2,1,0:T(8,128)S(1)}, f32[32,48,128]{2,1,0:T(8,128)S(1)}, u32[]{:S(2)}, u32[]{:S(2)}) collective-permute-start(f32[32,48,128]{2,1,0:T(8,128)S(1)} %pad_maximum_fusion.3), channel_id=1, source_target_pairs={{0,1},{1,0},{2,3},{3,2},{4,5},{5,4},{6,7},{7,6},{8,9},{9,8},{10,11... | collective-permute-start | bytes 2359304 | tf_op jit(solution)/shard_map/ppermute | solution.py:74
  63.1 18.6 %collective-permute-done.10 = f32[16,64,128]{2,1,0:T(8,128)} collective-permute-done((f32[16,64,128]{2,1,0:T(8,128)S(1)}, f32[16,64,128]{2,1,0:T(8,128)}, u32[]{:S(2)}, u32[]{:S(2)}) %collective-permute-start.10) | collective-permute-done | bytes 524320 | tf_op jit(solution)/shard_map/ppermute | solution.py:74
  81.7 5.3 %collective-permute-start.11 = (f32[16,64,128]{2,1,0:T(8,128)}, f32[16,64,128]{2,1,0:T(8,128)S(1)}, u32[]{:S(2)}, u32[]{:S(2)}) collective-permute-start(f32[16,64,128]{2,1,0:T(8,128)} %collective-permute-done.10), channel_id=1, source_target_pairs={{0,64},{1,192},{64,0},{65,128},{128,65},{129,193},{192,1},{193,129... | collective-permute-start | bytes 1572872 | tf_op jit(solution)/shard_map/ppermute | solution.py:74
  87.3 6.6 %collective-permute-done.11 = f32[16,64,128]{2,1,0:T(8,128)S(1)} collective-permute-done((f32[16,64,128]{2,1,0:T(8,128)}, f32[16,64,128]{2,1,0:T(8,128)S(1)}, u32[]{:S(2)}, u32[]{:S(2)}) %collective-permute-start.11) | collective-permute-done | bytes 524320 | tf_op jit(solution)/shard_map/ppermute | solution.py:74
  93.9 1.0 fusion.23
  94.9 1.6 fusion.12
  96.5 1.0 fusion.6
  97.7 2.3 %fusion.18 = f32[4,16,64,128]{3,2,1,0:T(8,128)S(1)} fusion(f32[4,128,128,1]{1,2,3,0:T(8,128)S(1)} %copy.23, f32[4,16,64,128]{3,2,1,0:T(8,128)S(1)} %fusion.6, f32[1,16,64,128]{3,2,1,0:T(8,128)S(1)} %bitcast.130, f32[1,16,64,128]{3,2,1,0:T(8,128)S(1)} %bitcast.128, f32[1,16,64,128]{3,2,1,0:T(8,128)} %bitcast.27, f32[1,16,64,128]{3,2,1,0:T(8,128)S(1)} %bitcast.126, ...), kind=kOutput, calls=%fused_computation.19 | convolution fusion | flops 405798912 | bytes 6553664 | tf_op jit(solution)/shard_map/uryw,uzw->uryz/dot_general | solution.py:178
  100.0 1.1 fusion.129
  101.1 2.0 %fusion.33 = f32[64,48,128]{2,1,0:T(8,128)S(1)} fusion(f32[4,64,16,128]{3,1,2,0:T(8,128)S(1)} %fusion.129, f32[4,16,48]{2,0,1:T(4,128)S(1)} %fusion.56), kind=kOutput, calls=%fused_computation.37 | convolution fusion | flops 150994944 | bytes 3682304 | tf_op jit(solution)/shard_map/urj,uryz->yjz/dot_general | solution.py:180
  103.1 1.9 %collective-permute-start.12 = (f32[32,48,128]{2,1,0:T(8,128)S(1)}, f32[32,48,128]{2,1,0:T(8,128)S(1)}, u32[]{:S(2)}, u32[]{:S(2)}) collective-permute-start(f32[32,48,128]{2,1,0:T(8,128)S(1)} %slice.115), channel_id=1, source_target_pairs={{0,1},{1,0},{2,3},{3,2},{4,5},{5,4},{6,7},{7,6},{8,9},{9,8},{10,11... | collective-permute-start | bytes 2359304 | tf_op jit(solution)/shard_map/ppermute | solution.py:74
  105.0 2.3 %collective-permute-done.12 = f32[32,48,128]{2,1,0:T(8,128)S(1)} collective-permute-done((f32[32,48,128]{2,1,0:T(8,128)S(1)}, f32[32,48,128]{2,1,0:T(8,128)S(1)}, u32[]{:S(2)}, u32[]{:S(2)}) %collective-permute-start.12) | collective-permute-done | bytes 786464 | tf_op jit(solution)/shard_map/ppermute | solution.py:74
  107.4 5.0 %collective-permute-start.13 = (f32[32,16,128]{2,1,0:T(8,128)S(1)}, f32[32,16,128]{2,1,0:T(8,128)S(1)}, u32[]{:S(2)}, u32[]{:S(2)}) collective-permute-start(f32[32,16,128]{2,1,0:T(8,128)S(1)} %get-tuple-element.47), channel_id=1, source_target_pairs={{64,128},{128,64},{65,129},{129,65},{192,194},{194,192},{193,195},... | collective-permute-start | bytes 786440 | tf_op jit(solution)/shard_map/ppermute | solution.py:74
  112.4 1.9 %collective-permute-start.14 = (f32[32,16,128]{2,1,0:T(8,128)S(1)}, f32[32,16,128]{2,1,0:T(8,128)S(1)}, u32[]{:S(2)}, u32[]{:S(2)}) collective-permute-start(f32[32,16,128]{2,1,0:T(8,128)S(1)} %get-tuple-element.48), channel_id=1, source_target_pairs={{0,64},{64,0},{1,65},{65,1},{128,192},{192,128},{129,193},{193,129... | collective-permute-start | bytes 786440 | tf_op jit(solution)/shard_map/ppermute | solution.py:74
  114.3 4.8 %collective-permute-done.13 = f32[32,16,128]{2,1,0:T(8,128)S(1)} collective-permute-done((f32[32,16,128]{2,1,0:T(8,128)S(1)}, f32[32,16,128]{2,1,0:T(8,128)S(1)}, u32[]{:S(2)}, u32[]{:S(2)}) %collective-permute-start.13) | collective-permute-done | bytes 262176 | tf_op jit(solution)/shard_map/ppermute | solution.py:74
  119.2 2.3 %collective-permute-done.14 = f32[32,16,128]{2,1,0:T(8,128)S(1)} collective-permute-done((f32[32,16,128]{2,1,0:T(8,128)S(1)}, f32[32,16,128]{2,1,0:T(8,128)S(1)}, u32[]{:S(2)}, u32[]{:S(2)}) %collective-permute-start.14) | collective-permute-done | bytes 262176 | tf_op jit(solution)/shard_map/ppermute | solution.py:74
  121.6 4.7 %collective-permute-start.15 = (f32[32,16,128]{2,1,0:T(8,128)S(1)}, f32[32,16,128]{2,1,0:T(8,128)S(1)}, u32[]{:S(2)}, u32[]{:S(2)}) collective-permute-start(f32[32,16,128]{2,1,0:T(8,128)S(1)} %fusion.55), channel_id=1, source_target_pairs={{64,128},{128,64},{65,129},{129,65},{192,194},{194,192},{193,195},... | collective-permute-start | bytes 786440 | tf_op jit(solution)/shard_map/ppermute | solution.py:74
  126.3 1.9 %collective-permute-start.16 = (f32[32,16,128]{2,1,0:T(8,128)S(1)}, f32[32,16,128]{2,1,0:T(8,128)S(1)}, u32[]{:S(2)}, u32[]{:S(2)}) collective-permute-start(f32[32,16,128]{2,1,0:T(8,128)S(1)} %fusion.55), channel_id=1, source_target_pairs={{0,64},{64,0},{1,65},{65,1},{128,192},{192,128},{129,193},{193,129... | collective-permute-start | bytes 786440 | tf_op jit(solution)/shard_map/ppermute | solution.py:74
  128.2 3.7 %collective-permute-done.15 = f32[32,16,128]{2,1,0:T(8,128)S(1)} collective-permute-done((f32[32,16,128]{2,1,0:T(8,128)S(1)}, f32[32,16,128]{2,1,0:T(8,128)S(1)}, u32[]{:S(2)}, u32[]{:S(2)}) %collective-permute-start.15) | collective-permute-done | bytes 262176 | tf_op jit(solution)/shard_map/ppermute | solution.py:74
  131.9 2.6 %collective-permute-done.16 = f32[32,16,128]{2,1,0:T(8,128)S(1)} collective-permute-done((f32[32,16,128]{2,1,0:T(8,128)S(1)}, f32[32,16,128]{2,1,0:T(8,128)S(1)}, u32[]{:S(2)}, u32[]{:S(2)}) %collective-permute-start.16) | collective-permute-done | bytes 262176 | tf_op jit(solution)/shard_map/ppermute | solution.py:74
  134.5 4.5 %collective-permute-start.17 = (f32[32,48,128]{2,1,0:T(8,128)S(1)}, f32[32,48,128]{2,1,0:T(8,128)S(1)}, u32[]{:S(2)}, u32[]{:S(2)}) collective-permute-start(f32[32,48,128]{2,1,0:T(8,128)S(1)} %pad_maximum_fusion.4), channel_id=1, source_target_pairs={{0,1},{1,0},{2,3},{3,2},{4,5},{5,4},{6,7},{7,6},{8,9},{9,8},{10,11... | collective-permute-start | bytes 2359304 | tf_op jit(solution)/shard_map/ppermute | solution.py:74
  139.1 1.7 collective-permute-done.17
  140.7 1.0 fusion.26
  141.7 1.6 fusion.9
  143.4 1.0 fusion.2
  144.4 2.3 %fusion.14 = f32[4,16,64,128]{3,2,1,0:T(8,128)S(1)} fusion(f32[4,128,128,1]{1,2,3,0:T(8,128)S(1)} %copy.23, f32[4,16,64,128]{3,2,1,0:T(8,128)S(1)} %fusion.2, f32[1,16,64,128]{3,2,1,0:T(8,128)S(1)} %bitcast.131, f32[1,16,64,128]{3,2,1,0:T(8,128)S(1)} %bitcast.129, f32[1,16,64,128]{3,2,1,0:T(8,128)} %bitcast.27, f32[1,16,64,128]{3,2,1,0:T(8,128)S(1)} %bitcast.127, ...), kind=kOutput, calls=%fused_computation.15 | convolution fusion | flops 405798912 | bytes 6553664 | tf_op jit(solution)/shard_map/uryw,uzw->uryz/dot_general | solution.py:178
  146.7 1.1 fusion.130
  147.7 2.0 %fusion.36 = f32[64,48,128]{2,1,0:T(8,128)S(1)} fusion(f32[4,64,16,128]{3,1,2,0:T(8,128)S(1)} %fusion.130, f32[4,16,48]{2,0,1:T(4,128)S(1)} %fusion.56), kind=kOutput, calls=%fused_computation.38 | convolution fusion | flops 150994944 | bytes 3682304 | tf_op jit(solution)/shard_map/urj,uryz->yjz/dot_general | solution.py:180
  149.8 2.3 %collective-permute-start.18 = (f32[32,48,128]{2,1,0:T(8,128)S(1)}, f32[32,48,128]{2,1,0:T(8,128)S(1)}, u32[]{:S(2)}, u32[]{:S(2)}) collective-permute-start(f32[32,48,128]{2,1,0:T(8,128)S(1)} %slice.122), channel_id=1, source_target_pairs={{0,1},{1,0},{2,3},{3,2},{4,5},{5,4},{6,7},{7,6},{8,9},{9,8},{10,11... | collective-permute-start | bytes 2359304 | tf_op jit(solution)/shard_map/ppermute | solution.py:74
  152.1 1.9 %collective-permute-done.18 = f32[32,48,128]{2,1,0:T(8,128)S(1)} collective-permute-done((f32[32,48,128]{2,1,0:T(8,128)S(1)}, f32[32,48,128]{2,1,0:T(8,128)S(1)}, u32[]{:S(2)}, u32[]{:S(2)}) %collective-permute-start.18) | collective-permute-done | bytes 786464 | tf_op jit(solution)/shard_map/ppermute | solution.py:74
  154.1 3.9 %collective-permute-start.19 = (f32[32,16,128]{2,1,0:T(8,128)S(1)}, f32[32,16,128]{2,1,0:T(8,128)S(1)}, u32[]{:S(2)}, u32[]{:S(2)}) collective-permute-start(f32[32,16,128]{2,1,0:T(8,128)S(1)} %get-tuple-element.45), channel_id=1, source_target_pairs={{64,128},{128,64},{65,129},{129,65},{192,194},{194,192},{193,195},... | collective-permute-start | bytes 786440 | tf_op jit(solution)/shard_map/ppermute | solution.py:74
  158.0 1.9 %collective-permute-start.20 = (f32[32,16,128]{2,1,0:T(8,128)S(1)}, f32[32,16,128]{2,1,0:T(8,128)S(1)}, u32[]{:S(2)}, u32[]{:S(2)}) collective-permute-start(f32[32,16,128]{2,1,0:T(8,128)S(1)} %get-tuple-element.46), channel_id=1, source_target_pairs={{0,64},{64,0},{1,65},{65,1},{128,192},{192,128},{129,193},{193,129... | collective-permute-start | bytes 786440 | tf_op jit(solution)/shard_map/ppermute | solution.py:74
  160.0 5.6 %collective-permute-done.19 = f32[32,16,128]{2,1,0:T(8,128)S(1)} collective-permute-done((f32[32,16,128]{2,1,0:T(8,128)S(1)}, f32[32,16,128]{2,1,0:T(8,128)S(1)}, u32[]{:S(2)}, u32[]{:S(2)}) %collective-permute-start.19) | collective-permute-done | bytes 262176 | tf_op jit(solution)/shard_map/ppermute | solution.py:74
  165.6 1.5 collective-permute-done.20
  167.2 0.2 fusion.60
  167.5 3.1 %collective-permute-start.21 = (f32[8,16,128]{2,0,1:T(8,128)S(1)}, f32[8,16,128]{2,0,1:T(8,128)S(1)}, u32[]{:S(2)}, u32[]{:S(2)}) collective-permute-start(f32[8,16,128]{2,0,1:T(8,128)S(1)} %get-tuple-element.61), channel_id=1, source_target_pairs={{0,0},{128,1},{64,64},{192,65},{1,128},{129,129},{65,192},{193,193... | collective-permute-start | bytes 196616 | tf_op jit(solution)/shard_map/ppermute | solution.py:74
  170.6 3.7 %collective-permute-start.22 = (f32[8,16,128]{2,0,1:T(8,128)S(1)}, f32[8,16,128]{2,0,1:T(8,128)S(1)}, u32[]{:S(2)}, u32[]{:S(2)}) collective-permute-start(f32[8,16,128]{2,0,1:T(8,128)S(1)} %get-tuple-element.62), channel_id=1, source_target_pairs={{64,0},{192,1},{0,64},{128,65},{65,128},{193,129},{1,192},{129,193... | collective-permute-start | bytes 196616 | tf_op jit(solution)/shard_map/ppermute | solution.py:74
  174.3 0.2 collective-permute-done.21
  174.6 2.8 %collective-permute-done.22 = f32[8,16,128]{2,0,1:T(8,128)S(1)} collective-permute-done((f32[8,16,128]{2,0,1:T(8,128)S(1)}, f32[8,16,128]{2,0,1:T(8,128)S(1)}, u32[]{:S(2)}, u32[]{:S(2)}) %collective-permute-start.22) | collective-permute-done | bytes 65568 | tf_op jit(solution)/shard_map/ppermute | solution.py:74
  177.4 0.7 maximum_bitcast_fusion.4
  (54 shorter events, 2.2 us)
Async XLA Ops:
  0.9 20.1 %collective-permute-start = (f32[8,32,128]{2,1,0:T(8,128)S(1)}, f32[8,32,128]{2,1,0:T(8,128)S(1)}, u32[]{:S(2)}, u32[]{:S(2)}) collective-permute-start(f32[8,32,128]{2,1,0:T(8,128)S(1)} %bitcast.122), channel_id=1, source_target_pairs={{0,256},{1,257},{2,258},{3,259},{4,260},{5,261},{6,262},{7,263},{8... | collective-permute-start | bytes 393224 | tf_op jit(solution)/shard_map/ppermute | solution.py:74
  11.6 33.9 %copy-start = (f32[8,3,31]{2,0,1:T(8,128)S(1)}, f32[8,3,31]{2,0,1:T(8,128)}, u32[]{:S(2)}) copy-start(f32[8,3,31]{2,0,1:T(8,128)} %param.6) | copy-start | bytes 8932
  11.6 35.2 %copy-start.5 = (s32[8,16]{1,0:T(8,128)S(1)}, s32[8,16]{1,0:T(8,128)}, u32[]{:S(2)}) copy-start(s32[8,16]{1,0:T(8,128)} %param.7) | copy-start | bytes 1540
  12.9 24.0 %collective-permute-start.3 = (f32[16,64,128]{2,1,0:T(8,128)S(1)}, f32[16,64,128]{2,1,0:T(8,128)S(1)}, u32[]{:S(2)}, u32[]{:S(2)}) collective-permute-start(f32[16,64,128]{2,1,0:T(8,128)S(1)} %get-tuple-element.28), channel_id=1, source_target_pairs={{0,0},{1,128},{64,64},{65,192},{128,1},{129,129},{192,65},{193,193... | collective-permute-start | bytes 1572872 | tf_op jit(solution)/shard_map/ppermute | solution.py:74
  18.4 19.4 %collective-permute-start.4 = (f32[16,64,128]{2,1,0:T(8,128)S(1)}, f32[16,64,128]{2,1,0:T(8,128)}, u32[]{:S(2)}, u32[]{:S(2)}) collective-permute-start(f32[16,64,128]{2,1,0:T(8,128)S(1)} %get-tuple-element.35), channel_id=1, source_target_pairs={{0,64},{1,192},{64,0},{65,128},{128,65},{129,193},{192,1},{193,129... | collective-permute-start | bytes 1572872 | tf_op jit(solution)/shard_map/ppermute | solution.py:74
  21.1 12.6 %collective-permute-start.1 = (f32[16,16,128]{2,1,0:T(8,128)S(1)}, f32[16,16,128]{2,1,0:T(8,128)S(1)}, u32[]{:S(2)}, u32[]{:S(2)}) collective-permute-start(f32[16,16,128]{2,1,0:T(8,128)S(1)} %get-tuple-element.57), channel_id=1, source_target_pairs={{0,0},{1,128},{64,64},{65,192},{128,1},{129,129},{192,65},{193,193... | collective-permute-start | bytes 393224 | tf_op jit(solution)/shard_map/ppermute | solution.py:74
  25.1 11.9 %collective-permute-start.2 = (f32[16,16,128]{2,1,0:T(8,128)S(1)}, f32[16,16,128]{2,1,0:T(8,128)S(1)}, u32[]{:S(2)}, u32[]{:S(2)}) collective-permute-start(f32[16,16,128]{2,1,0:T(8,128)S(1)} %get-tuple-element.58), channel_id=1, source_target_pairs={{0,64},{1,192},{64,0},{65,128},{128,65},{129,193},{192,1},{193,129... | collective-permute-start | bytes 393224 | tf_op jit(solution)/shard_map/ppermute | solution.py:74
  27.7 21.3 %collective-permute-start.7 = (f32[16,64,128]{2,1,0:T(8,128)S(1)}, f32[16,64,128]{2,1,0:T(8,128)}, u32[]{:S(2)}, u32[]{:S(2)}) collective-permute-start(f32[16,64,128]{2,1,0:T(8,128)S(1)} %get-tuple-element.28), channel_id=1, source_target_pairs={{0,256},{1,257},{2,258},{3,259},{4,260},{5,261},{6,262},{7,263},{8... | collective-permute-start | bytes 1572872 | tf_op jit(solution)/shard_map/ppermute | solution.py:74
  33.7 47.9 %collective-permute-start.10 = (f32[16,64,128]{2,1,0:T(8,128)S(1)}, f32[16,64,128]{2,1,0:T(8,128)}, u32[]{:S(2)}, u32[]{:S(2)}) collective-permute-start(f32[16,64,128]{2,1,0:T(8,128)S(1)} %get-tuple-element.35), channel_id=1, source_target_pairs={{0,256},{1,257},{2,258},{3,259},{4,260},{5,261},{6,262},{7,263},{8... | collective-permute-start | bytes 1572872 | tf_op jit(solution)/shard_map/ppermute | solution.py:74
  37.0 0.8 copy-start.1
  37.8 19.4 %collective-permute-start.5 = (f32[32,16,128]{2,1,0:T(8,128)S(1)}, f32[32,16,128]{2,1,0:T(8,128)S(1)}, u32[]{:S(2)}, u32[]{:S(2)}) collective-permute-start(f32[32,16,128]{2,1,0:T(8,128)S(1)} %pad_maximum_fusion.5), channel_id=1, source_target_pairs={{64,128},{128,64},{65,129},{129,65},{192,194},{194,192},{193,195},... | collective-permute-start | bytes 786440 | tf_op jit(solution)/shard_map/ppermute | solution.py:74
  43.6 13.6 %collective-permute-start.6 = (f32[32,16,128]{2,1,0:T(8,128)S(1)}, f32[32,16,128]{2,1,0:T(8,128)S(1)}, u32[]{:S(2)}, u32[]{:S(2)}) collective-permute-start(f32[32,16,128]{2,1,0:T(8,128)S(1)} %pad_maximum_fusion.5), channel_id=1, source_target_pairs={{0,64},{64,0},{1,65},{65,1},{128,192},{192,128},{129,193},{193,129... | collective-permute-start | bytes 786440 | tf_op jit(solution)/shard_map/ppermute | solution.py:74
  49.0 12.2 %collective-permute-start.8 = (f32[16,64,128]{2,1,0:T(8,128)}, f32[16,64,128]{2,1,0:T(8,128)S(1)}, u32[]{:S(2)}, u32[]{:S(2)}) collective-permute-start(f32[16,64,128]{2,1,0:T(8,128)} %collective-permute-done.7), channel_id=1, source_target_pairs={{0,0},{1,128},{64,64},{65,192},{128,1},{129,129},{192,65},{193,193... | collective-permute-start | bytes 1572872 | tf_op jit(solution)/shard_map/ppermute | solution.py:74
  61.2 25.8 %copy-start.3 = (f32[16,64,128]{2,1,0:T(8,128)}, f32[16,64,128]{2,1,0:T(8,128)S(1)}, u32[]{:S(2)}) copy-start(f32[16,64,128]{2,1,0:T(8,128)S(1)} %collective-permute-done.8) | copy-start | bytes 1572868
  61.2 32.7 %collective-permute-start.9 = (f32[32,48,128]{2,1,0:T(8,128)S(1)}, f32[32,48,128]{2,1,0:T(8,128)S(1)}, u32[]{:S(2)}, u32[]{:S(2)}) collective-permute-start(f32[32,48,128]{2,1,0:T(8,128)S(1)} %pad_maximum_fusion.3), channel_id=1, source_target_pairs={{0,1},{1,0},{2,3},{3,2},{4,5},{5,4},{6,7},{7,6},{8,9},{9,8},{10,11... | collective-permute-start | bytes 2359304 | tf_op jit(solution)/shard_map/ppermute | solution.py:74
  81.7 12.2 %collective-permute-start.11 = (f32[16,64,128]{2,1,0:T(8,128)}, f32[16,64,128]{2,1,0:T(8,128)S(1)}, u32[]{:S(2)}, u32[]{:S(2)}) collective-permute-start(f32[16,64,128]{2,1,0:T(8,128)} %collective-permute-done.10), channel_id=1, source_target_pairs={{0,64},{1,192},{64,0},{65,128},{128,65},{129,193},{192,1},{193,129... | collective-permute-start | bytes 1572872 | tf_op jit(solution)/shard_map/ppermute | solution.py:74
  96.5 1.0 copy-start.2
  96.5 1.2 copy-start.4
  103.1 4.2 %collective-permute-start.12 = (f32[32,48,128]{2,1,0:T(8,128)S(1)}, f32[32,48,128]{2,1,0:T(8,128)S(1)}, u32[]{:S(2)}, u32[]{:S(2)}) collective-permute-start(f32[32,48,128]{2,1,0:T(8,128)S(1)} %slice.115), channel_id=1, source_target_pairs={{0,1},{1,0},{2,3},{3,2},{4,5},{5,4},{6,7},{7,6},{8,9},{9,8},{10,11... | collective-permute-start | bytes 2359304 | tf_op jit(solution)/shard_map/ppermute | solution.py:74
  107.4 11.8 %collective-permute-start.13 = (f32[32,16,128]{2,1,0:T(8,128)S(1)}, f32[32,16,128]{2,1,0:T(8,128)S(1)}, u32[]{:S(2)}, u32[]{:S(2)}) collective-permute-start(f32[32,16,128]{2,1,0:T(8,128)S(1)} %get-tuple-element.47), channel_id=1, source_target_pairs={{64,128},{128,64},{65,129},{129,65},{192,194},{194,192},{193,195},... | collective-permute-start | bytes 786440 | tf_op jit(solution)/shard_map/ppermute | solution.py:74
  112.4 9.1 %collective-permute-start.14 = (f32[32,16,128]{2,1,0:T(8,128)S(1)}, f32[32,16,128]{2,1,0:T(8,128)S(1)}, u32[]{:S(2)}, u32[]{:S(2)}) collective-permute-start(f32[32,16,128]{2,1,0:T(8,128)S(1)} %get-tuple-element.48), channel_id=1, source_target_pairs={{0,64},{64,0},{1,65},{65,1},{128,192},{192,128},{129,193},{193,129... | collective-permute-start | bytes 786440 | tf_op jit(solution)/shard_map/ppermute | solution.py:74
  121.6 10.3 %collective-permute-start.15 = (f32[32,16,128]{2,1,0:T(8,128)S(1)}, f32[32,16,128]{2,1,0:T(8,128)S(1)}, u32[]{:S(2)}, u32[]{:S(2)}) collective-permute-start(f32[32,16,128]{2,1,0:T(8,128)S(1)} %fusion.55), channel_id=1, source_target_pairs={{64,128},{128,64},{65,129},{129,65},{192,194},{194,192},{193,195},... | collective-permute-start | bytes 786440 | tf_op jit(solution)/shard_map/ppermute | solution.py:74
  126.3 8.2 %collective-permute-start.16 = (f32[32,16,128]{2,1,0:T(8,128)S(1)}, f32[32,16,128]{2,1,0:T(8,128)S(1)}, u32[]{:S(2)}, u32[]{:S(2)}) collective-permute-start(f32[32,16,128]{2,1,0:T(8,128)S(1)} %fusion.55), channel_id=1, source_target_pairs={{0,64},{64,0},{1,65},{65,1},{128,192},{192,128},{129,193},{193,129... | collective-permute-start | bytes 786440 | tf_op jit(solution)/shard_map/ppermute | solution.py:74
  134.5 6.2 %collective-permute-start.17 = (f32[32,48,128]{2,1,0:T(8,128)S(1)}, f32[32,48,128]{2,1,0:T(8,128)S(1)}, u32[]{:S(2)}, u32[]{:S(2)}) collective-permute-start(f32[32,48,128]{2,1,0:T(8,128)S(1)} %pad_maximum_fusion.4), channel_id=1, source_target_pairs={{0,1},{1,0},{2,3},{3,2},{4,5},{5,4},{6,7},{7,6},{8,9},{9,8},{10,11... | collective-permute-start | bytes 2359304 | tf_op jit(solution)/shard_map/ppermute | solution.py:74
  149.8 4.2 %collective-permute-start.18 = (f32[32,48,128]{2,1,0:T(8,128)S(1)}, f32[32,48,128]{2,1,0:T(8,128)S(1)}, u32[]{:S(2)}, u32[]{:S(2)}) collective-permute-start(f32[32,48,128]{2,1,0:T(8,128)S(1)} %slice.122), channel_id=1, source_target_pairs={{0,1},{1,0},{2,3},{3,2},{4,5},{5,4},{6,7},{7,6},{8,9},{9,8},{10,11... | collective-permute-start | bytes 2359304 | tf_op jit(solution)/shard_map/ppermute | solution.py:74
  154.1 11.5 %collective-permute-start.19 = (f32[32,16,128]{2,1,0:T(8,128)S(1)}, f32[32,16,128]{2,1,0:T(8,128)S(1)}, u32[]{:S(2)}, u32[]{:S(2)}) collective-permute-start(f32[32,16,128]{2,1,0:T(8,128)S(1)} %get-tuple-element.45), channel_id=1, source_target_pairs={{64,128},{128,64},{65,129},{129,65},{192,194},{194,192},{193,195},... | collective-permute-start | bytes 786440 | tf_op jit(solution)/shard_map/ppermute | solution.py:74
  158.0 9.1 %collective-permute-start.20 = (f32[32,16,128]{2,1,0:T(8,128)S(1)}, f32[32,16,128]{2,1,0:T(8,128)S(1)}, u32[]{:S(2)}, u32[]{:S(2)}) collective-permute-start(f32[32,16,128]{2,1,0:T(8,128)S(1)} %get-tuple-element.46), channel_id=1, source_target_pairs={{0,64},{64,0},{1,65},{65,1},{128,192},{192,128},{129,193},{193,129... | collective-permute-start | bytes 786440 | tf_op jit(solution)/shard_map/ppermute | solution.py:74
  167.5 7.1 %collective-permute-start.21 = (f32[8,16,128]{2,0,1:T(8,128)S(1)}, f32[8,16,128]{2,0,1:T(8,128)S(1)}, u32[]{:S(2)}, u32[]{:S(2)}) collective-permute-start(f32[8,16,128]{2,0,1:T(8,128)S(1)} %get-tuple-element.61), channel_id=1, source_target_pairs={{0,0},{128,1},{64,64},{192,65},{1,128},{129,129},{65,192},{193,193... | collective-permute-start | bytes 196616 | tf_op jit(solution)/shard_map/ppermute | solution.py:74
  170.6 6.8 %collective-permute-start.22 = (f32[8,16,128]{2,0,1:T(8,128)S(1)}, f32[8,16,128]{2,0,1:T(8,128)S(1)}, u32[]{:S(2)}, u32[]{:S(2)}) collective-permute-start(f32[8,16,128]{2,0,1:T(8,128)S(1)} %get-tuple-element.62), channel_id=1, source_target_pairs={{64,0},{192,1},{0,64},{128,65},{65,128},{193,129},{1,192},{129,193... | collective-permute-start | bytes 196616 | tf_op jit(solution)/shard_map/ppermute | solution.py:74

commit v7 on v5

--- a/solution.py
+++ b/solution.py
@@ -107,11 +107,13 @@
 
     even = p % 2 == 0
     flipped = jnp.swapaxes(estimate, 0, 1)
-    both = by_h(flipped, send(flipped, SWAP_H), h)
-    current = jnp.concatenate(
-        ordered([send(piece(both, turn, 1), SPREAD[turn]) for turn in (0, 1)], even), 0
+    quarter = jnp.concatenate(
+        ordered([send(piece(flipped, turn, 1), SPREAD[turn]) for turn in (0, 1)], even), 0
     )
-    images = [send(piece(observed[0], turn, 0), SPREAD[turn]) for turn in (0, 1)]
+    current = by_h(quarter, send(quarter, SWAP_H), h)
+    images = [piece(observed[0], turn, 0) for turn in (0, 1)]
+    *images, _ = lax.optimization_barrier((*images, quarter))
+    images = [send(image, SPREAD[turn]) for turn, image in enumerate(images)]
     psf_taps, intersection, current = lax.optimization_barrier((psf_taps, intersection, current))
 
     kernels = psf_taps / jnp.sum(psf_taps, axis=2, keepdims=True)
@@ -122,7 +124,7 @@
     width = full_width // 2
     block = estimate.shape[1]
     place = jnp.arange(width, dtype=jnp.int32)
-    place = place // (2 * block) * block + place // block % 2 * width + place % block
+    place = place // (2 * block) * width + place % (2 * block)
     local_y = jnp.concatenate([place + core * (width // 2), place + (1 - core) * (width // 2)])
     all_y = jnp.arange(full_width, dtype=jnp.int32)
     all_z = jnp.arange(depth, dtype=jnp.int32)
@@ -174,13 +176,15 @@
         if iteration < ITERS - 1:
             current = current * (part + send(part, SWAP_H) + 1.0) * scale
 
-    own_h = (place // width == h)[:, None, None]
-    terms = current * scale * jnp.where(own_h, part + 1.0, part)
-    terms = ordered([terms[: 2 * block], terms[2 * block :]], even)
-    terms = [send(value, reverse(route)) for value, route in zip(terms, SPREAD)]
-    terms = jnp.concatenate(ordered(terms, x % 2 == 0), 1)
-    mine, other = ordered([terms[:block], terms[block:]], h == 0)
-    return jnp.swapaxes(mine + send(other, SWAP_H), 0, 1)
+    def own_half(value, mine):
+        return jnp.where((h == 0) == mine, value[: 2 * block], value[2 * block :])
+
+    total = own_half(part, True) + send(own_half(part, False), SWAP_H)
+    quarter = own_half(current, True) * (total + 1.0) * own_half(scale, True)
+
+    result = ordered([quarter[:block], quarter[block:]], even)
+    result = [send(value, reverse(route)) for value, route in zip(result, SPREAD)]
+    return jnp.swapaxes(jnp.concatenate(ordered(result, x % 2 == 0), 1), 0, 1)
 
 
 def solution(mesh):

time: 162 us -> 159 us (0.981)
  starting transfers between devices: 78.5 us -> 76.4 us
  waiting for transfers between devices: 60.7 us -> 62.5 us
    ppermute x21, starting transfers between devices: 78.5 us -> 76.4 us  [send(): return lax.ppermute(value, AXES, pairs)]
    ppermute x21, waiting for transfers between devices: 60.7 us -> 62.5 us  [send(): return lax.ppermute(value, AXES, pairs)]
  transfers between devices with their start and end apart: 21 -> 21, of which waited for: 17 -> 17; matrix products, arithmetic and copies ran while one was open for 4% -> 3% of each run, Pallas kernels for 0% -> 0%
where the time goes in v7:
time: 159 us; the launch traced here: 158 us
  starting transfers between devices  76.4 us (48%)
  waiting for transfers between devices  62.5 us (39%)
  matrix products  15.6 us (10%)
  local copies, waits for them, and re-layouts  2.22 us (1%)
    ppermute x21, starting transfers between devices, send(): return lax.ppermute(value, AXES, pairs)  76.4 us
    ppermute x21, waiting for transfers between devices, send(): return lax.ppermute(value, AXES, pairs)  62.5 us
    dot_general x2, matrix products, body(): blurred = jnp.einsum('uryz,uzw->uryw', blurred, mat_z, precision=HIGH)  3.68 us
  transfers between devices with their start and end apart: 21, of which 17 were waited for; matrix products, arithmetic and copies ran while one was open for 3% of the time, Pallas kernels for 0%

profile of v7, /device:TPU:57, one launch (start us, length us, event | category | flops | bytes accessed | tf_op | source)
XLA Modules:
  0.0 158.4 jit_solution(2687848761766427545)
XLA Ops:
  0.0 1.0 constant_dynamic-slice_fusion.1
  1.0 5.2 %collective-permute-start = (f32[8,16,128]{2,1,0:T(8,128)S(1)}, f32[8,16,128]{2,1,0:T(8,128)S(1)}, u32[]{:S(2)}, u32[]{:S(2)}) collective-permute-start(f32[8,16,128]{2,1,0:T(8,128)S(1)} %bitcast.109), channel_id=1, source_target_pairs={{0,0},{1,128},{64,64},{65,192},{128,1},{129,129},{192,65},{193,193... | collective-permute-start | bytes 196616 | tf_op jit(solution)/shard_map/ppermute | solution.py:74
  6.2 2.5 %collective-permute-start.1 = (f32[8,16,128]{2,1,0:T(8,128)S(1)}, f32[8,16,128]{2,1,0:T(8,128)S(1)}, u32[]{:S(2)}, u32[]{:S(2)}) collective-permute-start(f32[8,16,128]{2,1,0:T(8,128)S(1)} %bitcast.110), channel_id=1, source_target_pairs={{0,64},{1,192},{64,0},{65,128},{128,65},{129,193},{192,1},{193,129... | collective-permute-start | bytes 196616 | tf_op jit(solution)/shard_map/ppermute | solution.py:74
  9.2 3.8 %collective-permute-done.1 = f32[8,16,128]{2,1,0:T(8,128)S(1)} collective-permute-done((f32[8,16,128]{2,1,0:T(8,128)S(1)}, f32[8,16,128]{2,1,0:T(8,128)S(1)}, u32[]{:S(2)}, u32[]{:S(2)}) %collective-permute-start.1) | collective-permute-done | bytes 65568 | tf_op jit(solution)/shard_map/ppermute | solution.py:74
  13.1 10.6 %collective-permute-start.2 = (f32[16,16,128]{2,1,0:T(8,128)S(1)}, f32[16,16,128]{2,1,0:T(8,128)S(1)}, u32[]{:S(2)}, u32[]{:S(2)}) collective-permute-start(f32[16,16,128]{2,1,0:T(8,128)S(1)} %pad_maximum_fusion.3), channel_id=1, source_target_pairs={{0,256},{1,257},{2,258},{3,259},{4,260},{5,261},{6,262},{7,263},{8... | collective-permute-start | bytes 393224 | tf_op jit(solution)/shard_map/ppermute | solution.py:74
  23.7 0.1 dynamic-slice_bitcast_fusion
  23.9 1.9 %collective-permute-start.5 = (f32[16,64,128]{2,1,0:T(8,128)S(1)}, f32[16,64,128]{2,1,0:T(8,128)}, u32[]{:S(2)}, u32[]{:S(2)}) collective-permute-start(f32[16,64,128]{2,1,0:T(8,128)S(1)} %get-tuple-element.21), channel_id=1, source_target_pairs={{0,0},{1,128},{64,64},{65,192},{128,1},{129,129},{192,65},{193,193... | collective-permute-start | bytes 1572872 | tf_op jit(solution)/shard_map/ppermute | solution.py:74
  25.8 3.7 %collective-permute-start.6 = (f32[16,64,128]{2,1,0:T(8,128)S(1)}, f32[16,64,128]{2,1,0:T(8,128)}, u32[]{:S(2)}, u32[]{:S(2)}) collective-permute-start(f32[16,64,128]{2,1,0:T(8,128)S(1)} %get-tuple-element.22), channel_id=1, source_target_pairs={{0,64},{1,192},{64,0},{65,128},{128,65},{129,193},{192,1},{193,129... | collective-permute-start | bytes 1572872 | tf_op jit(solution)/shard_map/ppermute | solution.py:74
  29.5 3.1 %collective-permute-start.4 = (f32[32,16,128]{2,1,0:T(8,128)S(1)}, f32[32,16,128]{2,1,0:T(8,128)S(1)}, u32[]{:S(2)}, u32[]{:S(2)}) collective-permute-start(f32[32,16,128]{2,1,0:T(8,128)S(1)} %maximum_select_fusion), channel_id=1, source_target_pairs={{0,64},{64,0},{1,65},{65,1},{128,192},{192,128},{129,193},{193,129... | collective-permute-start | bytes 786440 | tf_op jit(solution)/shard_map/ppermute | solution.py:74
  32.6 3.5 %collective-permute-start.3 = (f32[32,16,128]{2,1,0:T(8,128)S(1)}, f32[32,16,128]{2,1,0:T(8,128)S(1)}, u32[]{:S(2)}, u32[]{:S(2)}) collective-permute-start(f32[32,16,128]{2,1,0:T(8,128)S(1)} %maximum_select_fusion), channel_id=1, source_target_pairs={{64,128},{128,64},{65,129},{129,65},{192,194},{194,192},{193,195},... | collective-permute-start | bytes 786440 | tf_op jit(solution)/shard_map/ppermute | solution.py:74
  36.3 0.2 fusion.58
  36.5 0.7 fusion.26
  37.2 0.2 fusion.72
  37.4 0.2 fusion.29
  37.6 0.4 fusion.24
  38.0 0.8 fusion
  38.8 0.2 fusion.51
  39.0 0.3 fusion.37
  39.3 0.1 convolution_bitcast_fusion.4
  39.4 0.2 fusion.16
  39.6 0.8 fusion.15
  40.4 3.0 %collective-permute-done.4 = f32[32,16,128]{2,1,0:T(8,128)S(1)} collective-permute-done((f32[32,16,128]{2,1,0:T(8,128)S(1)}, f32[32,16,128]{2,1,0:T(8,128)S(1)}, u32[]{:S(2)}, u32[]{:S(2)}) %collective-permute-start.4) | collective-permute-done | bytes 262176 | tf_op jit(solution)/shard_map/ppermute | solution.py:74
  43.4 1.4 collective-permute-done.3
  44.9 2.4 %collective-permute-start.7 = (f32[32,48,128]{2,1,0:T(8,128)S(1)}, f32[32,48,128]{2,1,0:T(8,128)S(1)}, u32[]{:S(2)}, u32[]{:S(2)}) collective-permute-start(f32[32,48,128]{2,1,0:T(8,128)S(1)} %pad_maximum_fusion.1), channel_id=1, source_target_pairs={{0,1},{1,0},{2,3},{3,2},{4,5},{5,4},{6,7},{7,6},{8,9},{9,8},{10,11... | collective-permute-start | bytes 2359304 | tf_op jit(solution)/shard_map/ppermute | solution.py:74
  47.5 1.7 %collective-permute-done.7 = f32[32,48,128]{2,1,0:T(8,128)S(1)} collective-permute-done((f32[32,48,128]{2,1,0:T(8,128)S(1)}, f32[32,48,128]{2,1,0:T(8,128)S(1)}, u32[]{:S(2)}, u32[]{:S(2)}) %collective-permute-start.7) | collective-permute-done | bytes 786464 | tf_op jit(solution)/shard_map/ppermute | solution.py:74
  49.2 0.6 fusion.1
  49.8 0.9 convolution_bitcast_fusion.3
  50.6 1.8 %fusion.12 = f32[2,16,64,128]{3,2,1,0:T(8,128)S(1)} fusion(f32[2,16,64,128]{3,2,1,0:T(8,128)S(1)} %convolution_bitcast_fusion.3, f32[1,16,64,128]{3,2,1,0:T(8,128)} %bitcast.26, f32[1,16,64,128]{3,2,1,0:T(8,128)} %bitcast.25, pred[2,16]{1,0:T(4,128)(4,1)S(1)} %bitcast.113, f32[2,128,128,1]{2,0,1,3:T(2,128)S(1)} %bitcast.107), kind=kOutput, calls=%fused_computation.21 | convolution fusion | flops 202375168 | bytes 3276832 | tf_op jit(solution)/shard_map/uryz,uzw->uryw/dot_general | solution.py:169
  52.5 0.6 fusion.88
  53.1 0.6 fusion.89
  53.6 1.4 convolution_bitcast_fusion.1
  55.1 2.3 %collective-permute-start.8 = (f32[32,48,128]{2,1,0:T(8,128)S(1)}, f32[32,48,128]{2,1,0:T(8,128)S(1)}, u32[]{:S(2)}, u32[]{:S(2)}) collective-permute-start(f32[32,48,128]{2,1,0:T(8,128)S(1)} %slice.109), channel_id=1, source_target_pairs={{0,1},{1,0},{2,3},{3,2},{4,5},{5,4},{6,7},{7,6},{8,9},{9,8},{10,11... | collective-permute-start | bytes 2359304 | tf_op jit(solution)/shard_map/ppermute | solution.py:74
  57.4 1.9 %collective-permute-done.8 = f32[32,48,128]{2,1,0:T(8,128)S(1)} collective-permute-done((f32[32,48,128]{2,1,0:T(8,128)S(1)}, f32[32,48,128]{2,1,0:T(8,128)S(1)}, u32[]{:S(2)}, u32[]{:S(2)}) %collective-permute-start.8) | collective-permute-done | bytes 786464 | tf_op jit(solution)/shard_map/ppermute | solution.py:74
  59.4 4.9 %collective-permute-start.10 = (f32[32,16,128]{2,1,0:T(8,128)S(1)}, f32[32,16,128]{2,1,0:T(8,128)S(1)}, u32[]{:S(2)}, u32[]{:S(2)}) collective-permute-start(f32[32,16,128]{2,1,0:T(8,128)S(1)} %get-tuple-element.38), channel_id=1, source_target_pairs={{0,64},{64,0},{1,65},{65,1},{128,192},{192,128},{129,193},{193,129... | collective-permute-start | bytes 786440 | tf_op jit(solution)/shard_map/ppermute | solution.py:74
  64.3 1.9 %collective-permute-start.9 = (f32[32,16,128]{2,1,0:T(8,128)S(1)}, f32[32,16,128]{2,1,0:T(8,128)S(1)}, u32[]{:S(2)}, u32[]{:S(2)}) collective-permute-start(f32[32,16,128]{2,1,0:T(8,128)S(1)} %get-tuple-element.37), channel_id=1, source_target_pairs={{64,128},{128,64},{65,129},{129,65},{192,194},{194,192},{193,195},... | collective-permute-start | bytes 786440 | tf_op jit(solution)/shard_map/ppermute | solution.py:74
  66.2 4.4 %collective-permute-done.10 = f32[32,16,128]{2,1,0:T(8,128)S(1)} collective-permute-done((f32[32,16,128]{2,1,0:T(8,128)S(1)}, f32[32,16,128]{2,1,0:T(8,128)S(1)}, u32[]{:S(2)}, u32[]{:S(2)}) %collective-permute-start.10) | collective-permute-done | bytes 262176 | tf_op jit(solution)/shard_map/ppermute | solution.py:74
  70.7 4.8 %collective-permute-done.9 = f32[32,16,128]{2,1,0:T(8,128)S(1)} collective-permute-done((f32[32,16,128]{2,1,0:T(8,128)S(1)}, f32[32,16,128]{2,1,0:T(8,128)S(1)}, u32[]{:S(2)}, u32[]{:S(2)}) %collective-permute-start.9) | collective-permute-done | bytes 262176 | tf_op jit(solution)/shard_map/ppermute | solution.py:74
  75.6 4.0 %collective-permute-start.11 = (f32[32,16,128]{2,1,0:T(8,128)S(1)}, f32[32,16,128]{2,1,0:T(8,128)S(1)}, u32[]{:S(2)}, u32[]{:S(2)}) collective-permute-start(f32[32,16,128]{2,1,0:T(8,128)S(1)} %fusion.28), channel_id=1, source_target_pairs={{0,256},{1,257},{2,258},{3,259},{4,260},{5,261},{6,262},{7,263},{8... | collective-permute-start | bytes 786440 | tf_op jit(solution)/shard_map/ppermute | solution.py:74
  79.5 13.0 %collective-permute-done.11 = f32[32,16,128]{2,1,0:T(8,128)S(1)} collective-permute-done((f32[32,16,128]{2,1,0:T(8,128)S(1)}, f32[32,16,128]{2,1,0:T(8,128)S(1)}, u32[]{:S(2)}, u32[]{:S(2)}) %collective-permute-start.11) | collective-permute-done | bytes 262176 | tf_op jit(solution)/shard_map/ppermute | solution.py:74
  92.6 1.9 %collective-permute-start.13 = (f32[32,16,128]{2,1,0:T(8,128)S(1)}, f32[32,16,128]{2,1,0:T(8,128)S(1)}, u32[]{:S(2)}, u32[]{:S(2)}) collective-permute-start(f32[32,16,128]{2,1,0:T(8,128)S(1)} %multiply_multiply_fusion), channel_id=1, source_target_pairs={{0,64},{64,0},{1,65},{65,1},{128,192},{192,128},{129,193},{193,129... | collective-permute-start | bytes 786440 | tf_op jit(solution)/shard_map/ppermute | solution.py:74
  94.5 3.2 %collective-permute-start.12 = (f32[32,16,128]{2,1,0:T(8,128)S(1)}, f32[32,16,128]{2,1,0:T(8,128)S(1)}, u32[]{:S(2)}, u32[]{:S(2)}) collective-permute-start(f32[32,16,128]{2,1,0:T(8,128)S(1)} %multiply_multiply_fusion), channel_id=1, source_target_pairs={{64,128},{128,64},{65,129},{129,65},{192,194},{194,192},{193,195},... | collective-permute-start | bytes 786440 | tf_op jit(solution)/shard_map/ppermute | solution.py:74
  97.7 4.1 %collective-permute-done.13 = f32[32,16,128]{2,1,0:T(8,128)S(1)} collective-permute-done((f32[32,16,128]{2,1,0:T(8,128)S(1)}, f32[32,16,128]{2,1,0:T(8,128)S(1)}, u32[]{:S(2)}, u32[]{:S(2)}) %collective-permute-start.13) | collective-permute-done | bytes 262176 | tf_op jit(solution)/shard_map/ppermute | solution.py:74
  101.8 4.0 %collective-permute-done.12 = f32[32,16,128]{2,1,0:T(8,128)S(1)} collective-permute-done((f32[32,16,128]{2,1,0:T(8,128)S(1)}, f32[32,16,128]{2,1,0:T(8,128)S(1)}, u32[]{:S(2)}, u32[]{:S(2)}) %collective-permute-start.12) | collective-permute-done | bytes 262176 | tf_op jit(solution)/shard_map/ppermute | solution.py:74
  105.9 3.5 %collective-permute-start.14 = (f32[32,48,128]{2,1,0:T(8,128)S(1)}, f32[32,48,128]{2,1,0:T(8,128)S(1)}, u32[]{:S(2)}, u32[]{:S(2)}) collective-permute-start(f32[32,48,128]{2,1,0:T(8,128)S(1)} %pad_maximum_fusion.2), channel_id=1, source_target_pairs={{0,1},{1,0},{2,3},{3,2},{4,5},{5,4},{6,7},{7,6},{8,9},{9,8},{10,11... | collective-permute-start | bytes 2359304 | tf_op jit(solution)/shard_map/ppermute | solution.py:74
  109.4 1.7 %collective-permute-done.14 = f32[32,48,128]{2,1,0:T(8,128)S(1)} collective-permute-done((f32[32,48,128]{2,1,0:T(8,128)S(1)}, f32[32,48,128]{2,1,0:T(8,128)S(1)}, u32[]{:S(2)}, u32[]{:S(2)}) %collective-permute-start.14) | collective-permute-done | bytes 786464 | tf_op jit(solution)/shard_map/ppermute | solution.py:74
  111.1 0.6 fusion.4
  111.7 0.9 convolution_bitcast_fusion.2
  112.6 1.8 %fusion.14 = f32[2,16,64,128]{3,2,1,0:T(8,128)S(1)} fusion(f32[2,16,64,128]{3,2,1,0:T(8,128)S(1)} %convolution_bitcast_fusion.2, f32[1,16,64,128]{3,2,1,0:T(8,128)} %bitcast.26, f32[1,16,64,128]{3,2,1,0:T(8,128)} %bitcast.25, pred[2,16]{1,0:T(4,128)(4,1)S(1)} %bitcast.114, f32[2,128,128,1]{2,0,1,3:T(2,128)S(1)} %bitcast.108), kind=kOutput, calls=%fused_computation.23 | convolution fusion | flops 202375168 | bytes 3276832 | tf_op jit(solution)/shard_map/uryz,uzw->uryw/dot_general | solution.py:169
  114.4 0.6 fusion.90
  115.0 0.6 fusion.91
  115.6 1.4 convolution_bitcast_fusion
  117.0 2.3 %collective-permute-start.15 = (f32[32,48,128]{2,1,0:T(8,128)S(1)}, f32[32,48,128]{2,1,0:T(8,128)S(1)}, u32[]{:S(2)}, u32[]{:S(2)}) collective-permute-start(f32[32,48,128]{2,1,0:T(8,128)S(1)} %slice.116), channel_id=1, source_target_pairs={{0,1},{1,0},{2,3},{3,2},{4,5},{5,4},{6,7},{7,6},{8,9},{9,8},{10,11... | collective-permute-start | bytes 2359304 | tf_op jit(solution)/shard_map/ppermute | solution.py:74
  119.3 1.9 %collective-permute-done.15 = f32[32,48,128]{2,1,0:T(8,128)S(1)} collective-permute-done((f32[32,48,128]{2,1,0:T(8,128)S(1)}, f32[32,48,128]{2,1,0:T(8,128)S(1)}, u32[]{:S(2)}, u32[]{:S(2)}) %collective-permute-start.15) | collective-permute-done | bytes 786464 | tf_op jit(solution)/shard_map/ppermute | solution.py:74
  121.3 1.9 %collective-permute-start.17 = (f32[32,16,128]{2,1,0:T(8,128)S(1)}, f32[32,16,128]{2,1,0:T(8,128)S(1)}, u32[]{:S(2)}, u32[]{:S(2)}) collective-permute-start(f32[32,16,128]{2,1,0:T(8,128)S(1)} %get-tuple-element.36), channel_id=1, source_target_pairs={{0,64},{64,0},{1,65},{65,1},{128,192},{192,128},{129,193},{193,129... | collective-permute-start | bytes 786440 | tf_op jit(solution)/shard_map/ppermute | solution.py:74
  123.2 3.8 %collective-permute-start.16 = (f32[32,16,128]{2,1,0:T(8,128)S(1)}, f32[32,16,128]{2,1,0:T(8,128)S(1)}, u32[]{:S(2)}, u32[]{:S(2)}) collective-permute-start(f32[32,16,128]{2,1,0:T(8,128)S(1)} %get-tuple-element.35), channel_id=1, source_target_pairs={{64,128},{128,64},{65,129},{129,65},{192,194},{194,192},{193,195},... | collective-permute-start | bytes 786440 | tf_op jit(solution)/shard_map/ppermute | solution.py:74
  127.1 3.7 %collective-permute-done.17 = f32[32,16,128]{2,1,0:T(8,128)S(1)} collective-permute-done((f32[32,16,128]{2,1,0:T(8,128)S(1)}, f32[32,16,128]{2,1,0:T(8,128)S(1)}, u32[]{:S(2)}, u32[]{:S(2)}) %collective-permute-start.17) | collective-permute-done | bytes 262176 | tf_op jit(solution)/shard_map/ppermute | solution.py:74
  130.7 4.0 %collective-permute-done.16 = f32[32,16,128]{2,1,0:T(8,128)S(1)} collective-permute-done((f32[32,16,128]{2,1,0:T(8,128)S(1)}, f32[32,16,128]{2,1,0:T(8,128)S(1)}, u32[]{:S(2)}, u32[]{:S(2)}) %collective-permute-start.16) | collective-permute-done | bytes 262176 | tf_op jit(solution)/shard_map/ppermute | solution.py:74
  134.8 6.3 %collective-permute-start.18 = (f32[16,16,128]{2,1,0:T(8,128)S(1)}, f32[16,16,128]{2,1,0:T(8,128)S(1)}, u32[]{:S(2)}, u32[]{:S(2)}) collective-permute-start(f32[16,16,128]{2,1,0:T(8,128)S(1)} %slice_select_fusion.1), channel_id=1, source_target_pairs={{0,256},{1,257},{2,258},{3,259},{4,260},{5,261},{6,262},{7,263},{8... | collective-permute-start | bytes 393224 | tf_op jit(solution)/shard_map/ppermute | solution.py:74
  141.1 4.0 %collective-permute-done.18 = f32[16,16,128]{2,1,0:T(8,128)S(1)} collective-permute-done((f32[16,16,128]{2,1,0:T(8,128)S(1)}, f32[16,16,128]{2,1,0:T(8,128)S(1)}, u32[]{:S(2)}, u32[]{:S(2)}) %collective-permute-start.18) | collective-permute-done | bytes 131104 | tf_op jit(solution)/shard_map/ppermute | solution.py:74
  145.2 5.6 %collective-permute-start.19 = (f32[8,16,128]{2,1,0:T(8,128)S(1)}, f32[8,16,128]{2,1,0:T(8,128)S(1)}, u32[]{:S(2)}, u32[]{:S(2)}) collective-permute-start(f32[8,16,128]{2,1,0:T(8,128)S(1)} %get-tuple-element.41), channel_id=1, source_target_pairs={{0,0},{128,1},{64,64},{192,65},{1,128},{129,129},{65,192},{193,193... | collective-permute-start | bytes 196616 | tf_op jit(solution)/shard_map/ppermute | solution.py:74
  150.8 1.9 %collective-permute-start.20 = (f32[8,16,128]{2,1,0:T(8,128)S(1)}, f32[8,16,128]{2,1,0:T(8,128)S(1)}, u32[]{:S(2)}, u32[]{:S(2)}) collective-permute-start(f32[8,16,128]{2,1,0:T(8,128)S(1)} %get-tuple-element.42), channel_id=1, source_target_pairs={{64,0},{192,1},{0,64},{128,65},{65,128},{193,129},{1,192},{129,193... | collective-permute-start | bytes 196616 | tf_op jit(solution)/shard_map/ppermute | solution.py:74
  152.8 0.2 collective-permute-done.19
  153.0 4.7 %collective-permute-done.20 = f32[8,16,128]{2,1,0:T(8,128)S(1)} collective-permute-done((f32[8,16,128]{2,1,0:T(8,128)S(1)}, f32[8,16,128]{2,1,0:T(8,128)S(1)}, u32[]{:S(2)}, u32[]{:S(2)}) %collective-permute-start.20) | collective-permute-done | bytes 65568 | tf_op jit(solution)/shard_map/ppermute | solution.py:74
  157.7 0.7 copy.9
  (45 shorter events, 1.5 us)
Async XLA Ops:
  0.0 23.7 %copy-start = (f32[1,32,64,128]{3,2,1,0:T(8,128)S(1)}, f32[1,32,64,128]{3,2,1,0:T(8,128)}, u32[]{:S(2)}) copy-start(f32[1,32,64,128]{3,2,1,0:T(8,128)} %param.5) | copy-start | bytes 3145732
  1.0 8.2 %collective-permute-start = (f32[8,16,128]{2,1,0:T(8,128)S(1)}, f32[8,16,128]{2,1,0:T(8,128)S(1)}, u32[]{:S(2)}, u32[]{:S(2)}) collective-permute-start(f32[8,16,128]{2,1,0:T(8,128)S(1)} %bitcast.109), channel_id=1, source_target_pairs={{0,0},{1,128},{64,64},{65,192},{128,1},{129,129},{192,65},{193,193... | collective-permute-start | bytes 196616 | tf_op jit(solution)/shard_map/ppermute | solution.py:74
  6.2 6.8 %collective-permute-start.1 = (f32[8,16,128]{2,1,0:T(8,128)S(1)}, f32[8,16,128]{2,1,0:T(8,128)S(1)}, u32[]{:S(2)}, u32[]{:S(2)}) collective-permute-start(f32[8,16,128]{2,1,0:T(8,128)S(1)} %bitcast.110), channel_id=1, source_target_pairs={{0,64},{1,192},{64,0},{65,128},{128,65},{129,193},{192,1},{193,129... | collective-permute-start | bytes 196616 | tf_op jit(solution)/shard_map/ppermute | solution.py:74
  9.2 26.9 %copy-start.1 = (f32[8,3,31]{2,0,1:T(8,128)S(1)}, f32[8,3,31]{2,0,1:T(8,128)}, u32[]{:S(2)}) copy-start(f32[8,3,31]{2,0,1:T(8,128)} %param.6) | copy-start | bytes 8932
  13.1 25.7 %copy-start.2 = (s32[8,16]{1,0:T(8,128)S(1)}, s32[8,16]{1,0:T(8,128)}, u32[]{:S(2)}) copy-start(s32[8,16]{1,0:T(8,128)} %param.7) | copy-start | bytes 1540
  13.1 16.4 %collective-permute-start.2 = (f32[16,16,128]{2,1,0:T(8,128)S(1)}, f32[16,16,128]{2,1,0:T(8,128)S(1)}, u32[]{:S(2)}, u32[]{:S(2)}) collective-permute-start(f32[16,16,128]{2,1,0:T(8,128)S(1)} %pad_maximum_fusion.3), channel_id=1, source_target_pairs={{0,256},{1,257},{2,258},{3,259},{4,260},{5,261},{6,262},{7,263},{8... | collective-permute-start | bytes 393224 | tf_op jit(solution)/shard_map/ppermute | solution.py:74
  23.9 21.0 %collective-permute-start.5 = (f32[16,64,128]{2,1,0:T(8,128)S(1)}, f32[16,64,128]{2,1,0:T(8,128)}, u32[]{:S(2)}, u32[]{:S(2)}) collective-permute-start(f32[16,64,128]{2,1,0:T(8,128)S(1)} %get-tuple-element.21), channel_id=1, source_target_pairs={{0,0},{1,128},{64,64},{65,192},{128,1},{129,129},{192,65},{193,193... | collective-permute-start | bytes 1572872 | tf_op jit(solution)/shard_map/ppermute | solution.py:74
  25.8 19.1 %collective-permute-start.6 = (f32[16,64,128]{2,1,0:T(8,128)S(1)}, f32[16,64,128]{2,1,0:T(8,128)}, u32[]{:S(2)}, u32[]{:S(2)}) collective-permute-start(f32[16,64,128]{2,1,0:T(8,128)S(1)} %get-tuple-element.22), channel_id=1, source_target_pairs={{0,64},{1,192},{64,0},{65,128},{128,65},{129,193},{192,1},{193,129... | collective-permute-start | bytes 1572872 | tf_op jit(solution)/shard_map/ppermute | solution.py:74
  29.5 13.9 %collective-permute-start.4 = (f32[32,16,128]{2,1,0:T(8,128)S(1)}, f32[32,16,128]{2,1,0:T(8,128)S(1)}, u32[]{:S(2)}, u32[]{:S(2)}) collective-permute-start(f32[32,16,128]{2,1,0:T(8,128)S(1)} %maximum_select_fusion), channel_id=1, source_target_pairs={{0,64},{64,0},{1,65},{65,1},{128,192},{192,128},{129,193},{193,129... | collective-permute-start | bytes 786440 | tf_op jit(solution)/shard_map/ppermute | solution.py:74
  32.6 12.3 %collective-permute-start.3 = (f32[32,16,128]{2,1,0:T(8,128)S(1)}, f32[32,16,128]{2,1,0:T(8,128)S(1)}, u32[]{:S(2)}, u32[]{:S(2)}) collective-permute-start(f32[32,16,128]{2,1,0:T(8,128)S(1)} %maximum_select_fusion), channel_id=1, source_target_pairs={{64,128},{128,64},{65,129},{129,65},{192,194},{194,192},{193,195},... | collective-permute-start | bytes 786440 | tf_op jit(solution)/shard_map/ppermute | solution.py:74
  44.9 4.3 %collective-permute-start.7 = (f32[32,48,128]{2,1,0:T(8,128)S(1)}, f32[32,48,128]{2,1,0:T(8,128)S(1)}, u32[]{:S(2)}, u32[]{:S(2)}) collective-permute-start(f32[32,48,128]{2,1,0:T(8,128)S(1)} %pad_maximum_fusion.1), channel_id=1, source_target_pairs={{0,1},{1,0},{2,3},{3,2},{4,5},{5,4},{6,7},{7,6},{8,9},{9,8},{10,11... | collective-permute-start | bytes 2359304 | tf_op jit(solution)/shard_map/ppermute | solution.py:74
  55.1 4.2 %collective-permute-start.8 = (f32[32,48,128]{2,1,0:T(8,128)S(1)}, f32[32,48,128]{2,1,0:T(8,128)S(1)}, u32[]{:S(2)}, u32[]{:S(2)}) collective-permute-start(f32[32,48,128]{2,1,0:T(8,128)S(1)} %slice.109), channel_id=1, source_target_pairs={{0,1},{1,0},{2,3},{3,2},{4,5},{5,4},{6,7},{7,6},{8,9},{9,8},{10,11... | collective-permute-start | bytes 2359304 | tf_op jit(solution)/shard_map/ppermute | solution.py:74
  59.4 11.3 %collective-permute-start.10 = (f32[32,16,128]{2,1,0:T(8,128)S(1)}, f32[32,16,128]{2,1,0:T(8,128)S(1)}, u32[]{:S(2)}, u32[]{:S(2)}) collective-permute-start(f32[32,16,128]{2,1,0:T(8,128)S(1)} %get-tuple-element.38), channel_id=1, source_target_pairs={{0,64},{64,0},{1,65},{65,1},{128,192},{192,128},{129,193},{193,129... | collective-permute-start | bytes 786440 | tf_op jit(solution)/shard_map/ppermute | solution.py:74
  64.3 11.2 %collective-permute-start.9 = (f32[32,16,128]{2,1,0:T(8,128)S(1)}, f32[32,16,128]{2,1,0:T(8,128)S(1)}, u32[]{:S(2)}, u32[]{:S(2)}) collective-permute-start(f32[32,16,128]{2,1,0:T(8,128)S(1)} %get-tuple-element.37), channel_id=1, source_target_pairs={{64,128},{128,64},{65,129},{129,65},{192,194},{194,192},{193,195},... | collective-permute-start | bytes 786440 | tf_op jit(solution)/shard_map/ppermute | solution.py:74
  75.6 17.0 %collective-permute-start.11 = (f32[32,16,128]{2,1,0:T(8,128)S(1)}, f32[32,16,128]{2,1,0:T(8,128)S(1)}, u32[]{:S(2)}, u32[]{:S(2)}) collective-permute-start(f32[32,16,128]{2,1,0:T(8,128)S(1)} %fusion.28), channel_id=1, source_target_pairs={{0,256},{1,257},{2,258},{3,259},{4,260},{5,261},{6,262},{7,263},{8... | collective-permute-start | bytes 786440 | tf_op jit(solution)/shard_map/ppermute | solution.py:74
  92.6 9.2 %collective-permute-start.13 = (f32[32,16,128]{2,1,0:T(8,128)S(1)}, f32[32,16,128]{2,1,0:T(8,128)S(1)}, u32[]{:S(2)}, u32[]{:S(2)}) collective-permute-start(f32[32,16,128]{2,1,0:T(8,128)S(1)} %multiply_multiply_fusion), channel_id=1, source_target_pairs={{0,64},{64,0},{1,65},{65,1},{128,192},{192,128},{129,193},{193,129... | collective-permute-start | bytes 786440 | tf_op jit(solution)/shard_map/ppermute | solution.py:74
  94.5 11.3 %collective-permute-start.12 = (f32[32,16,128]{2,1,0:T(8,128)S(1)}, f32[32,16,128]{2,1,0:T(8,128)S(1)}, u32[]{:S(2)}, u32[]{:S(2)}) collective-permute-start(f32[32,16,128]{2,1,0:T(8,128)S(1)} %multiply_multiply_fusion), channel_id=1, source_target_pairs={{64,128},{128,64},{65,129},{129,65},{192,194},{194,192},{193,195},... | collective-permute-start | bytes 786440 | tf_op jit(solution)/shard_map/ppermute | solution.py:74
  105.9 5.2 %collective-permute-start.14 = (f32[32,48,128]{2,1,0:T(8,128)S(1)}, f32[32,48,128]{2,1,0:T(8,128)S(1)}, u32[]{:S(2)}, u32[]{:S(2)}) collective-permute-start(f32[32,48,128]{2,1,0:T(8,128)S(1)} %pad_maximum_fusion.2), channel_id=1, source_target_pairs={{0,1},{1,0},{2,3},{3,2},{4,5},{5,4},{6,7},{7,6},{8,9},{9,8},{10,11... | collective-permute-start | bytes 2359304 | tf_op jit(solution)/shard_map/ppermute | solution.py:74
  117.0 4.2 %collective-permute-start.15 = (f32[32,48,128]{2,1,0:T(8,128)S(1)}, f32[32,48,128]{2,1,0:T(8,128)S(1)}, u32[]{:S(2)}, u32[]{:S(2)}) collective-permute-start(f32[32,48,128]{2,1,0:T(8,128)S(1)} %slice.116), channel_id=1, source_target_pairs={{0,1},{1,0},{2,3},{3,2},{4,5},{5,4},{6,7},{7,6},{8,9},{9,8},{10,11... | collective-permute-start | bytes 2359304 | tf_op jit(solution)/shard_map/ppermute | solution.py:74
  121.3 9.4 %collective-permute-start.17 = (f32[32,16,128]{2,1,0:T(8,128)S(1)}, f32[32,16,128]{2,1,0:T(8,128)S(1)}, u32[]{:S(2)}, u32[]{:S(2)}) collective-permute-start(f32[32,16,128]{2,1,0:T(8,128)S(1)} %get-tuple-element.36), channel_id=1, source_target_pairs={{0,64},{64,0},{1,65},{65,1},{128,192},{192,128},{129,193},{193,129... | collective-permute-start | bytes 786440 | tf_op jit(solution)/shard_map/ppermute | solution.py:74
  123.2 11.5 %collective-permute-start.16 = (f32[32,16,128]{2,1,0:T(8,128)S(1)}, f32[32,16,128]{2,1,0:T(8,128)S(1)}, u32[]{:S(2)}, u32[]{:S(2)}) collective-permute-start(f32[32,16,128]{2,1,0:T(8,128)S(1)} %get-tuple-element.35), channel_id=1, source_target_pairs={{64,128},{128,64},{65,129},{129,65},{192,194},{194,192},{193,195},... | collective-permute-start | bytes 786440 | tf_op jit(solution)/shard_map/ppermute | solution.py:74
  134.8 10.3 %collective-permute-start.18 = (f32[16,16,128]{2,1,0:T(8,128)S(1)}, f32[16,16,128]{2,1,0:T(8,128)S(1)}, u32[]{:S(2)}, u32[]{:S(2)}) collective-permute-start(f32[16,16,128]{2,1,0:T(8,128)S(1)} %slice_select_fusion.1), channel_id=1, source_target_pairs={{0,256},{1,257},{2,258},{3,259},{4,260},{5,261},{6,262},{7,263},{8... | collective-permute-start | bytes 393224 | tf_op jit(solution)/shard_map/ppermute | solution.py:74
  145.2 7.8 %collective-permute-start.19 = (f32[8,16,128]{2,1,0:T(8,128)S(1)}, f32[8,16,128]{2,1,0:T(8,128)S(1)}, u32[]{:S(2)}, u32[]{:S(2)}) collective-permute-start(f32[8,16,128]{2,1,0:T(8,128)S(1)} %get-tuple-element.41), channel_id=1, source_target_pairs={{0,0},{128,1},{64,64},{192,65},{1,128},{129,129},{65,192},{193,193... | collective-permute-start | bytes 196616 | tf_op jit(solution)/shard_map/ppermute | solution.py:74
  150.8 6.8 %collective-permute-start.20 = (f32[8,16,128]{2,1,0:T(8,128)S(1)}, f32[8,16,128]{2,1,0:T(8,128)S(1)}, u32[]{:S(2)}, u32[]{:S(2)}) collective-permute-start(f32[8,16,128]{2,1,0:T(8,128)S(1)} %get-tuple-element.42), channel_id=1, source_target_pairs={{64,0},{192,1},{0,64},{128,65},{65,128},{193,129},{1,192},{129,193... | collective-permute-start | bytes 196616 | tf_op jit(solution)/shard_map/ppermute | solution.py:74

commit v8 on v7

--- a/solution.py
+++ b/solution.py
@@ -112,7 +112,7 @@
     )
     current = by_h(quarter, send(quarter, SWAP_H), h)
     images = [piece(observed[0], turn, 0) for turn in (0, 1)]
-    *images, _ = lax.optimization_barrier((*images, quarter))
+    images[1], _ = lax.optimization_barrier((images[1], quarter))
     images = [send(image, SPREAD[turn]) for turn, image in enumerate(images)]
     psf_taps, intersection, current = lax.optimization_barrier((psf_taps, intersection, current))
 
@@ -162,16 +162,23 @@
             extended, scale, inside, mat_x, mat_y, mat_z, *images = lax.optimization_barrier(
                 (extended, scale, inside, mat_x, mat_y, mat_z, *images)
             )
-            images = jnp.stack(images)
+            images = lax.optimization_barrier(jnp.where(inside, jnp.stack(images), 0.0))
         extended = jnp.concatenate([extended, send(extended, SWAP_CORE)], 0)
         blurred = jnp.einsum("urj,yjz->uryz", mat_x, extended, precision=HIGH)
         blurred = jnp.einsum("urjz,uyj->uryz", blurred, mat_y, precision=HIGH)
         blurred = jnp.einsum("uryz,uzw->uryw", blurred, mat_z, precision=HIGH)
-        ratio = jnp.where(inside, images / jnp.where(inside, blurred, 1.0), 0.0)
+        ratio = images / jnp.where(inside, blurred, 1.0)
         back = jnp.einsum("uryw,uzw->uryz", ratio, mat_z, precision=HIGH)
-        back = jnp.einsum("uryz,uyj->urjz", back, mat_y, precision=HIGH)
-        back = jnp.einsum("urj,uryz->yjz", mat_x, back, precision=HIGH)
-        part = back[:width] + send(back[width:], SWAP_CORE)
+        own_part, other_part = (
+            jnp.einsum(
+                "urj,uryz->yjz",
+                mat_x,
+                jnp.einsum("uryz,uyj->urjz", back, columns, precision=HIGH),
+                precision=HIGH,
+            )
+            for columns in (mat_y[:, :, :width], mat_y[:, :, width:])
+        )
+        part = lax.optimization_barrier(own_part) + send(other_part, SWAP_CORE)
         part = part[:, SLAB : 2 * SLAB] + send(part[:, :SLAB], ODD) + send(part[:, 2 * SLAB :], EVEN)
         if iteration < ITERS - 1:
             current = current * (part + send(part, SWAP_H) + 1.0) * scale
@@ -182,9 +189,11 @@
     total = own_half(part, True) + send(own_half(part, False), SWAP_H)
     quarter = own_half(current, True) * (total + 1.0) * own_half(scale, True)
 
-    result = ordered([quarter[:block], quarter[block:]], even)
+    quarter = jnp.swapaxes(quarter, 0, 1)
+    result = ordered([quarter[:, :block], quarter[:, block:]], even)
+    result = lax.optimization_barrier(tuple(result))
     result = [send(value, reverse(route)) for value, route in zip(result, SPREAD)]
-    return jnp.swapaxes(jnp.concatenate(ordered(result, x % 2 == 0), 1), 0, 1)
+    return jnp.concatenate(ordered(result, x % 2 == 0), 0)
 
 
 def solution(mesh):

time: 159 us -> 157 us (0.987)
  waiting for transfers between devices: 62.5 us -> 57.5 us
  other arithmetic: 1.05 us -> 4.48 us
  local copies, waits for them, and re-layouts: 2.22 us -> 4.74 us
  matrix products: 15.6 us -> 13.9 us
    ppermute x21, waiting for transfers between devices: 62.5 us -> 57.5 us  [send(): return lax.ppermute(value, AXES, pairs)]
    dot_general x2, matrix products: 3.68 us -> 1.22 us  [body(): blurred = jnp.einsum('uryz,uzw->uryw', blurred, mat_z, precision=HIGH)]
    dot_general x4 -> x8, matrix products: 3.87 us -> 4.54 us  [the longest x4 3.01 us: body(): jnp.einsum('urj,uryz->yjz', mat_x, jnp.einsum('uryz,uyj->urjz', back, col...]
  transfers between devices with their start and end apart: 21 -> 21, of which waited for: 17 -> 14; matrix products, arithmetic and copies ran while one was open for 3% -> 8% of each run, Pallas kernels for 0% -> 0%
where the time goes in v8:
time: 157 us; the launch traced here: 156 us
  starting transfers between devices  74.9 us (48%)
  waiting for transfers between devices  57.5 us (37%)
  matrix products  13.9 us (9%)
  local copies, waits for them, and re-layouts  4.74 us (3%)
  other arithmetic  4.48 us (3%)
    ppermute x21, starting transfers between devices, send(): return lax.ppermute(value, AXES, pairs)  74.9 us
    ppermute x21, waiting for transfers between devices, send(): return lax.ppermute(value, AXES, pairs)  57.5 us
  transfers between devices with their start and end apart: 21, of which 14 were waited for; matrix products, arithmetic and copies ran while one was open for 8% of the time, Pallas kernels for 0%

profile of v8, /device:TPU:57, one launch (start us, length us, event | category | flops | bytes accessed | tf_op | source)
XLA Modules:
  0.0 156.3 jit_solution(2325744034555937557)
XLA Ops:
  0.0 0.9 constant_dynamic-slice_fusion.1
  0.9 4.9 %collective-permute-start.1 = (f32[8,16,128]{2,1,0:T(8,128)S(1)}, f32[8,16,128]{2,1,0:T(8,128)S(1)}, u32[]{:S(2)}, u32[]{:S(2)}) collective-permute-start(f32[8,16,128]{2,1,0:T(8,128)S(1)} %bitcast.140), channel_id=1, source_target_pairs={{0,64},{1,192},{64,0},{65,128},{128,65},{129,193},{192,1},{193,129... | collective-permute-start | bytes 196616 | tf_op jit(solution)/shard_map/ppermute | solution.py:74
  5.9 2.2 %collective-permute-start = (f32[8,16,128]{2,1,0:T(8,128)S(1)}, f32[8,16,128]{2,1,0:T(8,128)S(1)}, u32[]{:S(2)}, u32[]{:S(2)}) collective-permute-start(f32[8,16,128]{2,1,0:T(8,128)S(1)} %bitcast.141), channel_id=1, source_target_pairs={{0,0},{1,128},{64,64},{65,192},{128,1},{129,129},{192,65},{193,193... | collective-permute-start | bytes 196616 | tf_op jit(solution)/shard_map/ppermute | solution.py:74
  8.1 1.3 dynamic-slice_bitcast_fusion
  9.4 4.9 %collective-permute-start.5 = (f32[16,64,128]{2,1,0:T(8,128)S(1)}, f32[16,64,128]{2,1,0:T(8,128)S(1)}, u32[]{:S(2)}, u32[]{:S(2)}) collective-permute-start(f32[16,64,128]{2,1,0:T(8,128)S(1)} %get-tuple-element.36), channel_id=1, source_target_pairs={{0,0},{1,128},{64,64},{65,192},{128,1},{129,129},{192,65},{193,193... | collective-permute-start | bytes 1572872 | tf_op jit(solution)/shard_map/ppermute | solution.py:74
  14.7 10.6 %collective-permute-start.2 = (f32[16,16,128]{2,1,0:T(8,128)S(1)}, f32[16,16,128]{2,1,0:T(8,128)S(1)}, u32[]{:S(2)}, u32[]{:S(2)}) collective-permute-start(f32[16,16,128]{2,1,0:T(8,128)S(1)} %pad_maximum_fusion.2), channel_id=1, source_target_pairs={{0,256},{1,257},{2,258},{3,259},{4,260},{5,261},{6,262},{7,263},{8... | collective-permute-start | bytes 393224 | tf_op jit(solution)/shard_map/ppermute | solution.py:74
  25.5 2.2 %collective-permute-start.6 = (f32[16,64,128]{2,1,0:T(8,128)S(1)}, f32[16,64,128]{2,1,0:T(8,128)}, u32[]{:S(2)}, u32[]{:S(2)}) collective-permute-start(f32[16,64,128]{2,1,0:T(8,128)S(1)} %get-tuple-element.22), channel_id=1, source_target_pairs={{0,64},{1,192},{64,0},{65,128},{128,65},{129,193},{192,1},{193,129... | collective-permute-start | bytes 1572872 | tf_op jit(solution)/shard_map/ppermute | solution.py:74
  27.8 1.9 %collective-permute-start.4 = (f32[32,16,128]{2,1,0:T(8,128)S(1)}, f32[32,16,128]{2,1,0:T(8,128)S(1)}, u32[]{:S(2)}, u32[]{:S(2)}) collective-permute-start(f32[32,16,128]{2,1,0:T(8,128)S(1)} %maximum_select_fusion.1), channel_id=1, source_target_pairs={{0,64},{64,0},{1,65},{65,1},{128,192},{192,128},{129,193},{193,129... | collective-permute-start | bytes 786440 | tf_op jit(solution)/shard_map/ppermute | solution.py:74
  29.8 10.1 %collective-permute-start.3 = (f32[32,16,128]{2,1,0:T(8,128)S(1)}, f32[32,16,128]{2,1,0:T(8,128)}, u32[]{:S(2)}, u32[]{:S(2)}) collective-permute-start(f32[32,16,128]{2,1,0:T(8,128)S(1)} %maximum_select_fusion.1), channel_id=1, source_target_pairs={{64,128},{128,64},{65,129},{129,65},{192,194},{194,192},{193,195},... | collective-permute-start | bytes 786440 | tf_op jit(solution)/shard_map/ppermute | solution.py:74
  40.2 0.2 fusion.83
  40.7 0.4 fusion.18
  41.1 0.7 fusion.28
  41.8 0.8 fusion
  42.8 0.3 fusion.44
  43.4 0.8 fusion.13
  44.2 2.3 %collective-permute-done.3 = f32[32,16,128]{2,1,0:T(8,128)} collective-permute-done((f32[32,16,128]{2,1,0:T(8,128)S(1)}, f32[32,16,128]{2,1,0:T(8,128)}, u32[]{:S(2)}, u32[]{:S(2)}) %collective-permute-start.3) | collective-permute-done | bytes 262176 | tf_op jit(solution)/shard_map/ppermute | solution.py:74
  46.5 1.0 pad_maximum_fusion
  47.5 2.6 %collective-permute-start.7 = (f32[32,48,128]{2,1,0:T(8,128)S(1)}, f32[32,48,128]{2,1,0:T(8,128)S(1)}, u32[]{:S(2)}, u32[]{:S(2)}) collective-permute-start(f32[32,48,128]{2,1,0:T(8,128)S(1)} %pad_maximum_fusion), channel_id=1, source_target_pairs={{0,1},{1,0},{2,3},{3,2},{4,5},{5,4},{6,7},{7,6},{8,9},{9,8},{10,11... | collective-permute-start | bytes 2359304 | tf_op jit(solution)/shard_map/ppermute | solution.py:74
  50.2 1.3 maximum_select_fusion
  51.5 0.7 slice_bitcast_fusion
  52.3 0.6 fusion.1
  52.9 0.9 convolution_bitcast_fusion.1
  53.8 0.6 fusion.11
  54.4 0.6 fusion.40
  55.0 0.4 fusion.100
  55.4 0.8 convolution_bitcast_fusion.4
  56.1 2.0 %collective-permute-start.8 = (f32[32,48,128]{2,1,0:T(8,128)S(1)}, f32[32,48,128]{2,1,0:T(8,128)}, u32[]{:S(2)}, u32[]{:S(2)}) collective-permute-start(f32[32,48,128]{2,1,0:T(8,128)S(1)} %convolution_bitcast_fusion.4), channel_id=1, source_target_pairs={{0,1},{1,0},{2,3},{3,2},{4,5},{5,4},{6,7},{7,6},{8,9},{9,8},{10,11... | collective-permute-start | bytes 2359304 | tf_op jit(solution)/shard_map/ppermute | solution.py:74
  58.2 0.9 copy.24
  59.1 0.4 fusion.99
  59.5 0.8 convolution_bitcast_fusion.5
  60.2 0.2 collective-permute-done.8
  60.5 1.2 add.250
  61.7 5.5 %collective-permute-start.9 = (f32[32,16,128]{2,1,0:T(8,128)S(1)}, f32[32,16,128]{2,1,0:T(8,128)S(1)}, u32[]{:S(2)}, u32[]{:S(2)}) collective-permute-start(f32[32,16,128]{2,1,0:T(8,128)S(1)} %get-tuple-element.39), channel_id=1, source_target_pairs={{64,128},{128,64},{65,129},{129,65},{192,194},{194,192},{193,195},... | collective-permute-start | bytes 786440 | tf_op jit(solution)/shard_map/ppermute | solution.py:74
  67.2 1.9 %collective-permute-start.10 = (f32[32,16,128]{2,1,0:T(8,128)S(1)}, f32[32,16,128]{2,1,0:T(8,128)S(1)}, u32[]{:S(2)}, u32[]{:S(2)}) collective-permute-start(f32[32,16,128]{2,1,0:T(8,128)S(1)} %get-tuple-element.40), channel_id=1, source_target_pairs={{0,64},{64,0},{1,65},{65,1},{128,192},{192,128},{129,193},{193,129... | collective-permute-start | bytes 786440 | tf_op jit(solution)/shard_map/ppermute | solution.py:74
  69.1 4.3 %collective-permute-done.9 = f32[32,16,128]{2,1,0:T(8,128)S(1)} collective-permute-done((f32[32,16,128]{2,1,0:T(8,128)S(1)}, f32[32,16,128]{2,1,0:T(8,128)S(1)}, u32[]{:S(2)}, u32[]{:S(2)}) %collective-permute-start.9) | collective-permute-done | bytes 262176 | tf_op jit(solution)/shard_map/ppermute | solution.py:74
  73.4 3.0 %collective-permute-done.10 = f32[32,16,128]{2,1,0:T(8,128)S(1)} collective-permute-done((f32[32,16,128]{2,1,0:T(8,128)S(1)}, f32[32,16,128]{2,1,0:T(8,128)S(1)}, u32[]{:S(2)}, u32[]{:S(2)}) %collective-permute-start.10) | collective-permute-done | bytes 262176 | tf_op jit(solution)/shard_map/ppermute | solution.py:74
  76.5 1.9 %collective-permute-start.11 = (f32[32,16,128]{2,1,0:T(8,128)S(1)}, f32[32,16,128]{2,1,0:T(8,128)S(1)}, u32[]{:S(2)}, u32[]{:S(2)}) collective-permute-start(f32[32,16,128]{2,1,0:T(8,128)S(1)} %fusion.30), channel_id=1, source_target_pairs={{0,256},{1,257},{2,258},{3,259},{4,260},{5,261},{6,262},{7,263},{8... | collective-permute-start | bytes 786440 | tf_op jit(solution)/shard_map/ppermute | solution.py:74
  78.5 16.5 %collective-permute-done.11 = f32[32,16,128]{2,1,0:T(8,128)S(1)} collective-permute-done((f32[32,16,128]{2,1,0:T(8,128)S(1)}, f32[32,16,128]{2,1,0:T(8,128)S(1)}, u32[]{:S(2)}, u32[]{:S(2)}) %collective-permute-start.11) | collective-permute-done | bytes 262176 | tf_op jit(solution)/shard_map/ppermute | solution.py:74
  95.1 2.2 %collective-permute-start.13 = (f32[32,16,128]{2,1,0:T(8,128)S(1)}, f32[32,16,128]{2,1,0:T(8,128)S(1)}, u32[]{:S(2)}, u32[]{:S(2)}) collective-permute-start(f32[32,16,128]{2,1,0:T(8,128)S(1)} %multiply_multiply_fusion), channel_id=1, source_target_pairs={{0,64},{64,0},{1,65},{65,1},{128,192},{192,128},{129,193},{193,129... | collective-permute-start | bytes 786440 | tf_op jit(solution)/shard_map/ppermute | solution.py:74
  97.3 1.9 %collective-permute-start.12 = (f32[32,16,128]{2,1,0:T(8,128)S(1)}, f32[32,16,128]{2,1,0:T(8,128)S(1)}, u32[]{:S(2)}, u32[]{:S(2)}) collective-permute-start(f32[32,16,128]{2,1,0:T(8,128)S(1)} %multiply_multiply_fusion), channel_id=1, source_target_pairs={{64,128},{128,64},{65,129},{129,65},{192,194},{194,192},{193,195},... | collective-permute-start | bytes 786440 | tf_op jit(solution)/shard_map/ppermute | solution.py:74
  99.3 5.1 %collective-permute-done.13 = f32[32,16,128]{2,1,0:T(8,128)S(1)} collective-permute-done((f32[32,16,128]{2,1,0:T(8,128)S(1)}, f32[32,16,128]{2,1,0:T(8,128)S(1)}, u32[]{:S(2)}, u32[]{:S(2)}) %collective-permute-start.13) | collective-permute-done | bytes 262176 | tf_op jit(solution)/shard_map/ppermute | solution.py:74
  104.4 4.0 %collective-permute-done.12 = f32[32,16,128]{2,1,0:T(8,128)S(1)} collective-permute-done((f32[32,16,128]{2,1,0:T(8,128)S(1)}, f32[32,16,128]{2,1,0:T(8,128)S(1)}, u32[]{:S(2)}, u32[]{:S(2)}) %collective-permute-start.12) | collective-permute-done | bytes 262176 | tf_op jit(solution)/shard_map/ppermute | solution.py:74
  108.4 3.8 %collective-permute-start.14 = (f32[32,48,128]{2,1,0:T(8,128)S(1)}, f32[32,48,128]{2,1,0:T(8,128)S(1)}, u32[]{:S(2)}, u32[]{:S(2)}) collective-permute-start(f32[32,48,128]{2,1,0:T(8,128)S(1)} %pad_maximum_fusion.1), channel_id=1, source_target_pairs={{0,1},{1,0},{2,3},{3,2},{4,5},{5,4},{6,7},{7,6},{8,9},{9,8},{10,11... | collective-permute-start | bytes 2359304 | tf_op jit(solution)/shard_map/ppermute | solution.py:74
  112.2 1.7 %collective-permute-done.14 = f32[32,48,128]{2,1,0:T(8,128)S(1)} collective-permute-done((f32[32,48,128]{2,1,0:T(8,128)S(1)}, f32[32,48,128]{2,1,0:T(8,128)S(1)}, u32[]{:S(2)}, u32[]{:S(2)}) %collective-permute-start.14) | collective-permute-done | bytes 786464 | tf_op jit(solution)/shard_map/ppermute | solution.py:74
  113.9 0.6 fusion.4
  114.5 0.9 convolution_bitcast_fusion
  115.4 0.6 fusion.12
  116.0 0.6 fusion.38
  116.6 0.4 fusion.102
  117.0 0.8 convolution_bitcast_fusion.2
  117.8 2.3 %collective-permute-start.15 = (f32[32,48,128]{2,1,0:T(8,128)S(1)}, f32[32,48,128]{2,1,0:T(8,128)S(1)}, u32[]{:S(2)}, u32[]{:S(2)}) collective-permute-start(f32[32,48,128]{2,1,0:T(8,128)S(1)} %convolution_bitcast_fusion.2), channel_id=1, source_target_pairs={{0,1},{1,0},{2,3},{3,2},{4,5},{5,4},{6,7},{7,6},{8,9},{9,8},{10,11... | collective-permute-start | bytes 2359304 | tf_op jit(solution)/shard_map/ppermute | solution.py:74
  120.1 0.4 fusion.101
  120.5 0.8 convolution_bitcast_fusion.3
  121.2 0.7 collective-permute-done.15
  122.1 1.9 %collective-permute-start.16 = (f32[32,16,128]{2,1,0:T(8,128)S(1)}, f32[32,16,128]{2,1,0:T(8,128)S(1)}, u32[]{:S(2)}, u32[]{:S(2)}) collective-permute-start(f32[32,16,128]{2,1,0:T(8,128)S(1)} %get-tuple-element.37), channel_id=1, source_target_pairs={{64,128},{128,64},{65,129},{129,65},{192,194},{194,192},{193,195},... | collective-permute-start | bytes 786440 | tf_op jit(solution)/shard_map/ppermute | solution.py:74
  124.0 1.9 %collective-permute-start.17 = (f32[32,16,128]{2,1,0:T(8,128)S(1)}, f32[32,16,128]{2,1,0:T(8,128)S(1)}, u32[]{:S(2)}, u32[]{:S(2)}) collective-permute-start(f32[32,16,128]{2,1,0:T(8,128)S(1)} %get-tuple-element.38), channel_id=1, source_target_pairs={{0,64},{64,0},{1,65},{65,1},{128,192},{192,128},{129,193},{193,129... | collective-permute-start | bytes 786440 | tf_op jit(solution)/shard_map/ppermute | solution.py:74
  126.0 7.7 %collective-permute-done.16 = f32[32,16,128]{2,1,0:T(8,128)S(1)} collective-permute-done((f32[32,16,128]{2,1,0:T(8,128)S(1)}, f32[32,16,128]{2,1,0:T(8,128)S(1)}, u32[]{:S(2)}, u32[]{:S(2)}) %collective-permute-start.16) | collective-permute-done | bytes 262176 | tf_op jit(solution)/shard_map/ppermute | solution.py:74
  133.7 3.3 %collective-permute-start.18 = (f32[16,16,128]{2,1,0:T(8,128)S(1)}, f32[16,16,128]{2,1,0:T(8,128)S(1)}, u32[]{:S(2)}, u32[]{:S(2)}) collective-permute-start(f32[16,16,128]{2,1,0:T(8,128)S(1)} %slice_select_fusion.1), channel_id=1, source_target_pairs={{0,256},{1,257},{2,258},{3,259},{4,260},{5,261},{6,262},{7,263},{8... | collective-permute-start | bytes 393224 | tf_op jit(solution)/shard_map/ppermute | solution.py:74
  137.0 9.0 %collective-permute-done.18 = f32[16,16,128]{2,1,0:T(8,128)S(1)} collective-permute-done((f32[16,16,128]{2,1,0:T(8,128)S(1)}, f32[16,16,128]{2,1,0:T(8,128)S(1)}, u32[]{:S(2)}, u32[]{:S(2)}) %collective-permute-start.18) | collective-permute-done | bytes 131104 | tf_op jit(solution)/shard_map/ppermute | solution.py:74
  146.1 2.6 %collective-permute-start.19 = (f32[16,8,128]{2,0,1:T(8,128)S(1)}, f32[16,8,128]{2,0,1:T(8,128)S(1)}, u32[]{:S(2)}, u32[]{:S(2)}) collective-permute-start(f32[16,8,128]{2,0,1:T(8,128)S(1)} %get-tuple-element.31), channel_id=1, source_target_pairs={{0,0},{128,1},{64,64},{192,65},{1,128},{129,129},{65,192},{193,193... | collective-permute-start | bytes 196616 | tf_op jit(solution)/shard_map/ppermute | solution.py:74
  148.7 4.1 %collective-permute-start.20 = (f32[16,8,128]{2,0,1:T(8,128)S(1)}, f32[16,8,128]{2,0,1:T(8,128)S(1)}, u32[]{:S(2)}, u32[]{:S(2)}) collective-permute-start(f32[16,8,128]{2,0,1:T(8,128)S(1)} %get-tuple-element.32), channel_id=1, source_target_pairs={{64,0},{192,1},{0,64},{128,65},{65,128},{193,129},{1,192},{129,193... | collective-permute-start | bytes 196616 | tf_op jit(solution)/shard_map/ppermute | solution.py:74
  152.8 0.4 collective-permute-done.19
  153.2 2.4 %collective-permute-done.20 = f32[16,8,128]{2,0,1:T(8,128)S(1)} collective-permute-done((f32[16,8,128]{2,0,1:T(8,128)S(1)}, f32[16,8,128]{2,0,1:T(8,128)S(1)}, u32[]{:S(2)}, u32[]{:S(2)}) %collective-permute-start.20) | collective-permute-done | bytes 65568 | tf_op jit(solution)/shard_map/ppermute | solution.py:74
  155.5 0.7 copy.13
  (57 shorter events, 2.2 us)
Async XLA Ops:
  0.9 13.7 %collective-permute-start.1 = (f32[8,16,128]{2,1,0:T(8,128)S(1)}, f32[8,16,128]{2,1,0:T(8,128)S(1)}, u32[]{:S(2)}, u32[]{:S(2)}) collective-permute-start(f32[8,16,128]{2,1,0:T(8,128)S(1)} %bitcast.140), channel_id=1, source_target_pairs={{0,64},{1,192},{64,0},{65,128},{128,65},{129,193},{192,1},{193,129... | collective-permute-start | bytes 196616 | tf_op jit(solution)/shard_map/ppermute | solution.py:74
  5.9 8.8 %collective-permute-start = (f32[8,16,128]{2,1,0:T(8,128)S(1)}, f32[8,16,128]{2,1,0:T(8,128)S(1)}, u32[]{:S(2)}, u32[]{:S(2)}) collective-permute-start(f32[8,16,128]{2,1,0:T(8,128)S(1)} %bitcast.141), channel_id=1, source_target_pairs={{0,0},{1,128},{64,64},{65,192},{128,1},{129,129},{192,65},{193,193... | collective-permute-start | bytes 196616 | tf_op jit(solution)/shard_map/ppermute | solution.py:74
  9.4 30.5 %copy-start.3 = (f32[8,3,31]{2,0,1:T(8,128)S(1)}, f32[8,3,31]{2,0,1:T(8,128)}, u32[]{:S(2)}) copy-start(f32[8,3,31]{2,0,1:T(8,128)} %param.6) | copy-start | bytes 8932
  9.4 38.1 %collective-permute-start.5 = (f32[16,64,128]{2,1,0:T(8,128)S(1)}, f32[16,64,128]{2,1,0:T(8,128)S(1)}, u32[]{:S(2)}, u32[]{:S(2)}) collective-permute-start(f32[16,64,128]{2,1,0:T(8,128)S(1)} %get-tuple-element.36), channel_id=1, source_target_pairs={{0,0},{1,128},{64,64},{65,192},{128,1},{129,129},{192,65},{193,193... | collective-permute-start | bytes 1572872 | tf_op jit(solution)/shard_map/ppermute | solution.py:74
  14.7 27.9 %copy-start.6 = (s32[8,16]{1,0:T(8,128)S(1)}, s32[8,16]{1,0:T(8,128)}, u32[]{:S(2)}) copy-start(s32[8,16]{1,0:T(8,128)} %param.7) | copy-start | bytes 1540
  14.7 13.1 %collective-permute-start.2 = (f32[16,16,128]{2,1,0:T(8,128)S(1)}, f32[16,16,128]{2,1,0:T(8,128)S(1)}, u32[]{:S(2)}, u32[]{:S(2)}) collective-permute-start(f32[16,16,128]{2,1,0:T(8,128)S(1)} %pad_maximum_fusion.2), channel_id=1, source_target_pairs={{0,256},{1,257},{2,258},{3,259},{4,260},{5,261},{6,262},{7,263},{8... | collective-permute-start | bytes 393224 | tf_op jit(solution)/shard_map/ppermute | solution.py:74
  25.5 22.1 %collective-permute-start.6 = (f32[16,64,128]{2,1,0:T(8,128)S(1)}, f32[16,64,128]{2,1,0:T(8,128)}, u32[]{:S(2)}, u32[]{:S(2)}) collective-permute-start(f32[16,64,128]{2,1,0:T(8,128)S(1)} %get-tuple-element.22), channel_id=1, source_target_pairs={{0,64},{1,192},{64,0},{65,128},{128,65},{129,193},{192,1},{193,129... | collective-permute-start | bytes 1572872 | tf_op jit(solution)/shard_map/ppermute | solution.py:74
  27.8 16.3 %collective-permute-start.4 = (f32[32,16,128]{2,1,0:T(8,128)S(1)}, f32[32,16,128]{2,1,0:T(8,128)S(1)}, u32[]{:S(2)}, u32[]{:S(2)}) collective-permute-start(f32[32,16,128]{2,1,0:T(8,128)S(1)} %maximum_select_fusion.1), channel_id=1, source_target_pairs={{0,64},{64,0},{1,65},{65,1},{128,192},{192,128},{129,193},{193,129... | collective-permute-start | bytes 786440 | tf_op jit(solution)/shard_map/ppermute | solution.py:74
  29.8 16.7 %collective-permute-start.3 = (f32[32,16,128]{2,1,0:T(8,128)S(1)}, f32[32,16,128]{2,1,0:T(8,128)}, u32[]{:S(2)}, u32[]{:S(2)}) collective-permute-start(f32[32,16,128]{2,1,0:T(8,128)S(1)} %maximum_select_fusion.1), channel_id=1, source_target_pairs={{64,128},{128,64},{65,129},{129,65},{192,194},{194,192},{193,195},... | collective-permute-start | bytes 786440 | tf_op jit(solution)/shard_map/ppermute | solution.py:74
  42.6 11.8 %copy-start.1 = (f32[2,128,128]{2,0,1:T(2,128)}, f32[2,128,128]{2,0,1:T(2,128)S(1)}, u32[]{:S(2)}) copy-start(f32[2,128,128]{2,0,1:T(2,128)S(1)} %fusion) | copy-start | bytes 393220
  43.4 10.4 %copy-start.4 = (pred[2,16,1,1]{1,0,3,2:T(4,128)(4,1)}, pred[2,16,1,1]{1,0,3,2:T(4,128)(4,1)S(1)}, u32[]{:S(2)}) copy-start(pred[2,16,1,1]{1,0,3,2:T(4,128)(4,1)S(1)} %fusion.14) | copy-start | bytes 100
  47.5 2.7 %copy-start = (f32[16,64,128]{2,1,0:T(8,128)}, f32[16,64,128]{2,1,0:T(8,128)S(1)}, u32[]{:S(2)}) copy-start(f32[16,64,128]{2,1,0:T(8,128)S(1)} %collective-permute-done.5) | copy-start | bytes 1572868
  47.5 4.8 %collective-permute-start.7 = (f32[32,48,128]{2,1,0:T(8,128)S(1)}, f32[32,48,128]{2,1,0:T(8,128)S(1)}, u32[]{:S(2)}, u32[]{:S(2)}) collective-permute-start(f32[32,48,128]{2,1,0:T(8,128)S(1)} %pad_maximum_fusion), channel_id=1, source_target_pairs={{0,1},{1,0},{2,3},{3,2},{4,5},{5,4},{6,7},{7,6},{8,9},{9,8},{10,11... | collective-permute-start | bytes 2359304 | tf_op jit(solution)/shard_map/ppermute | solution.py:74
  56.1 4.3 %collective-permute-start.8 = (f32[32,48,128]{2,1,0:T(8,128)S(1)}, f32[32,48,128]{2,1,0:T(8,128)}, u32[]{:S(2)}, u32[]{:S(2)}) collective-permute-start(f32[32,48,128]{2,1,0:T(8,128)S(1)} %convolution_bitcast_fusion.4), channel_id=1, source_target_pairs={{0,1},{1,0},{2,3},{3,2},{4,5},{5,4},{6,7},{7,6},{8,9},{9,8},{10,11... | collective-permute-start | bytes 2359304 | tf_op jit(solution)/shard_map/ppermute | solution.py:74
  61.7 11.7 %collective-permute-start.9 = (f32[32,16,128]{2,1,0:T(8,128)S(1)}, f32[32,16,128]{2,1,0:T(8,128)S(1)}, u32[]{:S(2)}, u32[]{:S(2)}) collective-permute-start(f32[32,16,128]{2,1,0:T(8,128)S(1)} %get-tuple-element.39), channel_id=1, source_target_pairs={{64,128},{128,64},{65,129},{129,65},{192,194},{194,192},{193,195},... | collective-permute-start | bytes 786440 | tf_op jit(solution)/shard_map/ppermute | solution.py:74
  67.2 9.3 %collective-permute-start.10 = (f32[32,16,128]{2,1,0:T(8,128)S(1)}, f32[32,16,128]{2,1,0:T(8,128)S(1)}, u32[]{:S(2)}, u32[]{:S(2)}) collective-permute-start(f32[32,16,128]{2,1,0:T(8,128)S(1)} %get-tuple-element.40), channel_id=1, source_target_pairs={{0,64},{64,0},{1,65},{65,1},{128,192},{192,128},{129,193},{193,129... | collective-permute-start | bytes 786440 | tf_op jit(solution)/shard_map/ppermute | solution.py:74
  76.5 18.5 %collective-permute-start.11 = (f32[32,16,128]{2,1,0:T(8,128)S(1)}, f32[32,16,128]{2,1,0:T(8,128)S(1)}, u32[]{:S(2)}, u32[]{:S(2)}) collective-permute-start(f32[32,16,128]{2,1,0:T(8,128)S(1)} %fusion.30), channel_id=1, source_target_pairs={{0,256},{1,257},{2,258},{3,259},{4,260},{5,261},{6,262},{7,263},{8... | collective-permute-start | bytes 786440 | tf_op jit(solution)/shard_map/ppermute | solution.py:74
  95.1 9.3 %collective-permute-start.13 = (f32[32,16,128]{2,1,0:T(8,128)S(1)}, f32[32,16,128]{2,1,0:T(8,128)S(1)}, u32[]{:S(2)}, u32[]{:S(2)}) collective-permute-start(f32[32,16,128]{2,1,0:T(8,128)S(1)} %multiply_multiply_fusion), channel_id=1, source_target_pairs={{0,64},{64,0},{1,65},{65,1},{128,192},{192,128},{129,193},{193,129... | collective-permute-start | bytes 786440 | tf_op jit(solution)/shard_map/ppermute | solution.py:74
  97.3 11.1 %collective-permute-start.12 = (f32[32,16,128]{2,1,0:T(8,128)S(1)}, f32[32,16,128]{2,1,0:T(8,128)S(1)}, u32[]{:S(2)}, u32[]{:S(2)}) collective-permute-start(f32[32,16,128]{2,1,0:T(8,128)S(1)} %multiply_multiply_fusion), channel_id=1, source_target_pairs={{64,128},{128,64},{65,129},{129,65},{192,194},{194,192},{193,195},... | collective-permute-start | bytes 786440 | tf_op jit(solution)/shard_map/ppermute | solution.py:74
  108.4 5.5 %collective-permute-start.14 = (f32[32,48,128]{2,1,0:T(8,128)S(1)}, f32[32,48,128]{2,1,0:T(8,128)S(1)}, u32[]{:S(2)}, u32[]{:S(2)}) collective-permute-start(f32[32,48,128]{2,1,0:T(8,128)S(1)} %pad_maximum_fusion.1), channel_id=1, source_target_pairs={{0,1},{1,0},{2,3},{3,2},{4,5},{5,4},{6,7},{7,6},{8,9},{9,8},{10,11... | collective-permute-start | bytes 2359304 | tf_op jit(solution)/shard_map/ppermute | solution.py:74
  114.5 0.9 copy-start.2
  114.5 0.9 copy-start.5
  117.8 4.2 %collective-permute-start.15 = (f32[32,48,128]{2,1,0:T(8,128)S(1)}, f32[32,48,128]{2,1,0:T(8,128)S(1)}, u32[]{:S(2)}, u32[]{:S(2)}) collective-permute-start(f32[32,48,128]{2,1,0:T(8,128)S(1)} %convolution_bitcast_fusion.2), channel_id=1, source_target_pairs={{0,1},{1,0},{2,3},{3,2},{4,5},{5,4},{6,7},{7,6},{8,9},{9,8},{10,11... | collective-permute-start | bytes 2359304 | tf_op jit(solution)/shard_map/ppermute | solution.py:74
  122.1 11.5 %collective-permute-start.16 = (f32[32,16,128]{2,1,0:T(8,128)S(1)}, f32[32,16,128]{2,1,0:T(8,128)S(1)}, u32[]{:S(2)}, u32[]{:S(2)}) collective-permute-start(f32[32,16,128]{2,1,0:T(8,128)S(1)} %get-tuple-element.37), channel_id=1, source_target_pairs={{64,128},{128,64},{65,129},{129,65},{192,194},{194,192},{193,195},... | collective-permute-start | bytes 786440 | tf_op jit(solution)/shard_map/ppermute | solution.py:74
  124.0 9.6 %collective-permute-start.17 = (f32[32,16,128]{2,1,0:T(8,128)S(1)}, f32[32,16,128]{2,1,0:T(8,128)S(1)}, u32[]{:S(2)}, u32[]{:S(2)}) collective-permute-start(f32[32,16,128]{2,1,0:T(8,128)S(1)} %get-tuple-element.38), channel_id=1, source_target_pairs={{0,64},{64,0},{1,65},{65,1},{128,192},{192,128},{129,193},{193,129... | collective-permute-start | bytes 786440 | tf_op jit(solution)/shard_map/ppermute | solution.py:74
  133.7 12.3 %collective-permute-start.18 = (f32[16,16,128]{2,1,0:T(8,128)S(1)}, f32[16,16,128]{2,1,0:T(8,128)S(1)}, u32[]{:S(2)}, u32[]{:S(2)}) collective-permute-start(f32[16,16,128]{2,1,0:T(8,128)S(1)} %slice_select_fusion.1), channel_id=1, source_target_pairs={{0,256},{1,257},{2,258},{3,259},{4,260},{5,261},{6,262},{7,263},{8... | collective-permute-start | bytes 393224 | tf_op jit(solution)/shard_map/ppermute | solution.py:74
  146.1 7.1 %collective-permute-start.19 = (f32[16,8,128]{2,0,1:T(8,128)S(1)}, f32[16,8,128]{2,0,1:T(8,128)S(1)}, u32[]{:S(2)}, u32[]{:S(2)}) collective-permute-start(f32[16,8,128]{2,0,1:T(8,128)S(1)} %get-tuple-element.31), channel_id=1, source_target_pairs={{0,0},{128,1},{64,64},{192,65},{1,128},{129,129},{65,192},{193,193... | collective-permute-start | bytes 196616 | tf_op jit(solution)/shard_map/ppermute | solution.py:74
  148.7 6.8 %collective-permute-start.20 = (f32[16,8,128]{2,0,1:T(8,128)S(1)}, f32[16,8,128]{2,0,1:T(8,128)S(1)}, u32[]{:S(2)}, u32[]{:S(2)}) collective-permute-start(f32[16,8,128]{2,0,1:T(8,128)S(1)} %get-tuple-element.32), channel_id=1, source_target_pairs={{64,0},{192,1},{0,64},{128,65},{65,128},{193,129},{1,192},{129,193... | collective-permute-start | bytes 196616 | tf_op jit(solution)/shard_map/ppermute | solution.py:74

commit v9 on v8

--- a/solution.py
+++ b/solution.py
@@ -20,7 +20,7 @@
     return (p - column % 4) % 4
 
 
-def spread_pairs(turn):
+def spread_pairs(turn, cross=0):
     pairs = []
     for h in range(2):
         for column in range(COLS // 2):
@@ -30,7 +30,7 @@
                     pairs.append(
                         (
                             device(h, x, 2 * column + k),
-                            device(h, chip_x(column, p), 2 * column + x // 2),
+                            device(h ^ cross, chip_x(column, p), 2 * column + x // 2),
                         )
                     )
     return pairs
@@ -64,6 +64,7 @@
 
 
 SPREAD = [spread_pairs(0), spread_pairs(1)]
+CROSS = [spread_pairs(0, 1), spread_pairs(1, 1)]
 ODD = chip_pairs(1)
 EVEN = chip_pairs(0)
 SWAP_H = swap_pairs("h")
@@ -107,12 +108,14 @@
 
     even = p % 2 == 0
     flipped = jnp.swapaxes(estimate, 0, 1)
-    quarter = jnp.concatenate(
-        ordered([send(piece(flipped, turn, 1), SPREAD[turn]) for turn in (0, 1)], even), 0
-    )
-    current = by_h(quarter, send(quarter, SWAP_H), h)
+    sent = [piece(flipped, turn, 1) for turn in (0, 1)]
+    other, quarter = (
+        jnp.concatenate(ordered([send(value, route) for value, route in zip(sent, routes)], even), 0)
+        for routes in (CROSS, SPREAD)
+    )
+    current = by_h(quarter, other, h)
     images = [piece(observed[0], turn, 0) for turn in (0, 1)]
-    images[1], _ = lax.optimization_barrier((images[1], quarter))
+    *images, _ = lax.optimization_barrier((*images, quarter))
     images = [send(image, SPREAD[turn]) for turn, image in enumerate(images)]
     psf_taps, intersection, current = lax.optimization_barrier((psf_taps, intersection, current))
 
@@ -183,17 +186,21 @@
         if iteration < ITERS - 1:
             current = current * (part + send(part, SWAP_H) + 1.0) * scale
 
-    def own_half(value, mine):
-        return jnp.where((h == 0) == mine, value[: 2 * block], value[2 * block :])
-
-    total = own_half(part, True) + send(own_half(part, False), SWAP_H)
-    quarter = own_half(current, True) * (total + 1.0) * own_half(scale, True)
-
-    quarter = jnp.swapaxes(quarter, 0, 1)
-    result = ordered([quarter[:, :block], quarter[:, block:]], even)
-    result = lax.optimization_barrier(tuple(result))
-    result = [send(value, reverse(route)) for value, route in zip(result, SPREAD)]
-    return jnp.concatenate(ordered(result, x % 2 == 0), 0)
+    own_h = (place // width == h)[:, None, None]
+    terms = current * scale * jnp.where(own_h, part + 1.0, part)
+    low, high = terms[: 2 * block], terms[2 * block :]
+    near = jnp.where(h == 0, low, high)
+    far = jnp.where(h == 0, high, low)
+    far, near = (jnp.swapaxes(value, 0, 1) for value in (far, near))
+    far, near = (
+        [
+            send(value, reverse(route))
+            for value, route in zip(ordered([half_h[:, :block], half_h[:, block:]], even), routes)
+        ]
+        for half_h, routes in ((far, CROSS), (near, SPREAD))
+    )
+    far, near = (jnp.concatenate(ordered(value, x % 2 == 0), 0) for value in (far, near))
+    return near + far
 
 
 def solution(mesh):

time: 157 us -> 161 us (1.025); the launches traced: 156 us -> 158 us
  starting transfers between devices: 74.9 us -> 89.2 us
  waiting for transfers between devices: 57.5 us -> 44.6 us
    ppermute x21 -> x23, starting transfers between devices: 74.9 us -> 89.2 us  [send(): return lax.ppermute(value, AXES, pairs)]
    ppermute x21 -> x23, waiting for transfers between devices: 57.5 us -> 44.6 us  [send(): return lax.ppermute(value, AXES, pairs)]
  transfers between devices with their start and end apart: 21 -> 23, of which waited for: 14 -> 12; matrix products, arithmetic and copies ran while one was open for 8% -> 8% of each run, Pallas kernels for 0% -> 0%
where the time goes in v9:
time: 161 us; the launch traced here: 158 us
  starting transfers between devices  89.2 us (55%)
  waiting for transfers between devices  44.6 us (28%)
  matrix products  13.9 us (9%)
  local copies, waits for them, and re-layouts  4.74 us (3%)
  other arithmetic  4.52 us (3%)
    ppermute x23, starting transfers between devices, send(): return lax.ppermute(value, AXES, pairs)  89.2 us
    ppermute x23, waiting for transfers between devices, send(): return lax.ppermute(value, AXES, pairs)  44.6 us
  transfers between devices with their start and end apart: 23, of which 12 were waited for; matrix products, arithmetic and copies ran while one was open for 8% of the time, Pallas kernels for 0%

profile of v9, /device:TPU:57, one launch (start us, length us, event | category | flops | bytes accessed | tf_op | source)
XLA Modules:
  0.0 157.8 jit_solution(2629298283679073842)
XLA Ops:
  0.0 0.9 constant_dynamic-slice_fusion.1
  0.9 13.4 %collective-permute-start.3 = (f32[8,16,128]{2,1,0:T(8,128)S(1)}, f32[8,16,128]{2,1,0:T(8,128)S(1)}, u32[]{:S(2)}, u32[]{:S(2)}) collective-permute-start(f32[8,16,128]{2,1,0:T(8,128)S(1)} %bitcast.142), channel_id=1, source_target_pairs={{0,320},{1,448},{64,256},{65,384},{128,321},{129,449},{192,257},{1... | collective-permute-start | bytes 196616 | tf_op jit(solution)/shard_map/ppermute | solution.py:75
  14.3 1.9 %collective-permute-start.1 = (f32[8,16,128]{2,1,0:T(8,128)S(1)}, f32[8,16,128]{2,1,0:T(8,128)S(1)}, u32[]{:S(2)}, u32[]{:S(2)}) collective-permute-start(f32[8,16,128]{2,1,0:T(8,128)S(1)} %bitcast.143), channel_id=1, source_target_pairs={{0,64},{1,192},{64,0},{65,128},{128,65},{129,193},{192,1},{193,129... | collective-permute-start | bytes 196616 | tf_op jit(solution)/shard_map/ppermute | solution.py:75
  16.3 2.2 %collective-permute-start.2 = (f32[8,16,128]{2,1,0:T(8,128)S(1)}, f32[8,16,128]{2,1,0:T(8,128)S(1)}, u32[]{:S(2)}, u32[]{:S(2)}) collective-permute-start(f32[8,16,128]{2,1,0:T(8,128)S(1)} %bitcast.144), channel_id=1, source_target_pairs={{0,256},{1,384},{64,320},{65,448},{128,257},{129,385},{192,321},{1... | collective-permute-start | bytes 196616 | tf_op jit(solution)/shard_map/ppermute | solution.py:75
  18.5 4.9 %collective-permute-start = (f32[8,16,128]{2,1,0:T(8,128)S(1)}, f32[8,16,128]{2,1,0:T(8,128)S(1)}, u32[]{:S(2)}, u32[]{:S(2)}) collective-permute-start(f32[8,16,128]{2,1,0:T(8,128)S(1)} %bitcast.145), channel_id=1, source_target_pairs={{0,0},{1,128},{64,64},{65,192},{128,1},{129,129},{192,65},{193,193... | collective-permute-start | bytes 196616 | tf_op jit(solution)/shard_map/ppermute | solution.py:75
  23.3 1.3 dynamic-slice_bitcast_fusion
  24.7 2.2 %collective-permute-start.6 = (f32[16,64,128]{2,1,0:T(8,128)S(1)}, f32[16,64,128]{2,1,0:T(8,128)S(1)}, u32[]{:S(2)}, u32[]{:S(2)}) collective-permute-start(f32[16,64,128]{2,1,0:T(8,128)S(1)} %get-tuple-element.21), channel_id=1, source_target_pairs={{0,0},{1,128},{64,64},{65,192},{128,1},{129,129},{192,65},{193,193... | collective-permute-start | bytes 1572872 | tf_op jit(solution)/shard_map/ppermute | solution.py:75
  27.3 4.7 %collective-permute-start.7 = (f32[16,64,128]{2,1,0:T(8,128)S(1)}, f32[16,64,128]{2,1,0:T(8,128)}, u32[]{:S(2)}, u32[]{:S(2)}) collective-permute-start(f32[16,64,128]{2,1,0:T(8,128)S(1)} %get-tuple-element.22), channel_id=1, source_target_pairs={{0,64},{1,192},{64,0},{65,128},{128,65},{129,193},{192,1},{193,129... | collective-permute-start | bytes 1572872 | tf_op jit(solution)/shard_map/ppermute | solution.py:75
  32.1 1.9 %collective-permute-start.5 = (f32[32,16,128]{2,1,0:T(8,128)S(1)}, f32[32,16,128]{2,1,0:T(8,128)S(1)}, u32[]{:S(2)}, u32[]{:S(2)}) collective-permute-start(f32[32,16,128]{2,1,0:T(8,128)S(1)} %maximum_select_fusion.1), channel_id=1, source_target_pairs={{0,64},{64,0},{1,65},{65,1},{128,192},{192,128},{129,193},{193,129... | collective-permute-start | bytes 786440 | tf_op jit(solution)/shard_map/ppermute | solution.py:75
  34.1 7.0 %collective-permute-start.4 = (f32[32,16,128]{2,1,0:T(8,128)S(1)}, f32[32,16,128]{2,1,0:T(8,128)}, u32[]{:S(2)}, u32[]{:S(2)}) collective-permute-start(f32[32,16,128]{2,1,0:T(8,128)S(1)} %maximum_select_fusion.1), channel_id=1, source_target_pairs={{64,128},{128,64},{65,129},{129,65},{192,194},{194,192},{193,195},... | collective-permute-start | bytes 786440 | tf_op jit(solution)/shard_map/ppermute | solution.py:75
  41.5 0.2 fusion.81
  41.9 0.4 fusion.18
  42.3 0.7 fusion.28
  43.0 0.8 fusion
  44.0 0.3 fusion.42
  44.6 0.8 fusion.13
  45.4 2.4 %collective-permute-done.4 = f32[32,16,128]{2,1,0:T(8,128)} collective-permute-done((f32[32,16,128]{2,1,0:T(8,128)S(1)}, f32[32,16,128]{2,1,0:T(8,128)}, u32[]{:S(2)}, u32[]{:S(2)}) %collective-permute-start.4) | collective-permute-done | bytes 262176 | tf_op jit(solution)/shard_map/ppermute | solution.py:75
  47.8 1.0 pad_maximum_fusion
  48.9 2.5 %collective-permute-start.8 = (f32[32,48,128]{2,1,0:T(8,128)S(1)}, f32[32,48,128]{2,1,0:T(8,128)S(1)}, u32[]{:S(2)}, u32[]{:S(2)}) collective-permute-start(f32[32,48,128]{2,1,0:T(8,128)S(1)} %pad_maximum_fusion), channel_id=1, source_target_pairs={{0,1},{1,0},{2,3},{3,2},{4,5},{5,4},{6,7},{7,6},{8,9},{9,8},{10,11... | collective-permute-start | bytes 2359304 | tf_op jit(solution)/shard_map/ppermute | solution.py:75
  51.4 1.3 maximum_select_fusion
  52.8 0.7 slice_bitcast_fusion
  53.5 0.6 fusion.1
  54.1 0.9 convolution_bitcast_fusion.1
  55.0 0.6 fusion.11
  55.6 0.6 fusion.38
  56.2 0.4 fusion.99
  56.6 0.8 convolution_bitcast_fusion.4
  57.4 2.0 %collective-permute-start.9 = (f32[32,48,128]{2,1,0:T(8,128)S(1)}, f32[32,48,128]{2,1,0:T(8,128)}, u32[]{:S(2)}, u32[]{:S(2)}) collective-permute-start(f32[32,48,128]{2,1,0:T(8,128)S(1)} %convolution_bitcast_fusion.4), channel_id=1, source_target_pairs={{0,1},{1,0},{2,3},{3,2},{4,5},{5,4},{6,7},{7,6},{8,9},{9,8},{10,11... | collective-permute-start | bytes 2359304 | tf_op jit(solution)/shard_map/ppermute | solution.py:75
  59.4 0.9 copy.24
  60.3 0.4 fusion.98
  60.7 0.8 convolution_bitcast_fusion.5
  61.7 1.2 add.269
  62.9 7.1 %collective-permute-start.10 = (f32[32,16,128]{2,1,0:T(8,128)S(1)}, f32[32,16,128]{2,1,0:T(8,128)S(1)}, u32[]{:S(2)}, u32[]{:S(2)}) collective-permute-start(f32[32,16,128]{2,1,0:T(8,128)S(1)} %get-tuple-element.37), channel_id=1, source_target_pairs={{64,128},{128,64},{65,129},{129,65},{192,194},{194,192},{193,195},... | collective-permute-start | bytes 786440 | tf_op jit(solution)/shard_map/ppermute | solution.py:75
  70.0 1.9 %collective-permute-start.11 = (f32[32,16,128]{2,1,0:T(8,128)S(1)}, f32[32,16,128]{2,1,0:T(8,128)S(1)}, u32[]{:S(2)}, u32[]{:S(2)}) collective-permute-start(f32[32,16,128]{2,1,0:T(8,128)S(1)} %get-tuple-element.38), channel_id=1, source_target_pairs={{0,64},{64,0},{1,65},{65,1},{128,192},{192,128},{129,193},{193,129... | collective-permute-start | bytes 786440 | tf_op jit(solution)/shard_map/ppermute | solution.py:75
  72.0 4.6 %collective-permute-done.10 = f32[32,16,128]{2,1,0:T(8,128)S(1)} collective-permute-done((f32[32,16,128]{2,1,0:T(8,128)S(1)}, f32[32,16,128]{2,1,0:T(8,128)S(1)}, u32[]{:S(2)}, u32[]{:S(2)}) %collective-permute-start.10) | collective-permute-done | bytes 262176 | tf_op jit(solution)/shard_map/ppermute | solution.py:75
  76.6 2.7 %collective-permute-done.11 = f32[32,16,128]{2,1,0:T(8,128)S(1)} collective-permute-done((f32[32,16,128]{2,1,0:T(8,128)S(1)}, f32[32,16,128]{2,1,0:T(8,128)S(1)}, u32[]{:S(2)}, u32[]{:S(2)}) %collective-permute-start.11) | collective-permute-done | bytes 262176 | tf_op jit(solution)/shard_map/ppermute | solution.py:75
  79.4 3.6 %collective-permute-start.12 = (f32[32,16,128]{2,1,0:T(8,128)S(1)}, f32[32,16,128]{2,1,0:T(8,128)S(1)}, u32[]{:S(2)}, u32[]{:S(2)}) collective-permute-start(f32[32,16,128]{2,1,0:T(8,128)S(1)} %fusion.31), channel_id=1, source_target_pairs={{0,256},{1,257},{2,258},{3,259},{4,260},{5,261},{6,262},{7,263},{8... | collective-permute-start | bytes 786440 | tf_op jit(solution)/shard_map/ppermute | solution.py:75
  83.1 14.6 %collective-permute-done.12 = f32[32,16,128]{2,1,0:T(8,128)S(1)} collective-permute-done((f32[32,16,128]{2,1,0:T(8,128)S(1)}, f32[32,16,128]{2,1,0:T(8,128)S(1)}, u32[]{:S(2)}, u32[]{:S(2)}) %collective-permute-start.12) | collective-permute-done | bytes 262176 | tf_op jit(solution)/shard_map/ppermute | solution.py:75
  97.8 2.2 %collective-permute-start.14 = (f32[32,16,128]{2,1,0:T(8,128)S(1)}, f32[32,16,128]{2,1,0:T(8,128)S(1)}, u32[]{:S(2)}, u32[]{:S(2)}) collective-permute-start(f32[32,16,128]{2,1,0:T(8,128)S(1)} %multiply_multiply_fusion), channel_id=1, source_target_pairs={{0,64},{64,0},{1,65},{65,1},{128,192},{192,128},{129,193},{193,129... | collective-permute-start | bytes 786440 | tf_op jit(solution)/shard_map/ppermute | solution.py:75
  100.0 1.9 %collective-permute-start.13 = (f32[32,16,128]{2,1,0:T(8,128)S(1)}, f32[32,16,128]{2,1,0:T(8,128)S(1)}, u32[]{:S(2)}, u32[]{:S(2)}) collective-permute-start(f32[32,16,128]{2,1,0:T(8,128)S(1)} %multiply_multiply_fusion), channel_id=1, source_target_pairs={{64,128},{128,64},{65,129},{129,65},{192,194},{194,192},{193,195},... | collective-permute-start | bytes 786440 | tf_op jit(solution)/shard_map/ppermute | solution.py:75
  101.9 3.7 %collective-permute-done.14 = f32[32,16,128]{2,1,0:T(8,128)S(1)} collective-permute-done((f32[32,16,128]{2,1,0:T(8,128)S(1)}, f32[32,16,128]{2,1,0:T(8,128)S(1)}, u32[]{:S(2)}, u32[]{:S(2)}) %collective-permute-start.14) | collective-permute-done | bytes 262176 | tf_op jit(solution)/shard_map/ppermute | solution.py:75
  105.7 4.1 %collective-permute-done.13 = f32[32,16,128]{2,1,0:T(8,128)S(1)} collective-permute-done((f32[32,16,128]{2,1,0:T(8,128)S(1)}, f32[32,16,128]{2,1,0:T(8,128)S(1)}, u32[]{:S(2)}, u32[]{:S(2)}) %collective-permute-start.13) | collective-permute-done | bytes 262176 | tf_op jit(solution)/shard_map/ppermute | solution.py:75
  109.8 5.1 %collective-permute-start.15 = (f32[32,48,128]{2,1,0:T(8,128)S(1)}, f32[32,48,128]{2,1,0:T(8,128)S(1)}, u32[]{:S(2)}, u32[]{:S(2)}) collective-permute-start(f32[32,48,128]{2,1,0:T(8,128)S(1)} %pad_maximum_fusion.1), channel_id=1, source_target_pairs={{0,1},{1,0},{2,3},{3,2},{4,5},{5,4},{6,7},{7,6},{8,9},{9,8},{10,11... | collective-permute-start | bytes 2359304 | tf_op jit(solution)/shard_map/ppermute | solution.py:75
  114.9 1.7 %collective-permute-done.15 = f32[32,48,128]{2,1,0:T(8,128)S(1)} collective-permute-done((f32[32,48,128]{2,1,0:T(8,128)S(1)}, f32[32,48,128]{2,1,0:T(8,128)S(1)}, u32[]{:S(2)}, u32[]{:S(2)}) %collective-permute-start.15) | collective-permute-done | bytes 786464 | tf_op jit(solution)/shard_map/ppermute | solution.py:75
  116.6 0.6 fusion.4
  117.2 0.9 convolution_bitcast_fusion
  118.1 0.6 fusion.12
  118.7 0.6 fusion.36
  119.3 0.4 fusion.101
  119.7 0.8 convolution_bitcast_fusion.2
  120.4 2.3 %collective-permute-start.16 = (f32[32,48,128]{2,1,0:T(8,128)S(1)}, f32[32,48,128]{2,1,0:T(8,128)S(1)}, u32[]{:S(2)}, u32[]{:S(2)}) collective-permute-start(f32[32,48,128]{2,1,0:T(8,128)S(1)} %convolution_bitcast_fusion.2), channel_id=1, source_target_pairs={{0,1},{1,0},{2,3},{3,2},{4,5},{5,4},{6,7},{7,6},{8,9},{9,8},{10,11... | collective-permute-start | bytes 2359304 | tf_op jit(solution)/shard_map/ppermute | solution.py:75
  122.7 0.4 fusion.100
  123.1 0.8 convolution_bitcast_fusion.3
  123.9 0.7 collective-permute-done.16
  124.8 2.3 %collective-permute-start.17 = (f32[32,16,128]{2,1,0:T(8,128)S(1)}, f32[32,16,128]{2,1,0:T(8,128)S(1)}, u32[]{:S(2)}, u32[]{:S(2)}) collective-permute-start(f32[32,16,128]{2,1,0:T(8,128)S(1)} %get-tuple-element.35), channel_id=1, source_target_pairs={{64,128},{128,64},{65,129},{129,65},{192,194},{194,192},{193,195},... | collective-permute-start | bytes 786440 | tf_op jit(solution)/shard_map/ppermute | solution.py:75
  127.0 1.9 %collective-permute-start.18 = (f32[32,16,128]{2,1,0:T(8,128)S(1)}, f32[32,16,128]{2,1,0:T(8,128)S(1)}, u32[]{:S(2)}, u32[]{:S(2)}) collective-permute-start(f32[32,16,128]{2,1,0:T(8,128)S(1)} %get-tuple-element.36), channel_id=1, source_target_pairs={{0,64},{64,0},{1,65},{65,1},{128,192},{192,128},{129,193},{193,129... | collective-permute-start | bytes 786440 | tf_op jit(solution)/shard_map/ppermute | solution.py:75
  129.0 7.3 %collective-permute-done.17 = f32[32,16,128]{2,1,0:T(8,128)S(1)} collective-permute-done((f32[32,16,128]{2,1,0:T(8,128)S(1)}, f32[32,16,128]{2,1,0:T(8,128)S(1)}, u32[]{:S(2)}, u32[]{:S(2)}) %collective-permute-start.17) | collective-permute-done | bytes 262176 | tf_op jit(solution)/shard_map/ppermute | solution.py:75
  136.4 5.9 %collective-permute-start.21 = (f32[16,8,128]{2,0,1:T(8,128)S(1)}, f32[16,8,128]{2,0,1:T(8,128)S(1)}, u32[]{:S(2)}, u32[]{:S(2)}) collective-permute-start(f32[16,8,128]{2,0,1:T(8,128)S(1)} %get-tuple-element.43), channel_id=1, source_target_pairs={{256,0},{384,1},{320,64},{448,65},{257,128},{385,129},{321,192},{4... | collective-permute-start | bytes 196616 | tf_op jit(solution)/shard_map/ppermute | solution.py:75
  142.4 5.6 %collective-permute-start.22 = (f32[16,8,128]{2,0,1:T(8,128)S(1)}, f32[16,8,128]{2,0,1:T(8,128)S(1)}, u32[]{:S(2)}, u32[]{:S(2)}) collective-permute-start(f32[16,8,128]{2,0,1:T(8,128)S(1)} %get-tuple-element.44), channel_id=1, source_target_pairs={{320,0},{448,1},{256,64},{384,65},{321,128},{449,129},{257,192},{3... | collective-permute-start | bytes 196616 | tf_op jit(solution)/shard_map/ppermute | solution.py:75
  147.9 2.2 %collective-permute-start.19 = (f32[16,8,128]{2,0,1:T(8,128)S(1)}, f32[16,8,128]{2,0,1:T(8,128)S(1)}, u32[]{:S(2)}, u32[]{:S(2)}) collective-permute-start(f32[16,8,128]{2,0,1:T(8,128)S(1)} %get-tuple-element.47), channel_id=1, source_target_pairs={{0,0},{128,1},{64,64},{192,65},{1,128},{129,129},{65,192},{193,193... | collective-permute-start | bytes 196616 | tf_op jit(solution)/shard_map/ppermute | solution.py:75
  150.2 4.3 %collective-permute-start.20 = (f32[16,8,128]{2,0,1:T(8,128)S(1)}, f32[16,8,128]{2,0,1:T(8,128)S(1)}, u32[]{:S(2)}, u32[]{:S(2)}) collective-permute-start(f32[16,8,128]{2,0,1:T(8,128)S(1)} %get-tuple-element.48), channel_id=1, source_target_pairs={{64,0},{192,1},{0,64},{128,65},{65,128},{193,129},{1,192},{129,193... | collective-permute-start | bytes 196616 | tf_op jit(solution)/shard_map/ppermute | solution.py:75
  154.6 0.5 collective-permute-done.19
  155.0 1.9 %collective-permute-done.20 = f32[16,8,128]{2,0,1:T(8,128)S(1)} collective-permute-done((f32[16,8,128]{2,0,1:T(8,128)S(1)}, f32[16,8,128]{2,0,1:T(8,128)S(1)}, u32[]{:S(2)}, u32[]{:S(2)}) %collective-permute-start.20) | collective-permute-done | bytes 65568 | tf_op jit(solution)/shard_map/ppermute | solution.py:75
  157.0 0.7 copy.13
  (63 shorter events, 2.3 us)
Async XLA Ops:
  0.9 26.4 %collective-permute-start.3 = (f32[8,16,128]{2,1,0:T(8,128)S(1)}, f32[8,16,128]{2,1,0:T(8,128)S(1)}, u32[]{:S(2)}, u32[]{:S(2)}) collective-permute-start(f32[8,16,128]{2,1,0:T(8,128)S(1)} %bitcast.142), channel_id=1, source_target_pairs={{0,320},{1,448},{64,256},{65,384},{128,321},{129,449},{192,257},{1... | collective-permute-start | bytes 196616 | tf_op jit(solution)/shard_map/ppermute | solution.py:75
  14.3 17.8 %collective-permute-start.1 = (f32[8,16,128]{2,1,0:T(8,128)S(1)}, f32[8,16,128]{2,1,0:T(8,128)S(1)}, u32[]{:S(2)}, u32[]{:S(2)}) collective-permute-start(f32[8,16,128]{2,1,0:T(8,128)S(1)} %bitcast.143), channel_id=1, source_target_pairs={{0,64},{1,192},{64,0},{65,128},{128,65},{129,193},{192,1},{193,129... | collective-permute-start | bytes 196616 | tf_op jit(solution)/shard_map/ppermute | solution.py:75
  16.3 15.8 %collective-permute-start.2 = (f32[8,16,128]{2,1,0:T(8,128)S(1)}, f32[8,16,128]{2,1,0:T(8,128)S(1)}, u32[]{:S(2)}, u32[]{:S(2)}) collective-permute-start(f32[8,16,128]{2,1,0:T(8,128)S(1)} %bitcast.144), channel_id=1, source_target_pairs={{0,256},{1,384},{64,320},{65,448},{128,257},{129,385},{192,321},{1... | collective-permute-start | bytes 196616 | tf_op jit(solution)/shard_map/ppermute | solution.py:75
  18.5 13.6 %collective-permute-start = (f32[8,16,128]{2,1,0:T(8,128)S(1)}, f32[8,16,128]{2,1,0:T(8,128)S(1)}, u32[]{:S(2)}, u32[]{:S(2)}) collective-permute-start(f32[8,16,128]{2,1,0:T(8,128)S(1)} %bitcast.145), channel_id=1, source_target_pairs={{0,0},{1,128},{64,64},{65,192},{128,1},{129,129},{192,65},{193,193... | collective-permute-start | bytes 196616 | tf_op jit(solution)/shard_map/ppermute | solution.py:75
  24.7 16.4 %copy-start.3 = (f32[8,3,31]{2,0,1:T(8,128)S(1)}, f32[8,3,31]{2,0,1:T(8,128)}, u32[]{:S(2)}) copy-start(f32[8,3,31]{2,0,1:T(8,128)} %param.6) | copy-start | bytes 8932
  24.7 24.2 %collective-permute-start.6 = (f32[16,64,128]{2,1,0:T(8,128)S(1)}, f32[16,64,128]{2,1,0:T(8,128)S(1)}, u32[]{:S(2)}, u32[]{:S(2)}) collective-permute-start(f32[16,64,128]{2,1,0:T(8,128)S(1)} %get-tuple-element.21), channel_id=1, source_target_pairs={{0,0},{1,128},{64,64},{65,192},{128,1},{129,129},{192,65},{193,193... | collective-permute-start | bytes 1572872 | tf_op jit(solution)/shard_map/ppermute | solution.py:75
  27.3 16.5 %copy-start.6 = (s32[8,16]{1,0:T(8,128)S(1)}, s32[8,16]{1,0:T(8,128)}, u32[]{:S(2)}) copy-start(s32[8,16]{1,0:T(8,128)} %param.7) | copy-start | bytes 1540
  27.3 21.5 %collective-permute-start.7 = (f32[16,64,128]{2,1,0:T(8,128)S(1)}, f32[16,64,128]{2,1,0:T(8,128)}, u32[]{:S(2)}, u32[]{:S(2)}) collective-permute-start(f32[16,64,128]{2,1,0:T(8,128)S(1)} %get-tuple-element.22), channel_id=1, source_target_pairs={{0,64},{1,192},{64,0},{65,128},{128,65},{129,193},{192,1},{193,129... | collective-permute-start | bytes 1572872 | tf_op jit(solution)/shard_map/ppermute | solution.py:75
  32.1 13.3 %collective-permute-start.5 = (f32[32,16,128]{2,1,0:T(8,128)S(1)}, f32[32,16,128]{2,1,0:T(8,128)S(1)}, u32[]{:S(2)}, u32[]{:S(2)}) collective-permute-start(f32[32,16,128]{2,1,0:T(8,128)S(1)} %maximum_select_fusion.1), channel_id=1, source_target_pairs={{0,64},{64,0},{1,65},{65,1},{128,192},{192,128},{129,193},{193,129... | collective-permute-start | bytes 786440 | tf_op jit(solution)/shard_map/ppermute | solution.py:75
  34.1 13.8 %collective-permute-start.4 = (f32[32,16,128]{2,1,0:T(8,128)S(1)}, f32[32,16,128]{2,1,0:T(8,128)}, u32[]{:S(2)}, u32[]{:S(2)}) collective-permute-start(f32[32,16,128]{2,1,0:T(8,128)S(1)} %maximum_select_fusion.1), channel_id=1, source_target_pairs={{64,128},{128,64},{65,129},{129,65},{192,194},{194,192},{193,195},... | collective-permute-start | bytes 786440 | tf_op jit(solution)/shard_map/ppermute | solution.py:75
  43.8 11.8 %copy-start.1 = (f32[2,128,128]{2,0,1:T(2,128)}, f32[2,128,128]{2,0,1:T(2,128)S(1)}, u32[]{:S(2)}) copy-start(f32[2,128,128]{2,0,1:T(2,128)S(1)} %fusion) | copy-start | bytes 393220
  44.6 10.4 %copy-start.4 = (pred[2,16,1,1]{1,0,3,2:T(4,128)(4,1)}, pred[2,16,1,1]{1,0,3,2:T(4,128)(4,1)S(1)}, u32[]{:S(2)}) copy-start(pred[2,16,1,1]{1,0,3,2:T(4,128)(4,1)S(1)} %fusion.14) | copy-start | bytes 100
  48.8 2.6 %copy-start = (f32[16,64,128]{2,1,0:T(8,128)}, f32[16,64,128]{2,1,0:T(8,128)S(1)}, u32[]{:S(2)}) copy-start(f32[16,64,128]{2,1,0:T(8,128)S(1)} %collective-permute-done.6) | copy-start | bytes 1572868
  48.9 4.7 %collective-permute-start.8 = (f32[32,48,128]{2,1,0:T(8,128)S(1)}, f32[32,48,128]{2,1,0:T(8,128)S(1)}, u32[]{:S(2)}, u32[]{:S(2)}) collective-permute-start(f32[32,48,128]{2,1,0:T(8,128)S(1)} %pad_maximum_fusion), channel_id=1, source_target_pairs={{0,1},{1,0},{2,3},{3,2},{4,5},{5,4},{6,7},{7,6},{8,9},{9,8},{10,11... | collective-permute-start | bytes 2359304 | tf_op jit(solution)/shard_map/ppermute | solution.py:75
  57.4 4.3 %collective-permute-start.9 = (f32[32,48,128]{2,1,0:T(8,128)S(1)}, f32[32,48,128]{2,1,0:T(8,128)}, u32[]{:S(2)}, u32[]{:S(2)}) collective-permute-start(f32[32,48,128]{2,1,0:T(8,128)S(1)} %convolution_bitcast_fusion.4), channel_id=1, source_target_pairs={{0,1},{1,0},{2,3},{3,2},{4,5},{5,4},{6,7},{7,6},{8,9},{9,8},{10,11... | collective-permute-start | bytes 2359304 | tf_op jit(solution)/shard_map/ppermute | solution.py:75
  62.9 13.7 %collective-permute-start.10 = (f32[32,16,128]{2,1,0:T(8,128)S(1)}, f32[32,16,128]{2,1,0:T(8,128)S(1)}, u32[]{:S(2)}, u32[]{:S(2)}) collective-permute-start(f32[32,16,128]{2,1,0:T(8,128)S(1)} %get-tuple-element.37), channel_id=1, source_target_pairs={{64,128},{128,64},{65,129},{129,65},{192,194},{194,192},{193,195},... | collective-permute-start | bytes 786440 | tf_op jit(solution)/shard_map/ppermute | solution.py:75
  70.0 9.3 %collective-permute-start.11 = (f32[32,16,128]{2,1,0:T(8,128)S(1)}, f32[32,16,128]{2,1,0:T(8,128)S(1)}, u32[]{:S(2)}, u32[]{:S(2)}) collective-permute-start(f32[32,16,128]{2,1,0:T(8,128)S(1)} %get-tuple-element.38), channel_id=1, source_target_pairs={{0,64},{64,0},{1,65},{65,1},{128,192},{192,128},{129,193},{193,129... | collective-permute-start | bytes 786440 | tf_op jit(solution)/shard_map/ppermute | solution.py:75
  79.4 18.3 %collective-permute-start.12 = (f32[32,16,128]{2,1,0:T(8,128)S(1)}, f32[32,16,128]{2,1,0:T(8,128)S(1)}, u32[]{:S(2)}, u32[]{:S(2)}) collective-permute-start(f32[32,16,128]{2,1,0:T(8,128)S(1)} %fusion.31), channel_id=1, source_target_pairs={{0,256},{1,257},{2,258},{3,259},{4,260},{5,261},{6,262},{7,263},{8... | collective-permute-start | bytes 786440 | tf_op jit(solution)/shard_map/ppermute | solution.py:75
  97.8 7.9 %collective-permute-start.14 = (f32[32,16,128]{2,1,0:T(8,128)S(1)}, f32[32,16,128]{2,1,0:T(8,128)S(1)}, u32[]{:S(2)}, u32[]{:S(2)}) collective-permute-start(f32[32,16,128]{2,1,0:T(8,128)S(1)} %multiply_multiply_fusion), channel_id=1, source_target_pairs={{0,64},{64,0},{1,65},{65,1},{128,192},{192,128},{129,193},{193,129... | collective-permute-start | bytes 786440 | tf_op jit(solution)/shard_map/ppermute | solution.py:75
  100.0 9.7 %collective-permute-start.13 = (f32[32,16,128]{2,1,0:T(8,128)S(1)}, f32[32,16,128]{2,1,0:T(8,128)S(1)}, u32[]{:S(2)}, u32[]{:S(2)}) collective-permute-start(f32[32,16,128]{2,1,0:T(8,128)S(1)} %multiply_multiply_fusion), channel_id=1, source_target_pairs={{64,128},{128,64},{65,129},{129,65},{192,194},{194,192},{193,195},... | collective-permute-start | bytes 786440 | tf_op jit(solution)/shard_map/ppermute | solution.py:75
  109.8 6.8 %collective-permute-start.15 = (f32[32,48,128]{2,1,0:T(8,128)S(1)}, f32[32,48,128]{2,1,0:T(8,128)S(1)}, u32[]{:S(2)}, u32[]{:S(2)}) collective-permute-start(f32[32,48,128]{2,1,0:T(8,128)S(1)} %pad_maximum_fusion.1), channel_id=1, source_target_pairs={{0,1},{1,0},{2,3},{3,2},{4,5},{5,4},{6,7},{7,6},{8,9},{9,8},{10,11... | collective-permute-start | bytes 2359304 | tf_op jit(solution)/shard_map/ppermute | solution.py:75
  117.2 0.9 copy-start.2
  117.2 0.9 copy-start.5
  120.4 4.2 %collective-permute-start.16 = (f32[32,48,128]{2,1,0:T(8,128)S(1)}, f32[32,48,128]{2,1,0:T(8,128)S(1)}, u32[]{:S(2)}, u32[]{:S(2)}) collective-permute-start(f32[32,48,128]{2,1,0:T(8,128)S(1)} %convolution_bitcast_fusion.2), channel_id=1, source_target_pairs={{0,1},{1,0},{2,3},{3,2},{4,5},{5,4},{6,7},{7,6},{8,9},{9,8},{10,11... | collective-permute-start | bytes 2359304 | tf_op jit(solution)/shard_map/ppermute | solution.py:75
  124.8 11.5 %collective-permute-start.17 = (f32[32,16,128]{2,1,0:T(8,128)S(1)}, f32[32,16,128]{2,1,0:T(8,128)S(1)}, u32[]{:S(2)}, u32[]{:S(2)}) collective-permute-start(f32[32,16,128]{2,1,0:T(8,128)S(1)} %get-tuple-element.35), channel_id=1, source_target_pairs={{64,128},{128,64},{65,129},{129,65},{192,194},{194,192},{193,195},... | collective-permute-start | bytes 786440 | tf_op jit(solution)/shard_map/ppermute | solution.py:75
  127.0 9.3 %collective-permute-start.18 = (f32[32,16,128]{2,1,0:T(8,128)S(1)}, f32[32,16,128]{2,1,0:T(8,128)S(1)}, u32[]{:S(2)}, u32[]{:S(2)}) collective-permute-start(f32[32,16,128]{2,1,0:T(8,128)S(1)} %get-tuple-element.36), channel_id=1, source_target_pairs={{0,64},{64,0},{1,65},{65,1},{128,192},{192,128},{129,193},{193,129... | collective-permute-start | bytes 786440 | tf_op jit(solution)/shard_map/ppermute | solution.py:75
  136.4 18.1 %collective-permute-start.21 = (f32[16,8,128]{2,0,1:T(8,128)S(1)}, f32[16,8,128]{2,0,1:T(8,128)S(1)}, u32[]{:S(2)}, u32[]{:S(2)}) collective-permute-start(f32[16,8,128]{2,0,1:T(8,128)S(1)} %get-tuple-element.43), channel_id=1, source_target_pairs={{256,0},{384,1},{320,64},{448,65},{257,128},{385,129},{321,192},{4... | collective-permute-start | bytes 196616 | tf_op jit(solution)/shard_map/ppermute | solution.py:75
  142.4 12.2 %collective-permute-start.22 = (f32[16,8,128]{2,0,1:T(8,128)S(1)}, f32[16,8,128]{2,0,1:T(8,128)S(1)}, u32[]{:S(2)}, u32[]{:S(2)}) collective-permute-start(f32[16,8,128]{2,0,1:T(8,128)S(1)} %get-tuple-element.44), channel_id=1, source_target_pairs={{320,0},{448,1},{256,64},{384,65},{321,128},{449,129},{257,192},{3... | collective-permute-start | bytes 196616 | tf_op jit(solution)/shard_map/ppermute | solution.py:75
  147.9 7.1 %collective-permute-start.19 = (f32[16,8,128]{2,0,1:T(8,128)S(1)}, f32[16,8,128]{2,0,1:T(8,128)S(1)}, u32[]{:S(2)}, u32[]{:S(2)}) collective-permute-start(f32[16,8,128]{2,0,1:T(8,128)S(1)} %get-tuple-element.47), channel_id=1, source_target_pairs={{0,0},{128,1},{64,64},{192,65},{1,128},{129,129},{65,192},{193,193... | collective-permute-start | bytes 196616 | tf_op jit(solution)/shard_map/ppermute | solution.py:75
  150.2 6.8 %collective-permute-start.20 = (f32[16,8,128]{2,0,1:T(8,128)S(1)}, f32[16,8,128]{2,0,1:T(8,128)S(1)}, u32[]{:S(2)}, u32[]{:S(2)}) collective-permute-start(f32[16,8,128]{2,0,1:T(8,128)S(1)} %get-tuple-element.48), channel_id=1, source_target_pairs={{64,0},{192,1},{0,64},{128,65},{65,128},{193,129},{1,192},{129,193... | collective-permute-start | bytes 196616 | tf_op jit(solution)/shard_map/ppermute | solution.py:75

commit v10 on v8

--- a/solution.py
+++ b/solution.py
@@ -155,9 +155,12 @@
     own_masks = jnp.einsum("uv,vj->uj", picker, masks[:, SLAB : 2 * SLAB], precision=HIGHEST)
     inside = own_masks[:, :, None, None] > 0
 
+    def with_halo(field):
+        return jnp.concatenate([send(field, ODD), field, send(field, EVEN)], 1)
+
     scale = 1.0 / (weights + 1.0)
+    extended = with_halo(current)
     for iteration in range(ITERS):
-        extended = jnp.concatenate([send(current, ODD), current, send(current, EVEN)], 1)
         if iteration == 0:
             extended, scale, inside, mat_x, mat_y, mat_z, *images = lax.optimization_barrier(
                 (extended, scale, inside, mat_x, mat_y, mat_z, *images)
@@ -181,7 +184,17 @@
         part = lax.optimization_barrier(own_part) + send(other_part, SWAP_CORE)
         part = part[:, SLAB : 2 * SLAB] + send(part[:, :SLAB], ODD) + send(part[:, 2 * SLAB :], EVEN)
         if iteration < ITERS - 1:
-            current = current * (part + send(part, SWAP_H) + 1.0) * scale
+            pieces = lax.optimization_barrier((part[: 2 * block], part[2 * block :]))
+            received = [send(value, SWAP_H) for value in pieces]
+            chunks = []
+            for place_of, value in enumerate(pieces):
+                chunk = slice(2 * block * place_of, 2 * block * (place_of + 1))
+                if chunks:
+                    received[1], _ = lax.optimization_barrier((received[1], chunks[0]))
+                total = value + received[place_of] + 1.0
+                chunks.append(current[chunk] * total * scale[chunk])
+            current = jnp.concatenate(chunks, 0)
+            extended = jnp.concatenate([with_halo(chunk) for chunk in chunks], 0)
 
     def own_half(value, mine):
         return jnp.where((h == 0) == mine, value[: 2 * block], value[2 * block :])

time: 157 us -> 160 us (1.019); the launches traced: 156 us -> 157 us
  starting transfers between devices: 74.9 us -> 95.2 us
  waiting for transfers between devices: 57.5 us -> 38.2 us
    ppermute x21 -> x24, starting transfers between devices: 74.9 us -> 95.2 us  [send(): return lax.ppermute(value, AXES, pairs)]
    ppermute x21 -> x24, waiting for transfers between devices: 57.5 us -> 38.2 us  [send(): return lax.ppermute(value, AXES, pairs)]
  transfers between devices with their start and end apart: 21 -> 24, of which waited for: 14 -> 15; matrix products, arithmetic and copies ran while one was open for 8% -> 8% of each run, Pallas kernels for 0% -> 0%
where the time goes in v10:
time: 160 us; the launch traced here: 157 us
  starting transfers between devices  95.2 us (60%)
  waiting for transfers between devices  38.2 us (24%)
  matrix products  13.9 us (9%)
  local copies, waits for them, and re-layouts  4.73 us (3%)
  other arithmetic  4.48 us (3%)
    ppermute x24, starting transfers between devices, send(): return lax.ppermute(value, AXES, pairs)  95.2 us
    ppermute x24, waiting for transfers between devices, send(): return lax.ppermute(value, AXES, pairs)  38.2 us
  transfers between devices with their start and end apart: 24, of which 15 were waited for; matrix products, arithmetic and copies ran while one was open for 8% of the time, Pallas kernels for 0%

profile of v10, /device:TPU:57, one launch (start us, length us, event | category | flops | bytes accessed | tf_op | source)
XLA Modules:
  0.0 157.3 jit_solution(7341634304615465807)
XLA Ops:
  0.0 0.9 constant_dynamic-slice_fusion.1
  0.9 4.9 %collective-permute-start.1 = (f32[8,16,128]{2,1,0:T(8,128)S(1)}, f32[8,16,128]{2,1,0:T(8,128)S(1)}, u32[]{:S(2)}, u32[]{:S(2)}) collective-permute-start(f32[8,16,128]{2,1,0:T(8,128)S(1)} %bitcast.140), channel_id=1, source_target_pairs={{0,64},{1,192},{64,0},{65,128},{128,65},{129,193},{192,1},{193,129... | collective-permute-start | bytes 196616 | tf_op jit(solution)/shard_map/ppermute | solution.py:74
  5.9 2.2 %collective-permute-start = (f32[8,16,128]{2,1,0:T(8,128)S(1)}, f32[8,16,128]{2,1,0:T(8,128)S(1)}, u32[]{:S(2)}, u32[]{:S(2)}) collective-permute-start(f32[8,16,128]{2,1,0:T(8,128)S(1)} %bitcast.141), channel_id=1, source_target_pairs={{0,0},{1,128},{64,64},{65,192},{128,1},{129,129},{192,65},{193,193... | collective-permute-start | bytes 196616 | tf_op jit(solution)/shard_map/ppermute | solution.py:74
  8.1 1.3 dynamic-slice_bitcast_fusion
  9.4 4.9 %collective-permute-start.5 = (f32[16,64,128]{2,1,0:T(8,128)S(1)}, f32[16,64,128]{2,1,0:T(8,128)S(1)}, u32[]{:S(2)}, u32[]{:S(2)}) collective-permute-start(f32[16,64,128]{2,1,0:T(8,128)S(1)} %get-tuple-element.42), channel_id=1, source_target_pairs={{0,0},{1,128},{64,64},{65,192},{128,1},{129,129},{192,65},{193,193... | collective-permute-start | bytes 1572872 | tf_op jit(solution)/shard_map/ppermute | solution.py:74
  14.7 10.6 %collective-permute-start.2 = (f32[16,16,128]{2,1,0:T(8,128)S(1)}, f32[16,16,128]{2,1,0:T(8,128)S(1)}, u32[]{:S(2)}, u32[]{:S(2)}) collective-permute-start(f32[16,16,128]{2,1,0:T(8,128)S(1)} %pad_maximum_fusion.1), channel_id=1, source_target_pairs={{0,256},{1,257},{2,258},{3,259},{4,260},{5,261},{6,262},{7,263},{8... | collective-permute-start | bytes 393224 | tf_op jit(solution)/shard_map/ppermute | solution.py:74
  25.4 2.2 %collective-permute-start.6 = (f32[16,64,128]{2,1,0:T(8,128)S(1)}, f32[16,64,128]{2,1,0:T(8,128)}, u32[]{:S(2)}, u32[]{:S(2)}) collective-permute-start(f32[16,64,128]{2,1,0:T(8,128)S(1)} %get-tuple-element.25), channel_id=1, source_target_pairs={{0,64},{1,192},{64,0},{65,128},{128,65},{129,193},{192,1},{193,129... | collective-permute-start | bytes 1572872 | tf_op jit(solution)/shard_map/ppermute | solution.py:74
  27.8 1.9 %collective-permute-start.4 = (f32[32,16,128]{2,1,0:T(8,128)S(1)}, f32[32,16,128]{2,1,0:T(8,128)S(1)}, u32[]{:S(2)}, u32[]{:S(2)}) collective-permute-start(f32[32,16,128]{2,1,0:T(8,128)S(1)} %maximum_select_fusion.1), channel_id=1, source_target_pairs={{0,64},{64,0},{1,65},{65,1},{128,192},{192,128},{129,193},{193,129... | collective-permute-start | bytes 786440 | tf_op jit(solution)/shard_map/ppermute | solution.py:74
  29.7 10.1 %collective-permute-start.3 = (f32[32,16,128]{2,1,0:T(8,128)S(1)}, f32[32,16,128]{2,1,0:T(8,128)}, u32[]{:S(2)}, u32[]{:S(2)}) collective-permute-start(f32[32,16,128]{2,1,0:T(8,128)S(1)} %maximum_select_fusion.1), channel_id=1, source_target_pairs={{64,128},{128,64},{65,129},{129,65},{192,194},{194,192},{193,195},... | collective-permute-start | bytes 786440 | tf_op jit(solution)/shard_map/ppermute | solution.py:74
  40.6 0.4 fusion.24
  41.1 0.7 fusion.34
  41.8 0.8 fusion
  43.3 0.8 fusion.19
  44.1 2.4 %collective-permute-done.3 = f32[32,16,128]{2,1,0:T(8,128)} collective-permute-done((f32[32,16,128]{2,1,0:T(8,128)S(1)}, f32[32,16,128]{2,1,0:T(8,128)}, u32[]{:S(2)}, u32[]{:S(2)}) %collective-permute-start.3) | collective-permute-done | bytes 262176 | tf_op jit(solution)/shard_map/ppermute | solution.py:74
  46.5 1.0 pad_maximum_fusion
  47.6 2.6 %collective-permute-start.7 = (f32[32,48,128]{2,1,0:T(8,128)S(1)}, f32[32,48,128]{2,1,0:T(8,128)S(1)}, u32[]{:S(2)}, u32[]{:S(2)}) collective-permute-start(f32[32,48,128]{2,1,0:T(8,128)S(1)} %pad_maximum_fusion), channel_id=1, source_target_pairs={{0,1},{1,0},{2,3},{3,2},{4,5},{5,4},{6,7},{7,6},{8,9},{9,8},{10,11... | collective-permute-start | bytes 2359304 | tf_op jit(solution)/shard_map/ppermute | solution.py:74
  50.1 1.3 maximum_select_fusion
  51.5 0.7 slice_bitcast_fusion
  52.3 0.6 fusion.1
  52.8 0.9 convolution_bitcast_fusion.1
  53.7 0.6 fusion.17
  54.4 0.6 fusion.43
  55.0 0.4 fusion.104
  55.3 0.8 convolution_bitcast_fusion.4
  56.1 2.0 %collective-permute-start.8 = (f32[32,48,128]{2,1,0:T(8,128)S(1)}, f32[32,48,128]{2,1,0:T(8,128)}, u32[]{:S(2)}, u32[]{:S(2)}) collective-permute-start(f32[32,48,128]{2,1,0:T(8,128)S(1)} %convolution_bitcast_fusion.4), channel_id=1, source_target_pairs={{0,1},{1,0},{2,3},{3,2},{4,5},{5,4},{6,7},{7,6},{8,9},{9,8},{10,11... | collective-permute-start | bytes 2359304 | tf_op jit(solution)/shard_map/ppermute | solution.py:74
  58.2 0.9 copy.24
  59.1 0.4 fusion.103
  59.5 0.8 convolution_bitcast_fusion.5
  60.4 1.2 add.253
  61.7 5.5 %collective-permute-start.9 = (f32[32,16,128]{2,1,0:T(8,128)S(1)}, f32[32,16,128]{2,1,0:T(8,128)S(1)}, u32[]{:S(2)}, u32[]{:S(2)}) collective-permute-start(f32[32,16,128]{2,1,0:T(8,128)S(1)} %get-tuple-element.45), channel_id=1, source_target_pairs={{64,128},{128,64},{65,129},{129,65},{192,194},{194,192},{193,195},... | collective-permute-start | bytes 786440 | tf_op jit(solution)/shard_map/ppermute | solution.py:74
  67.2 1.9 %collective-permute-start.10 = (f32[32,16,128]{2,1,0:T(8,128)S(1)}, f32[32,16,128]{2,1,0:T(8,128)S(1)}, u32[]{:S(2)}, u32[]{:S(2)}) collective-permute-start(f32[32,16,128]{2,1,0:T(8,128)S(1)} %get-tuple-element.46), channel_id=1, source_target_pairs={{0,64},{64,0},{1,65},{65,1},{128,192},{192,128},{129,193},{193,129... | collective-permute-start | bytes 786440 | tf_op jit(solution)/shard_map/ppermute | solution.py:74
  69.1 4.3 %collective-permute-done.9 = f32[32,16,128]{2,1,0:T(8,128)S(1)} collective-permute-done((f32[32,16,128]{2,1,0:T(8,128)S(1)}, f32[32,16,128]{2,1,0:T(8,128)S(1)}, u32[]{:S(2)}, u32[]{:S(2)}) %collective-permute-start.9) | collective-permute-done | bytes 262176 | tf_op jit(solution)/shard_map/ppermute | solution.py:74
  73.4 3.1 %collective-permute-done.10 = f32[32,16,128]{2,1,0:T(8,128)S(1)} collective-permute-done((f32[32,16,128]{2,1,0:T(8,128)S(1)}, f32[32,16,128]{2,1,0:T(8,128)S(1)}, u32[]{:S(2)}, u32[]{:S(2)}) %collective-permute-start.10) | collective-permute-done | bytes 262176 | tf_op jit(solution)/shard_map/ppermute | solution.py:74
  76.5 1.9 %collective-permute-start.11 = (f32[16,16,128]{2,1,0:T(8,128)S(1)}, f32[16,16,128]{2,1,0:T(8,128)S(1)}, u32[]{:S(2)}, u32[]{:S(2)}) collective-permute-start(f32[16,16,128]{2,1,0:T(8,128)S(1)} %get-tuple-element.33), channel_id=1, source_target_pairs={{0,256},{1,257},{2,258},{3,259},{4,260},{5,261},{6,262},{7,263},{8... | collective-permute-start | bytes 393224 | tf_op jit(solution)/shard_map/ppermute | solution.py:74
  78.5 7.3 %collective-permute-start.12 = (f32[16,16,128]{2,1,0:T(8,128)S(1)}, f32[16,16,128]{2,1,0:T(8,128)S(1)}, u32[]{:S(2)}, u32[]{:S(2)}) collective-permute-start(f32[16,16,128]{2,1,0:T(8,128)S(1)} %get-tuple-element.35), channel_id=1, source_target_pairs={{0,256},{1,257},{2,258},{3,259},{4,260},{5,261},{6,262},{7,263},{8... | collective-permute-start | bytes 393224 | tf_op jit(solution)/shard_map/ppermute | solution.py:74
  85.7 3.2 %collective-permute-done.11 = f32[16,16,128]{2,1,0:T(8,128)S(1)} collective-permute-done((f32[16,16,128]{2,1,0:T(8,128)S(1)}, f32[16,16,128]{2,1,0:T(8,128)S(1)}, u32[]{:S(2)}, u32[]{:S(2)}) %collective-permute-start.11) | collective-permute-done | bytes 131104 | tf_op jit(solution)/shard_map/ppermute | solution.py:74
  88.9 3.1 %collective-permute-start.14 = (f32[16,16,128]{2,1,0:T(8,128)S(1)}, f32[16,16,128]{2,1,0:T(8,128)S(1)}, u32[]{:S(2)}, u32[]{:S(2)}) collective-permute-start(f32[16,16,128]{2,1,0:T(8,128)S(1)} %multiply_multiply_fusion.1), channel_id=1, source_target_pairs={{0,64},{64,0},{1,65},{65,1},{128,192},{192,128},{129,193},{193,129... | collective-permute-start | bytes 393224 | tf_op jit(solution)/shard_map/ppermute | solution.py:74
  92.1 1.9 %collective-permute-start.13 = (f32[16,16,128]{2,1,0:T(8,128)S(1)}, f32[16,16,128]{2,1,0:T(8,128)S(1)}, u32[]{:S(2)}, u32[]{:S(2)}) collective-permute-start(f32[16,16,128]{2,1,0:T(8,128)S(1)} %multiply_multiply_fusion.1), channel_id=1, source_target_pairs={{64,128},{128,64},{65,129},{129,65},{192,194},{194,192},{193,195},... | collective-permute-start | bytes 393224 | tf_op jit(solution)/shard_map/ppermute | solution.py:74
  94.4 2.8 %collective-permute-start.16 = (f32[16,16,128]{2,1,0:T(8,128)S(1)}, f32[16,16,128]{2,1,0:T(8,128)S(1)}, u32[]{:S(2)}, u32[]{:S(2)}) collective-permute-start(f32[16,16,128]{2,1,0:T(8,128)S(1)} %multiply_multiply_fusion), channel_id=1, source_target_pairs={{0,64},{64,0},{1,65},{65,1},{128,192},{192,128},{129,193},{193,129... | collective-permute-start | bytes 393224 | tf_op jit(solution)/shard_map/ppermute | solution.py:74
  97.2 4.2 %collective-permute-start.15 = (f32[16,16,128]{2,1,0:T(8,128)S(1)}, f32[16,16,128]{2,1,0:T(8,128)S(1)}, u32[]{:S(2)}, u32[]{:S(2)}) collective-permute-start(f32[16,16,128]{2,1,0:T(8,128)S(1)} %multiply_multiply_fusion), channel_id=1, source_target_pairs={{64,128},{128,64},{65,129},{129,65},{192,194},{194,192},{193,195},... | collective-permute-start | bytes 393224 | tf_op jit(solution)/shard_map/ppermute | solution.py:74
  101.5 3.5 %collective-permute-done.15 = f32[16,16,128]{2,1,0:T(8,128)S(1)} collective-permute-done((f32[16,16,128]{2,1,0:T(8,128)S(1)}, f32[16,16,128]{2,1,0:T(8,128)S(1)}, u32[]{:S(2)}, u32[]{:S(2)}) %collective-permute-start.15) | collective-permute-done | bytes 131104 | tf_op jit(solution)/shard_map/ppermute | solution.py:74
  105.1 7.1 %collective-permute-start.17 = (f32[32,48,128]{2,1,0:T(8,128)S(1)}, f32[32,48,128]{2,1,0:T(8,128)S(1)}, u32[]{:S(2)}, u32[]{:S(2)}) collective-permute-start(f32[32,48,128]{2,1,0:T(8,128)S(1)} %maximum_maximum_fusion), channel_id=1, source_target_pairs={{0,1},{1,0},{2,3},{3,2},{4,5},{5,4},{6,7},{7,6},{8,9},{9,8},{10,11... | collective-permute-start | bytes 2359304 | tf_op jit(solution)/shard_map/ppermute | solution.py:74
  112.2 1.7 %collective-permute-done.17 = f32[32,48,128]{2,1,0:T(8,128)S(1)} collective-permute-done((f32[32,48,128]{2,1,0:T(8,128)S(1)}, f32[32,48,128]{2,1,0:T(8,128)S(1)}, u32[]{:S(2)}, u32[]{:S(2)}) %collective-permute-start.17) | collective-permute-done | bytes 786464 | tf_op jit(solution)/shard_map/ppermute | solution.py:74
  113.9 0.6 fusion.4
  114.5 0.9 convolution_bitcast_fusion
  115.4 0.6 fusion.18
  116.0 0.6 fusion.41
  116.6 0.4 fusion.106
  117.0 0.8 convolution_bitcast_fusion.2
  117.7 2.3 %collective-permute-start.18 = (f32[32,48,128]{2,1,0:T(8,128)S(1)}, f32[32,48,128]{2,1,0:T(8,128)S(1)}, u32[]{:S(2)}, u32[]{:S(2)}) collective-permute-start(f32[32,48,128]{2,1,0:T(8,128)S(1)} %convolution_bitcast_fusion.2), channel_id=1, source_target_pairs={{0,1},{1,0},{2,3},{3,2},{4,5},{5,4},{6,7},{7,6},{8,9},{9,8},{10,11... | collective-permute-start | bytes 2359304 | tf_op jit(solution)/shard_map/ppermute | solution.py:74
  120.0 0.4 fusion.105
  120.4 0.8 convolution_bitcast_fusion.3
  121.2 0.7 collective-permute-done.18
  122.1 3.8 %collective-permute-start.19 = (f32[32,16,128]{2,1,0:T(8,128)S(1)}, f32[32,16,128]{2,1,0:T(8,128)S(1)}, u32[]{:S(2)}, u32[]{:S(2)}) collective-permute-start(f32[32,16,128]{2,1,0:T(8,128)S(1)} %get-tuple-element.43), channel_id=1, source_target_pairs={{64,128},{128,64},{65,129},{129,65},{192,194},{194,192},{193,195},... | collective-permute-start | bytes 786440 | tf_op jit(solution)/shard_map/ppermute | solution.py:74
  125.8 1.9 %collective-permute-start.20 = (f32[32,16,128]{2,1,0:T(8,128)S(1)}, f32[32,16,128]{2,1,0:T(8,128)S(1)}, u32[]{:S(2)}, u32[]{:S(2)}) collective-permute-start(f32[32,16,128]{2,1,0:T(8,128)S(1)} %get-tuple-element.44), channel_id=1, source_target_pairs={{0,64},{64,0},{1,65},{65,1},{128,192},{192,128},{129,193},{193,129... | collective-permute-start | bytes 786440 | tf_op jit(solution)/shard_map/ppermute | solution.py:74
  127.8 5.8 %collective-permute-done.19 = f32[32,16,128]{2,1,0:T(8,128)S(1)} collective-permute-done((f32[32,16,128]{2,1,0:T(8,128)S(1)}, f32[32,16,128]{2,1,0:T(8,128)S(1)}, u32[]{:S(2)}, u32[]{:S(2)}) %collective-permute-start.19) | collective-permute-done | bytes 262176 | tf_op jit(solution)/shard_map/ppermute | solution.py:74
  133.6 1.3 collective-permute-done.20
  135.0 3.5 %collective-permute-start.21 = (f32[16,16,128]{2,1,0:T(8,128)S(1)}, f32[16,16,128]{2,1,0:T(8,128)S(1)}, u32[]{:S(2)}, u32[]{:S(2)}) collective-permute-start(f32[16,16,128]{2,1,0:T(8,128)S(1)} %slice_select_fusion), channel_id=1, source_target_pairs={{0,256},{1,257},{2,258},{3,259},{4,260},{5,261},{6,262},{7,263},{8... | collective-permute-start | bytes 393224 | tf_op jit(solution)/shard_map/ppermute | solution.py:74
  138.5 6.7 %collective-permute-done.21 = f32[16,16,128]{2,1,0:T(8,128)S(1)} collective-permute-done((f32[16,16,128]{2,1,0:T(8,128)S(1)}, f32[16,16,128]{2,1,0:T(8,128)S(1)}, u32[]{:S(2)}, u32[]{:S(2)}) %collective-permute-start.21) | collective-permute-done | bytes 131104 | tf_op jit(solution)/shard_map/ppermute | solution.py:74
  145.3 4.4 %collective-permute-start.22 = (f32[16,8,128]{2,0,1:T(8,128)S(1)}, f32[16,8,128]{2,0,1:T(8,128)S(1)}, u32[]{:S(2)}, u32[]{:S(2)}) collective-permute-start(f32[16,8,128]{2,0,1:T(8,128)S(1)} %get-tuple-element.37), channel_id=1, source_target_pairs={{0,0},{128,1},{64,64},{192,65},{1,128},{129,129},{65,192},{193,193... | collective-permute-start | bytes 196616 | tf_op jit(solution)/shard_map/ppermute | solution.py:74
  149.7 2.1 %collective-permute-start.23 = (f32[16,8,128]{2,0,1:T(8,128)S(1)}, f32[16,8,128]{2,0,1:T(8,128)S(1)}, u32[]{:S(2)}, u32[]{:S(2)}) collective-permute-start(f32[16,8,128]{2,0,1:T(8,128)S(1)} %get-tuple-element.38), channel_id=1, source_target_pairs={{64,0},{192,1},{0,64},{128,65},{65,128},{193,129},{1,192},{129,193... | collective-permute-start | bytes 196616 | tf_op jit(solution)/shard_map/ppermute | solution.py:74
  151.8 0.9 collective-permute-done.22
  152.8 3.7 %collective-permute-done.23 = f32[16,8,128]{2,0,1:T(8,128)S(1)} collective-permute-done((f32[16,8,128]{2,0,1:T(8,128)S(1)}, f32[16,8,128]{2,0,1:T(8,128)S(1)}, u32[]{:S(2)}, u32[]{:S(2)}) %collective-permute-start.23) | collective-permute-done | bytes 65568 | tf_op jit(solution)/shard_map/ppermute | solution.py:74
  156.5 0.7 copy.13
  (65 shorter events, 3.2 us)
Async XLA Ops:
  0.9 13.7 %collective-permute-start.1 = (f32[8,16,128]{2,1,0:T(8,128)S(1)}, f32[8,16,128]{2,1,0:T(8,128)S(1)}, u32[]{:S(2)}, u32[]{:S(2)}) collective-permute-start(f32[8,16,128]{2,1,0:T(8,128)S(1)} %bitcast.140), channel_id=1, source_target_pairs={{0,64},{1,192},{64,0},{65,128},{128,65},{129,193},{192,1},{193,129... | collective-permute-start | bytes 196616 | tf_op jit(solution)/shard_map/ppermute | solution.py:74
  5.9 8.7 %collective-permute-start = (f32[8,16,128]{2,1,0:T(8,128)S(1)}, f32[8,16,128]{2,1,0:T(8,128)S(1)}, u32[]{:S(2)}, u32[]{:S(2)}) collective-permute-start(f32[8,16,128]{2,1,0:T(8,128)S(1)} %bitcast.141), channel_id=1, source_target_pairs={{0,0},{1,128},{64,64},{65,192},{128,1},{129,129},{192,65},{193,193... | collective-permute-start | bytes 196616 | tf_op jit(solution)/shard_map/ppermute | solution.py:74
  9.4 30.5 %copy-start.3 = (f32[8,3,31]{2,0,1:T(8,128)S(1)}, f32[8,3,31]{2,0,1:T(8,128)}, u32[]{:S(2)}) copy-start(f32[8,3,31]{2,0,1:T(8,128)} %param.6) | copy-start | bytes 8932
  9.4 38.2 %collective-permute-start.5 = (f32[16,64,128]{2,1,0:T(8,128)S(1)}, f32[16,64,128]{2,1,0:T(8,128)S(1)}, u32[]{:S(2)}, u32[]{:S(2)}) collective-permute-start(f32[16,64,128]{2,1,0:T(8,128)S(1)} %get-tuple-element.42), channel_id=1, source_target_pairs={{0,0},{1,128},{64,64},{65,192},{128,1},{129,129},{192,65},{193,193... | collective-permute-start | bytes 1572872 | tf_op jit(solution)/shard_map/ppermute | solution.py:74
  14.7 27.9 %copy-start.6 = (s32[8,16]{1,0:T(8,128)S(1)}, s32[8,16]{1,0:T(8,128)}, u32[]{:S(2)}) copy-start(s32[8,16]{1,0:T(8,128)} %param.7) | copy-start | bytes 1540
  14.7 13.1 %collective-permute-start.2 = (f32[16,16,128]{2,1,0:T(8,128)S(1)}, f32[16,16,128]{2,1,0:T(8,128)S(1)}, u32[]{:S(2)}, u32[]{:S(2)}) collective-permute-start(f32[16,16,128]{2,1,0:T(8,128)S(1)} %pad_maximum_fusion.1), channel_id=1, source_target_pairs={{0,256},{1,257},{2,258},{3,259},{4,260},{5,261},{6,262},{7,263},{8... | collective-permute-start | bytes 393224 | tf_op jit(solution)/shard_map/ppermute | solution.py:74
  25.4 22.1 %collective-permute-start.6 = (f32[16,64,128]{2,1,0:T(8,128)S(1)}, f32[16,64,128]{2,1,0:T(8,128)}, u32[]{:S(2)}, u32[]{:S(2)}) collective-permute-start(f32[16,64,128]{2,1,0:T(8,128)S(1)} %get-tuple-element.25), channel_id=1, source_target_pairs={{0,64},{1,192},{64,0},{65,128},{128,65},{129,193},{192,1},{193,129... | collective-permute-start | bytes 1572872 | tf_op jit(solution)/shard_map/ppermute | solution.py:74
  27.8 16.3 %collective-permute-start.4 = (f32[32,16,128]{2,1,0:T(8,128)S(1)}, f32[32,16,128]{2,1,0:T(8,128)S(1)}, u32[]{:S(2)}, u32[]{:S(2)}) collective-permute-start(f32[32,16,128]{2,1,0:T(8,128)S(1)} %maximum_select_fusion.1), channel_id=1, source_target_pairs={{0,64},{64,0},{1,65},{65,1},{128,192},{192,128},{129,193},{193,129... | collective-permute-start | bytes 786440 | tf_op jit(solution)/shard_map/ppermute | solution.py:74
  29.7 16.8 %collective-permute-start.3 = (f32[32,16,128]{2,1,0:T(8,128)S(1)}, f32[32,16,128]{2,1,0:T(8,128)}, u32[]{:S(2)}, u32[]{:S(2)}) collective-permute-start(f32[32,16,128]{2,1,0:T(8,128)S(1)} %maximum_select_fusion.1), channel_id=1, source_target_pairs={{64,128},{128,64},{65,129},{129,65},{192,194},{194,192},{193,195},... | collective-permute-start | bytes 786440 | tf_op jit(solution)/shard_map/ppermute | solution.py:74
  42.6 11.8 %copy-start.1 = (f32[2,128,128]{2,0,1:T(2,128)}, f32[2,128,128]{2,0,1:T(2,128)S(1)}, u32[]{:S(2)}) copy-start(f32[2,128,128]{2,0,1:T(2,128)S(1)} %fusion) | copy-start | bytes 393220
  43.3 10.4 %copy-start.4 = (pred[2,16,1,1]{1,0,3,2:T(4,128)(4,1)}, pred[2,16,1,1]{1,0,3,2:T(4,128)(4,1)S(1)}, u32[]{:S(2)}) copy-start(pred[2,16,1,1]{1,0,3,2:T(4,128)(4,1)S(1)} %fusion.20) | copy-start | bytes 100
  47.5 2.6 %copy-start = (f32[16,64,128]{2,1,0:T(8,128)}, f32[16,64,128]{2,1,0:T(8,128)S(1)}, u32[]{:S(2)}) copy-start(f32[16,64,128]{2,1,0:T(8,128)S(1)} %collective-permute-done.5) | copy-start | bytes 1572868
  47.6 4.7 %collective-permute-start.7 = (f32[32,48,128]{2,1,0:T(8,128)S(1)}, f32[32,48,128]{2,1,0:T(8,128)S(1)}, u32[]{:S(2)}, u32[]{:S(2)}) collective-permute-start(f32[32,48,128]{2,1,0:T(8,128)S(1)} %pad_maximum_fusion), channel_id=1, source_target_pairs={{0,1},{1,0},{2,3},{3,2},{4,5},{5,4},{6,7},{7,6},{8,9},{9,8},{10,11... | collective-permute-start | bytes 2359304 | tf_op jit(solution)/shard_map/ppermute | solution.py:74
  56.1 4.3 %collective-permute-start.8 = (f32[32,48,128]{2,1,0:T(8,128)S(1)}, f32[32,48,128]{2,1,0:T(8,128)}, u32[]{:S(2)}, u32[]{:S(2)}) collective-permute-start(f32[32,48,128]{2,1,0:T(8,128)S(1)} %convolution_bitcast_fusion.4), channel_id=1, source_target_pairs={{0,1},{1,0},{2,3},{3,2},{4,5},{5,4},{6,7},{7,6},{8,9},{9,8},{10,11... | collective-permute-start | bytes 2359304 | tf_op jit(solution)/shard_map/ppermute | solution.py:74
  61.7 11.7 %collective-permute-start.9 = (f32[32,16,128]{2,1,0:T(8,128)S(1)}, f32[32,16,128]{2,1,0:T(8,128)S(1)}, u32[]{:S(2)}, u32[]{:S(2)}) collective-permute-start(f32[32,16,128]{2,1,0:T(8,128)S(1)} %get-tuple-element.45), channel_id=1, source_target_pairs={{64,128},{128,64},{65,129},{129,65},{192,194},{194,192},{193,195},... | collective-permute-start | bytes 786440 | tf_op jit(solution)/shard_map/ppermute | solution.py:74
  67.2 9.3 %collective-permute-start.10 = (f32[32,16,128]{2,1,0:T(8,128)S(1)}, f32[32,16,128]{2,1,0:T(8,128)S(1)}, u32[]{:S(2)}, u32[]{:S(2)}) collective-permute-start(f32[32,16,128]{2,1,0:T(8,128)S(1)} %get-tuple-element.46), channel_id=1, source_target_pairs={{0,64},{64,0},{1,65},{65,1},{128,192},{192,128},{129,193},{193,129... | collective-permute-start | bytes 786440 | tf_op jit(solution)/shard_map/ppermute | solution.py:74
  76.5 12.4 %collective-permute-start.11 = (f32[16,16,128]{2,1,0:T(8,128)S(1)}, f32[16,16,128]{2,1,0:T(8,128)S(1)}, u32[]{:S(2)}, u32[]{:S(2)}) collective-permute-start(f32[16,16,128]{2,1,0:T(8,128)S(1)} %get-tuple-element.33), channel_id=1, source_target_pairs={{0,256},{1,257},{2,258},{3,259},{4,260},{5,261},{6,262},{7,263},{8... | collective-permute-start | bytes 393224 | tf_op jit(solution)/shard_map/ppermute | solution.py:74
  78.5 15.9 %collective-permute-start.12 = (f32[16,16,128]{2,1,0:T(8,128)S(1)}, f32[16,16,128]{2,1,0:T(8,128)S(1)}, u32[]{:S(2)}, u32[]{:S(2)}) collective-permute-start(f32[16,16,128]{2,1,0:T(8,128)S(1)} %get-tuple-element.35), channel_id=1, source_target_pairs={{0,256},{1,257},{2,258},{3,259},{4,260},{5,261},{6,262},{7,263},{8... | collective-permute-start | bytes 393224 | tf_op jit(solution)/shard_map/ppermute | solution.py:74
  88.9 12.5 %collective-permute-start.14 = (f32[16,16,128]{2,1,0:T(8,128)S(1)}, f32[16,16,128]{2,1,0:T(8,128)S(1)}, u32[]{:S(2)}, u32[]{:S(2)}) collective-permute-start(f32[16,16,128]{2,1,0:T(8,128)S(1)} %multiply_multiply_fusion.1), channel_id=1, source_target_pairs={{0,64},{64,0},{1,65},{65,1},{128,192},{192,128},{129,193},{193,129... | collective-permute-start | bytes 393224 | tf_op jit(solution)/shard_map/ppermute | solution.py:74
  92.1 9.4 %collective-permute-start.13 = (f32[16,16,128]{2,1,0:T(8,128)S(1)}, f32[16,16,128]{2,1,0:T(8,128)S(1)}, u32[]{:S(2)}, u32[]{:S(2)}) collective-permute-start(f32[16,16,128]{2,1,0:T(8,128)S(1)} %multiply_multiply_fusion.1), channel_id=1, source_target_pairs={{64,128},{128,64},{65,129},{129,65},{192,194},{194,192},{193,195},... | collective-permute-start | bytes 393224 | tf_op jit(solution)/shard_map/ppermute | solution.py:74
  94.4 7.1 %collective-permute-start.16 = (f32[16,16,128]{2,1,0:T(8,128)S(1)}, f32[16,16,128]{2,1,0:T(8,128)S(1)}, u32[]{:S(2)}, u32[]{:S(2)}) collective-permute-start(f32[16,16,128]{2,1,0:T(8,128)S(1)} %multiply_multiply_fusion), channel_id=1, source_target_pairs={{0,64},{64,0},{1,65},{65,1},{128,192},{192,128},{129,193},{193,129... | collective-permute-start | bytes 393224 | tf_op jit(solution)/shard_map/ppermute | solution.py:74
  97.2 7.8 %collective-permute-start.15 = (f32[16,16,128]{2,1,0:T(8,128)S(1)}, f32[16,16,128]{2,1,0:T(8,128)S(1)}, u32[]{:S(2)}, u32[]{:S(2)}) collective-permute-start(f32[16,16,128]{2,1,0:T(8,128)S(1)} %multiply_multiply_fusion), channel_id=1, source_target_pairs={{64,128},{128,64},{65,129},{129,65},{192,194},{194,192},{193,195},... | collective-permute-start | bytes 393224 | tf_op jit(solution)/shard_map/ppermute | solution.py:74
  105.1 8.8 %collective-permute-start.17 = (f32[32,48,128]{2,1,0:T(8,128)S(1)}, f32[32,48,128]{2,1,0:T(8,128)S(1)}, u32[]{:S(2)}, u32[]{:S(2)}) collective-permute-start(f32[32,48,128]{2,1,0:T(8,128)S(1)} %maximum_maximum_fusion), channel_id=1, source_target_pairs={{0,1},{1,0},{2,3},{3,2},{4,5},{5,4},{6,7},{7,6},{8,9},{9,8},{10,11... | collective-permute-start | bytes 2359304 | tf_op jit(solution)/shard_map/ppermute | solution.py:74
  114.5 0.9 copy-start.2
  114.5 0.9 copy-start.5
  117.7 4.2 %collective-permute-start.18 = (f32[32,48,128]{2,1,0:T(8,128)S(1)}, f32[32,48,128]{2,1,0:T(8,128)S(1)}, u32[]{:S(2)}, u32[]{:S(2)}) collective-permute-start(f32[32,48,128]{2,1,0:T(8,128)S(1)} %convolution_bitcast_fusion.2), channel_id=1, source_target_pairs={{0,1},{1,0},{2,3},{3,2},{4,5},{5,4},{6,7},{7,6},{8,9},{9,8},{10,11... | collective-permute-start | bytes 2359304 | tf_op jit(solution)/shard_map/ppermute | solution.py:74
  122.1 11.5 %collective-permute-start.19 = (f32[32,16,128]{2,1,0:T(8,128)S(1)}, f32[32,16,128]{2,1,0:T(8,128)S(1)}, u32[]{:S(2)}, u32[]{:S(2)}) collective-permute-start(f32[32,16,128]{2,1,0:T(8,128)S(1)} %get-tuple-element.43), channel_id=1, source_target_pairs={{64,128},{128,64},{65,129},{129,65},{192,194},{194,192},{193,195},... | collective-permute-start | bytes 786440 | tf_op jit(solution)/shard_map/ppermute | solution.py:74
  125.8 9.1 %collective-permute-start.20 = (f32[32,16,128]{2,1,0:T(8,128)S(1)}, f32[32,16,128]{2,1,0:T(8,128)S(1)}, u32[]{:S(2)}, u32[]{:S(2)}) collective-permute-start(f32[32,16,128]{2,1,0:T(8,128)S(1)} %get-tuple-element.44), channel_id=1, source_target_pairs={{0,64},{64,0},{1,65},{65,1},{128,192},{192,128},{129,193},{193,129... | collective-permute-start | bytes 786440 | tf_op jit(solution)/shard_map/ppermute | solution.py:74
  135.0 10.2 %collective-permute-start.21 = (f32[16,16,128]{2,1,0:T(8,128)S(1)}, f32[16,16,128]{2,1,0:T(8,128)S(1)}, u32[]{:S(2)}, u32[]{:S(2)}) collective-permute-start(f32[16,16,128]{2,1,0:T(8,128)S(1)} %slice_select_fusion), channel_id=1, source_target_pairs={{0,256},{1,257},{2,258},{3,259},{4,260},{5,261},{6,262},{7,263},{8... | collective-permute-start | bytes 393224 | tf_op jit(solution)/shard_map/ppermute | solution.py:74
  145.3 7.4 %collective-permute-start.22 = (f32[16,8,128]{2,0,1:T(8,128)S(1)}, f32[16,8,128]{2,0,1:T(8,128)S(1)}, u32[]{:S(2)}, u32[]{:S(2)}) collective-permute-start(f32[16,8,128]{2,0,1:T(8,128)S(1)} %get-tuple-element.37), channel_id=1, source_target_pairs={{0,0},{128,1},{64,64},{192,65},{1,128},{129,129},{65,192},{193,193... | collective-permute-start | bytes 196616 | tf_op jit(solution)/shard_map/ppermute | solution.py:74
  149.7 6.8 %collective-permute-start.23 = (f32[16,8,128]{2,0,1:T(8,128)S(1)}, f32[16,8,128]{2,0,1:T(8,128)S(1)}, u32[]{:S(2)}, u32[]{:S(2)}) collective-permute-start(f32[16,8,128]{2,0,1:T(8,128)S(1)} %get-tuple-element.38), channel_id=1, source_target_pairs={{64,0},{192,1},{0,64},{128,65},{65,128},{193,129},{1,192},{129,193... | collective-permute-start | bytes 196616 | tf_op jit(solution)/shard_map/ppermute | solution.py:74

commit v11 on v8

--- a/solution.py
+++ b/solution.py
@@ -1,6 +1,7 @@
 import jax
 import jax.numpy as jnp
 from jax import lax
+from jax.experimental.layout import Layout, with_layout_constraint
 from jax.sharding import PartitionSpec as P
 
 TX = 128
@@ -135,32 +136,45 @@
     mat_y = tap_matrix(own[:, 1], local_y[None, :] - all_y[:, None] + half)
     mat_z = tap_matrix(own[:, 2], all_z[:, None] - all_z[None, :] + half)
 
-    wide_rows = first_row + wide
-    tile = (wide_rows // TX)[:, None] == jnp.arange(intersection.shape[1], dtype=jnp.int32)[None, :]
-    tile = jnp.logical_and(tile, jnp.logical_and(wide_rows >= 0, wide_rows < rows)[:, None]).astype(jnp.float32)
-    masks = jnp.einsum("vt,jt->vj", intersection.astype(jnp.float32), tile, precision=HIGHEST)
-    weight_rows = jnp.einsum(
-        "vrj,vj->vr", tap_matrix(kernels[:, 0], slab[:, None] - wide[None, :] + half), masks, precision=HIGHEST
+    mat_x, mat_y, mat_own, mat_other, mat_z = (
+        with_layout_constraint(table, Layout((0, 1, 2)))
+        for table in (mat_x, mat_y, mat_y[:, :, :width], mat_y[:, :, width:], mat_z)
     )
+
+    def masks_of(intersection):
+        wide_rows = first_row + wide
+        tile = (wide_rows // TX)[:, None] == jnp.arange(intersection.shape[1], dtype=jnp.int32)[None, :]
+        tile = jnp.logical_and(tile, jnp.logical_and(wide_rows >= 0, wide_rows < rows)[:, None])
+        return jnp.einsum(
+            "vt,jt->vj", intersection.astype(jnp.float32), tile.astype(jnp.float32), precision=HIGHEST
+        )
 
     def coverage(kernel, places, length):
         source = places[:, None] - jnp.arange(taps, dtype=jnp.int32)[None, :] + half
         inside = jnp.logical_and(source >= 0, source < length).astype(jnp.float32)
         return jnp.einsum("yk,vk->vy", inside, kernel, precision=HIGHEST)
 
-    weight_cols = coverage(kernels[:, 1], local_y[:width], full_width)
-    weight_depth = coverage(kernels[:, 2], all_z, depth)
-    weight_plane = weight_cols[:, :, None] * weight_rows[:, None, :]
-    weights = jnp.einsum("vyx,vz->yxz", weight_plane, weight_depth, precision=HIGHEST)
-    own_masks = jnp.einsum("uv,vj->uj", picker, masks[:, SLAB : 2 * SLAB], precision=HIGHEST)
+    def scale_of(psf_taps, intersection):
+        kernels = psf_taps / jnp.sum(psf_taps, axis=2, keepdims=True)
+        weight_rows = jnp.einsum(
+            "vrj,vj->vr",
+            tap_matrix(kernels[:, 0], slab[:, None] - wide[None, :] + half),
+            masks_of(intersection),
+            precision=HIGHEST,
+        )
+        weight_cols = coverage(kernels[:, 1], local_y[:width], full_width)
+        weight_depth = coverage(kernels[:, 2], all_z, depth)
+        weight_plane = weight_cols[:, :, None] * weight_rows[:, None, :]
+        return 1.0 / (jnp.einsum("vyx,vz->yxz", weight_plane, weight_depth, precision=HIGHEST) + 1.0)
+
+    own_masks = jnp.einsum("uv,vj->uj", picker, masks_of(intersection)[:, SLAB : 2 * SLAB], precision=HIGHEST)
     inside = own_masks[:, :, None, None] > 0
 
-    scale = 1.0 / (weights + 1.0)
     for iteration in range(ITERS):
         extended = jnp.concatenate([send(current, ODD), current, send(current, EVEN)], 1)
         if iteration == 0:
-            extended, scale, inside, mat_x, mat_y, mat_z, *images = lax.optimization_barrier(
-                (extended, scale, inside, mat_x, mat_y, mat_z, *images)
+            extended, inside, mat_x, mat_y, mat_own, mat_other, mat_z, *images = lax.optimization_barrier(
+                (extended, inside, mat_x, mat_y, mat_own, mat_other, mat_z, *images)
             )
             images = lax.optimization_barrier(jnp.where(inside, jnp.stack(images), 0.0))
         extended = jnp.concatenate([extended, send(extended, SWAP_CORE)], 0)
@@ -176,10 +190,12 @@
                 jnp.einsum("uryz,uyj->urjz", back, columns, precision=HIGH),
                 precision=HIGH,
             )
-            for columns in (mat_y[:, :, :width], mat_y[:, :, width:])
+            for columns in (mat_own, mat_other)
         )
         part = lax.optimization_barrier(own_part) + send(other_part, SWAP_CORE)
         part = part[:, SLAB : 2 * SLAB] + send(part[:, :SLAB], ODD) + send(part[:, 2 * SLAB :], EVEN)
+        if iteration == 0:
+            scale = scale_of(*lax.optimization_barrier((psf_taps, intersection, part))[:2])
         if iteration < ITERS - 1:
             current = current * (part + send(part, SWAP_H) + 1.0) * scale
 

time: 157 us -> 155 us (0.987)
  starting transfers between devices: 74.9 us -> 83.1 us
  waiting for transfers between devices: 57.5 us -> 50.8 us
  other arithmetic: 4.48 us -> 1.36 us
  local copies, waits for them, and re-layouts: 4.74 us -> 3.12 us
    ppermute x21, starting transfers between devices: 74.9 us -> 83.1 us  [send(): return lax.ppermute(value, AXES, pairs)]
    ppermute x21, waiting for transfers between devices: 57.5 us -> 50.8 us  [send(): return lax.ppermute(value, AXES, pairs)]
  transfers between devices with their start and end apart: 21 -> 21, of which waited for: 14 -> 15; matrix products, arithmetic and copies ran while one was open for 8% -> 6% of each run, Pallas kernels for 0% -> 0%
where the time goes in v11:
time: 155 us; the launch traced here: 153 us
  starting transfers between devices  83.1 us (54%)
  waiting for transfers between devices  50.8 us (33%)
  matrix products  14.2 us (9%)
  local copies, waits for them, and re-layouts  3.12 us (2%)
    ppermute x21, starting transfers between devices, send(): return lax.ppermute(value, AXES, pairs)  83.1 us
    ppermute x21, waiting for transfers between devices, send(): return lax.ppermute(value, AXES, pairs)  50.8 us
  transfers between devices with their start and end apart: 21, of which 15 were waited for; matrix products, arithmetic and copies ran while one was open for 6% of the time, Pallas kernels for 0%

profile of v11, /device:TPU:57, one launch (start us, length us, event | category | flops | bytes accessed | tf_op | source)
XLA Modules:
  0.0 153.3 jit_solution(2557718133167719088)
XLA Ops:
  0.0 0.9 constant_dynamic-slice_fusion.1
  0.9 5.2 %collective-permute-start = (f32[8,16,128]{2,1,0:T(8,128)S(1)}, f32[8,16,128]{2,1,0:T(8,128)S(1)}, u32[]{:S(2)}, u32[]{:S(2)}) collective-permute-start(f32[8,16,128]{2,1,0:T(8,128)S(1)} %bitcast.155), channel_id=1, source_target_pairs={{0,0},{1,128},{64,64},{65,192},{128,1},{129,129},{192,65},{193,193... | collective-permute-start | bytes 196616 | tf_op jit(solution)/shard_map/ppermute | solution.py:75
  6.2 2.5 %collective-permute-start.1 = (f32[8,16,128]{2,1,0:T(8,128)S(1)}, f32[8,16,128]{2,1,0:T(8,128)S(1)}, u32[]{:S(2)}, u32[]{:S(2)}) collective-permute-start(f32[8,16,128]{2,1,0:T(8,128)S(1)} %bitcast.156), channel_id=1, source_target_pairs={{0,64},{1,192},{64,0},{65,128},{128,65},{129,193},{192,1},{193,129... | collective-permute-start | bytes 196616 | tf_op jit(solution)/shard_map/ppermute | solution.py:75
  8.6 1.3 dynamic-slice_bitcast_fusion
  9.9 3.7 %collective-permute-start.5 = (f32[16,64,128]{2,1,0:T(8,128)S(1)}, f32[16,64,128]{2,1,0:T(8,128)S(1)}, u32[]{:S(2)}, u32[]{:S(2)}) collective-permute-start(f32[16,64,128]{2,1,0:T(8,128)S(1)} %get-tuple-element.42), channel_id=1, source_target_pairs={{0,0},{1,128},{64,64},{65,192},{128,1},{129,129},{192,65},{193,193... | collective-permute-start | bytes 1572872 | tf_op jit(solution)/shard_map/ppermute | solution.py:75
  14.2 10.6 %collective-permute-start.2 = (f32[16,16,128]{2,1,0:T(8,128)S(1)}, f32[16,16,128]{2,1,0:T(8,128)S(1)}, u32[]{:S(2)}, u32[]{:S(2)}) collective-permute-start(f32[16,16,128]{2,1,0:T(8,128)S(1)} %pad_maximum_fusion.2), channel_id=1, source_target_pairs={{0,256},{1,257},{2,258},{3,259},{4,260},{5,261},{6,262},{7,263},{8... | collective-permute-start | bytes 393224 | tf_op jit(solution)/shard_map/ppermute | solution.py:75
  24.9 2.8 %collective-permute-start.6 = (f32[16,64,128]{2,1,0:T(8,128)S(1)}, f32[16,64,128]{2,1,0:T(8,128)S(1)}, u32[]{:S(2)}, u32[]{:S(2)}) collective-permute-start(f32[16,64,128]{2,1,0:T(8,128)S(1)} %get-tuple-element.25), channel_id=1, source_target_pairs={{0,64},{1,192},{64,0},{65,128},{128,65},{129,193},{192,1},{193,129... | collective-permute-start | bytes 1572872 | tf_op jit(solution)/shard_map/ppermute | solution.py:75
  27.8 2.6 %collective-permute-start.4 = (f32[32,16,128]{2,1,0:T(8,128)S(1)}, f32[32,16,128]{2,1,0:T(8,128)S(1)}, u32[]{:S(2)}, u32[]{:S(2)}) collective-permute-start(f32[32,16,128]{2,1,0:T(8,128)S(1)} %maximum_select_fusion.1), channel_id=1, source_target_pairs={{0,64},{64,0},{1,65},{65,1},{128,192},{192,128},{129,193},{193,129... | collective-permute-start | bytes 786440 | tf_op jit(solution)/shard_map/ppermute | solution.py:75
  30.4 7.7 %collective-permute-start.3 = (f32[32,16,128]{2,1,0:T(8,128)S(1)}, f32[32,16,128]{2,1,0:T(8,128)S(1)}, u32[]{:S(2)}, u32[]{:S(2)}) collective-permute-start(f32[32,16,128]{2,1,0:T(8,128)S(1)} %maximum_select_fusion.1), channel_id=1, source_target_pairs={{64,128},{128,64},{65,129},{129,65},{192,194},{194,192},{193,195},... | collective-permute-start | bytes 786440 | tf_op jit(solution)/shard_map/ppermute | solution.py:75
  38.2 0.2 fusion.77
  38.4 0.2 fusion.31
  38.6 0.4 fusion.18
  39.0 0.8 fusion
  40.2 1.6 %collective-permute-done.3 = f32[32,16,128]{2,1,0:T(8,128)S(1)} collective-permute-done((f32[32,16,128]{2,1,0:T(8,128)S(1)}, f32[32,16,128]{2,1,0:T(8,128)S(1)}, u32[]{:S(2)}, u32[]{:S(2)}) %collective-permute-start.3) | collective-permute-done | bytes 262176 | tf_op jit(solution)/shard_map/ppermute | solution.py:75
  41.9 5.4 %collective-permute-start.7 = (f32[32,48,128]{2,1,0:T(8,128)S(1)}, f32[32,48,128]{2,1,0:T(8,128)S(1)}, u32[]{:S(2)}, u32[]{:S(2)}) collective-permute-start(f32[32,48,128]{2,1,0:T(8,128)S(1)} %pad_maximum_fusion), channel_id=1, source_target_pairs={{0,1},{1,0},{2,3},{3,2},{4,5},{5,4},{6,7},{7,6},{8,9},{9,8},{10,11... | collective-permute-start | bytes 2359304 | tf_op jit(solution)/shard_map/ppermute | solution.py:75
  47.5 1.7 %collective-permute-done.7 = f32[32,48,128]{2,1,0:T(8,128)S(1)} collective-permute-done((f32[32,48,128]{2,1,0:T(8,128)S(1)}, f32[32,48,128]{2,1,0:T(8,128)S(1)}, u32[]{:S(2)}, u32[]{:S(2)}) %collective-permute-start.7) | collective-permute-done | bytes 786464 | tf_op jit(solution)/shard_map/ppermute | solution.py:75
  49.2 0.6 fusion.1
  49.8 0.9 convolution_bitcast_fusion.1
  50.7 0.6 fusion.11
  51.3 0.6 fusion.39
  51.9 0.4 fusion.46
  52.3 0.8 convolution_bitcast_fusion.4
  53.1 2.3 %collective-permute-start.8 = (f32[32,48,128]{2,1,0:T(8,128)S(1)}, f32[32,48,128]{2,1,0:T(8,128)S(1)}, u32[]{:S(2)}, u32[]{:S(2)}) collective-permute-start(f32[32,48,128]{2,1,0:T(8,128)S(1)} %convolution_bitcast_fusion.4), channel_id=1, source_target_pairs={{0,1},{1,0},{2,3},{3,2},{4,5},{5,4},{6,7},{7,6},{8,9},{9,8},{10,11... | collective-permute-start | bytes 2359304 | tf_op jit(solution)/shard_map/ppermute | solution.py:75
  55.4 0.4 fusion.52
  55.8 0.8 convolution_bitcast_fusion.5
  56.6 0.7 collective-permute-done.8
  57.4 1.9 %collective-permute-start.10 = (f32[32,16,128]{2,1,0:T(8,128)S(1)}, f32[32,16,128]{2,1,0:T(8,128)S(1)}, u32[]{:S(2)}, u32[]{:S(2)}) collective-permute-start(f32[32,16,128]{2,1,0:T(8,128)S(1)} %get-tuple-element.46), channel_id=1, source_target_pairs={{0,64},{64,0},{1,65},{65,1},{128,192},{192,128},{129,193},{193,129... | collective-permute-start | bytes 786440 | tf_op jit(solution)/shard_map/ppermute | solution.py:75
  59.3 6.0 %collective-permute-start.9 = (f32[32,16,128]{2,1,0:T(8,128)S(1)}, f32[32,16,128]{2,1,0:T(8,128)S(1)}, u32[]{:S(2)}, u32[]{:S(2)}) collective-permute-start(f32[32,16,128]{2,1,0:T(8,128)S(1)} %get-tuple-element.45), channel_id=1, source_target_pairs={{64,128},{128,64},{65,129},{129,65},{192,194},{194,192},{193,195},... | collective-permute-start | bytes 786440 | tf_op jit(solution)/shard_map/ppermute | solution.py:75
  65.3 1.5 collective-permute-done.10
  66.8 4.6 %collective-permute-done.9 = f32[32,16,128]{2,1,0:T(8,128)S(1)} collective-permute-done((f32[32,16,128]{2,1,0:T(8,128)S(1)}, f32[32,16,128]{2,1,0:T(8,128)S(1)}, u32[]{:S(2)}, u32[]{:S(2)}) %collective-permute-start.9) | collective-permute-done | bytes 262176 | tf_op jit(solution)/shard_map/ppermute | solution.py:75
  71.5 3.6 %collective-permute-start.11 = (f32[32,16,128]{2,1,0:T(8,128)S(1)}, f32[32,16,128]{2,1,0:T(8,128)S(1)}, u32[]{:S(2)}, u32[]{:S(2)}) collective-permute-start(f32[32,16,128]{2,1,0:T(8,128)S(1)} %fusion.30), channel_id=1, source_target_pairs={{0,256},{1,257},{2,258},{3,259},{4,260},{5,261},{6,262},{7,263},{8... | collective-permute-start | bytes 786440 | tf_op jit(solution)/shard_map/ppermute | solution.py:75
  75.3 0.2 fusion.86
  75.5 0.2 fusion.75
  75.7 0.7 fusion.28
  76.4 0.2 fusion.54
  76.8 0.8 fusion.13
  77.6 11.8 %collective-permute-done.11 = f32[32,16,128]{2,1,0:T(8,128)S(1)} collective-permute-done((f32[32,16,128]{2,1,0:T(8,128)S(1)}, f32[32,16,128]{2,1,0:T(8,128)S(1)}, u32[]{:S(2)}, u32[]{:S(2)}) %collective-permute-start.11) | collective-permute-done | bytes 262176 | tf_op jit(solution)/shard_map/ppermute | solution.py:75
  89.4 1.9 %collective-permute-start.13 = (f32[32,16,128]{2,1,0:T(8,128)S(1)}, f32[32,16,128]{2,1,0:T(8,128)S(1)}, u32[]{:S(2)}, u32[]{:S(2)}) collective-permute-start(f32[32,16,128]{2,1,0:T(8,128)S(1)} %multiply_multiply_fusion), channel_id=1, source_target_pairs={{0,64},{64,0},{1,65},{65,1},{128,192},{192,128},{129,193},{193,129... | collective-permute-start | bytes 786440 | tf_op jit(solution)/shard_map/ppermute | solution.py:75
  91.4 2.9 %collective-permute-start.12 = (f32[32,16,128]{2,1,0:T(8,128)S(1)}, f32[32,16,128]{2,1,0:T(8,128)S(1)}, u32[]{:S(2)}, u32[]{:S(2)}) collective-permute-start(f32[32,16,128]{2,1,0:T(8,128)S(1)} %multiply_multiply_fusion), channel_id=1, source_target_pairs={{64,128},{128,64},{65,129},{129,65},{192,194},{194,192},{193,195},... | collective-permute-start | bytes 786440 | tf_op jit(solution)/shard_map/ppermute | solution.py:75
  94.3 2.7 %collective-permute-done.13 = f32[32,16,128]{2,1,0:T(8,128)S(1)} collective-permute-done((f32[32,16,128]{2,1,0:T(8,128)S(1)}, f32[32,16,128]{2,1,0:T(8,128)S(1)}, u32[]{:S(2)}, u32[]{:S(2)}) %collective-permute-start.13) | collective-permute-done | bytes 262176 | tf_op jit(solution)/shard_map/ppermute | solution.py:75
  97.0 4.0 %collective-permute-done.12 = f32[32,16,128]{2,1,0:T(8,128)S(1)} collective-permute-done((f32[32,16,128]{2,1,0:T(8,128)S(1)}, f32[32,16,128]{2,1,0:T(8,128)S(1)}, u32[]{:S(2)}, u32[]{:S(2)}) %collective-permute-start.12) | collective-permute-done | bytes 262176 | tf_op jit(solution)/shard_map/ppermute | solution.py:75
  101.1 5.2 %collective-permute-start.14 = (f32[32,48,128]{2,1,0:T(8,128)S(1)}, f32[32,48,128]{2,1,0:T(8,128)S(1)}, u32[]{:S(2)}, u32[]{:S(2)}) collective-permute-start(f32[32,48,128]{2,1,0:T(8,128)S(1)} %pad_maximum_fusion.1), channel_id=1, source_target_pairs={{0,1},{1,0},{2,3},{3,2},{4,5},{5,4},{6,7},{7,6},{8,9},{9,8},{10,11... | collective-permute-start | bytes 2359304 | tf_op jit(solution)/shard_map/ppermute | solution.py:75
  106.2 1.7 %collective-permute-done.14 = f32[32,48,128]{2,1,0:T(8,128)S(1)} collective-permute-done((f32[32,48,128]{2,1,0:T(8,128)S(1)}, f32[32,48,128]{2,1,0:T(8,128)S(1)}, u32[]{:S(2)}, u32[]{:S(2)}) %collective-permute-start.14) | collective-permute-done | bytes 786464 | tf_op jit(solution)/shard_map/ppermute | solution.py:75
  108.0 0.6 fusion.4
  108.5 0.9 convolution_bitcast_fusion
  109.4 0.6 fusion.12
  110.0 0.6 fusion.36
  110.6 0.4 fusion.44
  111.1 0.8 convolution_bitcast_fusion.2
  111.8 2.3 %collective-permute-start.15 = (f32[32,48,128]{2,1,0:T(8,128)S(1)}, f32[32,48,128]{2,1,0:T(8,128)S(1)}, u32[]{:S(2)}, u32[]{:S(2)}) collective-permute-start(f32[32,48,128]{2,1,0:T(8,128)S(1)} %convolution_bitcast_fusion.2), channel_id=1, source_target_pairs={{0,1},{1,0},{2,3},{3,2},{4,5},{5,4},{6,7},{7,6},{8,9},{9,8},{10,11... | collective-permute-start | bytes 2359304 | tf_op jit(solution)/shard_map/ppermute | solution.py:75
  114.1 0.4 fusion.50
  114.6 0.8 convolution_bitcast_fusion.3
  115.3 0.7 collective-permute-done.15
  116.1 1.9 %collective-permute-start.17 = (f32[32,16,128]{2,1,0:T(8,128)S(1)}, f32[32,16,128]{2,1,0:T(8,128)S(1)}, u32[]{:S(2)}, u32[]{:S(2)}) collective-permute-start(f32[32,16,128]{2,1,0:T(8,128)S(1)} %get-tuple-element.44), channel_id=1, source_target_pairs={{0,64},{64,0},{1,65},{65,1},{128,192},{192,128},{129,193},{193,129... | collective-permute-start | bytes 786440 | tf_op jit(solution)/shard_map/ppermute | solution.py:75
  118.1 3.7 %collective-permute-start.16 = (f32[32,16,128]{2,1,0:T(8,128)S(1)}, f32[32,16,128]{2,1,0:T(8,128)S(1)}, u32[]{:S(2)}, u32[]{:S(2)}) collective-permute-start(f32[32,16,128]{2,1,0:T(8,128)S(1)} %get-tuple-element.43), channel_id=1, source_target_pairs={{64,128},{128,64},{65,129},{129,65},{192,194},{194,192},{193,195},... | collective-permute-start | bytes 786440 | tf_op jit(solution)/shard_map/ppermute | solution.py:75
  121.8 3.8 %collective-permute-done.17 = f32[32,16,128]{2,1,0:T(8,128)S(1)} collective-permute-done((f32[32,16,128]{2,1,0:T(8,128)S(1)}, f32[32,16,128]{2,1,0:T(8,128)S(1)}, u32[]{:S(2)}, u32[]{:S(2)}) %collective-permute-start.17) | collective-permute-done | bytes 262176 | tf_op jit(solution)/shard_map/ppermute | solution.py:75
  125.5 4.0 %collective-permute-done.16 = f32[32,16,128]{2,1,0:T(8,128)S(1)} collective-permute-done((f32[32,16,128]{2,1,0:T(8,128)S(1)}, f32[32,16,128]{2,1,0:T(8,128)S(1)}, u32[]{:S(2)}, u32[]{:S(2)}) %collective-permute-start.16) | collective-permute-done | bytes 262176 | tf_op jit(solution)/shard_map/ppermute | solution.py:75
  129.7 5.2 %collective-permute-start.18 = (f32[16,16,128]{2,1,0:T(8,128)S(1)}, f32[16,16,128]{2,1,0:T(8,128)S(1)}, u32[]{:S(2)}, u32[]{:S(2)}) collective-permute-start(f32[16,16,128]{2,1,0:T(8,128)S(1)} %slice_select_fusion.2), channel_id=1, source_target_pairs={{0,256},{1,257},{2,258},{3,259},{4,260},{5,261},{6,262},{7,263},{8... | collective-permute-start | bytes 393224 | tf_op jit(solution)/shard_map/ppermute | solution.py:75
  134.9 8.2 %collective-permute-done.18 = f32[16,16,128]{2,1,0:T(8,128)S(1)} collective-permute-done((f32[16,16,128]{2,1,0:T(8,128)S(1)}, f32[16,16,128]{2,1,0:T(8,128)S(1)}, u32[]{:S(2)}, u32[]{:S(2)}) %collective-permute-start.18) | collective-permute-done | bytes 131104 | tf_op jit(solution)/shard_map/ppermute | solution.py:75
  143.2 2.6 %collective-permute-start.19 = (f32[16,8,128]{2,0,1:T(8,128)S(1)}, f32[16,8,128]{2,0,1:T(8,128)S(1)}, u32[]{:S(2)}, u32[]{:S(2)}) collective-permute-start(f32[16,8,128]{2,0,1:T(8,128)S(1)} %get-tuple-element.37), channel_id=1, source_target_pairs={{0,0},{128,1},{64,64},{192,65},{1,128},{129,129},{65,192},{193,193... | collective-permute-start | bytes 196616 | tf_op jit(solution)/shard_map/ppermute | solution.py:75
  145.8 3.0 %collective-permute-start.20 = (f32[16,8,128]{2,0,1:T(8,128)S(1)}, f32[16,8,128]{2,0,1:T(8,128)S(1)}, u32[]{:S(2)}, u32[]{:S(2)}) collective-permute-start(f32[16,8,128]{2,0,1:T(8,128)S(1)} %get-tuple-element.38), channel_id=1, source_target_pairs={{64,0},{192,1},{0,64},{128,65},{65,128},{193,129},{1,192},{129,193... | collective-permute-start | bytes 196616 | tf_op jit(solution)/shard_map/ppermute | solution.py:75
  148.7 1.5 collective-permute-done.19
  150.2 2.3 %collective-permute-done.20 = f32[16,8,128]{2,0,1:T(8,128)S(1)} collective-permute-done((f32[16,8,128]{2,0,1:T(8,128)S(1)}, f32[16,8,128]{2,0,1:T(8,128)S(1)}, u32[]{:S(2)}, u32[]{:S(2)}) %collective-permute-start.20) | collective-permute-done | bytes 65568 | tf_op jit(solution)/shard_map/ppermute | solution.py:75
  152.6 0.7 copy.12
  (51 shorter events, 2.0 us)
Async XLA Ops:
  0.9 13.2 %collective-permute-start = (f32[8,16,128]{2,1,0:T(8,128)S(1)}, f32[8,16,128]{2,1,0:T(8,128)S(1)}, u32[]{:S(2)}, u32[]{:S(2)}) collective-permute-start(f32[8,16,128]{2,1,0:T(8,128)S(1)} %bitcast.155), channel_id=1, source_target_pairs={{0,0},{1,128},{64,64},{65,192},{128,1},{129,129},{192,65},{193,193... | collective-permute-start | bytes 196616 | tf_op jit(solution)/shard_map/ppermute | solution.py:75
  6.2 8.0 %collective-permute-start.1 = (f32[8,16,128]{2,1,0:T(8,128)S(1)}, f32[8,16,128]{2,1,0:T(8,128)S(1)}, u32[]{:S(2)}, u32[]{:S(2)}) collective-permute-start(f32[8,16,128]{2,1,0:T(8,128)S(1)} %bitcast.156), channel_id=1, source_target_pairs={{0,64},{1,192},{64,0},{65,128},{128,65},{129,193},{192,1},{193,129... | collective-permute-start | bytes 196616 | tf_op jit(solution)/shard_map/ppermute | solution.py:75
  9.9 28.2 %copy-start = (f32[8,3,31]{2,0,1:T(8,128)S(1)}, f32[8,3,31]{2,0,1:T(8,128)}, u32[]{:S(2)}) copy-start(f32[8,3,31]{2,0,1:T(8,128)} %param.6) | copy-start | bytes 8932
  9.9 32.0 %collective-permute-start.5 = (f32[16,64,128]{2,1,0:T(8,128)S(1)}, f32[16,64,128]{2,1,0:T(8,128)S(1)}, u32[]{:S(2)}, u32[]{:S(2)}) collective-permute-start(f32[16,64,128]{2,1,0:T(8,128)S(1)} %get-tuple-element.42), channel_id=1, source_target_pairs={{0,0},{1,128},{64,64},{65,192},{128,1},{129,129},{192,65},{193,193... | collective-permute-start | bytes 1572872 | tf_op jit(solution)/shard_map/ppermute | solution.py:75
  14.1 25.7 %copy-start.1 = (s32[8,16]{1,0:T(8,128)S(1)}, s32[8,16]{1,0:T(8,128)}, u32[]{:S(2)}) copy-start(s32[8,16]{1,0:T(8,128)} %param.7) | copy-start | bytes 1540
  14.2 13.6 %collective-permute-start.2 = (f32[16,16,128]{2,1,0:T(8,128)S(1)}, f32[16,16,128]{2,1,0:T(8,128)S(1)}, u32[]{:S(2)}, u32[]{:S(2)}) collective-permute-start(f32[16,16,128]{2,1,0:T(8,128)S(1)} %pad_maximum_fusion.2), channel_id=1, source_target_pairs={{0,256},{1,257},{2,258},{3,259},{4,260},{5,261},{6,262},{7,263},{8... | collective-permute-start | bytes 393224 | tf_op jit(solution)/shard_map/ppermute | solution.py:75
  24.9 17.0 %collective-permute-start.6 = (f32[16,64,128]{2,1,0:T(8,128)S(1)}, f32[16,64,128]{2,1,0:T(8,128)S(1)}, u32[]{:S(2)}, u32[]{:S(2)}) collective-permute-start(f32[16,64,128]{2,1,0:T(8,128)S(1)} %get-tuple-element.25), channel_id=1, source_target_pairs={{0,64},{1,192},{64,0},{65,128},{128,65},{129,193},{192,1},{193,129... | collective-permute-start | bytes 1572872 | tf_op jit(solution)/shard_map/ppermute | solution.py:75
  27.8 12.5 %collective-permute-start.4 = (f32[32,16,128]{2,1,0:T(8,128)S(1)}, f32[32,16,128]{2,1,0:T(8,128)S(1)}, u32[]{:S(2)}, u32[]{:S(2)}) collective-permute-start(f32[32,16,128]{2,1,0:T(8,128)S(1)} %maximum_select_fusion.1), channel_id=1, source_target_pairs={{0,64},{64,0},{1,65},{65,1},{128,192},{192,128},{129,193},{193,129... | collective-permute-start | bytes 786440 | tf_op jit(solution)/shard_map/ppermute | solution.py:75
  30.4 11.5 %collective-permute-start.3 = (f32[32,16,128]{2,1,0:T(8,128)S(1)}, f32[32,16,128]{2,1,0:T(8,128)S(1)}, u32[]{:S(2)}, u32[]{:S(2)}) collective-permute-start(f32[32,16,128]{2,1,0:T(8,128)S(1)} %maximum_select_fusion.1), channel_id=1, source_target_pairs={{64,128},{128,64},{65,129},{129,65},{192,194},{194,192},{193,195},... | collective-permute-start | bytes 786440 | tf_op jit(solution)/shard_map/ppermute | solution.py:75
  41.9 7.3 %collective-permute-start.7 = (f32[32,48,128]{2,1,0:T(8,128)S(1)}, f32[32,48,128]{2,1,0:T(8,128)S(1)}, u32[]{:S(2)}, u32[]{:S(2)}) collective-permute-start(f32[32,48,128]{2,1,0:T(8,128)S(1)} %pad_maximum_fusion), channel_id=1, source_target_pairs={{0,1},{1,0},{2,3},{3,2},{4,5},{5,4},{6,7},{7,6},{8,9},{9,8},{10,11... | collective-permute-start | bytes 2359304 | tf_op jit(solution)/shard_map/ppermute | solution.py:75
  53.1 4.2 %collective-permute-start.8 = (f32[32,48,128]{2,1,0:T(8,128)S(1)}, f32[32,48,128]{2,1,0:T(8,128)S(1)}, u32[]{:S(2)}, u32[]{:S(2)}) collective-permute-start(f32[32,48,128]{2,1,0:T(8,128)S(1)} %convolution_bitcast_fusion.4), channel_id=1, source_target_pairs={{0,1},{1,0},{2,3},{3,2},{4,5},{5,4},{6,7},{7,6},{8,9},{9,8},{10,11... | collective-permute-start | bytes 2359304 | tf_op jit(solution)/shard_map/ppermute | solution.py:75
  57.4 9.4 %collective-permute-start.10 = (f32[32,16,128]{2,1,0:T(8,128)S(1)}, f32[32,16,128]{2,1,0:T(8,128)S(1)}, u32[]{:S(2)}, u32[]{:S(2)}) collective-permute-start(f32[32,16,128]{2,1,0:T(8,128)S(1)} %get-tuple-element.46), channel_id=1, source_target_pairs={{0,64},{64,0},{1,65},{65,1},{128,192},{192,128},{129,193},{193,129... | collective-permute-start | bytes 786440 | tf_op jit(solution)/shard_map/ppermute | solution.py:75
  59.3 12.1 %collective-permute-start.9 = (f32[32,16,128]{2,1,0:T(8,128)S(1)}, f32[32,16,128]{2,1,0:T(8,128)S(1)}, u32[]{:S(2)}, u32[]{:S(2)}) collective-permute-start(f32[32,16,128]{2,1,0:T(8,128)S(1)} %get-tuple-element.45), channel_id=1, source_target_pairs={{64,128},{128,64},{65,129},{129,65},{192,194},{194,192},{193,195},... | collective-permute-start | bytes 786440 | tf_op jit(solution)/shard_map/ppermute | solution.py:75
  71.5 17.9 %collective-permute-start.11 = (f32[32,16,128]{2,1,0:T(8,128)S(1)}, f32[32,16,128]{2,1,0:T(8,128)S(1)}, u32[]{:S(2)}, u32[]{:S(2)}) collective-permute-start(f32[32,16,128]{2,1,0:T(8,128)S(1)} %fusion.30), channel_id=1, source_target_pairs={{0,256},{1,257},{2,258},{3,259},{4,260},{5,261},{6,262},{7,263},{8... | collective-permute-start | bytes 786440 | tf_op jit(solution)/shard_map/ppermute | solution.py:75
  89.4 7.5 %collective-permute-start.13 = (f32[32,16,128]{2,1,0:T(8,128)S(1)}, f32[32,16,128]{2,1,0:T(8,128)S(1)}, u32[]{:S(2)}, u32[]{:S(2)}) collective-permute-start(f32[32,16,128]{2,1,0:T(8,128)S(1)} %multiply_multiply_fusion), channel_id=1, source_target_pairs={{0,64},{64,0},{1,65},{65,1},{128,192},{192,128},{129,193},{193,129... | collective-permute-start | bytes 786440 | tf_op jit(solution)/shard_map/ppermute | solution.py:75
  91.4 9.7 %collective-permute-start.12 = (f32[32,16,128]{2,1,0:T(8,128)S(1)}, f32[32,16,128]{2,1,0:T(8,128)S(1)}, u32[]{:S(2)}, u32[]{:S(2)}) collective-permute-start(f32[32,16,128]{2,1,0:T(8,128)S(1)} %multiply_multiply_fusion), channel_id=1, source_target_pairs={{64,128},{128,64},{65,129},{129,65},{192,194},{194,192},{193,195},... | collective-permute-start | bytes 786440 | tf_op jit(solution)/shard_map/ppermute | solution.py:75
  101.1 6.9 %collective-permute-start.14 = (f32[32,48,128]{2,1,0:T(8,128)S(1)}, f32[32,48,128]{2,1,0:T(8,128)S(1)}, u32[]{:S(2)}, u32[]{:S(2)}) collective-permute-start(f32[32,48,128]{2,1,0:T(8,128)S(1)} %pad_maximum_fusion.1), channel_id=1, source_target_pairs={{0,1},{1,0},{2,3},{3,2},{4,5},{5,4},{6,7},{7,6},{8,9},{9,8},{10,11... | collective-permute-start | bytes 2359304 | tf_op jit(solution)/shard_map/ppermute | solution.py:75
  111.8 4.2 %collective-permute-start.15 = (f32[32,48,128]{2,1,0:T(8,128)S(1)}, f32[32,48,128]{2,1,0:T(8,128)S(1)}, u32[]{:S(2)}, u32[]{:S(2)}) collective-permute-start(f32[32,48,128]{2,1,0:T(8,128)S(1)} %convolution_bitcast_fusion.2), channel_id=1, source_target_pairs={{0,1},{1,0},{2,3},{3,2},{4,5},{5,4},{6,7},{7,6},{8,9},{9,8},{10,11... | collective-permute-start | bytes 2359304 | tf_op jit(solution)/shard_map/ppermute | solution.py:75
  116.1 9.4 %collective-permute-start.17 = (f32[32,16,128]{2,1,0:T(8,128)S(1)}, f32[32,16,128]{2,1,0:T(8,128)S(1)}, u32[]{:S(2)}, u32[]{:S(2)}) collective-permute-start(f32[32,16,128]{2,1,0:T(8,128)S(1)} %get-tuple-element.44), channel_id=1, source_target_pairs={{0,64},{64,0},{1,65},{65,1},{128,192},{192,128},{129,193},{193,129... | collective-permute-start | bytes 786440 | tf_op jit(solution)/shard_map/ppermute | solution.py:75
  118.1 11.5 %collective-permute-start.16 = (f32[32,16,128]{2,1,0:T(8,128)S(1)}, f32[32,16,128]{2,1,0:T(8,128)S(1)}, u32[]{:S(2)}, u32[]{:S(2)}) collective-permute-start(f32[32,16,128]{2,1,0:T(8,128)S(1)} %get-tuple-element.43), channel_id=1, source_target_pairs={{64,128},{128,64},{65,129},{129,65},{192,194},{194,192},{193,195},... | collective-permute-start | bytes 786440 | tf_op jit(solution)/shard_map/ppermute | solution.py:75
  129.7 13.4 %collective-permute-start.18 = (f32[16,16,128]{2,1,0:T(8,128)S(1)}, f32[16,16,128]{2,1,0:T(8,128)S(1)}, u32[]{:S(2)}, u32[]{:S(2)}) collective-permute-start(f32[16,16,128]{2,1,0:T(8,128)S(1)} %slice_select_fusion.2), channel_id=1, source_target_pairs={{0,256},{1,257},{2,258},{3,259},{4,260},{5,261},{6,262},{7,263},{8... | collective-permute-start | bytes 393224 | tf_op jit(solution)/shard_map/ppermute | solution.py:75
  143.2 7.1 %collective-permute-start.19 = (f32[16,8,128]{2,0,1:T(8,128)S(1)}, f32[16,8,128]{2,0,1:T(8,128)S(1)}, u32[]{:S(2)}, u32[]{:S(2)}) collective-permute-start(f32[16,8,128]{2,0,1:T(8,128)S(1)} %get-tuple-element.37), channel_id=1, source_target_pairs={{0,0},{128,1},{64,64},{192,65},{1,128},{129,129},{65,192},{193,193... | collective-permute-start | bytes 196616 | tf_op jit(solution)/shard_map/ppermute | solution.py:75
  145.8 6.8 %collective-permute-start.20 = (f32[16,8,128]{2,0,1:T(8,128)S(1)}, f32[16,8,128]{2,0,1:T(8,128)S(1)}, u32[]{:S(2)}, u32[]{:S(2)}) collective-permute-start(f32[16,8,128]{2,0,1:T(8,128)S(1)} %get-tuple-element.38), channel_id=1, source_target_pairs={{64,0},{192,1},{0,64},{128,65},{65,128},{193,129},{1,192},{129,193... | collective-permute-start | bytes 196616 | tf_op jit(solution)/shard_map/ppermute | solution.py:75

commit v12 on v11

--- a/solution.py
+++ b/solution.py
@@ -113,7 +113,7 @@
     )
     current = by_h(quarter, send(quarter, SWAP_H), h)
     images = [piece(observed[0], turn, 0) for turn in (0, 1)]
-    images[1], _ = lax.optimization_barrier((images[1], quarter))
+    *images, _ = lax.optimization_barrier((*images, quarter))
     images = [send(image, SPREAD[turn]) for turn, image in enumerate(images)]
     psf_taps, intersection, current = lax.optimization_barrier((psf_taps, intersection, current))
 
@@ -207,7 +207,7 @@
 
     quarter = jnp.swapaxes(quarter, 0, 1)
     result = ordered([quarter[:, :block], quarter[:, block:]], even)
-    result = lax.optimization_barrier(tuple(result))
+    result = [with_layout_constraint(value, Layout((0, 1, 2))) for value in result]
     result = [send(value, reverse(route)) for value, route in zip(result, SPREAD)]
     return jnp.concatenate(ordered(result, x % 2 == 0), 0)
 

time: 155 us -> 159 us (1.026)
  the two profiles are of different devices: /device:TPU:57 before, /device:TPU:33 now
where the time goes in v12:
time: 159 us; the launch traced here: 158 us
  starting transfers between devices  78.1 us (49%)
  waiting for transfers between devices  56.5 us (36%)
  matrix products  17.2 us (11%)
  other arithmetic  3.1 us (2%)
  local copies, waits for them, and re-layouts  2.48 us (2%)
    ppermute x21, starting transfers between devices, send(): return lax.ppermute(value, AXES, pairs)  78.1 us
    ppermute x21, waiting for transfers between devices, send(): return lax.ppermute(value, AXES, pairs)  56.5 us
  transfers between devices with their start and end apart: 21, of which 15 were waited for; matrix products, arithmetic and copies ran while one was open for 6% of the time, Pallas kernels for 0%

profile of v12, /device:TPU:33, one launch (start us, length us, event | category | flops | bytes accessed | tf_op | source)
XLA Modules:
  0.0 158.2 jit_solution(16047002012957776263)
XLA Ops:
  0.0 1.0 dynamic-slice_bitcast_fusion.3
  1.0 5.2 %collective-permute-start = (f32[8,16,128]{2,0,1:T(8,128)S(1)}, f32[8,16,128]{2,0,1:T(8,128)S(1)}, u32[]{:S(2)}, u32[]{:S(2)}) collective-permute-start(f32[8,16,128]{2,0,1:T(8,128)S(1)} %get-tuple-element.51), channel_id=1, source_target_pairs={{0,0},{1,128},{64,64},{65,192},{128,1},{129,129},{192,65},{193,193... | collective-permute-start | bytes 196616 | tf_op jit(solution)/shard_map/ppermute | solution.py:75
  6.2 2.5 %collective-permute-start.1 = (f32[8,16,128]{2,0,1:T(8,128)S(1)}, f32[8,16,128]{2,0,1:T(8,128)S(1)}, u32[]{:S(2)}, u32[]{:S(2)}) collective-permute-start(f32[8,16,128]{2,0,1:T(8,128)S(1)} %get-tuple-element.52), channel_id=1, source_target_pairs={{0,64},{1,192},{64,0},{65,128},{128,65},{129,193},{192,1},{193,129... | collective-permute-start | bytes 196616 | tf_op jit(solution)/shard_map/ppermute | solution.py:75
  8.9 0.6 subtract_add_fusion.4
  9.8 3.1 %collective-permute-done.1 = f32[8,16,128]{2,0,1:T(8,128)S(1)} collective-permute-done((f32[8,16,128]{2,0,1:T(8,128)S(1)}, f32[8,16,128]{2,0,1:T(8,128)S(1)}, u32[]{:S(2)}, u32[]{:S(2)}) %collective-permute-start.1) | collective-permute-done | bytes 65568 | tf_op jit(solution)/shard_map/ppermute | solution.py:75
  13.1 10.6 %collective-permute-start.2 = (f32[16,16,128]{2,0,1:T(8,128)S(1)}, f32[16,16,128]{2,0,1:T(8,128)S(1)}, u32[]{:S(2)}, u32[]{:S(2)}) collective-permute-start(f32[16,16,128]{2,0,1:T(8,128)S(1)} %pad_maximum_fusion.2), channel_id=1, source_target_pairs={{0,256},{1,257},{2,258},{3,259},{4,260},{5,261},{6,262},{7,263},{8... | collective-permute-start | bytes 393224 | tf_op jit(solution)/shard_map/ppermute | solution.py:75
  23.8 1.9 %collective-permute-start.5 = (f32[16,64,128]{2,1,0:T(8,128)S(1)}, f32[16,64,128]{2,1,0:T(8,128)S(1)}, u32[]{:S(2)}, u32[]{:S(2)}) collective-permute-start(f32[16,64,128]{2,1,0:T(8,128)S(1)} %get-tuple-element.24), channel_id=1, source_target_pairs={{0,0},{1,128},{64,64},{65,192},{128,1},{129,129},{192,65},{193,193... | collective-permute-start | bytes 1572872 | tf_op jit(solution)/shard_map/ppermute | solution.py:75
  25.8 3.7 %collective-permute-start.6 = (f32[16,64,128]{2,1,0:T(8,128)S(1)}, f32[16,64,128]{2,1,0:T(8,128)S(1)}, u32[]{:S(2)}, u32[]{:S(2)}) collective-permute-start(f32[16,64,128]{2,1,0:T(8,128)S(1)} %get-tuple-element.25), channel_id=1, source_target_pairs={{0,64},{1,192},{64,0},{65,128},{128,65},{129,193},{192,1},{193,129... | collective-permute-start | bytes 1572872 | tf_op jit(solution)/shard_map/ppermute | solution.py:75
  29.5 3.8 %collective-permute-start.3 = (f32[32,16,128]{2,0,1:T(8,128)S(1)}, f32[32,16,128]{2,0,1:T(8,128)S(1)}, u32[]{:S(2)}, u32[]{:S(2)}) collective-permute-start(f32[32,16,128]{2,0,1:T(8,128)S(1)} %maximum_select_fusion.1), channel_id=1, source_target_pairs={{64,128},{128,64},{65,129},{129,65},{192,194},{194,192},{193,195},... | collective-permute-start | bytes 786440 | tf_op jit(solution)/shard_map/ppermute | solution.py:75
  33.2 1.9 %collective-permute-start.4 = (f32[32,16,128]{2,0,1:T(8,128)S(1)}, f32[32,16,128]{2,0,1:T(8,128)S(1)}, u32[]{:S(2)}, u32[]{:S(2)}) collective-permute-start(f32[32,16,128]{2,0,1:T(8,128)S(1)} %maximum_select_fusion.1), channel_id=1, source_target_pairs={{0,64},{64,0},{1,65},{65,1},{128,192},{192,128},{129,193},{193,129... | collective-permute-start | bytes 786440 | tf_op jit(solution)/shard_map/ppermute | solution.py:75
  35.5 0.4 fusion.12
  35.9 0.8 fusion
  36.7 0.9 fusion.25
  37.7 0.9 fusion.8
  38.7 1.2 collective-permute-done.3
  39.9 3.2 %collective-permute-done.4 = f32[32,16,128]{2,0,1:T(8,128)S(1)} collective-permute-done((f32[32,16,128]{2,0,1:T(8,128)S(1)}, f32[32,16,128]{2,0,1:T(8,128)S(1)}, u32[]{:S(2)}, u32[]{:S(2)}) %collective-permute-start.4) | collective-permute-done | bytes 262176 | tf_op jit(solution)/shard_map/ppermute | solution.py:75
  43.2 2.6 %collective-permute-start.7 = (f32[32,48,128]{2,0,1:T(8,128)S(1)}, f32[32,48,128]{2,0,1:T(8,128)S(1)}, u32[]{:S(2)}, u32[]{:S(2)}) collective-permute-start(f32[32,48,128]{2,0,1:T(8,128)S(1)} %pad_maximum_fusion), channel_id=1, source_target_pairs={{0,1},{1,0},{2,3},{3,2},{4,5},{5,4},{6,7},{7,6},{8,9},{9,8},{10,11... | collective-permute-start | bytes 2359304 | tf_op jit(solution)/shard_map/ppermute | solution.py:75
  46.0 1.7 %collective-permute-done.7 = f32[32,48,128]{2,0,1:T(8,128)S(1)} collective-permute-done((f32[32,48,128]{2,0,1:T(8,128)S(1)}, f32[32,48,128]{2,0,1:T(8,128)S(1)}, u32[]{:S(2)}, u32[]{:S(2)}) %collective-permute-start.7) | collective-permute-done | bytes 786464 | tf_op jit(solution)/shard_map/ppermute | solution.py:75
  47.9 1.5 fusion.3
  49.3 0.9 convolution_bitcast_fusion.1
  50.2 0.6 fusion.5
  50.8 0.6 fusion.33
  51.4 0.4 fusion.39
  51.9 0.8 convolution_bitcast_fusion.4
  52.6 0.3 copy.75
  52.9 2.3 %collective-permute-start.8 = (f32[32,48,128]{2,0,1:T(8,128)S(1)}, f32[32,48,128]{2,0,1:T(8,128)S(1)}, u32[]{:S(2)}, u32[]{:S(2)}) collective-permute-start(f32[32,48,128]{2,0,1:T(8,128)S(1)} %bitcast.157), channel_id=1, source_target_pairs={{0,1},{1,0},{2,3},{3,2},{4,5},{5,4},{6,7},{7,6},{8,9},{9,8},{10,11... | collective-permute-start | bytes 2359304 | tf_op jit(solution)/shard_map/ppermute | solution.py:75
  55.2 0.4 fusion.45
  55.6 0.8 convolution_bitcast_fusion.5
  56.4 0.3 copy.76
  56.7 0.4 collective-permute-done.8
  57.3 6.2 %collective-permute-start.10 = (f32[32,16,128]{2,0,1:T(8,128)S(1)}, f32[32,16,128]{2,0,1:T(8,128)S(1)}, u32[]{:S(2)}, u32[]{:S(2)}) collective-permute-start(f32[32,16,128]{2,0,1:T(8,128)S(1)} %get-tuple-element.44), channel_id=1, source_target_pairs={{0,64},{64,0},{1,65},{65,1},{128,192},{192,128},{129,193},{193,129... | collective-permute-start | bytes 786440 | tf_op jit(solution)/shard_map/ppermute | solution.py:75
  63.5 1.9 %collective-permute-start.9 = (f32[32,16,128]{2,0,1:T(8,128)S(1)}, f32[32,16,128]{2,0,1:T(8,128)S(1)}, u32[]{:S(2)}, u32[]{:S(2)}) collective-permute-start(f32[32,16,128]{2,0,1:T(8,128)S(1)} %get-tuple-element.43), channel_id=1, source_target_pairs={{64,128},{128,64},{65,129},{129,65},{192,194},{194,192},{193,195},... | collective-permute-start | bytes 786440 | tf_op jit(solution)/shard_map/ppermute | solution.py:75
  65.4 4.4 %collective-permute-done.10 = f32[32,16,128]{2,0,1:T(8,128)S(1)} collective-permute-done((f32[32,16,128]{2,0,1:T(8,128)S(1)}, f32[32,16,128]{2,0,1:T(8,128)S(1)}, u32[]{:S(2)}, u32[]{:S(2)}) %collective-permute-start.10) | collective-permute-done | bytes 262176 | tf_op jit(solution)/shard_map/ppermute | solution.py:75
  69.8 6.0 %collective-permute-done.9 = f32[32,16,128]{2,0,1:T(8,128)S(1)} collective-permute-done((f32[32,16,128]{2,0,1:T(8,128)S(1)}, f32[32,16,128]{2,0,1:T(8,128)S(1)}, u32[]{:S(2)}, u32[]{:S(2)}) %collective-permute-start.9) | collective-permute-done | bytes 262176 | tf_op jit(solution)/shard_map/ppermute | solution.py:75
  75.9 1.9 %collective-permute-start.11 = (f32[32,16,128]{2,0,1:T(8,128)S(1)}, f32[32,16,128]{2,0,1:T(8,128)S(1)}, u32[]{:S(2)}, u32[]{:S(2)}) collective-permute-start(f32[32,16,128]{2,0,1:T(8,128)S(1)} %fusion.24), channel_id=1, source_target_pairs={{0,256},{1,257},{2,258},{3,259},{4,260},{5,261},{6,262},{7,263},{8... | collective-permute-start | bytes 786440 | tf_op jit(solution)/shard_map/ppermute | solution.py:75
  78.2 0.7 fusion.22
  79.9 0.6 fusion.7
  80.5 9.9 %collective-permute-done.11 = f32[32,16,128]{2,0,1:T(8,128)S(1)} collective-permute-done((f32[32,16,128]{2,0,1:T(8,128)S(1)}, f32[32,16,128]{2,0,1:T(8,128)S(1)}, u32[]{:S(2)}, u32[]{:S(2)}) %collective-permute-start.11) | collective-permute-done | bytes 262176 | tf_op jit(solution)/shard_map/ppermute | solution.py:75
  90.5 7.0 %collective-permute-start.12 = (f32[32,16,128]{2,0,1:T(8,128)S(1)}, f32[32,16,128]{2,0,1:T(8,128)S(1)}, u32[]{:S(2)}, u32[]{:S(2)}) collective-permute-start(f32[32,16,128]{2,0,1:T(8,128)S(1)} %multiply_multiply_fusion), channel_id=1, source_target_pairs={{64,128},{128,64},{65,129},{129,65},{192,194},{194,192},{193,195},... | collective-permute-start | bytes 786440 | tf_op jit(solution)/shard_map/ppermute | solution.py:75
  97.5 1.9 %collective-permute-start.13 = (f32[32,16,128]{2,0,1:T(8,128)S(1)}, f32[32,16,128]{2,0,1:T(8,128)S(1)}, u32[]{:S(2)}, u32[]{:S(2)}) collective-permute-start(f32[32,16,128]{2,0,1:T(8,128)S(1)} %multiply_multiply_fusion), channel_id=1, source_target_pairs={{0,64},{64,0},{1,65},{65,1},{128,192},{192,128},{129,193},{193,129... | collective-permute-start | bytes 786440 | tf_op jit(solution)/shard_map/ppermute | solution.py:75
  99.5 3.2 %collective-permute-done.12 = f32[32,16,128]{2,0,1:T(8,128)S(1)} collective-permute-done((f32[32,16,128]{2,0,1:T(8,128)S(1)}, f32[32,16,128]{2,0,1:T(8,128)S(1)}, u32[]{:S(2)}, u32[]{:S(2)}) %collective-permute-start.12) | collective-permute-done | bytes 262176 | tf_op jit(solution)/shard_map/ppermute | solution.py:75
  102.7 3.8 %collective-permute-done.13 = f32[32,16,128]{2,0,1:T(8,128)S(1)} collective-permute-done((f32[32,16,128]{2,0,1:T(8,128)S(1)}, f32[32,16,128]{2,0,1:T(8,128)S(1)}, u32[]{:S(2)}, u32[]{:S(2)}) %collective-permute-start.13) | collective-permute-done | bytes 262176 | tf_op jit(solution)/shard_map/ppermute | solution.py:75
  106.6 3.8 %collective-permute-start.14 = (f32[32,48,128]{2,0,1:T(8,128)S(1)}, f32[32,48,128]{2,0,1:T(8,128)S(1)}, u32[]{:S(2)}, u32[]{:S(2)}) collective-permute-start(f32[32,48,128]{2,0,1:T(8,128)S(1)} %pad_maximum_fusion.1), channel_id=1, source_target_pairs={{0,1},{1,0},{2,3},{3,2},{4,5},{5,4},{6,7},{7,6},{8,9},{9,8},{10,11... | collective-permute-start | bytes 2359304 | tf_op jit(solution)/shard_map/ppermute | solution.py:75
  110.3 1.7 %collective-permute-done.14 = f32[32,48,128]{2,0,1:T(8,128)S(1)} collective-permute-done((f32[32,48,128]{2,0,1:T(8,128)S(1)}, f32[32,48,128]{2,0,1:T(8,128)S(1)}, u32[]{:S(2)}, u32[]{:S(2)}) %collective-permute-start.14) | collective-permute-done | bytes 786464 | tf_op jit(solution)/shard_map/ppermute | solution.py:75
  112.2 1.5 fusion.1
  113.6 0.9 convolution_bitcast_fusion
  114.5 0.6 fusion.6
  115.1 0.6 fusion.30
  115.7 0.4 fusion.37
  116.2 0.8 convolution_bitcast_fusion.2
  117.2 2.3 %collective-permute-start.15 = (f32[32,48,128]{2,0,1:T(8,128)S(1)}, f32[32,48,128]{2,0,1:T(8,128)S(1)}, u32[]{:S(2)}, u32[]{:S(2)}) collective-permute-start(f32[32,48,128]{2,0,1:T(8,128)S(1)} %bitcast.156), channel_id=1, source_target_pairs={{0,1},{1,0},{2,3},{3,2},{4,5},{5,4},{6,7},{7,6},{8,9},{9,8},{10,11... | collective-permute-start | bytes 2359304 | tf_op jit(solution)/shard_map/ppermute | solution.py:75
  119.5 0.4 fusion.43
  119.9 0.8 convolution_bitcast_fusion.3
  120.7 0.3 copy.74
  120.9 0.4 collective-permute-done.15
  121.6 3.3 %collective-permute-start.16 = (f32[32,16,128]{2,0,1:T(8,128)S(1)}, f32[32,16,128]{2,0,1:T(8,128)S(1)}, u32[]{:S(2)}, u32[]{:S(2)}) collective-permute-start(f32[32,16,128]{2,0,1:T(8,128)S(1)} %get-tuple-element.41), channel_id=1, source_target_pairs={{64,128},{128,64},{65,129},{129,65},{192,194},{194,192},{193,195},... | collective-permute-start | bytes 786440 | tf_op jit(solution)/shard_map/ppermute | solution.py:75
  124.9 1.9 %collective-permute-start.17 = (f32[32,16,128]{2,0,1:T(8,128)S(1)}, f32[32,16,128]{2,0,1:T(8,128)S(1)}, u32[]{:S(2)}, u32[]{:S(2)}) collective-permute-start(f32[32,16,128]{2,0,1:T(8,128)S(1)} %get-tuple-element.42), channel_id=1, source_target_pairs={{0,64},{64,0},{1,65},{65,1},{128,192},{192,128},{129,193},{193,129... | collective-permute-start | bytes 786440 | tf_op jit(solution)/shard_map/ppermute | solution.py:75
  126.8 7.5 %collective-permute-done.16 = f32[32,16,128]{2,0,1:T(8,128)S(1)} collective-permute-done((f32[32,16,128]{2,0,1:T(8,128)S(1)}, f32[32,16,128]{2,0,1:T(8,128)S(1)}, u32[]{:S(2)}, u32[]{:S(2)}) %collective-permute-start.16) | collective-permute-done | bytes 262176 | tf_op jit(solution)/shard_map/ppermute | solution.py:75
  134.4 4.8 %collective-permute-start.18 = (f32[16,16,128]{2,0,1:T(8,128)S(1)}, f32[16,16,128]{2,0,1:T(8,128)S(1)}, u32[]{:S(2)}, u32[]{:S(2)}) collective-permute-start(f32[16,16,128]{2,0,1:T(8,128)S(1)} %slice_select_fusion.2), channel_id=1, source_target_pairs={{0,256},{1,257},{2,258},{3,259},{4,260},{5,261},{6,262},{7,263},{8... | collective-permute-start | bytes 393224 | tf_op jit(solution)/shard_map/ppermute | solution.py:75
  139.2 4.8 %collective-permute-done.18 = f32[16,16,128]{2,0,1:T(8,128)S(1)} collective-permute-done((f32[16,16,128]{2,0,1:T(8,128)S(1)}, f32[16,16,128]{2,0,1:T(8,128)S(1)}, u32[]{:S(2)}, u32[]{:S(2)}) %collective-permute-start.18) | collective-permute-done | bytes 131104 | tf_op jit(solution)/shard_map/ppermute | solution.py:75
  144.1 6.6 %collective-permute-start.19 = (f32[16,8,128]{2,1,0:T(8,128)S(1)}, f32[16,8,128]{2,1,0:T(8,128)S(1)}, u32[]{:S(2)}, u32[]{:S(2)}) collective-permute-start(f32[16,8,128]{2,1,0:T(8,128)S(1)} %get-tuple-element.47), channel_id=1, source_target_pairs={{0,0},{128,1},{64,64},{192,65},{1,128},{129,129},{65,192},{193,193... | collective-permute-start | bytes 196616 | tf_op jit(solution)/shard_map/ppermute | solution.py:75
  150.7 1.9 %collective-permute-start.20 = (f32[16,8,128]{2,1,0:T(8,128)S(1)}, f32[16,8,128]{2,1,0:T(8,128)S(1)}, u32[]{:S(2)}, u32[]{:S(2)}) collective-permute-start(f32[16,8,128]{2,1,0:T(8,128)S(1)} %get-tuple-element.48), channel_id=1, source_target_pairs={{64,0},{192,1},{0,64},{128,65},{65,128},{193,129},{1,192},{129,193... | collective-permute-start | bytes 196616 | tf_op jit(solution)/shard_map/ppermute | solution.py:75
  152.7 4.9 %collective-permute-done.20 = f32[16,8,128]{2,1,0:T(8,128)S(1)} collective-permute-done((f32[16,8,128]{2,1,0:T(8,128)S(1)}, f32[16,8,128]{2,1,0:T(8,128)S(1)}, u32[]{:S(2)}, u32[]{:S(2)}) %collective-permute-start.20) | collective-permute-done | bytes 65568 | tf_op jit(solution)/shard_map/ppermute | solution.py:75
  157.5 0.7 pad_maximum_fusion.3
  (72 shorter events, 3.7 us)
Async XLA Ops:
  0.0 23.7 %copy-start = (f32[1,32,64,128]{3,2,1,0:T(8,128)S(1)}, f32[1,32,64,128]{3,2,1,0:T(8,128)}, u32[]{:S(2)}) copy-start(f32[1,32,64,128]{3,2,1,0:T(8,128)} %param.5) | copy-start | bytes 3145732
  1.0 8.9 %collective-permute-start = (f32[8,16,128]{2,0,1:T(8,128)S(1)}, f32[8,16,128]{2,0,1:T(8,128)S(1)}, u32[]{:S(2)}, u32[]{:S(2)}) collective-permute-start(f32[8,16,128]{2,0,1:T(8,128)S(1)} %get-tuple-element.51), channel_id=1, source_target_pairs={{0,0},{1,128},{64,64},{65,192},{128,1},{129,129},{192,65},{193,193... | collective-permute-start | bytes 196616 | tf_op jit(solution)/shard_map/ppermute | solution.py:75
  6.2 6.8 %collective-permute-start.1 = (f32[8,16,128]{2,0,1:T(8,128)S(1)}, f32[8,16,128]{2,0,1:T(8,128)S(1)}, u32[]{:S(2)}, u32[]{:S(2)}) collective-permute-start(f32[8,16,128]{2,0,1:T(8,128)S(1)} %get-tuple-element.52), channel_id=1, source_target_pairs={{0,64},{1,192},{64,0},{65,128},{128,65},{129,193},{192,1},{193,129... | collective-permute-start | bytes 196616 | tf_op jit(solution)/shard_map/ppermute | solution.py:75
  8.9 4.1 %copy-start.3 = (pred[48]{0:T(512)(128)(4,1)}, pred[48]{0:T(512)(128)(4,1)S(1)}, u32[]{:S(2)}) copy-start(pred[48]{0:T(512)(128)(4,1)S(1)} %get-tuple-element.37) | copy-start | bytes 148
  9.6 3.5 %copy-start.5 = (s32[48]{0:T(128)}, s32[48]{0:T(128)S(1)}, u32[]{:S(2)}) copy-start(s32[48]{0:T(128)S(1)} %and_select_fusion.2) | copy-start | bytes 580
  9.6 3.5 %copy-start.7 = (s32[32]{0:T(128)}, s32[32]{0:T(128)S(1)}, u32[]{:S(2)}) copy-start(s32[32]{0:T(128)S(1)} %get-tuple-element.58) | copy-start | bytes 388
  9.8 26.8 %copy-start.9 = (s32[2]{0:T(128)}, s32[2]{0:T(128)S(1)}, u32[]{:S(2)}) copy-start(s32[2]{0:T(128)S(1)} %add_add_fusion) | copy-start | bytes 28
  9.8 25.3 %copy-start.1 = (f32[8,3,31]{2,0,1:T(8,128)S(1)}, f32[8,3,31]{2,0,1:T(8,128)}, u32[]{:S(2)}) copy-start(f32[8,3,31]{2,0,1:T(8,128)} %param.6) | copy-start | bytes 8932
  13.1 24.5 %copy-start.2 = (s32[8,16]{1,0:T(8,128)S(1)}, s32[8,16]{1,0:T(8,128)}, u32[]{:S(2)}) copy-start(s32[8,16]{1,0:T(8,128)} %param.7) | copy-start | bytes 1540
  13.1 16.4 %collective-permute-start.2 = (f32[16,16,128]{2,0,1:T(8,128)S(1)}, f32[16,16,128]{2,0,1:T(8,128)S(1)}, u32[]{:S(2)}, u32[]{:S(2)}) collective-permute-start(f32[16,16,128]{2,0,1:T(8,128)S(1)} %pad_maximum_fusion.2), channel_id=1, source_target_pairs={{0,256},{1,257},{2,258},{3,259},{4,260},{5,261},{6,262},{7,263},{8... | collective-permute-start | bytes 393224 | tf_op jit(solution)/shard_map/ppermute | solution.py:75
  23.8 19.4 %collective-permute-start.5 = (f32[16,64,128]{2,1,0:T(8,128)S(1)}, f32[16,64,128]{2,1,0:T(8,128)S(1)}, u32[]{:S(2)}, u32[]{:S(2)}) collective-permute-start(f32[16,64,128]{2,1,0:T(8,128)S(1)} %get-tuple-element.24), channel_id=1, source_target_pairs={{0,0},{1,128},{64,64},{65,192},{128,1},{129,129},{192,65},{193,193... | collective-permute-start | bytes 1572872 | tf_op jit(solution)/shard_map/ppermute | solution.py:75
  25.8 17.5 %collective-permute-start.6 = (f32[16,64,128]{2,1,0:T(8,128)S(1)}, f32[16,64,128]{2,1,0:T(8,128)S(1)}, u32[]{:S(2)}, u32[]{:S(2)}) collective-permute-start(f32[16,64,128]{2,1,0:T(8,128)S(1)} %get-tuple-element.25), channel_id=1, source_target_pairs={{0,64},{1,192},{64,0},{65,128},{128,65},{129,193},{192,1},{193,129... | collective-permute-start | bytes 1572872 | tf_op jit(solution)/shard_map/ppermute | solution.py:75
  29.5 10.4 %collective-permute-start.3 = (f32[32,16,128]{2,0,1:T(8,128)S(1)}, f32[32,16,128]{2,0,1:T(8,128)S(1)}, u32[]{:S(2)}, u32[]{:S(2)}) collective-permute-start(f32[32,16,128]{2,0,1:T(8,128)S(1)} %maximum_select_fusion.1), channel_id=1, source_target_pairs={{64,128},{128,64},{65,129},{129,65},{192,194},{194,192},{193,195},... | collective-permute-start | bytes 786440 | tf_op jit(solution)/shard_map/ppermute | solution.py:75
  33.2 9.9 %collective-permute-start.4 = (f32[32,16,128]{2,0,1:T(8,128)S(1)}, f32[32,16,128]{2,0,1:T(8,128)S(1)}, u32[]{:S(2)}, u32[]{:S(2)}) collective-permute-start(f32[32,16,128]{2,0,1:T(8,128)S(1)} %maximum_select_fusion.1), channel_id=1, source_target_pairs={{0,64},{64,0},{1,65},{65,1},{128,192},{192,128},{129,193},{193,129... | collective-permute-start | bytes 786440 | tf_op jit(solution)/shard_map/ppermute | solution.py:75
  43.2 4.5 %collective-permute-start.7 = (f32[32,48,128]{2,0,1:T(8,128)S(1)}, f32[32,48,128]{2,0,1:T(8,128)S(1)}, u32[]{:S(2)}, u32[]{:S(2)}) collective-permute-start(f32[32,48,128]{2,0,1:T(8,128)S(1)} %pad_maximum_fusion), channel_id=1, source_target_pairs={{0,1},{1,0},{2,3},{3,2},{4,5},{5,4},{6,7},{7,6},{8,9},{9,8},{10,11... | collective-permute-start | bytes 2359304 | tf_op jit(solution)/shard_map/ppermute | solution.py:75
  52.9 4.2 %collective-permute-start.8 = (f32[32,48,128]{2,0,1:T(8,128)S(1)}, f32[32,48,128]{2,0,1:T(8,128)S(1)}, u32[]{:S(2)}, u32[]{:S(2)}) collective-permute-start(f32[32,48,128]{2,0,1:T(8,128)S(1)} %bitcast.157), channel_id=1, source_target_pairs={{0,1},{1,0},{2,3},{3,2},{4,5},{5,4},{6,7},{7,6},{8,9},{9,8},{10,11... | collective-permute-start | bytes 2359304 | tf_op jit(solution)/shard_map/ppermute | solution.py:75
  57.2 20.8 %copy-start.8 = (s32[32]{0:T(128)S(1)}, s32[32]{0:T(128)}, u32[]{:S(2)}) copy-start(s32[32]{0:T(128)} %copy-done.7) | copy-start | bytes 388
  57.2 21.8 %copy-start.4 = (pred[48]{0:T(512)(128)(4,1)S(1)}, pred[48]{0:T(512)(128)(4,1)}, u32[]{:S(2)}) copy-start(pred[48]{0:T(512)(128)(4,1)} %copy-done.3) | copy-start | bytes 148
  57.2 21.7 %copy-start.6 = (s32[48]{0:T(128)S(1)}, s32[48]{0:T(128)}, u32[]{:S(2)}) copy-start(s32[48]{0:T(128)} %copy-done.5) | copy-start | bytes 580
  57.3 12.5 %collective-permute-start.10 = (f32[32,16,128]{2,0,1:T(8,128)S(1)}, f32[32,16,128]{2,0,1:T(8,128)S(1)}, u32[]{:S(2)}, u32[]{:S(2)}) collective-permute-start(f32[32,16,128]{2,0,1:T(8,128)S(1)} %get-tuple-element.44), channel_id=1, source_target_pairs={{0,64},{64,0},{1,65},{65,1},{128,192},{192,128},{129,193},{193,129... | collective-permute-start | bytes 786440 | tf_op jit(solution)/shard_map/ppermute | solution.py:75
  63.5 12.4 %collective-permute-start.9 = (f32[32,16,128]{2,0,1:T(8,128)S(1)}, f32[32,16,128]{2,0,1:T(8,128)S(1)}, u32[]{:S(2)}, u32[]{:S(2)}) collective-permute-start(f32[32,16,128]{2,0,1:T(8,128)S(1)} %get-tuple-element.43), channel_id=1, source_target_pairs={{64,128},{128,64},{65,129},{129,65},{192,194},{194,192},{193,195},... | collective-permute-start | bytes 786440 | tf_op jit(solution)/shard_map/ppermute | solution.py:75
  75.9 14.5 %collective-permute-start.11 = (f32[32,16,128]{2,0,1:T(8,128)S(1)}, f32[32,16,128]{2,0,1:T(8,128)S(1)}, u32[]{:S(2)}, u32[]{:S(2)}) collective-permute-start(f32[32,16,128]{2,0,1:T(8,128)S(1)} %fusion.24), channel_id=1, source_target_pairs={{0,256},{1,257},{2,258},{3,259},{4,260},{5,261},{6,262},{7,263},{8... | collective-permute-start | bytes 786440 | tf_op jit(solution)/shard_map/ppermute | solution.py:75
  90.5 12.2 %collective-permute-start.12 = (f32[32,16,128]{2,0,1:T(8,128)S(1)}, f32[32,16,128]{2,0,1:T(8,128)S(1)}, u32[]{:S(2)}, u32[]{:S(2)}) collective-permute-start(f32[32,16,128]{2,0,1:T(8,128)S(1)} %multiply_multiply_fusion), channel_id=1, source_target_pairs={{64,128},{128,64},{65,129},{129,65},{192,194},{194,192},{193,195},... | collective-permute-start | bytes 786440 | tf_op jit(solution)/shard_map/ppermute | solution.py:75
  97.5 9.0 %collective-permute-start.13 = (f32[32,16,128]{2,0,1:T(8,128)S(1)}, f32[32,16,128]{2,0,1:T(8,128)S(1)}, u32[]{:S(2)}, u32[]{:S(2)}) collective-permute-start(f32[32,16,128]{2,0,1:T(8,128)S(1)} %multiply_multiply_fusion), channel_id=1, source_target_pairs={{0,64},{64,0},{1,65},{65,1},{128,192},{192,128},{129,193},{193,129... | collective-permute-start | bytes 786440 | tf_op jit(solution)/shard_map/ppermute | solution.py:75
  106.6 5.5 %collective-permute-start.14 = (f32[32,48,128]{2,0,1:T(8,128)S(1)}, f32[32,48,128]{2,0,1:T(8,128)S(1)}, u32[]{:S(2)}, u32[]{:S(2)}) collective-permute-start(f32[32,48,128]{2,0,1:T(8,128)S(1)} %pad_maximum_fusion.1), channel_id=1, source_target_pairs={{0,1},{1,0},{2,3},{3,2},{4,5},{5,4},{6,7},{7,6},{8,9},{9,8},{10,11... | collective-permute-start | bytes 2359304 | tf_op jit(solution)/shard_map/ppermute | solution.py:75
  117.2 4.2 %collective-permute-start.15 = (f32[32,48,128]{2,0,1:T(8,128)S(1)}, f32[32,48,128]{2,0,1:T(8,128)S(1)}, u32[]{:S(2)}, u32[]{:S(2)}) collective-permute-start(f32[32,48,128]{2,0,1:T(8,128)S(1)} %bitcast.156), channel_id=1, source_target_pairs={{0,1},{1,0},{2,3},{3,2},{4,5},{5,4},{6,7},{7,6},{8,9},{9,8},{10,11... | collective-permute-start | bytes 2359304 | tf_op jit(solution)/shard_map/ppermute | solution.py:75
  121.6 12.7 %collective-permute-start.16 = (f32[32,16,128]{2,0,1:T(8,128)S(1)}, f32[32,16,128]{2,0,1:T(8,128)S(1)}, u32[]{:S(2)}, u32[]{:S(2)}) collective-permute-start(f32[32,16,128]{2,0,1:T(8,128)S(1)} %get-tuple-element.41), channel_id=1, source_target_pairs={{64,128},{128,64},{65,129},{129,65},{192,194},{194,192},{193,195},... | collective-permute-start | bytes 786440 | tf_op jit(solution)/shard_map/ppermute | solution.py:75
  124.9 9.4 %collective-permute-start.17 = (f32[32,16,128]{2,0,1:T(8,128)S(1)}, f32[32,16,128]{2,0,1:T(8,128)S(1)}, u32[]{:S(2)}, u32[]{:S(2)}) collective-permute-start(f32[32,16,128]{2,0,1:T(8,128)S(1)} %get-tuple-element.42), channel_id=1, source_target_pairs={{0,64},{64,0},{1,65},{65,1},{128,192},{192,128},{129,193},{193,129... | collective-permute-start | bytes 786440 | tf_op jit(solution)/shard_map/ppermute | solution.py:75
  134.4 9.7 %collective-permute-start.18 = (f32[16,16,128]{2,0,1:T(8,128)S(1)}, f32[16,16,128]{2,0,1:T(8,128)S(1)}, u32[]{:S(2)}, u32[]{:S(2)}) collective-permute-start(f32[16,16,128]{2,0,1:T(8,128)S(1)} %slice_select_fusion.2), channel_id=1, source_target_pairs={{0,256},{1,257},{2,258},{3,259},{4,260},{5,261},{6,262},{7,263},{8... | collective-permute-start | bytes 393224 | tf_op jit(solution)/shard_map/ppermute | solution.py:75
  144.1 8.5 %collective-permute-start.19 = (f32[16,8,128]{2,1,0:T(8,128)S(1)}, f32[16,8,128]{2,1,0:T(8,128)S(1)}, u32[]{:S(2)}, u32[]{:S(2)}) collective-permute-start(f32[16,8,128]{2,1,0:T(8,128)S(1)} %get-tuple-element.47), channel_id=1, source_target_pairs={{0,0},{128,1},{64,64},{192,65},{1,128},{129,129},{65,192},{193,193... | collective-permute-start | bytes 196616 | tf_op jit(solution)/shard_map/ppermute | solution.py:75
  150.7 6.8 %collective-permute-start.20 = (f32[16,8,128]{2,1,0:T(8,128)S(1)}, f32[16,8,128]{2,1,0:T(8,128)S(1)}, u32[]{:S(2)}, u32[]{:S(2)}) collective-permute-start(f32[16,8,128]{2,1,0:T(8,128)S(1)} %get-tuple-element.48), channel_id=1, source_target_pairs={{64,0},{192,1},{0,64},{128,65},{65,128},{193,129},{1,192},{129,193... | collective-permute-start | bytes 196616 | tf_op jit(solution)/shard_map/ppermute | solution.py:75

commit v13 on v11

--- a/solution.py
+++ b/solution.py
@@ -192,8 +192,14 @@
             )
             for columns in (mat_own, mat_other)
         )
-        part = lax.optimization_barrier(own_part) + send(other_part, SWAP_CORE)
-        part = part[:, SLAB : 2 * SLAB] + send(part[:, :SLAB], ODD) + send(part[:, 2 * SLAB :], EVEN)
+        own_part = lax.optimization_barrier(own_part)
+        other_part = send(other_part, SWAP_CORE)
+        to_odd, kept, to_even = (
+            own_part[:, start : start + SLAB] + other_part[:, start : start + SLAB]
+            for start in range(0, 3 * SLAB, SLAB)
+        )
+        terms = [kept, send(to_odd, ODD), send(to_even, EVEN)]
+        part = sum(terms)
         if iteration == 0:
             scale = scale_of(*lax.optimization_barrier((psf_taps, intersection, part))[:2])
         if iteration < ITERS - 1:
@@ -202,8 +208,8 @@
     def own_half(value, mine):
         return jnp.where((h == 0) == mine, value[: 2 * block], value[2 * block :])
 
-    total = own_half(part, True) + send(own_half(part, False), SWAP_H)
-    quarter = own_half(current, True) * (total + 1.0) * own_half(scale, True)
+    far, near = (sum(own_half(term, mine) for term in terms) for mine in (False, True))
+    quarter = own_half(current, True) * (near + send(far, SWAP_H) + 1.0) * own_half(scale, True)
 
     quarter = jnp.swapaxes(quarter, 0, 1)
     result = ordered([quarter[:, :block], quarter[:, block:]], even)

time: 155 us -> 154 us (level)
  starting transfers between devices: 83.1 us -> 77.1 us
  waiting for transfers between devices: 50.8 us -> 56.5 us
    ppermute x21, starting transfers between devices: 83.1 us -> 77.1 us  [send(): return lax.ppermute(value, AXES, pairs)]
    ppermute x21, waiting for transfers between devices: 50.8 us -> 56.5 us  [send(): return lax.ppermute(value, AXES, pairs)]
where the time goes in v13:
time: 154 us; the launch traced here: 153 us
  starting transfers between devices  77.1 us (50%)
  waiting for transfers between devices  56.5 us (37%)
  matrix products  14.2 us (9%)
  local copies, waits for them, and re-layouts  3.05 us (2%)
    ppermute x21, starting transfers between devices, send(): return lax.ppermute(value, AXES, pairs)  77.1 us
    ppermute x21, waiting for transfers between devices, send(): return lax.ppermute(value, AXES, pairs)  56.5 us
  transfers between devices with their start and end apart: 21, of which 15 were waited for; matrix products, arithmetic and copies ran while one was open for 6% of the time, Pallas kernels for 0%

profile of v13, /device:TPU:57, one launch (start us, length us, event | category | flops | bytes accessed | tf_op | source)
XLA Modules:
  0.0 153.0 jit_solution(2044513519598827566)
XLA Ops:
  0.0 0.9 constant_dynamic-slice_fusion.1
  0.9 5.2 %collective-permute-start = (f32[8,16,128]{2,1,0:T(8,128)S(1)}, f32[8,16,128]{2,1,0:T(8,128)S(1)}, u32[]{:S(2)}, u32[]{:S(2)}) collective-permute-start(f32[8,16,128]{2,1,0:T(8,128)S(1)} %bitcast.155), channel_id=1, source_target_pairs={{0,0},{1,128},{64,64},{65,192},{128,1},{129,129},{192,65},{193,193... | collective-permute-start | bytes 196616 | tf_op jit(solution)/shard_map/ppermute | solution.py:75
  6.2 2.5 %collective-permute-start.1 = (f32[8,16,128]{2,1,0:T(8,128)S(1)}, f32[8,16,128]{2,1,0:T(8,128)S(1)}, u32[]{:S(2)}, u32[]{:S(2)}) collective-permute-start(f32[8,16,128]{2,1,0:T(8,128)S(1)} %bitcast.156), channel_id=1, source_target_pairs={{0,64},{1,192},{64,0},{65,128},{128,65},{129,193},{192,1},{193,129... | collective-permute-start | bytes 196616 | tf_op jit(solution)/shard_map/ppermute | solution.py:75
  8.6 1.3 dynamic-slice_bitcast_fusion
  9.9 3.7 %collective-permute-start.5 = (f32[16,64,128]{2,1,0:T(8,128)S(1)}, f32[16,64,128]{2,1,0:T(8,128)S(1)}, u32[]{:S(2)}, u32[]{:S(2)}) collective-permute-start(f32[16,64,128]{2,1,0:T(8,128)S(1)} %get-tuple-element.47), channel_id=1, source_target_pairs={{0,0},{1,128},{64,64},{65,192},{128,1},{129,129},{192,65},{193,193... | collective-permute-start | bytes 1572872 | tf_op jit(solution)/shard_map/ppermute | solution.py:75
  14.2 10.6 %collective-permute-start.2 = (f32[16,16,128]{2,1,0:T(8,128)S(1)}, f32[16,16,128]{2,1,0:T(8,128)S(1)}, u32[]{:S(2)}, u32[]{:S(2)}) collective-permute-start(f32[16,16,128]{2,1,0:T(8,128)S(1)} %pad_maximum_fusion.2), channel_id=1, source_target_pairs={{0,256},{1,257},{2,258},{3,259},{4,260},{5,261},{6,262},{7,263},{8... | collective-permute-start | bytes 393224 | tf_op jit(solution)/shard_map/ppermute | solution.py:75
  24.9 2.8 %collective-permute-start.6 = (f32[16,64,128]{2,1,0:T(8,128)S(1)}, f32[16,64,128]{2,1,0:T(8,128)S(1)}, u32[]{:S(2)}, u32[]{:S(2)}) collective-permute-start(f32[16,64,128]{2,1,0:T(8,128)S(1)} %get-tuple-element.25), channel_id=1, source_target_pairs={{0,64},{1,192},{64,0},{65,128},{128,65},{129,193},{192,1},{193,129... | collective-permute-start | bytes 1572872 | tf_op jit(solution)/shard_map/ppermute | solution.py:75
  27.8 8.4 %collective-permute-start.3 = (f32[32,16,128]{2,1,0:T(8,128)S(1)}, f32[32,16,128]{2,1,0:T(8,128)S(1)}, u32[]{:S(2)}, u32[]{:S(2)}) collective-permute-start(f32[32,16,128]{2,1,0:T(8,128)S(1)} %maximum_select_fusion.1), channel_id=1, source_target_pairs={{64,128},{128,64},{65,129},{129,65},{192,194},{194,192},{193,195},... | collective-permute-start | bytes 786440 | tf_op jit(solution)/shard_map/ppermute | solution.py:75
  36.2 1.9 %collective-permute-start.4 = (f32[32,16,128]{2,1,0:T(8,128)S(1)}, f32[32,16,128]{2,1,0:T(8,128)S(1)}, u32[]{:S(2)}, u32[]{:S(2)}) collective-permute-start(f32[32,16,128]{2,1,0:T(8,128)S(1)} %maximum_select_fusion.1), channel_id=1, source_target_pairs={{0,64},{64,0},{1,65},{65,1},{128,192},{192,128},{129,193},{193,129... | collective-permute-start | bytes 786440 | tf_op jit(solution)/shard_map/ppermute | solution.py:75
  38.2 0.2 fusion.77
  38.4 0.4 fusion.18
  38.8 0.8 fusion
  39.6 0.2 fusion.31
  40.2 2.0 %collective-permute-done.3 = f32[32,16,128]{2,1,0:T(8,128)S(1)} collective-permute-done((f32[32,16,128]{2,1,0:T(8,128)S(1)}, f32[32,16,128]{2,1,0:T(8,128)S(1)}, u32[]{:S(2)}, u32[]{:S(2)}) %collective-permute-start.3) | collective-permute-done | bytes 262176 | tf_op jit(solution)/shard_map/ppermute | solution.py:75
  42.2 4.0 %collective-permute-done.4 = f32[32,16,128]{2,1,0:T(8,128)S(1)} collective-permute-done((f32[32,16,128]{2,1,0:T(8,128)S(1)}, f32[32,16,128]{2,1,0:T(8,128)S(1)}, u32[]{:S(2)}, u32[]{:S(2)}) %collective-permute-start.4) | collective-permute-done | bytes 262176 | tf_op jit(solution)/shard_map/ppermute | solution.py:75
  46.4 2.4 %collective-permute-start.7 = (f32[32,48,128]{2,1,0:T(8,128)S(1)}, f32[32,48,128]{2,1,0:T(8,128)S(1)}, u32[]{:S(2)}, u32[]{:S(2)}) collective-permute-start(f32[32,48,128]{2,1,0:T(8,128)S(1)} %pad_maximum_fusion), channel_id=1, source_target_pairs={{0,1},{1,0},{2,3},{3,2},{4,5},{5,4},{6,7},{7,6},{8,9},{9,8},{10,11... | collective-permute-start | bytes 2359304 | tf_op jit(solution)/shard_map/ppermute | solution.py:75
  48.9 1.7 %collective-permute-done.7 = f32[32,48,128]{2,1,0:T(8,128)S(1)} collective-permute-done((f32[32,48,128]{2,1,0:T(8,128)S(1)}, f32[32,48,128]{2,1,0:T(8,128)S(1)}, u32[]{:S(2)}, u32[]{:S(2)}) %collective-permute-start.7) | collective-permute-done | bytes 786464 | tf_op jit(solution)/shard_map/ppermute | solution.py:75
  50.7 0.6 fusion.1
  51.2 0.9 convolution_bitcast_fusion.1
  52.1 0.6 fusion.11
  52.7 0.6 fusion.39
  53.3 0.4 fusion.46
  53.8 0.8 convolution_bitcast_fusion.4
  54.5 2.3 %collective-permute-start.8 = (f32[32,48,128]{2,1,0:T(8,128)S(1)}, f32[32,48,128]{2,1,0:T(8,128)S(1)}, u32[]{:S(2)}, u32[]{:S(2)}) collective-permute-start(f32[32,48,128]{2,1,0:T(8,128)S(1)} %convolution_bitcast_fusion.4), channel_id=1, source_target_pairs={{0,1},{1,0},{2,3},{3,2},{4,5},{5,4},{6,7},{7,6},{8,9},{9,8},{10,11... | collective-permute-start | bytes 2359304 | tf_op jit(solution)/shard_map/ppermute | solution.py:75
  56.8 0.4 fusion.52
  57.3 0.8 convolution_bitcast_fusion.5
  58.0 0.7 collective-permute-done.8
  58.8 1.9 %collective-permute-start.10 = (f32[32,16,128]{2,1,0:T(8,128)S(1)}, f32[32,16,128]{2,1,0:T(8,128)S(1)}, u32[]{:S(2)}, u32[]{:S(2)}) collective-permute-start(f32[32,16,128]{2,1,0:T(8,128)S(1)} %get-tuple-element.45), channel_id=1, source_target_pairs={{0,64},{64,0},{1,65},{65,1},{128,192},{192,128},{129,193},{193,129... | collective-permute-start | bytes 786440 | tf_op jit(solution)/shard_map/ppermute | solution.py:75
  60.7 4.7 %collective-permute-start.9 = (f32[32,16,128]{2,1,0:T(8,128)S(1)}, f32[32,16,128]{2,1,0:T(8,128)S(1)}, u32[]{:S(2)}, u32[]{:S(2)}) collective-permute-start(f32[32,16,128]{2,1,0:T(8,128)S(1)} %get-tuple-element.44), channel_id=1, source_target_pairs={{64,128},{128,64},{65,129},{129,65},{192,194},{194,192},{193,195},... | collective-permute-start | bytes 786440 | tf_op jit(solution)/shard_map/ppermute | solution.py:75
  65.4 2.8 %collective-permute-done.10 = f32[32,16,128]{2,1,0:T(8,128)S(1)} collective-permute-done((f32[32,16,128]{2,1,0:T(8,128)S(1)}, f32[32,16,128]{2,1,0:T(8,128)S(1)}, u32[]{:S(2)}, u32[]{:S(2)}) %collective-permute-start.10) | collective-permute-done | bytes 262176 | tf_op jit(solution)/shard_map/ppermute | solution.py:75
  68.2 4.0 %collective-permute-done.9 = f32[32,16,128]{2,1,0:T(8,128)S(1)} collective-permute-done((f32[32,16,128]{2,1,0:T(8,128)S(1)}, f32[32,16,128]{2,1,0:T(8,128)S(1)}, u32[]{:S(2)}, u32[]{:S(2)}) %collective-permute-start.9) | collective-permute-done | bytes 262176 | tf_op jit(solution)/shard_map/ppermute | solution.py:75
  72.3 2.8 %collective-permute-start.11 = (f32[32,16,128]{2,1,0:T(8,128)S(1)}, f32[32,16,128]{2,1,0:T(8,128)S(1)}, u32[]{:S(2)}, u32[]{:S(2)}) collective-permute-start(f32[32,16,128]{2,1,0:T(8,128)S(1)} %fusion.30), channel_id=1, source_target_pairs={{0,256},{1,257},{2,258},{3,259},{4,260},{5,261},{6,262},{7,263},{8... | collective-permute-start | bytes 786440 | tf_op jit(solution)/shard_map/ppermute | solution.py:75
  75.3 0.2 fusion.75
  75.5 0.7 fusion.28
  76.2 0.2 fusion.86
  76.4 0.3 fusion.54
  76.8 0.8 fusion.13
  77.6 13.6 %collective-permute-done.11 = f32[32,16,128]{2,1,0:T(8,128)S(1)} collective-permute-done((f32[32,16,128]{2,1,0:T(8,128)S(1)}, f32[32,16,128]{2,1,0:T(8,128)S(1)}, u32[]{:S(2)}, u32[]{:S(2)}) %collective-permute-start.11) | collective-permute-done | bytes 262176 | tf_op jit(solution)/shard_map/ppermute | solution.py:75
  91.3 2.2 %collective-permute-start.12 = (f32[32,16,128]{2,1,0:T(8,128)S(1)}, f32[32,16,128]{2,1,0:T(8,128)S(1)}, u32[]{:S(2)}, u32[]{:S(2)}) collective-permute-start(f32[32,16,128]{2,1,0:T(8,128)S(1)} %multiply_multiply_fusion), channel_id=1, source_target_pairs={{64,128},{128,64},{65,129},{129,65},{192,194},{194,192},{193,195},... | collective-permute-start | bytes 786440 | tf_op jit(solution)/shard_map/ppermute | solution.py:75
  93.5 1.9 %collective-permute-start.13 = (f32[32,16,128]{2,1,0:T(8,128)S(1)}, f32[32,16,128]{2,1,0:T(8,128)S(1)}, u32[]{:S(2)}, u32[]{:S(2)}) collective-permute-start(f32[32,16,128]{2,1,0:T(8,128)S(1)} %multiply_multiply_fusion), channel_id=1, source_target_pairs={{0,64},{64,0},{1,65},{65,1},{128,192},{192,128},{129,193},{193,129... | collective-permute-start | bytes 786440 | tf_op jit(solution)/shard_map/ppermute | solution.py:75
  95.4 7.3 %collective-permute-done.12 = f32[32,16,128]{2,1,0:T(8,128)S(1)} collective-permute-done((f32[32,16,128]{2,1,0:T(8,128)S(1)}, f32[32,16,128]{2,1,0:T(8,128)S(1)}, u32[]{:S(2)}, u32[]{:S(2)}) %collective-permute-start.12) | collective-permute-done | bytes 262176 | tf_op jit(solution)/shard_map/ppermute | solution.py:75
  102.7 3.5 %collective-permute-start.14 = (f32[32,48,128]{2,1,0:T(8,128)S(1)}, f32[32,48,128]{2,1,0:T(8,128)S(1)}, u32[]{:S(2)}, u32[]{:S(2)}) collective-permute-start(f32[32,48,128]{2,1,0:T(8,128)S(1)} %pad_maximum_fusion.1), channel_id=1, source_target_pairs={{0,1},{1,0},{2,3},{3,2},{4,5},{5,4},{6,7},{7,6},{8,9},{9,8},{10,11... | collective-permute-start | bytes 2359304 | tf_op jit(solution)/shard_map/ppermute | solution.py:75
  106.2 1.7 %collective-permute-done.14 = f32[32,48,128]{2,1,0:T(8,128)S(1)} collective-permute-done((f32[32,48,128]{2,1,0:T(8,128)S(1)}, f32[32,48,128]{2,1,0:T(8,128)S(1)}, u32[]{:S(2)}, u32[]{:S(2)}) %collective-permute-start.14) | collective-permute-done | bytes 786464 | tf_op jit(solution)/shard_map/ppermute | solution.py:75
  107.9 0.6 fusion.4
  108.5 0.9 convolution_bitcast_fusion
  109.4 0.6 fusion.12
  110.0 0.6 fusion.36
  110.6 0.4 fusion.44
  111.0 0.8 convolution_bitcast_fusion.2
  111.8 2.3 %collective-permute-start.15 = (f32[32,48,128]{2,1,0:T(8,128)S(1)}, f32[32,48,128]{2,1,0:T(8,128)S(1)}, u32[]{:S(2)}, u32[]{:S(2)}) collective-permute-start(f32[32,48,128]{2,1,0:T(8,128)S(1)} %convolution_bitcast_fusion.2), channel_id=1, source_target_pairs={{0,1},{1,0},{2,3},{3,2},{4,5},{5,4},{6,7},{7,6},{8,9},{9,8},{10,11... | collective-permute-start | bytes 2359304 | tf_op jit(solution)/shard_map/ppermute | solution.py:75
  114.1 0.4 fusion.50
  114.5 0.8 convolution_bitcast_fusion.3
  115.3 0.7 collective-permute-done.15
  116.1 6.4 %collective-permute-start.16 = (f32[32,16,128]{2,1,0:T(8,128)S(1)}, f32[32,16,128]{2,1,0:T(8,128)S(1)}, u32[]{:S(2)}, u32[]{:S(2)}) collective-permute-start(f32[32,16,128]{2,1,0:T(8,128)S(1)} %get-tuple-element.43), channel_id=1, source_target_pairs={{64,128},{128,64},{65,129},{129,65},{192,194},{194,192},{193,195},... | collective-permute-start | bytes 786440 | tf_op jit(solution)/shard_map/ppermute | solution.py:75
  122.5 1.9 %collective-permute-start.17 = (f32[32,16,128]{2,1,0:T(8,128)S(1)}, f32[32,16,128]{2,1,0:T(8,128)S(1)}, u32[]{:S(2)}, u32[]{:S(2)}) collective-permute-start(f32[32,16,128]{2,1,0:T(8,128)S(1)} %get-tuple-element.42), channel_id=1, source_target_pairs={{0,64},{64,0},{1,65},{65,1},{128,192},{192,128},{129,193},{193,129... | collective-permute-start | bytes 786440 | tf_op jit(solution)/shard_map/ppermute | solution.py:75
  124.5 4.4 %collective-permute-done.16 = f32[32,16,128]{2,1,0:T(8,128)S(1)} collective-permute-done((f32[32,16,128]{2,1,0:T(8,128)S(1)}, f32[32,16,128]{2,1,0:T(8,128)S(1)}, u32[]{:S(2)}, u32[]{:S(2)}) %collective-permute-start.16) | collective-permute-done | bytes 262176 | tf_op jit(solution)/shard_map/ppermute | solution.py:75
  128.9 2.7 %collective-permute-done.17 = f32[32,16,128]{2,1,0:T(8,128)S(1)} collective-permute-done((f32[32,16,128]{2,1,0:T(8,128)S(1)}, f32[32,16,128]{2,1,0:T(8,128)S(1)}, u32[]{:S(2)}, u32[]{:S(2)}) %collective-permute-start.17) | collective-permute-done | bytes 262176 | tf_op jit(solution)/shard_map/ppermute | solution.py:75
  131.7 2.8 %collective-permute-start.18 = (f32[16,16,128]{2,1,0:T(8,128)S(1)}, f32[16,16,128]{2,1,0:T(8,128)S(1)}, u32[]{:S(2)}, u32[]{:S(2)}) collective-permute-start(f32[16,16,128]{2,1,0:T(8,128)S(1)} %select_add_fusion), channel_id=1, source_target_pairs={{0,256},{1,257},{2,258},{3,259},{4,260},{5,261},{6,262},{7,263},{8... | collective-permute-start | bytes 393224 | tf_op jit(solution)/shard_map/ppermute | solution.py:75
  134.5 6.8 %collective-permute-done.18 = f32[16,16,128]{2,1,0:T(8,128)S(1)} collective-permute-done((f32[16,16,128]{2,1,0:T(8,128)S(1)}, f32[16,16,128]{2,1,0:T(8,128)S(1)}, u32[]{:S(2)}, u32[]{:S(2)}) %collective-permute-start.18) | collective-permute-done | bytes 131104 | tf_op jit(solution)/shard_map/ppermute | solution.py:75
  141.4 4.0 %collective-permute-start.19 = (f32[16,8,128]{2,0,1:T(8,128)S(1)}, f32[16,8,128]{2,0,1:T(8,128)S(1)}, u32[]{:S(2)}, u32[]{:S(2)}) collective-permute-start(f32[16,8,128]{2,0,1:T(8,128)S(1)} %get-tuple-element.37), channel_id=1, source_target_pairs={{0,0},{128,1},{64,64},{192,65},{1,128},{129,129},{65,192},{193,193... | collective-permute-start | bytes 196616 | tf_op jit(solution)/shard_map/ppermute | solution.py:75
  145.4 2.8 %collective-permute-start.20 = (f32[16,8,128]{2,0,1:T(8,128)S(1)}, f32[16,8,128]{2,0,1:T(8,128)S(1)}, u32[]{:S(2)}, u32[]{:S(2)}) collective-permute-start(f32[16,8,128]{2,0,1:T(8,128)S(1)} %get-tuple-element.38), channel_id=1, source_target_pairs={{64,0},{192,1},{0,64},{128,65},{65,128},{193,129},{1,192},{129,193... | collective-permute-start | bytes 196616 | tf_op jit(solution)/shard_map/ppermute | solution.py:75
  148.3 0.2 collective-permute-done.19
  148.5 3.7 %collective-permute-done.20 = f32[16,8,128]{2,0,1:T(8,128)S(1)} collective-permute-done((f32[16,8,128]{2,0,1:T(8,128)S(1)}, f32[16,8,128]{2,0,1:T(8,128)S(1)}, u32[]{:S(2)}, u32[]{:S(2)}) %collective-permute-start.20) | collective-permute-done | bytes 65568 | tf_op jit(solution)/shard_map/ppermute | solution.py:75
  152.2 0.7 copy.12
  (48 shorter events, 2.0 us)
Async XLA Ops:
  0.9 13.2 %collective-permute-start = (f32[8,16,128]{2,1,0:T(8,128)S(1)}, f32[8,16,128]{2,1,0:T(8,128)S(1)}, u32[]{:S(2)}, u32[]{:S(2)}) collective-permute-start(f32[8,16,128]{2,1,0:T(8,128)S(1)} %bitcast.155), channel_id=1, source_target_pairs={{0,0},{1,128},{64,64},{65,192},{128,1},{129,129},{192,65},{193,193... | collective-permute-start | bytes 196616 | tf_op jit(solution)/shard_map/ppermute | solution.py:75
  6.2 8.0 %collective-permute-start.1 = (f32[8,16,128]{2,1,0:T(8,128)S(1)}, f32[8,16,128]{2,1,0:T(8,128)S(1)}, u32[]{:S(2)}, u32[]{:S(2)}) collective-permute-start(f32[8,16,128]{2,1,0:T(8,128)S(1)} %bitcast.156), channel_id=1, source_target_pairs={{0,64},{1,192},{64,0},{65,128},{128,65},{129,193},{192,1},{193,129... | collective-permute-start | bytes 196616 | tf_op jit(solution)/shard_map/ppermute | solution.py:75
  9.9 28.2 %copy-start = (f32[8,3,31]{2,0,1:T(8,128)S(1)}, f32[8,3,31]{2,0,1:T(8,128)}, u32[]{:S(2)}) copy-start(f32[8,3,31]{2,0,1:T(8,128)} %param.6) | copy-start | bytes 8932
  9.9 36.4 %collective-permute-start.5 = (f32[16,64,128]{2,1,0:T(8,128)S(1)}, f32[16,64,128]{2,1,0:T(8,128)S(1)}, u32[]{:S(2)}, u32[]{:S(2)}) collective-permute-start(f32[16,64,128]{2,1,0:T(8,128)S(1)} %get-tuple-element.47), channel_id=1, source_target_pairs={{0,0},{1,128},{64,64},{65,192},{128,1},{129,129},{192,65},{193,193... | collective-permute-start | bytes 1572872 | tf_op jit(solution)/shard_map/ppermute | solution.py:75
  14.1 25.7 %copy-start.1 = (s32[8,16]{1,0:T(8,128)S(1)}, s32[8,16]{1,0:T(8,128)}, u32[]{:S(2)}) copy-start(s32[8,16]{1,0:T(8,128)} %param.7) | copy-start | bytes 1540
  14.2 13.6 %collective-permute-start.2 = (f32[16,16,128]{2,1,0:T(8,128)S(1)}, f32[16,16,128]{2,1,0:T(8,128)S(1)}, u32[]{:S(2)}, u32[]{:S(2)}) collective-permute-start(f32[16,16,128]{2,1,0:T(8,128)S(1)} %pad_maximum_fusion.2), channel_id=1, source_target_pairs={{0,256},{1,257},{2,258},{3,259},{4,260},{5,261},{6,262},{7,263},{8... | collective-permute-start | bytes 393224 | tf_op jit(solution)/shard_map/ppermute | solution.py:75
  24.9 21.4 %collective-permute-start.6 = (f32[16,64,128]{2,1,0:T(8,128)S(1)}, f32[16,64,128]{2,1,0:T(8,128)S(1)}, u32[]{:S(2)}, u32[]{:S(2)}) collective-permute-start(f32[16,64,128]{2,1,0:T(8,128)S(1)} %get-tuple-element.25), channel_id=1, source_target_pairs={{0,64},{1,192},{64,0},{65,128},{128,65},{129,193},{192,1},{193,129... | collective-permute-start | bytes 1572872 | tf_op jit(solution)/shard_map/ppermute | solution.py:75
  27.8 14.5 %collective-permute-start.3 = (f32[32,16,128]{2,1,0:T(8,128)S(1)}, f32[32,16,128]{2,1,0:T(8,128)S(1)}, u32[]{:S(2)}, u32[]{:S(2)}) collective-permute-start(f32[32,16,128]{2,1,0:T(8,128)S(1)} %maximum_select_fusion.1), channel_id=1, source_target_pairs={{64,128},{128,64},{65,129},{129,65},{192,194},{194,192},{193,195},... | collective-permute-start | bytes 786440 | tf_op jit(solution)/shard_map/ppermute | solution.py:75
  36.2 10.1 %collective-permute-start.4 = (f32[32,16,128]{2,1,0:T(8,128)S(1)}, f32[32,16,128]{2,1,0:T(8,128)S(1)}, u32[]{:S(2)}, u32[]{:S(2)}) collective-permute-start(f32[32,16,128]{2,1,0:T(8,128)S(1)} %maximum_select_fusion.1), channel_id=1, source_target_pairs={{0,64},{64,0},{1,65},{65,1},{128,192},{192,128},{129,193},{193,129... | collective-permute-start | bytes 786440 | tf_op jit(solution)/shard_map/ppermute | solution.py:75
  46.4 4.3 %collective-permute-start.7 = (f32[32,48,128]{2,1,0:T(8,128)S(1)}, f32[32,48,128]{2,1,0:T(8,128)S(1)}, u32[]{:S(2)}, u32[]{:S(2)}) collective-permute-start(f32[32,48,128]{2,1,0:T(8,128)S(1)} %pad_maximum_fusion), channel_id=1, source_target_pairs={{0,1},{1,0},{2,3},{3,2},{4,5},{5,4},{6,7},{7,6},{8,9},{9,8},{10,11... | collective-permute-start | bytes 2359304 | tf_op jit(solution)/shard_map/ppermute | solution.py:75
  54.5 4.2 %collective-permute-start.8 = (f32[32,48,128]{2,1,0:T(8,128)S(1)}, f32[32,48,128]{2,1,0:T(8,128)S(1)}, u32[]{:S(2)}, u32[]{:S(2)}) collective-permute-start(f32[32,48,128]{2,1,0:T(8,128)S(1)} %convolution_bitcast_fusion.4), channel_id=1, source_target_pairs={{0,1},{1,0},{2,3},{3,2},{4,5},{5,4},{6,7},{7,6},{8,9},{9,8},{10,11... | collective-permute-start | bytes 2359304 | tf_op jit(solution)/shard_map/ppermute | solution.py:75
  58.8 9.4 %collective-permute-start.10 = (f32[32,16,128]{2,1,0:T(8,128)S(1)}, f32[32,16,128]{2,1,0:T(8,128)S(1)}, u32[]{:S(2)}, u32[]{:S(2)}) collective-permute-start(f32[32,16,128]{2,1,0:T(8,128)S(1)} %get-tuple-element.45), channel_id=1, source_target_pairs={{0,64},{64,0},{1,65},{65,1},{128,192},{192,128},{129,193},{193,129... | collective-permute-start | bytes 786440 | tf_op jit(solution)/shard_map/ppermute | solution.py:75
  60.7 11.5 %collective-permute-start.9 = (f32[32,16,128]{2,1,0:T(8,128)S(1)}, f32[32,16,128]{2,1,0:T(8,128)S(1)}, u32[]{:S(2)}, u32[]{:S(2)}) collective-permute-start(f32[32,16,128]{2,1,0:T(8,128)S(1)} %get-tuple-element.44), channel_id=1, source_target_pairs={{64,128},{128,64},{65,129},{129,65},{192,194},{194,192},{193,195},... | collective-permute-start | bytes 786440 | tf_op jit(solution)/shard_map/ppermute | solution.py:75
  72.3 18.9 %collective-permute-start.11 = (f32[32,16,128]{2,1,0:T(8,128)S(1)}, f32[32,16,128]{2,1,0:T(8,128)S(1)}, u32[]{:S(2)}, u32[]{:S(2)}) collective-permute-start(f32[32,16,128]{2,1,0:T(8,128)S(1)} %fusion.30), channel_id=1, source_target_pairs={{0,256},{1,257},{2,258},{3,259},{4,260},{5,261},{6,262},{7,263},{8... | collective-permute-start | bytes 786440 | tf_op jit(solution)/shard_map/ppermute | solution.py:75
  91.3 11.4 %collective-permute-start.12 = (f32[32,16,128]{2,1,0:T(8,128)S(1)}, f32[32,16,128]{2,1,0:T(8,128)S(1)}, u32[]{:S(2)}, u32[]{:S(2)}) collective-permute-start(f32[32,16,128]{2,1,0:T(8,128)S(1)} %multiply_multiply_fusion), channel_id=1, source_target_pairs={{64,128},{128,64},{65,129},{129,65},{192,194},{194,192},{193,195},... | collective-permute-start | bytes 786440 | tf_op jit(solution)/shard_map/ppermute | solution.py:75
  93.5 9.2 %collective-permute-start.13 = (f32[32,16,128]{2,1,0:T(8,128)S(1)}, f32[32,16,128]{2,1,0:T(8,128)S(1)}, u32[]{:S(2)}, u32[]{:S(2)}) collective-permute-start(f32[32,16,128]{2,1,0:T(8,128)S(1)} %multiply_multiply_fusion), channel_id=1, source_target_pairs={{0,64},{64,0},{1,65},{65,1},{128,192},{192,128},{129,193},{193,129... | collective-permute-start | bytes 786440 | tf_op jit(solution)/shard_map/ppermute | solution.py:75
  102.7 5.2 %collective-permute-start.14 = (f32[32,48,128]{2,1,0:T(8,128)S(1)}, f32[32,48,128]{2,1,0:T(8,128)S(1)}, u32[]{:S(2)}, u32[]{:S(2)}) collective-permute-start(f32[32,48,128]{2,1,0:T(8,128)S(1)} %pad_maximum_fusion.1), channel_id=1, source_target_pairs={{0,1},{1,0},{2,3},{3,2},{4,5},{5,4},{6,7},{7,6},{8,9},{9,8},{10,11... | collective-permute-start | bytes 2359304 | tf_op jit(solution)/shard_map/ppermute | solution.py:75
  111.8 4.2 %collective-permute-start.15 = (f32[32,48,128]{2,1,0:T(8,128)S(1)}, f32[32,48,128]{2,1,0:T(8,128)S(1)}, u32[]{:S(2)}, u32[]{:S(2)}) collective-permute-start(f32[32,48,128]{2,1,0:T(8,128)S(1)} %convolution_bitcast_fusion.2), channel_id=1, source_target_pairs={{0,1},{1,0},{2,3},{3,2},{4,5},{5,4},{6,7},{7,6},{8,9},{9,8},{10,11... | collective-permute-start | bytes 2359304 | tf_op jit(solution)/shard_map/ppermute | solution.py:75
  116.1 12.8 %collective-permute-start.16 = (f32[32,16,128]{2,1,0:T(8,128)S(1)}, f32[32,16,128]{2,1,0:T(8,128)S(1)}, u32[]{:S(2)}, u32[]{:S(2)}) collective-permute-start(f32[32,16,128]{2,1,0:T(8,128)S(1)} %get-tuple-element.43), channel_id=1, source_target_pairs={{64,128},{128,64},{65,129},{129,65},{192,194},{194,192},{193,195},... | collective-permute-start | bytes 786440 | tf_op jit(solution)/shard_map/ppermute | solution.py:75
  122.5 9.1 %collective-permute-start.17 = (f32[32,16,128]{2,1,0:T(8,128)S(1)}, f32[32,16,128]{2,1,0:T(8,128)S(1)}, u32[]{:S(2)}, u32[]{:S(2)}) collective-permute-start(f32[32,16,128]{2,1,0:T(8,128)S(1)} %get-tuple-element.42), channel_id=1, source_target_pairs={{0,64},{64,0},{1,65},{65,1},{128,192},{192,128},{129,193},{193,129... | collective-permute-start | bytes 786440 | tf_op jit(solution)/shard_map/ppermute | solution.py:75
  131.7 9.6 %collective-permute-start.18 = (f32[16,16,128]{2,1,0:T(8,128)S(1)}, f32[16,16,128]{2,1,0:T(8,128)S(1)}, u32[]{:S(2)}, u32[]{:S(2)}) collective-permute-start(f32[16,16,128]{2,1,0:T(8,128)S(1)} %select_add_fusion), channel_id=1, source_target_pairs={{0,256},{1,257},{2,258},{3,259},{4,260},{5,261},{6,262},{7,263},{8... | collective-permute-start | bytes 393224 | tf_op jit(solution)/shard_map/ppermute | solution.py:75
  141.4 7.1 %collective-permute-start.19 = (f32[16,8,128]{2,0,1:T(8,128)S(1)}, f32[16,8,128]{2,0,1:T(8,128)S(1)}, u32[]{:S(2)}, u32[]{:S(2)}) collective-permute-start(f32[16,8,128]{2,0,1:T(8,128)S(1)} %get-tuple-element.37), channel_id=1, source_target_pairs={{0,0},{128,1},{64,64},{192,65},{1,128},{129,129},{65,192},{193,193... | collective-permute-start | bytes 196616 | tf_op jit(solution)/shard_map/ppermute | solution.py:75
  145.4 6.8 %collective-permute-start.20 = (f32[16,8,128]{2,0,1:T(8,128)S(1)}, f32[16,8,128]{2,0,1:T(8,128)S(1)}, u32[]{:S(2)}, u32[]{:S(2)}) collective-permute-start(f32[16,8,128]{2,0,1:T(8,128)S(1)} %get-tuple-element.38), channel_id=1, source_target_pairs={{64,0},{192,1},{0,64},{128,65},{65,128},{193,129},{1,192},{129,193... | collective-permute-start | bytes 196616 | tf_op jit(solution)/shard_map/ppermute | solution.py:75

commit v14 on v13

--- a/solution.py
+++ b/solution.py
@@ -102,15 +102,12 @@
     def piece(value, turn, axis):
         return lax.dynamic_slice_in_dim(value, SLAB * ((x + turn) % 2), SLAB, axis)
 
-    def ordered(pair, first):
-        one, two = pair
-        return jnp.where(first, one, two), jnp.where(first, two, one)
+    def joined(pair, first, axis):
+        return jnp.where(first, jnp.concatenate(pair, axis), jnp.concatenate(pair[::-1], axis))
 
     even = p % 2 == 0
     flipped = jnp.swapaxes(estimate, 0, 1)
-    quarter = jnp.concatenate(
-        ordered([send(piece(flipped, turn, 1), SPREAD[turn]) for turn in (0, 1)], even), 0
-    )
+    quarter = joined([send(piece(flipped, turn, 1), SPREAD[turn]) for turn in (0, 1)], even, 0)
     current = by_h(quarter, send(quarter, SWAP_H), h)
     images = [piece(observed[0], turn, 0) for turn in (0, 1)]
     images[1], _ = lax.optimization_barrier((images[1], quarter))
@@ -209,13 +206,17 @@
         return jnp.where((h == 0) == mine, value[: 2 * block], value[2 * block :])
 
     far, near = (sum(own_half(term, mine) for term in terms) for mine in (False, True))
-    quarter = own_half(current, True) * (near + send(far, SWAP_H) + 1.0) * own_half(scale, True)
-
-    quarter = jnp.swapaxes(quarter, 0, 1)
-    result = ordered([quarter[:, :block], quarter[:, block:]], even)
-    result = lax.optimization_barrier(tuple(result))
+    received = send(far, SWAP_H)
+
+    result = []
+    for first in (even, jnp.logical_not(even)):
+        old, mine, other, factor = (
+            jnp.where(first, value[:block], value[block:])
+            for value in (own_half(current, True), near, received, own_half(scale, True))
+        )
+        result.append(old * (mine + other + 1.0) * factor)
     result = [send(value, reverse(route)) for value, route in zip(result, SPREAD)]
-    return jnp.concatenate(ordered(result, x % 2 == 0), 0)
+    return jnp.swapaxes(joined(result, x % 2 == 0, 1), 0, 1)
 
 
 def solution(mesh):

time: 154 us -> 154 us (level)
  no operation moved by 1% of the time
where the time goes in v14:
time: 154 us; the launch traced here: 153 us
  starting transfers between devices  77 us (50%)
  waiting for transfers between devices  56.5 us (37%)
  matrix products  14.2 us (9%)
  local copies, waits for them, and re-layouts  3.05 us (2%)
    ppermute x21, starting transfers between devices, send(): return lax.ppermute(value, AXES, pairs)  77 us
    ppermute x21, waiting for transfers between devices, send(): return lax.ppermute(value, AXES, pairs)  56.5 us
  transfers between devices with their start and end apart: 21, of which 15 were waited for; matrix products, arithmetic and copies ran while one was open for 6% of the time, Pallas kernels for 0%

profile of v14, /device:TPU:57, one launch (start us, length us, event | category | flops | bytes accessed | tf_op | source)
XLA Modules:
  0.0 152.9 jit_solution(10761934090496644533)
XLA Ops:
  0.0 0.9 constant_dynamic-slice_fusion.1
  0.9 5.2 %collective-permute-start = (f32[8,16,128]{2,1,0:T(8,128)S(1)}, f32[8,16,128]{2,1,0:T(8,128)S(1)}, u32[]{:S(2)}, u32[]{:S(2)}) collective-permute-start(f32[8,16,128]{2,1,0:T(8,128)S(1)} %bitcast.155), channel_id=1, source_target_pairs={{0,0},{1,128},{64,64},{65,192},{128,1},{129,129},{192,65},{193,193... | collective-permute-start | bytes 196616 | tf_op jit(solution)/shard_map/ppermute | solution.py:75
  6.2 2.5 %collective-permute-start.1 = (f32[8,16,128]{2,1,0:T(8,128)S(1)}, f32[8,16,128]{2,1,0:T(8,128)S(1)}, u32[]{:S(2)}, u32[]{:S(2)}) collective-permute-start(f32[8,16,128]{2,1,0:T(8,128)S(1)} %bitcast.156), channel_id=1, source_target_pairs={{0,64},{1,192},{64,0},{65,128},{128,65},{129,193},{192,1},{193,129... | collective-permute-start | bytes 196616 | tf_op jit(solution)/shard_map/ppermute | solution.py:75
  8.6 1.3 dynamic-slice_bitcast_fusion
  9.9 3.7 %collective-permute-start.5 = (f32[16,64,128]{2,1,0:T(8,128)S(1)}, f32[16,64,128]{2,1,0:T(8,128)S(1)}, u32[]{:S(2)}, u32[]{:S(2)}) collective-permute-start(f32[16,64,128]{2,1,0:T(8,128)S(1)} %get-tuple-element.43), channel_id=1, source_target_pairs={{0,0},{1,128},{64,64},{65,192},{128,1},{129,129},{192,65},{193,193... | collective-permute-start | bytes 1572872 | tf_op jit(solution)/shard_map/ppermute | solution.py:75
  14.1 10.6 %collective-permute-start.2 = (f32[16,16,128]{2,1,0:T(8,128)S(1)}, f32[16,16,128]{2,1,0:T(8,128)S(1)}, u32[]{:S(2)}, u32[]{:S(2)}) collective-permute-start(f32[16,16,128]{2,1,0:T(8,128)S(1)} %maximum_select_fusion.2), channel_id=1, source_target_pairs={{0,256},{1,257},{2,258},{3,259},{4,260},{5,261},{6,262},{7,263},{8... | collective-permute-start | bytes 393224 | tf_op jit(solution)/shard_map/ppermute | solution.py:75
  24.9 2.8 %collective-permute-start.6 = (f32[16,64,128]{2,1,0:T(8,128)S(1)}, f32[16,64,128]{2,1,0:T(8,128)S(1)}, u32[]{:S(2)}, u32[]{:S(2)}) collective-permute-start(f32[16,64,128]{2,1,0:T(8,128)S(1)} %get-tuple-element.23), channel_id=1, source_target_pairs={{0,64},{1,192},{64,0},{65,128},{128,65},{129,193},{192,1},{193,129... | collective-permute-start | bytes 1572872 | tf_op jit(solution)/shard_map/ppermute | solution.py:75
  27.7 8.4 %collective-permute-start.3 = (f32[32,16,128]{2,1,0:T(8,128)S(1)}, f32[32,16,128]{2,1,0:T(8,128)S(1)}, u32[]{:S(2)}, u32[]{:S(2)}) collective-permute-start(f32[32,16,128]{2,1,0:T(8,128)S(1)} %maximum_select_fusion.1), channel_id=1, source_target_pairs={{64,128},{128,64},{65,129},{129,65},{192,194},{194,192},{193,195},... | collective-permute-start | bytes 786440 | tf_op jit(solution)/shard_map/ppermute | solution.py:75
  36.1 1.9 %collective-permute-start.4 = (f32[32,16,128]{2,1,0:T(8,128)S(1)}, f32[32,16,128]{2,1,0:T(8,128)S(1)}, u32[]{:S(2)}, u32[]{:S(2)}) collective-permute-start(f32[32,16,128]{2,1,0:T(8,128)S(1)} %maximum_select_fusion.1), channel_id=1, source_target_pairs={{0,64},{64,0},{1,65},{65,1},{128,192},{192,128},{129,193},{193,129... | collective-permute-start | bytes 786440 | tf_op jit(solution)/shard_map/ppermute | solution.py:75
  38.2 0.2 fusion.75
  38.4 0.4 fusion.18
  38.8 0.8 fusion
  39.6 0.2 fusion.31
  40.2 2.0 %collective-permute-done.3 = f32[32,16,128]{2,1,0:T(8,128)S(1)} collective-permute-done((f32[32,16,128]{2,1,0:T(8,128)S(1)}, f32[32,16,128]{2,1,0:T(8,128)S(1)}, u32[]{:S(2)}, u32[]{:S(2)}) %collective-permute-start.3) | collective-permute-done | bytes 262176 | tf_op jit(solution)/shard_map/ppermute | solution.py:75
  42.2 4.0 %collective-permute-done.4 = f32[32,16,128]{2,1,0:T(8,128)S(1)} collective-permute-done((f32[32,16,128]{2,1,0:T(8,128)S(1)}, f32[32,16,128]{2,1,0:T(8,128)S(1)}, u32[]{:S(2)}, u32[]{:S(2)}) %collective-permute-start.4) | collective-permute-done | bytes 262176 | tf_op jit(solution)/shard_map/ppermute | solution.py:75
  46.3 2.4 %collective-permute-start.7 = (f32[32,48,128]{2,1,0:T(8,128)S(1)}, f32[32,48,128]{2,1,0:T(8,128)S(1)}, u32[]{:S(2)}, u32[]{:S(2)}) collective-permute-start(f32[32,48,128]{2,1,0:T(8,128)S(1)} %pad_maximum_fusion), channel_id=1, source_target_pairs={{0,1},{1,0},{2,3},{3,2},{4,5},{5,4},{6,7},{7,6},{8,9},{9,8},{10,11... | collective-permute-start | bytes 2359304 | tf_op jit(solution)/shard_map/ppermute | solution.py:75
  48.9 1.7 %collective-permute-done.7 = f32[32,48,128]{2,1,0:T(8,128)S(1)} collective-permute-done((f32[32,48,128]{2,1,0:T(8,128)S(1)}, f32[32,48,128]{2,1,0:T(8,128)S(1)}, u32[]{:S(2)}, u32[]{:S(2)}) %collective-permute-start.7) | collective-permute-done | bytes 786464 | tf_op jit(solution)/shard_map/ppermute | solution.py:75
  50.6 0.6 fusion.1
  51.2 0.9 convolution_bitcast_fusion.1
  52.1 0.6 fusion.11
  52.7 0.6 fusion.37
  53.3 0.4 fusion.44
  53.7 0.8 convolution_bitcast_fusion.4
  54.5 2.3 %collective-permute-start.8 = (f32[32,48,128]{2,1,0:T(8,128)S(1)}, f32[32,48,128]{2,1,0:T(8,128)S(1)}, u32[]{:S(2)}, u32[]{:S(2)}) collective-permute-start(f32[32,48,128]{2,1,0:T(8,128)S(1)} %convolution_bitcast_fusion.4), channel_id=1, source_target_pairs={{0,1},{1,0},{2,3},{3,2},{4,5},{5,4},{6,7},{7,6},{8,9},{9,8},{10,11... | collective-permute-start | bytes 2359304 | tf_op jit(solution)/shard_map/ppermute | solution.py:75
  56.8 0.4 fusion.50
  57.2 0.8 convolution_bitcast_fusion.5
  58.0 0.7 collective-permute-done.8
  58.8 1.9 %collective-permute-start.10 = (f32[32,16,128]{2,1,0:T(8,128)S(1)}, f32[32,16,128]{2,1,0:T(8,128)S(1)}, u32[]{:S(2)}, u32[]{:S(2)}) collective-permute-start(f32[32,16,128]{2,1,0:T(8,128)S(1)} %get-tuple-element.41), channel_id=1, source_target_pairs={{0,64},{64,0},{1,65},{65,1},{128,192},{192,128},{129,193},{193,129... | collective-permute-start | bytes 786440 | tf_op jit(solution)/shard_map/ppermute | solution.py:75
  60.7 4.7 %collective-permute-start.9 = (f32[32,16,128]{2,1,0:T(8,128)S(1)}, f32[32,16,128]{2,1,0:T(8,128)S(1)}, u32[]{:S(2)}, u32[]{:S(2)}) collective-permute-start(f32[32,16,128]{2,1,0:T(8,128)S(1)} %get-tuple-element.40), channel_id=1, source_target_pairs={{64,128},{128,64},{65,129},{129,65},{192,194},{194,192},{193,195},... | collective-permute-start | bytes 786440 | tf_op jit(solution)/shard_map/ppermute | solution.py:75
  65.4 2.8 %collective-permute-done.10 = f32[32,16,128]{2,1,0:T(8,128)S(1)} collective-permute-done((f32[32,16,128]{2,1,0:T(8,128)S(1)}, f32[32,16,128]{2,1,0:T(8,128)S(1)}, u32[]{:S(2)}, u32[]{:S(2)}) %collective-permute-start.10) | collective-permute-done | bytes 262176 | tf_op jit(solution)/shard_map/ppermute | solution.py:75
  68.2 4.0 %collective-permute-done.9 = f32[32,16,128]{2,1,0:T(8,128)S(1)} collective-permute-done((f32[32,16,128]{2,1,0:T(8,128)S(1)}, f32[32,16,128]{2,1,0:T(8,128)S(1)}, u32[]{:S(2)}, u32[]{:S(2)}) %collective-permute-start.9) | collective-permute-done | bytes 262176 | tf_op jit(solution)/shard_map/ppermute | solution.py:75
  72.3 2.8 %collective-permute-start.11 = (f32[32,16,128]{2,1,0:T(8,128)S(1)}, f32[32,16,128]{2,1,0:T(8,128)S(1)}, u32[]{:S(2)}, u32[]{:S(2)}) collective-permute-start(f32[32,16,128]{2,1,0:T(8,128)S(1)} %fusion.30), channel_id=1, source_target_pairs={{0,256},{1,257},{2,258},{3,259},{4,260},{5,261},{6,262},{7,263},{8... | collective-permute-start | bytes 786440 | tf_op jit(solution)/shard_map/ppermute | solution.py:75
  75.3 0.2 fusion.73
  75.5 0.7 fusion.28
  76.2 0.2 fusion.84
  76.4 0.3 fusion.52
  76.8 0.8 fusion.13
  77.6 13.6 %collective-permute-done.11 = f32[32,16,128]{2,1,0:T(8,128)S(1)} collective-permute-done((f32[32,16,128]{2,1,0:T(8,128)S(1)}, f32[32,16,128]{2,1,0:T(8,128)S(1)}, u32[]{:S(2)}, u32[]{:S(2)}) %collective-permute-start.11) | collective-permute-done | bytes 262176 | tf_op jit(solution)/shard_map/ppermute | solution.py:75
  91.3 2.2 %collective-permute-start.12 = (f32[32,16,128]{2,1,0:T(8,128)S(1)}, f32[32,16,128]{2,1,0:T(8,128)S(1)}, u32[]{:S(2)}, u32[]{:S(2)}) collective-permute-start(f32[32,16,128]{2,1,0:T(8,128)S(1)} %multiply_multiply_fusion), channel_id=1, source_target_pairs={{64,128},{128,64},{65,129},{129,65},{192,194},{194,192},{193,195},... | collective-permute-start | bytes 786440 | tf_op jit(solution)/shard_map/ppermute | solution.py:75
  93.5 1.9 %collective-permute-start.13 = (f32[32,16,128]{2,1,0:T(8,128)S(1)}, f32[32,16,128]{2,1,0:T(8,128)S(1)}, u32[]{:S(2)}, u32[]{:S(2)}) collective-permute-start(f32[32,16,128]{2,1,0:T(8,128)S(1)} %multiply_multiply_fusion), channel_id=1, source_target_pairs={{0,64},{64,0},{1,65},{65,1},{128,192},{192,128},{129,193},{193,129... | collective-permute-start | bytes 786440 | tf_op jit(solution)/shard_map/ppermute | solution.py:75
  95.4 7.3 %collective-permute-done.12 = f32[32,16,128]{2,1,0:T(8,128)S(1)} collective-permute-done((f32[32,16,128]{2,1,0:T(8,128)S(1)}, f32[32,16,128]{2,1,0:T(8,128)S(1)}, u32[]{:S(2)}, u32[]{:S(2)}) %collective-permute-start.12) | collective-permute-done | bytes 262176 | tf_op jit(solution)/shard_map/ppermute | solution.py:75
  102.7 3.5 %collective-permute-start.14 = (f32[32,48,128]{2,1,0:T(8,128)S(1)}, f32[32,48,128]{2,1,0:T(8,128)S(1)}, u32[]{:S(2)}, u32[]{:S(2)}) collective-permute-start(f32[32,48,128]{2,1,0:T(8,128)S(1)} %pad_maximum_fusion.1), channel_id=1, source_target_pairs={{0,1},{1,0},{2,3},{3,2},{4,5},{5,4},{6,7},{7,6},{8,9},{9,8},{10,11... | collective-permute-start | bytes 2359304 | tf_op jit(solution)/shard_map/ppermute | solution.py:75
  106.2 1.7 %collective-permute-done.14 = f32[32,48,128]{2,1,0:T(8,128)S(1)} collective-permute-done((f32[32,48,128]{2,1,0:T(8,128)S(1)}, f32[32,48,128]{2,1,0:T(8,128)S(1)}, u32[]{:S(2)}, u32[]{:S(2)}) %collective-permute-start.14) | collective-permute-done | bytes 786464 | tf_op jit(solution)/shard_map/ppermute | solution.py:75
  107.9 0.6 fusion.4
  108.5 0.9 convolution_bitcast_fusion
  109.4 0.6 fusion.12
  110.0 0.6 fusion.34
  110.6 0.4 fusion.42
  111.0 0.8 convolution_bitcast_fusion.2
  111.8 2.3 %collective-permute-start.15 = (f32[32,48,128]{2,1,0:T(8,128)S(1)}, f32[32,48,128]{2,1,0:T(8,128)S(1)}, u32[]{:S(2)}, u32[]{:S(2)}) collective-permute-start(f32[32,48,128]{2,1,0:T(8,128)S(1)} %convolution_bitcast_fusion.2), channel_id=1, source_target_pairs={{0,1},{1,0},{2,3},{3,2},{4,5},{5,4},{6,7},{7,6},{8,9},{9,8},{10,11... | collective-permute-start | bytes 2359304 | tf_op jit(solution)/shard_map/ppermute | solution.py:75
  114.1 0.4 fusion.48
  114.5 0.8 convolution_bitcast_fusion.3
  115.3 0.7 collective-permute-done.15
  116.1 6.5 %collective-permute-start.16 = (f32[32,16,128]{2,1,0:T(8,128)S(1)}, f32[32,16,128]{2,1,0:T(8,128)S(1)}, u32[]{:S(2)}, u32[]{:S(2)}) collective-permute-start(f32[32,16,128]{2,1,0:T(8,128)S(1)} %get-tuple-element.39), channel_id=1, source_target_pairs={{64,128},{128,64},{65,129},{129,65},{192,194},{194,192},{193,195},... | collective-permute-start | bytes 786440 | tf_op jit(solution)/shard_map/ppermute | solution.py:75
  122.5 1.9 %collective-permute-start.17 = (f32[32,16,128]{2,1,0:T(8,128)S(1)}, f32[32,16,128]{2,1,0:T(8,128)S(1)}, u32[]{:S(2)}, u32[]{:S(2)}) collective-permute-start(f32[32,16,128]{2,1,0:T(8,128)S(1)} %get-tuple-element.38), channel_id=1, source_target_pairs={{0,64},{64,0},{1,65},{65,1},{128,192},{192,128},{129,193},{193,129... | collective-permute-start | bytes 786440 | tf_op jit(solution)/shard_map/ppermute | solution.py:75
  124.5 4.4 %collective-permute-done.16 = f32[32,16,128]{2,1,0:T(8,128)S(1)} collective-permute-done((f32[32,16,128]{2,1,0:T(8,128)S(1)}, f32[32,16,128]{2,1,0:T(8,128)S(1)}, u32[]{:S(2)}, u32[]{:S(2)}) %collective-permute-start.16) | collective-permute-done | bytes 262176 | tf_op jit(solution)/shard_map/ppermute | solution.py:75
  128.9 2.7 %collective-permute-done.17 = f32[32,16,128]{2,1,0:T(8,128)S(1)} collective-permute-done((f32[32,16,128]{2,1,0:T(8,128)S(1)}, f32[32,16,128]{2,1,0:T(8,128)S(1)}, u32[]{:S(2)}, u32[]{:S(2)}) %collective-permute-start.17) | collective-permute-done | bytes 262176 | tf_op jit(solution)/shard_map/ppermute | solution.py:75
  131.7 2.7 %collective-permute-start.18 = (f32[16,16,128]{2,1,0:T(8,128)S(1)}, f32[16,16,128]{2,1,0:T(8,128)S(1)}, u32[]{:S(2)}, u32[]{:S(2)}) collective-permute-start(f32[16,16,128]{2,1,0:T(8,128)S(1)} %get-tuple-element.45), channel_id=1, source_target_pairs={{0,256},{1,257},{2,258},{3,259},{4,260},{5,261},{6,262},{7,263},{8... | collective-permute-start | bytes 393224 | tf_op jit(solution)/shard_map/ppermute | solution.py:75
  134.4 6.9 %collective-permute-done.18 = f32[16,16,128]{2,1,0:T(8,128)S(1)} collective-permute-done((f32[16,16,128]{2,1,0:T(8,128)S(1)}, f32[16,16,128]{2,1,0:T(8,128)S(1)}, u32[]{:S(2)}, u32[]{:S(2)}) %collective-permute-start.18) | collective-permute-done | bytes 131104 | tf_op jit(solution)/shard_map/ppermute | solution.py:75
  141.3 4.0 %collective-permute-start.19 = (f32[8,16,128]{2,1,0:T(8,128)S(1)}, f32[8,16,128]{2,1,0:T(8,128)S(1)}, u32[]{:S(2)}, u32[]{:S(2)}) collective-permute-start(f32[8,16,128]{2,1,0:T(8,128)S(1)} %get-tuple-element.46), channel_id=1, source_target_pairs={{0,0},{128,1},{64,64},{192,65},{1,128},{129,129},{65,192},{193,193... | collective-permute-start | bytes 196616 | tf_op jit(solution)/shard_map/ppermute | solution.py:75
  145.3 2.9 %collective-permute-start.20 = (f32[8,16,128]{2,1,0:T(8,128)S(1)}, f32[8,16,128]{2,1,0:T(8,128)S(1)}, u32[]{:S(2)}, u32[]{:S(2)}) collective-permute-start(f32[8,16,128]{2,1,0:T(8,128)S(1)} %get-tuple-element.47), channel_id=1, source_target_pairs={{64,0},{192,1},{0,64},{128,65},{65,128},{193,129},{1,192},{129,193... | collective-permute-start | bytes 196616 | tf_op jit(solution)/shard_map/ppermute | solution.py:75
  148.2 0.2 collective-permute-done.19
  148.4 3.7 %collective-permute-done.20 = f32[8,16,128]{2,1,0:T(8,128)S(1)} collective-permute-done((f32[8,16,128]{2,1,0:T(8,128)S(1)}, f32[8,16,128]{2,1,0:T(8,128)S(1)}, u32[]{:S(2)}, u32[]{:S(2)}) %collective-permute-start.20) | collective-permute-done | bytes 65568 | tf_op jit(solution)/shard_map/ppermute | solution.py:75
  152.1 0.7 copy.12
  (47 shorter events, 1.9 us)
Async XLA Ops:
  0.9 13.2 %collective-permute-start = (f32[8,16,128]{2,1,0:T(8,128)S(1)}, f32[8,16,128]{2,1,0:T(8,128)S(1)}, u32[]{:S(2)}, u32[]{:S(2)}) collective-permute-start(f32[8,16,128]{2,1,0:T(8,128)S(1)} %bitcast.155), channel_id=1, source_target_pairs={{0,0},{1,128},{64,64},{65,192},{128,1},{129,129},{192,65},{193,193... | collective-permute-start | bytes 196616 | tf_op jit(solution)/shard_map/ppermute | solution.py:75
  6.2 8.0 %collective-permute-start.1 = (f32[8,16,128]{2,1,0:T(8,128)S(1)}, f32[8,16,128]{2,1,0:T(8,128)S(1)}, u32[]{:S(2)}, u32[]{:S(2)}) collective-permute-start(f32[8,16,128]{2,1,0:T(8,128)S(1)} %bitcast.156), channel_id=1, source_target_pairs={{0,64},{1,192},{64,0},{65,128},{128,65},{129,193},{192,1},{193,129... | collective-permute-start | bytes 196616 | tf_op jit(solution)/shard_map/ppermute | solution.py:75
  9.9 28.1 %copy-start = (f32[8,3,31]{2,0,1:T(8,128)S(1)}, f32[8,3,31]{2,0,1:T(8,128)}, u32[]{:S(2)}) copy-start(f32[8,3,31]{2,0,1:T(8,128)} %param.6) | copy-start | bytes 8932
  9.9 29.8 %copy-start.1 = (s32[8,16]{1,0:T(8,128)S(1)}, s32[8,16]{1,0:T(8,128)}, u32[]{:S(2)}) copy-start(s32[8,16]{1,0:T(8,128)} %param.7) | copy-start | bytes 1540
  9.9 36.4 %collective-permute-start.5 = (f32[16,64,128]{2,1,0:T(8,128)S(1)}, f32[16,64,128]{2,1,0:T(8,128)S(1)}, u32[]{:S(2)}, u32[]{:S(2)}) collective-permute-start(f32[16,64,128]{2,1,0:T(8,128)S(1)} %get-tuple-element.43), channel_id=1, source_target_pairs={{0,0},{1,128},{64,64},{65,192},{128,1},{129,129},{192,65},{193,193... | collective-permute-start | bytes 1572872 | tf_op jit(solution)/shard_map/ppermute | solution.py:75
  14.1 13.6 %collective-permute-start.2 = (f32[16,16,128]{2,1,0:T(8,128)S(1)}, f32[16,16,128]{2,1,0:T(8,128)S(1)}, u32[]{:S(2)}, u32[]{:S(2)}) collective-permute-start(f32[16,16,128]{2,1,0:T(8,128)S(1)} %maximum_select_fusion.2), channel_id=1, source_target_pairs={{0,256},{1,257},{2,258},{3,259},{4,260},{5,261},{6,262},{7,263},{8... | collective-permute-start | bytes 393224 | tf_op jit(solution)/shard_map/ppermute | solution.py:75
  24.9 21.4 %collective-permute-start.6 = (f32[16,64,128]{2,1,0:T(8,128)S(1)}, f32[16,64,128]{2,1,0:T(8,128)S(1)}, u32[]{:S(2)}, u32[]{:S(2)}) collective-permute-start(f32[16,64,128]{2,1,0:T(8,128)S(1)} %get-tuple-element.23), channel_id=1, source_target_pairs={{0,64},{1,192},{64,0},{65,128},{128,65},{129,193},{192,1},{193,129... | collective-permute-start | bytes 1572872 | tf_op jit(solution)/shard_map/ppermute | solution.py:75
  27.7 14.5 %collective-permute-start.3 = (f32[32,16,128]{2,1,0:T(8,128)S(1)}, f32[32,16,128]{2,1,0:T(8,128)S(1)}, u32[]{:S(2)}, u32[]{:S(2)}) collective-permute-start(f32[32,16,128]{2,1,0:T(8,128)S(1)} %maximum_select_fusion.1), channel_id=1, source_target_pairs={{64,128},{128,64},{65,129},{129,65},{192,194},{194,192},{193,195},... | collective-permute-start | bytes 786440 | tf_op jit(solution)/shard_map/ppermute | solution.py:75
  36.1 10.1 %collective-permute-start.4 = (f32[32,16,128]{2,1,0:T(8,128)S(1)}, f32[32,16,128]{2,1,0:T(8,128)S(1)}, u32[]{:S(2)}, u32[]{:S(2)}) collective-permute-start(f32[32,16,128]{2,1,0:T(8,128)S(1)} %maximum_select_fusion.1), channel_id=1, source_target_pairs={{0,64},{64,0},{1,65},{65,1},{128,192},{192,128},{129,193},{193,129... | collective-permute-start | bytes 786440 | tf_op jit(solution)/shard_map/ppermute | solution.py:75
  46.3 4.3 %collective-permute-start.7 = (f32[32,48,128]{2,1,0:T(8,128)S(1)}, f32[32,48,128]{2,1,0:T(8,128)S(1)}, u32[]{:S(2)}, u32[]{:S(2)}) collective-permute-start(f32[32,48,128]{2,1,0:T(8,128)S(1)} %pad_maximum_fusion), channel_id=1, source_target_pairs={{0,1},{1,0},{2,3},{3,2},{4,5},{5,4},{6,7},{7,6},{8,9},{9,8},{10,11... | collective-permute-start | bytes 2359304 | tf_op jit(solution)/shard_map/ppermute | solution.py:75
  54.5 4.2 %collective-permute-start.8 = (f32[32,48,128]{2,1,0:T(8,128)S(1)}, f32[32,48,128]{2,1,0:T(8,128)S(1)}, u32[]{:S(2)}, u32[]{:S(2)}) collective-permute-start(f32[32,48,128]{2,1,0:T(8,128)S(1)} %convolution_bitcast_fusion.4), channel_id=1, source_target_pairs={{0,1},{1,0},{2,3},{3,2},{4,5},{5,4},{6,7},{7,6},{8,9},{9,8},{10,11... | collective-permute-start | bytes 2359304 | tf_op jit(solution)/shard_map/ppermute | solution.py:75
  58.8 9.4 %collective-permute-start.10 = (f32[32,16,128]{2,1,0:T(8,128)S(1)}, f32[32,16,128]{2,1,0:T(8,128)S(1)}, u32[]{:S(2)}, u32[]{:S(2)}) collective-permute-start(f32[32,16,128]{2,1,0:T(8,128)S(1)} %get-tuple-element.41), channel_id=1, source_target_pairs={{0,64},{64,0},{1,65},{65,1},{128,192},{192,128},{129,193},{193,129... | collective-permute-start | bytes 786440 | tf_op jit(solution)/shard_map/ppermute | solution.py:75
  60.7 11.5 %collective-permute-start.9 = (f32[32,16,128]{2,1,0:T(8,128)S(1)}, f32[32,16,128]{2,1,0:T(8,128)S(1)}, u32[]{:S(2)}, u32[]{:S(2)}) collective-permute-start(f32[32,16,128]{2,1,0:T(8,128)S(1)} %get-tuple-element.40), channel_id=1, source_target_pairs={{64,128},{128,64},{65,129},{129,65},{192,194},{194,192},{193,195},... | collective-permute-start | bytes 786440 | tf_op jit(solution)/shard_map/ppermute | solution.py:75
  72.3 18.9 %collective-permute-start.11 = (f32[32,16,128]{2,1,0:T(8,128)S(1)}, f32[32,16,128]{2,1,0:T(8,128)S(1)}, u32[]{:S(2)}, u32[]{:S(2)}) collective-permute-start(f32[32,16,128]{2,1,0:T(8,128)S(1)} %fusion.30), channel_id=1, source_target_pairs={{0,256},{1,257},{2,258},{3,259},{4,260},{5,261},{6,262},{7,263},{8... | collective-permute-start | bytes 786440 | tf_op jit(solution)/shard_map/ppermute | solution.py:75
  91.3 11.4 %collective-permute-start.12 = (f32[32,16,128]{2,1,0:T(8,128)S(1)}, f32[32,16,128]{2,1,0:T(8,128)S(1)}, u32[]{:S(2)}, u32[]{:S(2)}) collective-permute-start(f32[32,16,128]{2,1,0:T(8,128)S(1)} %multiply_multiply_fusion), channel_id=1, source_target_pairs={{64,128},{128,64},{65,129},{129,65},{192,194},{194,192},{193,195},... | collective-permute-start | bytes 786440 | tf_op jit(solution)/shard_map/ppermute | solution.py:75
  93.5 9.2 %collective-permute-start.13 = (f32[32,16,128]{2,1,0:T(8,128)S(1)}, f32[32,16,128]{2,1,0:T(8,128)S(1)}, u32[]{:S(2)}, u32[]{:S(2)}) collective-permute-start(f32[32,16,128]{2,1,0:T(8,128)S(1)} %multiply_multiply_fusion), channel_id=1, source_target_pairs={{0,64},{64,0},{1,65},{65,1},{128,192},{192,128},{129,193},{193,129... | collective-permute-start | bytes 786440 | tf_op jit(solution)/shard_map/ppermute | solution.py:75
  102.7 5.2 %collective-permute-start.14 = (f32[32,48,128]{2,1,0:T(8,128)S(1)}, f32[32,48,128]{2,1,0:T(8,128)S(1)}, u32[]{:S(2)}, u32[]{:S(2)}) collective-permute-start(f32[32,48,128]{2,1,0:T(8,128)S(1)} %pad_maximum_fusion.1), channel_id=1, source_target_pairs={{0,1},{1,0},{2,3},{3,2},{4,5},{5,4},{6,7},{7,6},{8,9},{9,8},{10,11... | collective-permute-start | bytes 2359304 | tf_op jit(solution)/shard_map/ppermute | solution.py:75
  111.8 4.2 %collective-permute-start.15 = (f32[32,48,128]{2,1,0:T(8,128)S(1)}, f32[32,48,128]{2,1,0:T(8,128)S(1)}, u32[]{:S(2)}, u32[]{:S(2)}) collective-permute-start(f32[32,48,128]{2,1,0:T(8,128)S(1)} %convolution_bitcast_fusion.2), channel_id=1, source_target_pairs={{0,1},{1,0},{2,3},{3,2},{4,5},{5,4},{6,7},{7,6},{8,9},{9,8},{10,11... | collective-permute-start | bytes 2359304 | tf_op jit(solution)/shard_map/ppermute | solution.py:75
  116.1 12.8 %collective-permute-start.16 = (f32[32,16,128]{2,1,0:T(8,128)S(1)}, f32[32,16,128]{2,1,0:T(8,128)S(1)}, u32[]{:S(2)}, u32[]{:S(2)}) collective-permute-start(f32[32,16,128]{2,1,0:T(8,128)S(1)} %get-tuple-element.39), channel_id=1, source_target_pairs={{64,128},{128,64},{65,129},{129,65},{192,194},{194,192},{193,195},... | collective-permute-start | bytes 786440 | tf_op jit(solution)/shard_map/ppermute | solution.py:75
  122.5 9.1 %collective-permute-start.17 = (f32[32,16,128]{2,1,0:T(8,128)S(1)}, f32[32,16,128]{2,1,0:T(8,128)S(1)}, u32[]{:S(2)}, u32[]{:S(2)}) collective-permute-start(f32[32,16,128]{2,1,0:T(8,128)S(1)} %get-tuple-element.38), channel_id=1, source_target_pairs={{0,64},{64,0},{1,65},{65,1},{128,192},{192,128},{129,193},{193,129... | collective-permute-start | bytes 786440 | tf_op jit(solution)/shard_map/ppermute | solution.py:75
  131.7 9.6 %collective-permute-start.18 = (f32[16,16,128]{2,1,0:T(8,128)S(1)}, f32[16,16,128]{2,1,0:T(8,128)S(1)}, u32[]{:S(2)}, u32[]{:S(2)}) collective-permute-start(f32[16,16,128]{2,1,0:T(8,128)S(1)} %get-tuple-element.45), channel_id=1, source_target_pairs={{0,256},{1,257},{2,258},{3,259},{4,260},{5,261},{6,262},{7,263},{8... | collective-permute-start | bytes 393224 | tf_op jit(solution)/shard_map/ppermute | solution.py:75
  141.3 7.1 %collective-permute-start.19 = (f32[8,16,128]{2,1,0:T(8,128)S(1)}, f32[8,16,128]{2,1,0:T(8,128)S(1)}, u32[]{:S(2)}, u32[]{:S(2)}) collective-permute-start(f32[8,16,128]{2,1,0:T(8,128)S(1)} %get-tuple-element.46), channel_id=1, source_target_pairs={{0,0},{128,1},{64,64},{192,65},{1,128},{129,129},{65,192},{193,193... | collective-permute-start | bytes 196616 | tf_op jit(solution)/shard_map/ppermute | solution.py:75
  145.3 6.8 %collective-permute-start.20 = (f32[8,16,128]{2,1,0:T(8,128)S(1)}, f32[8,16,128]{2,1,0:T(8,128)S(1)}, u32[]{:S(2)}, u32[]{:S(2)}) collective-permute-start(f32[8,16,128]{2,1,0:T(8,128)S(1)} %get-tuple-element.47), channel_id=1, source_target_pairs={{64,0},{192,1},{0,64},{128,65},{65,128},{193,129},{1,192},{129,193... | collective-permute-start | bytes 196616 | tf_op jit(solution)/shard_map/ppermute | solution.py:75

commit v15 on v14

--- a/solution.py
+++ b/solution.py
@@ -110,7 +110,8 @@
     quarter = joined([send(piece(flipped, turn, 1), SPREAD[turn]) for turn in (0, 1)], even, 0)
     current = by_h(quarter, send(quarter, SWAP_H), h)
     images = [piece(observed[0], turn, 0) for turn in (0, 1)]
-    images[1], _ = lax.optimization_barrier((images[1], quarter))
+    images[0], _ = lax.optimization_barrier((images[0], quarter))
+    images[1], _ = lax.optimization_barrier((images[1], current))
     images = [send(image, SPREAD[turn]) for turn, image in enumerate(images)]
     psf_taps, intersection, current = lax.optimization_barrier((psf_taps, intersection, current))
 

time: 154 us -> 159 us (1.032)
  waiting for transfers between devices: 56.5 us -> 61.5 us
  starting transfers between devices: 77 us -> 78.6 us
    ppermute x21, waiting for transfers between devices: 56.5 us -> 61.5 us  [send(): return lax.ppermute(value, AXES, pairs)]
  transfers between devices with their start and end apart: 21 -> 21, of which waited for: 15 -> 18; matrix products, arithmetic and copies ran while one was open for 6% -> 5% of each run, Pallas kernels for 0% -> 0%
where the time goes in v15:
time: 159 us; the launch traced here: 158 us
  starting transfers between devices  78.6 us (49%)
  waiting for transfers between devices  61.5 us (39%)
  matrix products  14.2 us (9%)
  local copies, waits for them, and re-layouts  1.98 us (1%)
    ppermute x21, starting transfers between devices, send(): return lax.ppermute(value, AXES, pairs)  78.6 us
    ppermute x21, waiting for transfers between devices, send(): return lax.ppermute(value, AXES, pairs)  61.5 us
  transfers between devices with their start and end apart: 21, of which 18 were waited for; matrix products, arithmetic and copies ran while one was open for 5% of the time, Pallas kernels for 0%

profile of v15, /device:TPU:57, one launch (start us, length us, event | category | flops | bytes accessed | tf_op | source)
XLA Modules:
  0.0 158.3 jit_solution(1026342769185928595)
XLA Ops:
  0.0 1.0 constant_dynamic-slice_fusion.1
  1.0 5.2 %collective-permute-start = (f32[8,16,128]{2,1,0:T(8,128)S(1)}, f32[8,16,128]{2,1,0:T(8,128)S(1)}, u32[]{:S(2)}, u32[]{:S(2)}) collective-permute-start(f32[8,16,128]{2,1,0:T(8,128)S(1)} %bitcast.155), channel_id=1, source_target_pairs={{0,0},{1,128},{64,64},{65,192},{128,1},{129,129},{192,65},{193,193... | collective-permute-start | bytes 196616 | tf_op jit(solution)/shard_map/ppermute | solution.py:75
  6.2 2.5 %collective-permute-start.1 = (f32[8,16,128]{2,1,0:T(8,128)S(1)}, f32[8,16,128]{2,1,0:T(8,128)S(1)}, u32[]{:S(2)}, u32[]{:S(2)}) collective-permute-start(f32[8,16,128]{2,1,0:T(8,128)S(1)} %bitcast.156), channel_id=1, source_target_pairs={{0,64},{1,192},{64,0},{65,128},{128,65},{129,193},{192,1},{193,129... | collective-permute-start | bytes 196616 | tf_op jit(solution)/shard_map/ppermute | solution.py:75
  9.3 3.8 %collective-permute-done.1 = f32[8,16,128]{2,1,0:T(8,128)S(1)} collective-permute-done((f32[8,16,128]{2,1,0:T(8,128)S(1)}, f32[8,16,128]{2,1,0:T(8,128)S(1)}, u32[]{:S(2)}, u32[]{:S(2)}) %collective-permute-start.1) | collective-permute-done | bytes 65568 | tf_op jit(solution)/shard_map/ppermute | solution.py:75
  13.1 10.6 %collective-permute-start.2 = (f32[16,16,128]{2,1,0:T(8,128)S(1)}, f32[16,16,128]{2,1,0:T(8,128)S(1)}, u32[]{:S(2)}, u32[]{:S(2)}) collective-permute-start(f32[16,16,128]{2,1,0:T(8,128)S(1)} %maximum_select_fusion.2), channel_id=1, source_target_pairs={{0,256},{1,257},{2,258},{3,259},{4,260},{5,261},{6,262},{7,263},{8... | collective-permute-start | bytes 393224 | tf_op jit(solution)/shard_map/ppermute | solution.py:75
  23.8 1.9 %collective-permute-start.5 = (f32[16,64,128]{2,1,0:T(8,128)S(1)}, f32[16,64,128]{2,1,0:T(8,128)S(1)}, u32[]{:S(2)}, u32[]{:S(2)}) collective-permute-start(f32[16,64,128]{2,1,0:T(8,128)S(1)} %get-tuple-element.24), channel_id=1, source_target_pairs={{0,0},{1,128},{64,64},{65,192},{128,1},{129,129},{192,65},{193,193... | collective-permute-start | bytes 1572872 | tf_op jit(solution)/shard_map/ppermute | solution.py:75
  25.8 0.4 collective-permute-done.2
  26.2 7.9 %collective-permute-start.3 = (f32[32,16,128]{2,1,0:T(8,128)S(1)}, f32[32,16,128]{2,1,0:T(8,128)S(1)}, u32[]{:S(2)}, u32[]{:S(2)}) collective-permute-start(f32[32,16,128]{2,1,0:T(8,128)S(1)} %maximum_select_fusion.1), channel_id=1, source_target_pairs={{64,128},{128,64},{65,129},{129,65},{192,194},{194,192},{193,195},... | collective-permute-start | bytes 786440 | tf_op jit(solution)/shard_map/ppermute | solution.py:75
  34.1 1.9 %collective-permute-start.4 = (f32[32,16,128]{2,1,0:T(8,128)S(1)}, f32[32,16,128]{2,1,0:T(8,128)S(1)}, u32[]{:S(2)}, u32[]{:S(2)}) collective-permute-start(f32[32,16,128]{2,1,0:T(8,128)S(1)} %maximum_select_fusion.1), channel_id=1, source_target_pairs={{0,64},{64,0},{1,65},{65,1},{128,192},{192,128},{129,193},{193,129... | collective-permute-start | bytes 786440 | tf_op jit(solution)/shard_map/ppermute | solution.py:75
  36.2 0.2 fusion.75
  36.4 0.4 fusion.18
  36.8 0.8 fusion
  37.6 1.9 %collective-permute-start.6 = (f32[16,64,128]{2,1,0:T(8,128)S(1)}, f32[16,64,128]{2,1,0:T(8,128)S(1)}, u32[]{:S(2)}, u32[]{:S(2)}) collective-permute-start(f32[16,64,128]{2,1,0:T(8,128)S(1)} %get-tuple-element.25), channel_id=1, source_target_pairs={{0,64},{1,192},{64,0},{65,128},{128,65},{129,193},{192,1},{193,129... | collective-permute-start | bytes 1572872 | tf_op jit(solution)/shard_map/ppermute | solution.py:75
  40.2 0.3 collective-permute-done.3
  40.5 3.6 %collective-permute-done.4 = f32[32,16,128]{2,1,0:T(8,128)S(1)} collective-permute-done((f32[32,16,128]{2,1,0:T(8,128)S(1)}, f32[32,16,128]{2,1,0:T(8,128)S(1)}, u32[]{:S(2)}, u32[]{:S(2)}) %collective-permute-start.4) | collective-permute-done | bytes 262176 | tf_op jit(solution)/shard_map/ppermute | solution.py:75
  44.1 5.2 %collective-permute-done.6 = f32[16,64,128]{2,1,0:T(8,128)S(1)} collective-permute-done((f32[16,64,128]{2,1,0:T(8,128)S(1)}, f32[16,64,128]{2,1,0:T(8,128)S(1)}, u32[]{:S(2)}, u32[]{:S(2)}) %collective-permute-start.6) | collective-permute-done | bytes 524320 | tf_op jit(solution)/shard_map/ppermute | solution.py:75
  49.3 3.0 %collective-permute-start.7 = (f32[32,48,128]{2,1,0:T(8,128)S(1)}, f32[32,48,128]{2,1,0:T(8,128)S(1)}, u32[]{:S(2)}, u32[]{:S(2)}) collective-permute-start(f32[32,48,128]{2,1,0:T(8,128)S(1)} %pad_maximum_fusion), channel_id=1, source_target_pairs={{0,1},{1,0},{2,3},{3,2},{4,5},{5,4},{6,7},{7,6},{8,9},{9,8},{10,11... | collective-permute-start | bytes 2359304 | tf_op jit(solution)/shard_map/ppermute | solution.py:75
  52.4 1.7 %collective-permute-done.7 = f32[32,48,128]{2,1,0:T(8,128)S(1)} collective-permute-done((f32[32,48,128]{2,1,0:T(8,128)S(1)}, f32[32,48,128]{2,1,0:T(8,128)S(1)}, u32[]{:S(2)}, u32[]{:S(2)}) %collective-permute-start.7) | collective-permute-done | bytes 786464 | tf_op jit(solution)/shard_map/ppermute | solution.py:75
  54.2 0.6 fusion.1
  54.7 0.9 convolution_bitcast_fusion.1
  55.6 0.6 fusion.11
  56.2 0.6 fusion.37
  56.8 0.4 fusion.44
  57.3 0.8 convolution_bitcast_fusion.4
  58.0 2.3 %collective-permute-start.8 = (f32[32,48,128]{2,1,0:T(8,128)S(1)}, f32[32,48,128]{2,1,0:T(8,128)S(1)}, u32[]{:S(2)}, u32[]{:S(2)}) collective-permute-start(f32[32,48,128]{2,1,0:T(8,128)S(1)} %convolution_bitcast_fusion.4), channel_id=1, source_target_pairs={{0,1},{1,0},{2,3},{3,2},{4,5},{5,4},{6,7},{7,6},{8,9},{9,8},{10,11... | collective-permute-start | bytes 2359304 | tf_op jit(solution)/shard_map/ppermute | solution.py:75
  60.3 0.4 fusion.50
  60.8 0.8 convolution_bitcast_fusion.5
  61.5 0.7 collective-permute-done.8
  62.3 1.9 %collective-permute-start.10 = (f32[32,16,128]{2,1,0:T(8,128)S(1)}, f32[32,16,128]{2,1,0:T(8,128)S(1)}, u32[]{:S(2)}, u32[]{:S(2)}) collective-permute-start(f32[32,16,128]{2,1,0:T(8,128)S(1)} %get-tuple-element.43), channel_id=1, source_target_pairs={{0,64},{64,0},{1,65},{65,1},{128,192},{192,128},{129,193},{193,129... | collective-permute-start | bytes 786440 | tf_op jit(solution)/shard_map/ppermute | solution.py:75
  64.2 4.8 %collective-permute-start.9 = (f32[32,16,128]{2,1,0:T(8,128)S(1)}, f32[32,16,128]{2,1,0:T(8,128)S(1)}, u32[]{:S(2)}, u32[]{:S(2)}) collective-permute-start(f32[32,16,128]{2,1,0:T(8,128)S(1)} %get-tuple-element.42), channel_id=1, source_target_pairs={{64,128},{128,64},{65,129},{129,65},{192,194},{194,192},{193,195},... | collective-permute-start | bytes 786440 | tf_op jit(solution)/shard_map/ppermute | solution.py:75
  69.0 2.7 %collective-permute-done.10 = f32[32,16,128]{2,1,0:T(8,128)S(1)} collective-permute-done((f32[32,16,128]{2,1,0:T(8,128)S(1)}, f32[32,16,128]{2,1,0:T(8,128)S(1)}, u32[]{:S(2)}, u32[]{:S(2)}) %collective-permute-start.10) | collective-permute-done | bytes 262176 | tf_op jit(solution)/shard_map/ppermute | solution.py:75
  71.7 3.7 %collective-permute-done.9 = f32[32,16,128]{2,1,0:T(8,128)S(1)} collective-permute-done((f32[32,16,128]{2,1,0:T(8,128)S(1)}, f32[32,16,128]{2,1,0:T(8,128)S(1)}, u32[]{:S(2)}, u32[]{:S(2)}) %collective-permute-start.9) | collective-permute-done | bytes 262176 | tf_op jit(solution)/shard_map/ppermute | solution.py:75
  75.5 3.5 %collective-permute-start.11 = (f32[32,16,128]{2,1,0:T(8,128)S(1)}, f32[32,16,128]{2,1,0:T(8,128)S(1)}, u32[]{:S(2)}, u32[]{:S(2)}) collective-permute-start(f32[32,16,128]{2,1,0:T(8,128)S(1)} %fusion.30), channel_id=1, source_target_pairs={{0,256},{1,257},{2,258},{3,259},{4,260},{5,261},{6,262},{7,263},{8... | collective-permute-start | bytes 786440 | tf_op jit(solution)/shard_map/ppermute | solution.py:75
  79.4 0.7 fusion.28
  80.1 0.2 fusion.84
  80.3 0.3 fusion.52
  80.7 0.8 fusion.13
  81.5 11.9 %collective-permute-done.11 = f32[32,16,128]{2,1,0:T(8,128)S(1)} collective-permute-done((f32[32,16,128]{2,1,0:T(8,128)S(1)}, f32[32,16,128]{2,1,0:T(8,128)S(1)}, u32[]{:S(2)}, u32[]{:S(2)}) %collective-permute-start.11) | collective-permute-done | bytes 262176 | tf_op jit(solution)/shard_map/ppermute | solution.py:75
  93.5 5.2 %collective-permute-start.12 = (f32[32,16,128]{2,1,0:T(8,128)S(1)}, f32[32,16,128]{2,1,0:T(8,128)S(1)}, u32[]{:S(2)}, u32[]{:S(2)}) collective-permute-start(f32[32,16,128]{2,1,0:T(8,128)S(1)} %multiply_multiply_fusion), channel_id=1, source_target_pairs={{64,128},{128,64},{65,129},{129,65},{192,194},{194,192},{193,195},... | collective-permute-start | bytes 786440 | tf_op jit(solution)/shard_map/ppermute | solution.py:75
  98.7 1.9 %collective-permute-start.13 = (f32[32,16,128]{2,1,0:T(8,128)S(1)}, f32[32,16,128]{2,1,0:T(8,128)S(1)}, u32[]{:S(2)}, u32[]{:S(2)}) collective-permute-start(f32[32,16,128]{2,1,0:T(8,128)S(1)} %multiply_multiply_fusion), channel_id=1, source_target_pairs={{0,64},{64,0},{1,65},{65,1},{128,192},{192,128},{129,193},{193,129... | collective-permute-start | bytes 786440 | tf_op jit(solution)/shard_map/ppermute | solution.py:75
  100.6 3.1 %collective-permute-done.12 = f32[32,16,128]{2,1,0:T(8,128)S(1)} collective-permute-done((f32[32,16,128]{2,1,0:T(8,128)S(1)}, f32[32,16,128]{2,1,0:T(8,128)S(1)}, u32[]{:S(2)}, u32[]{:S(2)}) %collective-permute-start.12) | collective-permute-done | bytes 262176 | tf_op jit(solution)/shard_map/ppermute | solution.py:75
  103.7 3.8 %collective-permute-done.13 = f32[32,16,128]{2,1,0:T(8,128)S(1)} collective-permute-done((f32[32,16,128]{2,1,0:T(8,128)S(1)}, f32[32,16,128]{2,1,0:T(8,128)S(1)}, u32[]{:S(2)}, u32[]{:S(2)}) %collective-permute-start.13) | collective-permute-done | bytes 262176 | tf_op jit(solution)/shard_map/ppermute | solution.py:75
  107.5 3.9 %collective-permute-start.14 = (f32[32,48,128]{2,1,0:T(8,128)S(1)}, f32[32,48,128]{2,1,0:T(8,128)S(1)}, u32[]{:S(2)}, u32[]{:S(2)}) collective-permute-start(f32[32,48,128]{2,1,0:T(8,128)S(1)} %pad_maximum_fusion.1), channel_id=1, source_target_pairs={{0,1},{1,0},{2,3},{3,2},{4,5},{5,4},{6,7},{7,6},{8,9},{9,8},{10,11... | collective-permute-start | bytes 2359304 | tf_op jit(solution)/shard_map/ppermute | solution.py:75
  111.4 1.7 %collective-permute-done.14 = f32[32,48,128]{2,1,0:T(8,128)S(1)} collective-permute-done((f32[32,48,128]{2,1,0:T(8,128)S(1)}, f32[32,48,128]{2,1,0:T(8,128)S(1)}, u32[]{:S(2)}, u32[]{:S(2)}) %collective-permute-start.14) | collective-permute-done | bytes 786464 | tf_op jit(solution)/shard_map/ppermute | solution.py:75
  113.1 0.6 fusion.4
  113.7 0.9 convolution_bitcast_fusion
  114.6 0.6 fusion.12
  115.2 0.6 fusion.34
  115.8 0.4 fusion.42
  116.3 0.8 convolution_bitcast_fusion.2
  117.0 2.3 %collective-permute-start.15 = (f32[32,48,128]{2,1,0:T(8,128)S(1)}, f32[32,48,128]{2,1,0:T(8,128)S(1)}, u32[]{:S(2)}, u32[]{:S(2)}) collective-permute-start(f32[32,48,128]{2,1,0:T(8,128)S(1)} %convolution_bitcast_fusion.2), channel_id=1, source_target_pairs={{0,1},{1,0},{2,3},{3,2},{4,5},{5,4},{6,7},{7,6},{8,9},{9,8},{10,11... | collective-permute-start | bytes 2359304 | tf_op jit(solution)/shard_map/ppermute | solution.py:75
  119.3 0.4 fusion.48
  119.7 0.8 convolution_bitcast_fusion.3
  120.5 0.7 collective-permute-done.15
  121.3 3.5 %collective-permute-start.16 = (f32[32,16,128]{2,1,0:T(8,128)S(1)}, f32[32,16,128]{2,1,0:T(8,128)S(1)}, u32[]{:S(2)}, u32[]{:S(2)}) collective-permute-start(f32[32,16,128]{2,1,0:T(8,128)S(1)} %get-tuple-element.41), channel_id=1, source_target_pairs={{64,128},{128,64},{65,129},{129,65},{192,194},{194,192},{193,195},... | collective-permute-start | bytes 786440 | tf_op jit(solution)/shard_map/ppermute | solution.py:75
  124.8 1.9 %collective-permute-start.17 = (f32[32,16,128]{2,1,0:T(8,128)S(1)}, f32[32,16,128]{2,1,0:T(8,128)S(1)}, u32[]{:S(2)}, u32[]{:S(2)}) collective-permute-start(f32[32,16,128]{2,1,0:T(8,128)S(1)} %get-tuple-element.40), channel_id=1, source_target_pairs={{0,64},{64,0},{1,65},{65,1},{128,192},{192,128},{129,193},{193,129... | collective-permute-start | bytes 786440 | tf_op jit(solution)/shard_map/ppermute | solution.py:75
  126.8 6.0 %collective-permute-done.16 = f32[32,16,128]{2,1,0:T(8,128)S(1)} collective-permute-done((f32[32,16,128]{2,1,0:T(8,128)S(1)}, f32[32,16,128]{2,1,0:T(8,128)S(1)}, u32[]{:S(2)}, u32[]{:S(2)}) %collective-permute-start.16) | collective-permute-done | bytes 262176 | tf_op jit(solution)/shard_map/ppermute | solution.py:75
  132.8 1.1 collective-permute-done.17
  134.0 5.1 %collective-permute-start.18 = (f32[16,16,128]{2,1,0:T(8,128)S(1)}, f32[16,16,128]{2,1,0:T(8,128)S(1)}, u32[]{:S(2)}, u32[]{:S(2)}) collective-permute-start(f32[16,16,128]{2,1,0:T(8,128)S(1)} %get-tuple-element.47), channel_id=1, source_target_pairs={{0,256},{1,257},{2,258},{3,259},{4,260},{5,261},{6,262},{7,263},{8... | collective-permute-start | bytes 393224 | tf_op jit(solution)/shard_map/ppermute | solution.py:75
  139.1 7.9 %collective-permute-done.18 = f32[16,16,128]{2,1,0:T(8,128)S(1)} collective-permute-done((f32[16,16,128]{2,1,0:T(8,128)S(1)}, f32[16,16,128]{2,1,0:T(8,128)S(1)}, u32[]{:S(2)}, u32[]{:S(2)}) %collective-permute-start.18) | collective-permute-done | bytes 131104 | tf_op jit(solution)/shard_map/ppermute | solution.py:75
  147.1 3.6 %collective-permute-start.19 = (f32[8,16,128]{2,1,0:T(8,128)S(1)}, f32[8,16,128]{2,1,0:T(8,128)S(1)}, u32[]{:S(2)}, u32[]{:S(2)}) collective-permute-start(f32[8,16,128]{2,1,0:T(8,128)S(1)} %get-tuple-element.48), channel_id=1, source_target_pairs={{0,0},{128,1},{64,64},{192,65},{1,128},{129,129},{65,192},{193,193... | collective-permute-start | bytes 196616 | tf_op jit(solution)/shard_map/ppermute | solution.py:75
  150.7 3.7 %collective-permute-start.20 = (f32[8,16,128]{2,1,0:T(8,128)S(1)}, f32[8,16,128]{2,1,0:T(8,128)S(1)}, u32[]{:S(2)}, u32[]{:S(2)}) collective-permute-start(f32[8,16,128]{2,1,0:T(8,128)S(1)} %get-tuple-element.49), channel_id=1, source_target_pairs={{64,0},{192,1},{0,64},{128,65},{65,128},{193,129},{1,192},{129,193... | collective-permute-start | bytes 196616 | tf_op jit(solution)/shard_map/ppermute | solution.py:75
  154.4 3.1 %collective-permute-done.20 = f32[8,16,128]{2,1,0:T(8,128)S(1)} collective-permute-done((f32[8,16,128]{2,1,0:T(8,128)S(1)}, f32[8,16,128]{2,1,0:T(8,128)S(1)}, u32[]{:S(2)}, u32[]{:S(2)}) %collective-permute-start.20) | collective-permute-done | bytes 65568 | tf_op jit(solution)/shard_map/ppermute | solution.py:75
  157.5 0.7 copy.12
  (49 shorter events, 2.4 us)
Async XLA Ops:
  0.0 23.7 %copy-start = (f32[1,32,64,128]{3,2,1,0:T(8,128)S(1)}, f32[1,32,64,128]{3,2,1,0:T(8,128)}, u32[]{:S(2)}) copy-start(f32[1,32,64,128]{3,2,1,0:T(8,128)} %param.5) | copy-start | bytes 3145732
  1.0 8.3 %collective-permute-start = (f32[8,16,128]{2,1,0:T(8,128)S(1)}, f32[8,16,128]{2,1,0:T(8,128)S(1)}, u32[]{:S(2)}, u32[]{:S(2)}) collective-permute-start(f32[8,16,128]{2,1,0:T(8,128)S(1)} %bitcast.155), channel_id=1, source_target_pairs={{0,0},{1,128},{64,64},{65,192},{128,1},{129,129},{192,65},{193,193... | collective-permute-start | bytes 196616 | tf_op jit(solution)/shard_map/ppermute | solution.py:75
  6.2 6.8 %collective-permute-start.1 = (f32[8,16,128]{2,1,0:T(8,128)S(1)}, f32[8,16,128]{2,1,0:T(8,128)S(1)}, u32[]{:S(2)}, u32[]{:S(2)}) collective-permute-start(f32[8,16,128]{2,1,0:T(8,128)S(1)} %bitcast.156), channel_id=1, source_target_pairs={{0,64},{1,192},{64,0},{65,128},{128,65},{129,193},{192,1},{193,129... | collective-permute-start | bytes 196616 | tf_op jit(solution)/shard_map/ppermute | solution.py:75
  13.1 23.0 %copy-start.1 = (f32[8,3,31]{2,0,1:T(8,128)S(1)}, f32[8,3,31]{2,0,1:T(8,128)}, u32[]{:S(2)}) copy-start(f32[8,3,31]{2,0,1:T(8,128)} %param.6) | copy-start | bytes 8932
  13.1 13.1 %collective-permute-start.2 = (f32[16,16,128]{2,1,0:T(8,128)S(1)}, f32[16,16,128]{2,1,0:T(8,128)S(1)}, u32[]{:S(2)}, u32[]{:S(2)}) collective-permute-start(f32[16,16,128]{2,1,0:T(8,128)S(1)} %maximum_select_fusion.2), channel_id=1, source_target_pairs={{0,256},{1,257},{2,258},{3,259},{4,260},{5,261},{6,262},{7,263},{8... | collective-permute-start | bytes 393224 | tf_op jit(solution)/shard_map/ppermute | solution.py:75
  23.8 15.9 %copy-start.2 = (s32[8,16]{1,0:T(8,128)S(1)}, s32[8,16]{1,0:T(8,128)}, u32[]{:S(2)}) copy-start(s32[8,16]{1,0:T(8,128)} %param.7) | copy-start | bytes 1540
  23.8 20.3 %collective-permute-start.5 = (f32[16,64,128]{2,1,0:T(8,128)S(1)}, f32[16,64,128]{2,1,0:T(8,128)S(1)}, u32[]{:S(2)}, u32[]{:S(2)}) collective-permute-start(f32[16,64,128]{2,1,0:T(8,128)S(1)} %get-tuple-element.24), channel_id=1, source_target_pairs={{0,0},{1,128},{64,64},{65,192},{128,1},{129,129},{192,65},{193,193... | collective-permute-start | bytes 1572872 | tf_op jit(solution)/shard_map/ppermute | solution.py:75
  26.2 14.3 %collective-permute-start.3 = (f32[32,16,128]{2,1,0:T(8,128)S(1)}, f32[32,16,128]{2,1,0:T(8,128)S(1)}, u32[]{:S(2)}, u32[]{:S(2)}) collective-permute-start(f32[32,16,128]{2,1,0:T(8,128)S(1)} %maximum_select_fusion.1), channel_id=1, source_target_pairs={{64,128},{128,64},{65,129},{129,65},{192,194},{194,192},{193,195},... | collective-permute-start | bytes 786440 | tf_op jit(solution)/shard_map/ppermute | solution.py:75
  34.1 9.9 %collective-permute-start.4 = (f32[32,16,128]{2,1,0:T(8,128)S(1)}, f32[32,16,128]{2,1,0:T(8,128)S(1)}, u32[]{:S(2)}, u32[]{:S(2)}) collective-permute-start(f32[32,16,128]{2,1,0:T(8,128)S(1)} %maximum_select_fusion.1), channel_id=1, source_target_pairs={{0,64},{64,0},{1,65},{65,1},{128,192},{192,128},{129,193},{193,129... | collective-permute-start | bytes 786440 | tf_op jit(solution)/shard_map/ppermute | solution.py:75
  37.6 11.7 %collective-permute-start.6 = (f32[16,64,128]{2,1,0:T(8,128)S(1)}, f32[16,64,128]{2,1,0:T(8,128)S(1)}, u32[]{:S(2)}, u32[]{:S(2)}) collective-permute-start(f32[16,64,128]{2,1,0:T(8,128)S(1)} %get-tuple-element.25), channel_id=1, source_target_pairs={{0,64},{1,192},{64,0},{65,128},{128,65},{129,193},{192,1},{193,129... | collective-permute-start | bytes 1572872 | tf_op jit(solution)/shard_map/ppermute | solution.py:75
  49.3 4.9 %collective-permute-start.7 = (f32[32,48,128]{2,1,0:T(8,128)S(1)}, f32[32,48,128]{2,1,0:T(8,128)S(1)}, u32[]{:S(2)}, u32[]{:S(2)}) collective-permute-start(f32[32,48,128]{2,1,0:T(8,128)S(1)} %pad_maximum_fusion), channel_id=1, source_target_pairs={{0,1},{1,0},{2,3},{3,2},{4,5},{5,4},{6,7},{7,6},{8,9},{9,8},{10,11... | collective-permute-start | bytes 2359304 | tf_op jit(solution)/shard_map/ppermute | solution.py:75
  58.0 4.2 %collective-permute-start.8 = (f32[32,48,128]{2,1,0:T(8,128)S(1)}, f32[32,48,128]{2,1,0:T(8,128)S(1)}, u32[]{:S(2)}, u32[]{:S(2)}) collective-permute-start(f32[32,48,128]{2,1,0:T(8,128)S(1)} %convolution_bitcast_fusion.4), channel_id=1, source_target_pairs={{0,1},{1,0},{2,3},{3,2},{4,5},{5,4},{6,7},{7,6},{8,9},{9,8},{10,11... | collective-permute-start | bytes 2359304 | tf_op jit(solution)/shard_map/ppermute | solution.py:75
  62.3 9.4 %collective-permute-start.10 = (f32[32,16,128]{2,1,0:T(8,128)S(1)}, f32[32,16,128]{2,1,0:T(8,128)S(1)}, u32[]{:S(2)}, u32[]{:S(2)}) collective-permute-start(f32[32,16,128]{2,1,0:T(8,128)S(1)} %get-tuple-element.43), channel_id=1, source_target_pairs={{0,64},{64,0},{1,65},{65,1},{128,192},{192,128},{129,193},{193,129... | collective-permute-start | bytes 786440 | tf_op jit(solution)/shard_map/ppermute | solution.py:75
  64.2 11.2 %collective-permute-start.9 = (f32[32,16,128]{2,1,0:T(8,128)S(1)}, f32[32,16,128]{2,1,0:T(8,128)S(1)}, u32[]{:S(2)}, u32[]{:S(2)}) collective-permute-start(f32[32,16,128]{2,1,0:T(8,128)S(1)} %get-tuple-element.42), channel_id=1, source_target_pairs={{64,128},{128,64},{65,129},{129,65},{192,194},{194,192},{193,195},... | collective-permute-start | bytes 786440 | tf_op jit(solution)/shard_map/ppermute | solution.py:75
  75.5 17.9 %collective-permute-start.11 = (f32[32,16,128]{2,1,0:T(8,128)S(1)}, f32[32,16,128]{2,1,0:T(8,128)S(1)}, u32[]{:S(2)}, u32[]{:S(2)}) collective-permute-start(f32[32,16,128]{2,1,0:T(8,128)S(1)} %fusion.30), channel_id=1, source_target_pairs={{0,256},{1,257},{2,258},{3,259},{4,260},{5,261},{6,262},{7,263},{8... | collective-permute-start | bytes 786440 | tf_op jit(solution)/shard_map/ppermute | solution.py:75
  93.5 10.2 %collective-permute-start.12 = (f32[32,16,128]{2,1,0:T(8,128)S(1)}, f32[32,16,128]{2,1,0:T(8,128)S(1)}, u32[]{:S(2)}, u32[]{:S(2)}) collective-permute-start(f32[32,16,128]{2,1,0:T(8,128)S(1)} %multiply_multiply_fusion), channel_id=1, source_target_pairs={{64,128},{128,64},{65,129},{129,65},{192,194},{194,192},{193,195},... | collective-permute-start | bytes 786440 | tf_op jit(solution)/shard_map/ppermute | solution.py:75
  98.7 8.8 %collective-permute-start.13 = (f32[32,16,128]{2,1,0:T(8,128)S(1)}, f32[32,16,128]{2,1,0:T(8,128)S(1)}, u32[]{:S(2)}, u32[]{:S(2)}) collective-permute-start(f32[32,16,128]{2,1,0:T(8,128)S(1)} %multiply_multiply_fusion), channel_id=1, source_target_pairs={{0,64},{64,0},{1,65},{65,1},{128,192},{192,128},{129,193},{193,129... | collective-permute-start | bytes 786440 | tf_op jit(solution)/shard_map/ppermute | solution.py:75
  107.5 5.6 %collective-permute-start.14 = (f32[32,48,128]{2,1,0:T(8,128)S(1)}, f32[32,48,128]{2,1,0:T(8,128)S(1)}, u32[]{:S(2)}, u32[]{:S(2)}) collective-permute-start(f32[32,48,128]{2,1,0:T(8,128)S(1)} %pad_maximum_fusion.1), channel_id=1, source_target_pairs={{0,1},{1,0},{2,3},{3,2},{4,5},{5,4},{6,7},{7,6},{8,9},{9,8},{10,11... | collective-permute-start | bytes 2359304 | tf_op jit(solution)/shard_map/ppermute | solution.py:75
  117.0 4.2 %collective-permute-start.15 = (f32[32,48,128]{2,1,0:T(8,128)S(1)}, f32[32,48,128]{2,1,0:T(8,128)S(1)}, u32[]{:S(2)}, u32[]{:S(2)}) collective-permute-start(f32[32,48,128]{2,1,0:T(8,128)S(1)} %convolution_bitcast_fusion.2), channel_id=1, source_target_pairs={{0,1},{1,0},{2,3},{3,2},{4,5},{5,4},{6,7},{7,6},{8,9},{9,8},{10,11... | collective-permute-start | bytes 2359304 | tf_op jit(solution)/shard_map/ppermute | solution.py:75
  121.3 11.5 %collective-permute-start.16 = (f32[32,16,128]{2,1,0:T(8,128)S(1)}, f32[32,16,128]{2,1,0:T(8,128)S(1)}, u32[]{:S(2)}, u32[]{:S(2)}) collective-permute-start(f32[32,16,128]{2,1,0:T(8,128)S(1)} %get-tuple-element.41), channel_id=1, source_target_pairs={{64,128},{128,64},{65,129},{129,65},{192,194},{194,192},{193,195},... | collective-permute-start | bytes 786440 | tf_op jit(solution)/shard_map/ppermute | solution.py:75
  124.8 9.1 %collective-permute-start.17 = (f32[32,16,128]{2,1,0:T(8,128)S(1)}, f32[32,16,128]{2,1,0:T(8,128)S(1)}, u32[]{:S(2)}, u32[]{:S(2)}) collective-permute-start(f32[32,16,128]{2,1,0:T(8,128)S(1)} %get-tuple-element.40), channel_id=1, source_target_pairs={{0,64},{64,0},{1,65},{65,1},{128,192},{192,128},{129,193},{193,129... | collective-permute-start | bytes 786440 | tf_op jit(solution)/shard_map/ppermute | solution.py:75
  134.0 13.1 %collective-permute-start.18 = (f32[16,16,128]{2,1,0:T(8,128)S(1)}, f32[16,16,128]{2,1,0:T(8,128)S(1)}, u32[]{:S(2)}, u32[]{:S(2)}) collective-permute-start(f32[16,16,128]{2,1,0:T(8,128)S(1)} %get-tuple-element.47), channel_id=1, source_target_pairs={{0,256},{1,257},{2,258},{3,259},{4,260},{5,261},{6,262},{7,263},{8... | collective-permute-start | bytes 393224 | tf_op jit(solution)/shard_map/ppermute | solution.py:75
  147.1 7.3 %collective-permute-start.19 = (f32[8,16,128]{2,1,0:T(8,128)S(1)}, f32[8,16,128]{2,1,0:T(8,128)S(1)}, u32[]{:S(2)}, u32[]{:S(2)}) collective-permute-start(f32[8,16,128]{2,1,0:T(8,128)S(1)} %get-tuple-element.48), channel_id=1, source_target_pairs={{0,0},{128,1},{64,64},{192,65},{1,128},{129,129},{65,192},{193,193... | collective-permute-start | bytes 196616 | tf_op jit(solution)/shard_map/ppermute | solution.py:75
  150.7 6.8 %collective-permute-start.20 = (f32[8,16,128]{2,1,0:T(8,128)S(1)}, f32[8,16,128]{2,1,0:T(8,128)S(1)}, u32[]{:S(2)}, u32[]{:S(2)}) collective-permute-start(f32[8,16,128]{2,1,0:T(8,128)S(1)} %get-tuple-element.49), channel_id=1, source_target_pairs={{64,0},{192,1},{0,64},{128,65},{65,128},{193,129},{1,192},{129,193... | collective-permute-start | bytes 196616 | tf_op jit(solution)/shard_map/ppermute | solution.py:75

commit v16 on v14

--- a/solution.py
+++ b/solution.py
@@ -195,7 +195,7 @@
             own_part[:, start : start + SLAB] + other_part[:, start : start + SLAB]
             for start in range(0, 3 * SLAB, SLAB)
         )
-        terms = [kept, send(to_odd, ODD), send(to_even, EVEN)]
+        terms = [kept, send(to_even, EVEN), send(to_odd, ODD)]
         part = sum(terms)
         if iteration == 0:
             scale = scale_of(*lax.optimization_barrier((psf_taps, intersection, part))[:2])

time: 154 us -> 154 us (level)
  starting transfers between devices: 77 us -> 74.3 us
    ppermute x21, starting transfers between devices: 77 us -> 74.3 us  [send(): return lax.ppermute(value, AXES, pairs)]
where the time goes in v16:
time: 154 us; the launch traced here: 152 us
  starting transfers between devices  74.3 us (48%)
  waiting for transfers between devices  57.9 us (38%)
  matrix products  14.2 us (9%)
  local copies, waits for them, and re-layouts  3.05 us (2%)
    ppermute x21, starting transfers between devices, send(): return lax.ppermute(value, AXES, pairs)  74.3 us
    ppermute x21, waiting for transfers between devices, send(): return lax.ppermute(value, AXES, pairs)  57.9 us
  transfers between devices with their start and end apart: 21, of which 15 were waited for; matrix products, arithmetic and copies ran while one was open for 6% of the time, Pallas kernels for 0%

profile of v16, /device:TPU:57, one launch (start us, length us, event | category | flops | bytes accessed | tf_op | source)
XLA Modules:
  0.0 151.5 jit_solution(2050409858436171111)
XLA Ops:
  0.0 0.9 constant_dynamic-slice_fusion.1
  0.9 5.2 %collective-permute-start = (f32[8,16,128]{2,1,0:T(8,128)S(1)}, f32[8,16,128]{2,1,0:T(8,128)S(1)}, u32[]{:S(2)}, u32[]{:S(2)}) collective-permute-start(f32[8,16,128]{2,1,0:T(8,128)S(1)} %bitcast.155), channel_id=1, source_target_pairs={{0,0},{1,128},{64,64},{65,192},{128,1},{129,129},{192,65},{193,193... | collective-permute-start | bytes 196616 | tf_op jit(solution)/shard_map/ppermute | solution.py:75
  6.2 2.5 %collective-permute-start.1 = (f32[8,16,128]{2,1,0:T(8,128)S(1)}, f32[8,16,128]{2,1,0:T(8,128)S(1)}, u32[]{:S(2)}, u32[]{:S(2)}) collective-permute-start(f32[8,16,128]{2,1,0:T(8,128)S(1)} %bitcast.156), channel_id=1, source_target_pairs={{0,64},{1,192},{64,0},{65,128},{128,65},{129,193},{192,1},{193,129... | collective-permute-start | bytes 196616 | tf_op jit(solution)/shard_map/ppermute | solution.py:75
  8.6 1.3 dynamic-slice_bitcast_fusion
  9.9 3.7 %collective-permute-start.5 = (f32[16,64,128]{2,1,0:T(8,128)S(1)}, f32[16,64,128]{2,1,0:T(8,128)S(1)}, u32[]{:S(2)}, u32[]{:S(2)}) collective-permute-start(f32[16,64,128]{2,1,0:T(8,128)S(1)} %get-tuple-element.43), channel_id=1, source_target_pairs={{0,0},{1,128},{64,64},{65,192},{128,1},{129,129},{192,65},{193,193... | collective-permute-start | bytes 1572872 | tf_op jit(solution)/shard_map/ppermute | solution.py:75
  14.1 10.6 %collective-permute-start.2 = (f32[16,16,128]{2,1,0:T(8,128)S(1)}, f32[16,16,128]{2,1,0:T(8,128)S(1)}, u32[]{:S(2)}, u32[]{:S(2)}) collective-permute-start(f32[16,16,128]{2,1,0:T(8,128)S(1)} %maximum_select_fusion.2), channel_id=1, source_target_pairs={{0,256},{1,257},{2,258},{3,259},{4,260},{5,261},{6,262},{7,263},{8... | collective-permute-start | bytes 393224 | tf_op jit(solution)/shard_map/ppermute | solution.py:75
  24.9 2.8 %collective-permute-start.6 = (f32[16,64,128]{2,1,0:T(8,128)S(1)}, f32[16,64,128]{2,1,0:T(8,128)S(1)}, u32[]{:S(2)}, u32[]{:S(2)}) collective-permute-start(f32[16,64,128]{2,1,0:T(8,128)S(1)} %get-tuple-element.23), channel_id=1, source_target_pairs={{0,64},{1,192},{64,0},{65,128},{128,65},{129,193},{192,1},{193,129... | collective-permute-start | bytes 1572872 | tf_op jit(solution)/shard_map/ppermute | solution.py:75
  27.7 8.4 %collective-permute-start.3 = (f32[32,16,128]{2,1,0:T(8,128)S(1)}, f32[32,16,128]{2,1,0:T(8,128)S(1)}, u32[]{:S(2)}, u32[]{:S(2)}) collective-permute-start(f32[32,16,128]{2,1,0:T(8,128)S(1)} %maximum_select_fusion.1), channel_id=1, source_target_pairs={{64,128},{128,64},{65,129},{129,65},{192,194},{194,192},{193,195},... | collective-permute-start | bytes 786440 | tf_op jit(solution)/shard_map/ppermute | solution.py:75
  36.1 1.9 %collective-permute-start.4 = (f32[32,16,128]{2,1,0:T(8,128)S(1)}, f32[32,16,128]{2,1,0:T(8,128)S(1)}, u32[]{:S(2)}, u32[]{:S(2)}) collective-permute-start(f32[32,16,128]{2,1,0:T(8,128)S(1)} %maximum_select_fusion.1), channel_id=1, source_target_pairs={{0,64},{64,0},{1,65},{65,1},{128,192},{192,128},{129,193},{193,129... | collective-permute-start | bytes 786440 | tf_op jit(solution)/shard_map/ppermute | solution.py:75
  38.2 0.2 fusion.75
  38.4 0.4 fusion.18
  38.8 0.8 fusion
  39.6 0.2 fusion.31
  40.2 2.0 %collective-permute-done.3 = f32[32,16,128]{2,1,0:T(8,128)S(1)} collective-permute-done((f32[32,16,128]{2,1,0:T(8,128)S(1)}, f32[32,16,128]{2,1,0:T(8,128)S(1)}, u32[]{:S(2)}, u32[]{:S(2)}) %collective-permute-start.3) | collective-permute-done | bytes 262176 | tf_op jit(solution)/shard_map/ppermute | solution.py:75
  42.2 4.0 %collective-permute-done.4 = f32[32,16,128]{2,1,0:T(8,128)S(1)} collective-permute-done((f32[32,16,128]{2,1,0:T(8,128)S(1)}, f32[32,16,128]{2,1,0:T(8,128)S(1)}, u32[]{:S(2)}, u32[]{:S(2)}) %collective-permute-start.4) | collective-permute-done | bytes 262176 | tf_op jit(solution)/shard_map/ppermute | solution.py:75
  46.3 2.4 %collective-permute-start.7 = (f32[32,48,128]{2,1,0:T(8,128)S(1)}, f32[32,48,128]{2,1,0:T(8,128)S(1)}, u32[]{:S(2)}, u32[]{:S(2)}) collective-permute-start(f32[32,48,128]{2,1,0:T(8,128)S(1)} %pad_maximum_fusion), channel_id=1, source_target_pairs={{0,1},{1,0},{2,3},{3,2},{4,5},{5,4},{6,7},{7,6},{8,9},{9,8},{10,11... | collective-permute-start | bytes 2359304 | tf_op jit(solution)/shard_map/ppermute | solution.py:75
  48.9 1.7 %collective-permute-done.7 = f32[32,48,128]{2,1,0:T(8,128)S(1)} collective-permute-done((f32[32,48,128]{2,1,0:T(8,128)S(1)}, f32[32,48,128]{2,1,0:T(8,128)S(1)}, u32[]{:S(2)}, u32[]{:S(2)}) %collective-permute-start.7) | collective-permute-done | bytes 786464 | tf_op jit(solution)/shard_map/ppermute | solution.py:75
  50.6 0.6 fusion.1
  51.2 0.9 convolution_bitcast_fusion.1
  52.1 0.6 fusion.11
  52.7 0.6 fusion.37
  53.3 0.4 fusion.44
  53.7 0.8 convolution_bitcast_fusion.4
  54.5 2.3 %collective-permute-start.8 = (f32[32,48,128]{2,1,0:T(8,128)S(1)}, f32[32,48,128]{2,1,0:T(8,128)S(1)}, u32[]{:S(2)}, u32[]{:S(2)}) collective-permute-start(f32[32,48,128]{2,1,0:T(8,128)S(1)} %convolution_bitcast_fusion.4), channel_id=1, source_target_pairs={{0,1},{1,0},{2,3},{3,2},{4,5},{5,4},{6,7},{7,6},{8,9},{9,8},{10,11... | collective-permute-start | bytes 2359304 | tf_op jit(solution)/shard_map/ppermute | solution.py:75
  56.8 0.4 fusion.50
  57.2 0.8 convolution_bitcast_fusion.5
  58.0 0.7 collective-permute-done.8
  58.8 3.1 %collective-permute-start.10 = (f32[32,16,128]{2,1,0:T(8,128)S(1)}, f32[32,16,128]{2,1,0:T(8,128)S(1)}, u32[]{:S(2)}, u32[]{:S(2)}) collective-permute-start(f32[32,16,128]{2,1,0:T(8,128)S(1)} %get-tuple-element.41), channel_id=1, source_target_pairs={{64,128},{128,64},{65,129},{129,65},{192,194},{194,192},{193,195},... | collective-permute-start | bytes 786440 | tf_op jit(solution)/shard_map/ppermute | solution.py:75
  61.9 1.9 %collective-permute-start.9 = (f32[32,16,128]{2,1,0:T(8,128)S(1)}, f32[32,16,128]{2,1,0:T(8,128)S(1)}, u32[]{:S(2)}, u32[]{:S(2)}) collective-permute-start(f32[32,16,128]{2,1,0:T(8,128)S(1)} %get-tuple-element.40), channel_id=1, source_target_pairs={{0,64},{64,0},{1,65},{65,1},{128,192},{192,128},{129,193},{193,129... | collective-permute-start | bytes 786440 | tf_op jit(solution)/shard_map/ppermute | solution.py:75
  63.8 6.4 %collective-permute-done.10 = f32[32,16,128]{2,1,0:T(8,128)S(1)} collective-permute-done((f32[32,16,128]{2,1,0:T(8,128)S(1)}, f32[32,16,128]{2,1,0:T(8,128)S(1)}, u32[]{:S(2)}, u32[]{:S(2)}) %collective-permute-start.10) | collective-permute-done | bytes 262176 | tf_op jit(solution)/shard_map/ppermute | solution.py:75
  70.3 0.7 collective-permute-done.9
  71.1 2.9 %collective-permute-start.11 = (f32[32,16,128]{2,1,0:T(8,128)S(1)}, f32[32,16,128]{2,1,0:T(8,128)S(1)}, u32[]{:S(2)}, u32[]{:S(2)}) collective-permute-start(f32[32,16,128]{2,1,0:T(8,128)S(1)} %fusion.30), channel_id=1, source_target_pairs={{0,256},{1,257},{2,258},{3,259},{4,260},{5,261},{6,262},{7,263},{8... | collective-permute-start | bytes 786440 | tf_op jit(solution)/shard_map/ppermute | solution.py:75
  74.1 0.2 fusion.73
  74.3 0.7 fusion.28
  75.1 0.2 fusion.84
  75.3 0.3 fusion.52
  75.7 0.8 fusion.13
  76.4 13.8 %collective-permute-done.11 = f32[32,16,128]{2,1,0:T(8,128)S(1)} collective-permute-done((f32[32,16,128]{2,1,0:T(8,128)S(1)}, f32[32,16,128]{2,1,0:T(8,128)S(1)}, u32[]{:S(2)}, u32[]{:S(2)}) %collective-permute-start.11) | collective-permute-done | bytes 262176 | tf_op jit(solution)/shard_map/ppermute | solution.py:75
  90.3 1.9 %collective-permute-start.12 = (f32[32,16,128]{2,1,0:T(8,128)S(1)}, f32[32,16,128]{2,1,0:T(8,128)S(1)}, u32[]{:S(2)}, u32[]{:S(2)}) collective-permute-start(f32[32,16,128]{2,1,0:T(8,128)S(1)} %multiply_multiply_fusion), channel_id=1, source_target_pairs={{64,128},{128,64},{65,129},{129,65},{192,194},{194,192},{193,195},... | collective-permute-start | bytes 786440 | tf_op jit(solution)/shard_map/ppermute | solution.py:75
  92.2 1.9 %collective-permute-start.13 = (f32[32,16,128]{2,1,0:T(8,128)S(1)}, f32[32,16,128]{2,1,0:T(8,128)S(1)}, u32[]{:S(2)}, u32[]{:S(2)}) collective-permute-start(f32[32,16,128]{2,1,0:T(8,128)S(1)} %multiply_multiply_fusion), channel_id=1, source_target_pairs={{0,64},{64,0},{1,65},{65,1},{128,192},{192,128},{129,193},{193,129... | collective-permute-start | bytes 786440 | tf_op jit(solution)/shard_map/ppermute | solution.py:75
  94.1 7.5 %collective-permute-done.12 = f32[32,16,128]{2,1,0:T(8,128)S(1)} collective-permute-done((f32[32,16,128]{2,1,0:T(8,128)S(1)}, f32[32,16,128]{2,1,0:T(8,128)S(1)}, u32[]{:S(2)}, u32[]{:S(2)}) %collective-permute-start.12) | collective-permute-done | bytes 262176 | tf_op jit(solution)/shard_map/ppermute | solution.py:75
  101.7 3.7 %collective-permute-start.14 = (f32[32,48,128]{2,1,0:T(8,128)S(1)}, f32[32,48,128]{2,1,0:T(8,128)S(1)}, u32[]{:S(2)}, u32[]{:S(2)}) collective-permute-start(f32[32,48,128]{2,1,0:T(8,128)S(1)} %pad_maximum_fusion.1), channel_id=1, source_target_pairs={{0,1},{1,0},{2,3},{3,2},{4,5},{5,4},{6,7},{7,6},{8,9},{9,8},{10,11... | collective-permute-start | bytes 2359304 | tf_op jit(solution)/shard_map/ppermute | solution.py:75
  105.5 1.7 %collective-permute-done.14 = f32[32,48,128]{2,1,0:T(8,128)S(1)} collective-permute-done((f32[32,48,128]{2,1,0:T(8,128)S(1)}, f32[32,48,128]{2,1,0:T(8,128)S(1)}, u32[]{:S(2)}, u32[]{:S(2)}) %collective-permute-start.14) | collective-permute-done | bytes 786464 | tf_op jit(solution)/shard_map/ppermute | solution.py:75
  107.2 0.6 fusion.4
  107.7 0.9 convolution_bitcast_fusion
  108.6 0.6 fusion.12
  109.2 0.6 fusion.34
  109.8 0.4 fusion.42
  110.3 0.8 convolution_bitcast_fusion.2
  111.0 2.3 %collective-permute-start.15 = (f32[32,48,128]{2,1,0:T(8,128)S(1)}, f32[32,48,128]{2,1,0:T(8,128)S(1)}, u32[]{:S(2)}, u32[]{:S(2)}) collective-permute-start(f32[32,48,128]{2,1,0:T(8,128)S(1)} %convolution_bitcast_fusion.2), channel_id=1, source_target_pairs={{0,1},{1,0},{2,3},{3,2},{4,5},{5,4},{6,7},{7,6},{8,9},{9,8},{10,11... | collective-permute-start | bytes 2359304 | tf_op jit(solution)/shard_map/ppermute | solution.py:75
  113.3 0.4 fusion.48
  113.8 0.8 convolution_bitcast_fusion.3
  114.5 0.7 collective-permute-done.15
  115.3 1.9 %collective-permute-start.16 = (f32[32,16,128]{2,1,0:T(8,128)S(1)}, f32[32,16,128]{2,1,0:T(8,128)S(1)}, u32[]{:S(2)}, u32[]{:S(2)}) collective-permute-start(f32[32,16,128]{2,1,0:T(8,128)S(1)} %get-tuple-element.39), channel_id=1, source_target_pairs={{0,64},{64,0},{1,65},{65,1},{128,192},{192,128},{129,193},{193,129... | collective-permute-start | bytes 786440 | tf_op jit(solution)/shard_map/ppermute | solution.py:75
  117.3 6.2 %collective-permute-start.17 = (f32[32,16,128]{2,1,0:T(8,128)S(1)}, f32[32,16,128]{2,1,0:T(8,128)S(1)}, u32[]{:S(2)}, u32[]{:S(2)}) collective-permute-start(f32[32,16,128]{2,1,0:T(8,128)S(1)} %get-tuple-element.38), channel_id=1, source_target_pairs={{64,128},{128,64},{65,129},{129,65},{192,194},{194,192},{193,195},... | collective-permute-start | bytes 786440 | tf_op jit(solution)/shard_map/ppermute | solution.py:75
  123.5 1.3 collective-permute-done.16
  124.8 4.7 %collective-permute-done.17 = f32[32,16,128]{2,1,0:T(8,128)S(1)} collective-permute-done((f32[32,16,128]{2,1,0:T(8,128)S(1)}, f32[32,16,128]{2,1,0:T(8,128)S(1)}, u32[]{:S(2)}, u32[]{:S(2)}) %collective-permute-start.17) | collective-permute-done | bytes 262176 | tf_op jit(solution)/shard_map/ppermute | solution.py:75
  129.5 2.7 %collective-permute-start.18 = (f32[16,16,128]{2,1,0:T(8,128)S(1)}, f32[16,16,128]{2,1,0:T(8,128)S(1)}, u32[]{:S(2)}, u32[]{:S(2)}) collective-permute-start(f32[16,16,128]{2,1,0:T(8,128)S(1)} %get-tuple-element.45), channel_id=1, source_target_pairs={{0,256},{1,257},{2,258},{3,259},{4,260},{5,261},{6,262},{7,263},{8... | collective-permute-start | bytes 393224 | tf_op jit(solution)/shard_map/ppermute | solution.py:75
  132.3 9.7 %collective-permute-done.18 = f32[16,16,128]{2,1,0:T(8,128)S(1)} collective-permute-done((f32[16,16,128]{2,1,0:T(8,128)S(1)}, f32[16,16,128]{2,1,0:T(8,128)S(1)}, u32[]{:S(2)}, u32[]{:S(2)}) %collective-permute-start.18) | collective-permute-done | bytes 131104 | tf_op jit(solution)/shard_map/ppermute | solution.py:75
  142.0 1.9 %collective-permute-start.19 = (f32[8,16,128]{2,1,0:T(8,128)S(1)}, f32[8,16,128]{2,1,0:T(8,128)S(1)}, u32[]{:S(2)}, u32[]{:S(2)}) collective-permute-start(f32[8,16,128]{2,1,0:T(8,128)S(1)} %get-tuple-element.46), channel_id=1, source_target_pairs={{0,0},{128,1},{64,64},{192,65},{1,128},{129,129},{65,192},{193,193... | collective-permute-start | bytes 196616 | tf_op jit(solution)/shard_map/ppermute | solution.py:75
  144.0 3.9 %collective-permute-start.20 = (f32[8,16,128]{2,1,0:T(8,128)S(1)}, f32[8,16,128]{2,1,0:T(8,128)S(1)}, u32[]{:S(2)}, u32[]{:S(2)}) collective-permute-start(f32[8,16,128]{2,1,0:T(8,128)S(1)} %get-tuple-element.47), channel_id=1, source_target_pairs={{64,0},{192,1},{0,64},{128,65},{65,128},{193,129},{1,192},{129,193... | collective-permute-start | bytes 196616 | tf_op jit(solution)/shard_map/ppermute | solution.py:75
  147.9 1.2 collective-permute-done.19
  149.1 1.6 %collective-permute-done.20 = f32[8,16,128]{2,1,0:T(8,128)S(1)} collective-permute-done((f32[8,16,128]{2,1,0:T(8,128)S(1)}, f32[8,16,128]{2,1,0:T(8,128)S(1)}, u32[]{:S(2)}, u32[]{:S(2)}) %collective-permute-start.20) | collective-permute-done | bytes 65568 | tf_op jit(solution)/shard_map/ppermute | solution.py:75
  150.8 0.7 copy.12
  (47 shorter events, 1.9 us)
Async XLA Ops:
  0.9 13.2 %collective-permute-start = (f32[8,16,128]{2,1,0:T(8,128)S(1)}, f32[8,16,128]{2,1,0:T(8,128)S(1)}, u32[]{:S(2)}, u32[]{:S(2)}) collective-permute-start(f32[8,16,128]{2,1,0:T(8,128)S(1)} %bitcast.155), channel_id=1, source_target_pairs={{0,0},{1,128},{64,64},{65,192},{128,1},{129,129},{192,65},{193,193... | collective-permute-start | bytes 196616 | tf_op jit(solution)/shard_map/ppermute | solution.py:75
  6.2 8.0 %collective-permute-start.1 = (f32[8,16,128]{2,1,0:T(8,128)S(1)}, f32[8,16,128]{2,1,0:T(8,128)S(1)}, u32[]{:S(2)}, u32[]{:S(2)}) collective-permute-start(f32[8,16,128]{2,1,0:T(8,128)S(1)} %bitcast.156), channel_id=1, source_target_pairs={{0,64},{1,192},{64,0},{65,128},{128,65},{129,193},{192,1},{193,129... | collective-permute-start | bytes 196616 | tf_op jit(solution)/shard_map/ppermute | solution.py:75
  9.9 28.1 %copy-start = (f32[8,3,31]{2,0,1:T(8,128)S(1)}, f32[8,3,31]{2,0,1:T(8,128)}, u32[]{:S(2)}) copy-start(f32[8,3,31]{2,0,1:T(8,128)} %param.6) | copy-start | bytes 8932
  9.9 29.8 %copy-start.1 = (s32[8,16]{1,0:T(8,128)S(1)}, s32[8,16]{1,0:T(8,128)}, u32[]{:S(2)}) copy-start(s32[8,16]{1,0:T(8,128)} %param.7) | copy-start | bytes 1540
  9.9 36.4 %collective-permute-start.5 = (f32[16,64,128]{2,1,0:T(8,128)S(1)}, f32[16,64,128]{2,1,0:T(8,128)S(1)}, u32[]{:S(2)}, u32[]{:S(2)}) collective-permute-start(f32[16,64,128]{2,1,0:T(8,128)S(1)} %get-tuple-element.43), channel_id=1, source_target_pairs={{0,0},{1,128},{64,64},{65,192},{128,1},{129,129},{192,65},{193,193... | collective-permute-start | bytes 1572872 | tf_op jit(solution)/shard_map/ppermute | solution.py:75
  14.1 13.6 %collective-permute-start.2 = (f32[16,16,128]{2,1,0:T(8,128)S(1)}, f32[16,16,128]{2,1,0:T(8,128)S(1)}, u32[]{:S(2)}, u32[]{:S(2)}) collective-permute-start(f32[16,16,128]{2,1,0:T(8,128)S(1)} %maximum_select_fusion.2), channel_id=1, source_target_pairs={{0,256},{1,257},{2,258},{3,259},{4,260},{5,261},{6,262},{7,263},{8... | collective-permute-start | bytes 393224 | tf_op jit(solution)/shard_map/ppermute | solution.py:75
  24.9 21.4 %collective-permute-start.6 = (f32[16,64,128]{2,1,0:T(8,128)S(1)}, f32[16,64,128]{2,1,0:T(8,128)S(1)}, u32[]{:S(2)}, u32[]{:S(2)}) collective-permute-start(f32[16,64,128]{2,1,0:T(8,128)S(1)} %get-tuple-element.23), channel_id=1, source_target_pairs={{0,64},{1,192},{64,0},{65,128},{128,65},{129,193},{192,1},{193,129... | collective-permute-start | bytes 1572872 | tf_op jit(solution)/shard_map/ppermute | solution.py:75
  27.7 14.5 %collective-permute-start.3 = (f32[32,16,128]{2,1,0:T(8,128)S(1)}, f32[32,16,128]{2,1,0:T(8,128)S(1)}, u32[]{:S(2)}, u32[]{:S(2)}) collective-permute-start(f32[32,16,128]{2,1,0:T(8,128)S(1)} %maximum_select_fusion.1), channel_id=1, source_target_pairs={{64,128},{128,64},{65,129},{129,65},{192,194},{194,192},{193,195},... | collective-permute-start | bytes 786440 | tf_op jit(solution)/shard_map/ppermute | solution.py:75
  36.1 10.1 %collective-permute-start.4 = (f32[32,16,128]{2,1,0:T(8,128)S(1)}, f32[32,16,128]{2,1,0:T(8,128)S(1)}, u32[]{:S(2)}, u32[]{:S(2)}) collective-permute-start(f32[32,16,128]{2,1,0:T(8,128)S(1)} %maximum_select_fusion.1), channel_id=1, source_target_pairs={{0,64},{64,0},{1,65},{65,1},{128,192},{192,128},{129,193},{193,129... | collective-permute-start | bytes 786440 | tf_op jit(solution)/shard_map/ppermute | solution.py:75
  46.3 4.3 %collective-permute-start.7 = (f32[32,48,128]{2,1,0:T(8,128)S(1)}, f32[32,48,128]{2,1,0:T(8,128)S(1)}, u32[]{:S(2)}, u32[]{:S(2)}) collective-permute-start(f32[32,48,128]{2,1,0:T(8,128)S(1)} %pad_maximum_fusion), channel_id=1, source_target_pairs={{0,1},{1,0},{2,3},{3,2},{4,5},{5,4},{6,7},{7,6},{8,9},{9,8},{10,11... | collective-permute-start | bytes 2359304 | tf_op jit(solution)/shard_map/ppermute | solution.py:75
  54.5 4.2 %collective-permute-start.8 = (f32[32,48,128]{2,1,0:T(8,128)S(1)}, f32[32,48,128]{2,1,0:T(8,128)S(1)}, u32[]{:S(2)}, u32[]{:S(2)}) collective-permute-start(f32[32,48,128]{2,1,0:T(8,128)S(1)} %convolution_bitcast_fusion.4), channel_id=1, source_target_pairs={{0,1},{1,0},{2,3},{3,2},{4,5},{5,4},{6,7},{7,6},{8,9},{9,8},{10,11... | collective-permute-start | bytes 2359304 | tf_op jit(solution)/shard_map/ppermute | solution.py:75
  58.8 11.5 %collective-permute-start.10 = (f32[32,16,128]{2,1,0:T(8,128)S(1)}, f32[32,16,128]{2,1,0:T(8,128)S(1)}, u32[]{:S(2)}, u32[]{:S(2)}) collective-permute-start(f32[32,16,128]{2,1,0:T(8,128)S(1)} %get-tuple-element.41), channel_id=1, source_target_pairs={{64,128},{128,64},{65,129},{129,65},{192,194},{194,192},{193,195},... | collective-permute-start | bytes 786440 | tf_op jit(solution)/shard_map/ppermute | solution.py:75
  61.9 9.1 %collective-permute-start.9 = (f32[32,16,128]{2,1,0:T(8,128)S(1)}, f32[32,16,128]{2,1,0:T(8,128)S(1)}, u32[]{:S(2)}, u32[]{:S(2)}) collective-permute-start(f32[32,16,128]{2,1,0:T(8,128)S(1)} %get-tuple-element.40), channel_id=1, source_target_pairs={{0,64},{64,0},{1,65},{65,1},{128,192},{192,128},{129,193},{193,129... | collective-permute-start | bytes 786440 | tf_op jit(solution)/shard_map/ppermute | solution.py:75
  71.1 19.1 %collective-permute-start.11 = (f32[32,16,128]{2,1,0:T(8,128)S(1)}, f32[32,16,128]{2,1,0:T(8,128)S(1)}, u32[]{:S(2)}, u32[]{:S(2)}) collective-permute-start(f32[32,16,128]{2,1,0:T(8,128)S(1)} %fusion.30), channel_id=1, source_target_pairs={{0,256},{1,257},{2,258},{3,259},{4,260},{5,261},{6,262},{7,263},{8... | collective-permute-start | bytes 786440 | tf_op jit(solution)/shard_map/ppermute | solution.py:75
  90.3 11.4 %collective-permute-start.12 = (f32[32,16,128]{2,1,0:T(8,128)S(1)}, f32[32,16,128]{2,1,0:T(8,128)S(1)}, u32[]{:S(2)}, u32[]{:S(2)}) collective-permute-start(f32[32,16,128]{2,1,0:T(8,128)S(1)} %multiply_multiply_fusion), channel_id=1, source_target_pairs={{64,128},{128,64},{65,129},{129,65},{192,194},{194,192},{193,195},... | collective-permute-start | bytes 786440 | tf_op jit(solution)/shard_map/ppermute | solution.py:75
  92.2 9.5 %collective-permute-start.13 = (f32[32,16,128]{2,1,0:T(8,128)S(1)}, f32[32,16,128]{2,1,0:T(8,128)S(1)}, u32[]{:S(2)}, u32[]{:S(2)}) collective-permute-start(f32[32,16,128]{2,1,0:T(8,128)S(1)} %multiply_multiply_fusion), channel_id=1, source_target_pairs={{0,64},{64,0},{1,65},{65,1},{128,192},{192,128},{129,193},{193,129... | collective-permute-start | bytes 786440 | tf_op jit(solution)/shard_map/ppermute | solution.py:75
  101.7 5.5 %collective-permute-start.14 = (f32[32,48,128]{2,1,0:T(8,128)S(1)}, f32[32,48,128]{2,1,0:T(8,128)S(1)}, u32[]{:S(2)}, u32[]{:S(2)}) collective-permute-start(f32[32,48,128]{2,1,0:T(8,128)S(1)} %pad_maximum_fusion.1), channel_id=1, source_target_pairs={{0,1},{1,0},{2,3},{3,2},{4,5},{5,4},{6,7},{7,6},{8,9},{9,8},{10,11... | collective-permute-start | bytes 2359304 | tf_op jit(solution)/shard_map/ppermute | solution.py:75
  111.0 4.2 %collective-permute-start.15 = (f32[32,48,128]{2,1,0:T(8,128)S(1)}, f32[32,48,128]{2,1,0:T(8,128)S(1)}, u32[]{:S(2)}, u32[]{:S(2)}) collective-permute-start(f32[32,48,128]{2,1,0:T(8,128)S(1)} %convolution_bitcast_fusion.2), channel_id=1, source_target_pairs={{0,1},{1,0},{2,3},{3,2},{4,5},{5,4},{6,7},{7,6},{8,9},{9,8},{10,11... | collective-permute-start | bytes 2359304 | tf_op jit(solution)/shard_map/ppermute | solution.py:75
  115.3 9.4 %collective-permute-start.16 = (f32[32,16,128]{2,1,0:T(8,128)S(1)}, f32[32,16,128]{2,1,0:T(8,128)S(1)}, u32[]{:S(2)}, u32[]{:S(2)}) collective-permute-start(f32[32,16,128]{2,1,0:T(8,128)S(1)} %get-tuple-element.39), channel_id=1, source_target_pairs={{0,64},{64,0},{1,65},{65,1},{128,192},{192,128},{129,193},{193,129... | collective-permute-start | bytes 786440 | tf_op jit(solution)/shard_map/ppermute | solution.py:75
  117.3 12.2 %collective-permute-start.17 = (f32[32,16,128]{2,1,0:T(8,128)S(1)}, f32[32,16,128]{2,1,0:T(8,128)S(1)}, u32[]{:S(2)}, u32[]{:S(2)}) collective-permute-start(f32[32,16,128]{2,1,0:T(8,128)S(1)} %get-tuple-element.38), channel_id=1, source_target_pairs={{64,128},{128,64},{65,129},{129,65},{192,194},{194,192},{193,195},... | collective-permute-start | bytes 786440 | tf_op jit(solution)/shard_map/ppermute | solution.py:75
  129.5 12.4 %collective-permute-start.18 = (f32[16,16,128]{2,1,0:T(8,128)S(1)}, f32[16,16,128]{2,1,0:T(8,128)S(1)}, u32[]{:S(2)}, u32[]{:S(2)}) collective-permute-start(f32[16,16,128]{2,1,0:T(8,128)S(1)} %get-tuple-element.45), channel_id=1, source_target_pairs={{0,256},{1,257},{2,258},{3,259},{4,260},{5,261},{6,262},{7,263},{8... | collective-permute-start | bytes 393224 | tf_op jit(solution)/shard_map/ppermute | solution.py:75
  142.0 7.1 %collective-permute-start.19 = (f32[8,16,128]{2,1,0:T(8,128)S(1)}, f32[8,16,128]{2,1,0:T(8,128)S(1)}, u32[]{:S(2)}, u32[]{:S(2)}) collective-permute-start(f32[8,16,128]{2,1,0:T(8,128)S(1)} %get-tuple-element.46), channel_id=1, source_target_pairs={{0,0},{128,1},{64,64},{192,65},{1,128},{129,129},{65,192},{193,193... | collective-permute-start | bytes 196616 | tf_op jit(solution)/shard_map/ppermute | solution.py:75
  144.0 6.8 %collective-permute-start.20 = (f32[8,16,128]{2,1,0:T(8,128)S(1)}, f32[8,16,128]{2,1,0:T(8,128)S(1)}, u32[]{:S(2)}, u32[]{:S(2)}) collective-permute-start(f32[8,16,128]{2,1,0:T(8,128)S(1)} %get-tuple-element.47), channel_id=1, source_target_pairs={{64,0},{192,1},{0,64},{128,65},{65,128},{193,129},{1,192},{129,193... | collective-permute-start | bytes 196616 | tf_op jit(solution)/shard_map/ppermute | solution.py:75
